TPU v7x, 512 devices: a whole 4x8x8 slice. The times are simulated.
512 devices in a mesh: dp: 8 (over z_hi, core), tensor: 64 (over z_lo, y, x).
Axes of the slice: x: 4, y: 8, z: 8 (z_hi: 4, z_lo: 2; z = z_hi * 2 + z_lo), core: 2. Of those that a mesh axis runs over, the one named last changes fastest.
Arguments:
- tokens: bfloat16 [2048, 4096], P(('dp', 'tensor')), may hold values from -6 to 6
- cotangent: bfloat16 [2048, 4096], P(('dp', 'tensor')), may hold values from -3 to 3
- gate_weight: bfloat16 [4096, 16384], P(None, 'tensor'), may hold values from -0.09375 to 0.09375
- up_weight: bfloat16 [4096, 16384], P(None, 'tensor'), may hold values from -0.09375 to 0.09375
- down_weight: bfloat16 [16384, 4096], P('tensor', 'dp'), may hold values from -0.75 to 0.75
Outputs:
- input_grad: bfloat16 [2048, 4096], P(('dp', 'tensor'))
- down_grad: float32 [16384, 4096], P('tensor', 'dp')
All inputs are finite; a program needn't handle non-finite values.
Results may differ from a plain program's by a relative error of at most 0.015.
Values may be sent and summed in bfloat16 or wider, within the bound.
No kernel may reach another device: no remote copies, remote signals or barrier semaphores. Data moves between devices by JAX's collectives and lax.ppermute only.
A program may use at most 64 MiB of HBM per device.

v0:
```python
import jax
import jax.numpy as jnp
from jax import lax
from jax.sharding import PartitionSpec as P


def on_device(tokens, cotangent, gate_weight, up_weight, down_weight):
    input_piece = lax.all_gather(tokens, "tensor", axis=0, tiled=True)
    cot_piece = lax.all_gather(cotangent, "tensor", axis=0, tiled=True)
    gate_piece = jnp.dot(input_piece, gate_weight, preferred_element_type=jnp.float32)
    up_piece = jnp.dot(input_piece, up_weight, preferred_element_type=jnp.float32)
    d_hidden = lax.dot_general(
        cot_piece,
        lax.all_gather(down_weight, "dp", axis=1, tiled=True),
        (((1,), (1,)), ((), ())),
        preferred_element_type=jnp.float32,
    )
    sigma = jax.nn.sigmoid(gate_piece)
    silu_val = gate_piece * sigma
    hidden = (silu_val * up_piece).astype(jnp.bfloat16)
    d_up = (d_hidden * silu_val).astype(jnp.bfloat16)
    d_gate = (d_hidden * up_piece * sigma * (1.0 + gate_piece * (1.0 - sigma))).astype(jnp.bfloat16)
    term = lax.dot_general(
        d_gate, gate_weight, (((1,), (1,)), ((), ())), preferred_element_type=jnp.float32
    )
    input_grad = lax.psum_scatter(
        term
        + lax.dot_general(
            d_up, up_weight, (((1,), (1,)), ((), ())), preferred_element_type=jnp.float32
        ),
        "tensor",
        scatter_dimension=0,
        tiled=True,
    ).astype(jnp.bfloat16)
    partial_value = lax.dot_general(
        hidden, cot_piece, (((0,), (0,)), ((), ())), preferred_element_type=jnp.float32
    )
    down_grad = lax.psum_scatter(
        partial_value.astype(jnp.bfloat16), "dp", scatter_dimension=1, tiled=True
    ).astype(jnp.float32)
    return (input_grad, down_grad)


def solution(mesh):
    placed = (
        P(("dp", "tensor"), None),
        P(("dp", "tensor"), None),
        P(None, "tensor"),
        P(None, "tensor"),
        P("tensor", "dp"),
    )
    return jax.shard_map(
        on_device,
        mesh=mesh,
        in_specs=placed,
        out_specs=(P(("dp", "tensor"), None), P("tensor", "dp")),
        check_vma=False,
    )
```

profile of v0, /device:TPU:128, one launch (start us, length us, event | category | flops | bytes accessed | tf_op | source)
XLA Modules:
  0.0 1032.5 jit_solution(10270897696493263800)
XLA Ops:
  7.2 0.0 copy-start
  7.2 0.0 all-gather.10.cloned.1.call-start
  7.2 0.7 all-gather.10.cloned.1.call-update
  7.9 0.0 all-gather.8.cloned.1.call-start
  8.0 0.7 all-gather.8.cloned.1.call-update
  8.7 0.0 all-gather.6.cloned.1.call-start
  8.7 0.7 all-gather.6.cloned.1.call-update
  9.4 0.0 reduce-scatter.2.cloned.1.call-start
  9.4 1.3 dynamic-slice
  11.4 303.9 %all-gather.10.cloned.1.call-done = bf16[64,4,4096]{2,1,0:T(4,128)(2,1)} async-done(((bf16[1,4,4096]{2,1,0:T(4,128)(2,1)}), bf16[64,4,4096]{2,1,0:T(4,128)(2,1)}) %all-gather.10.cloned.1.call-update) | async-done | bytes 2097168 | tf_op jit(solution)/shard_map/all_gather | solution.py:8
  315.2 4.0 reshape.7
  319.3 297.9 %all-gather.8.cloned.1.call-done = bf16[64,4,4096]{2,1,0:T(4,128)(2,1)} async-done(((bf16[1,4,4096]{2,1,0:T(4,128)(2,1)}), bf16[64,4,4096]{2,1,0:T(4,128)(2,1)}) %all-gather.8.cloned.1.call-update) | async-done | bytes 2097168 | tf_op jit(solution)/shard_map/all_gather | solution.py:9
  617.1 4.0 reshape.5
  621.1 0.0 copy-done
  621.1 0.0 copy-start.2
  621.1 0.0 copy-start.3
  621.1 2.4 fusion.10
  623.5 0.0 copy-done.2
  623.6 0.4 copy-done.3
  623.9 0.0 copy-start.1
  623.9 0.7 fusion.9
  624.7 0.9 copy-done.1
  625.5 2.1 convolution_convert_fusion
  627.6 0.0 reduce-scatter.2.cloned.1.call-update
  627.7 27.9 %all-gather.6.cloned.1.call-done = bf16[256,4096]{1,0:T(8,128)(2,1)} async-done(((bf16[256,512]{1,0:T(8,128)(2,1)}), bf16[256,4096]{1,0:T(8,128)(2,1)}) %all-gather.6.cloned.1.call-update) | async-done | bytes 2097168 | tf_op jit(solution)/shard_map/all_gather | solution.py:14
  655.6 3.0 fusion.8
  658.5 0.0 copy-start.4
  658.6 0.8 fusion.1
  659.3 0.8 copy-done.4
  660.1 2.7 convolution_add_fusion
  662.9 359.9 %all-reduce.2 = bf16[256,4096]{1,0:T(8,128)(2,1)} all-reduce(f32[256,4096]{1,0:T(8,128)} %convolution_add_fusion), channel_id=2, replica_groups=mesh['dp'=8,'tensor'=64] {'tensor'}, use_global_device_ids=true, to_apply=%region_0.0.clone | all-reduce | flops 1048576 | bytes 6291456
  1022.7 1.5 dynamic-slice_convert_fusion
  1024.2 0.0 reduce-scatter.2.cloned.1.call-done
  1024.2 1.8 convert_element_type.23
Async XLA Ops:
  7.2 613.9 %copy-start = (bf16[4096,256]{1,0:T(8,128)(2,1)S(1)}, bf16[4096,256]{1,0:T(8,128)(2,1)}, u32[]{:S(2)}) copy-start(bf16[4096,256]{1,0:T(8,128)(2,1)} %param.7) | copy-start | bytes 6291460
  7.2 308.1 %all-gather.10.cloned.1.call-start = ((), (), s32[]{:S(2)}) async-start(), calls=%async_computation.4 | async-start | bytes 2129920 | tf_op jit(solution)/shard_map/all_gather | solution.py:8
  7.9 609.2 %all-gather.8.cloned.1.call-start = ((), (), s32[]{:S(2)}) async-start(), calls=%async_computation.3 | async-start | bytes 2129920 | tf_op jit(solution)/shard_map/all_gather | solution.py:9
  8.7 646.9 %all-gather.6.cloned.1.call-start = ((), (), s32[]{:S(2)}) async-start(), calls=%async_computation.1 | async-start | bytes 2359296 | tf_op jit(solution)/shard_map/all_gather | solution.py:14
  9.4 1014.8 %reduce-scatter.2.cloned.1.call-start = ((), (), s32[]{:S(2)}) async-start(), calls=%async_computation.2 | async-start | bytes 2359296 | tf_op jit(solution)/shard_map/reduce_scatter | solution.py:38
  621.1 2.5 copy-start.2
  621.1 2.9 copy-start.3
  623.9 1.6 copy-start.1
  658.5 1.6 copy-start.4
Sparse Core Ops, SparseCore 0:
  10.1 305.1 all-gather.9
  317.3 299.7 all-gather.7
  619.3 36.2 all-gather.5
  658.3 41.1 reduce-scatter.1
where the time goes:
time: 1030 us
  waiting for transfers between devices  632 us (61%)
  blocking collectives  360 us (35%)
  between operations  14.5 us (1%)
  local copies, waits for them, and re-layouts  12.8 us (1%)
  matrix products  11.7 us (1%)
    unnamed x1, blocking collectives  360 us
    all_gather x1, waiting for transfers between devices, on_device(): input_piece = lax.all_gather(tokens, 'tensor', axis=0, tiled=True)  304 us
    all_gather x1, waiting for transfers between devices, on_device(): cot_piece = lax.all_gather(cotangent, 'tensor', axis=0, tiled=True)  298 us
    all_gather x1, waiting for transfers between devices, on_device(): lax.all_gather(down_weight, 'dp', axis=1, tiled=True)  27.9 us
  transfers between devices with their start and end apart: 4, of which 3 were waited for; matrix products, arithmetic and copies ran while one was open for 2% of the time, Pallas kernels for 0%

commit v1 on v0

v1 whole, which is shorter than its diff:
```python
import jax
import jax.numpy as jnp
from jax import lax
from jax.sharding import PartitionSpec as P


def contract(a, b, ca, cb):
    return lax.dot_general(a, b, (((ca,), (cb,)), ((), ())), preferred_element_type=jnp.float32)


def on_device(tokens, cotangent, gate_weight, up_weight, down_weight):
    n = lax.axis_size("tensor")
    rows, d = tokens.shape
    down_rows = lax.all_gather(down_weight, "dp", axis=1, tiled=True)
    both = jnp.concatenate([tokens, cotangent], axis=0)
    sent = jnp.broadcast_to(both[None], (n, 2 * rows, d))
    got = lax.all_to_all(sent, "tensor", 0, 0)
    input_piece = got[:, :rows].reshape(n * rows, d)
    cot_piece = got[:, rows:].reshape(n * rows, d)
    gate_piece = contract(input_piece, gate_weight, 1, 0)
    up_piece = contract(input_piece, up_weight, 1, 0)
    sigma = jax.nn.sigmoid(gate_piece)
    silu_val = gate_piece * sigma
    hidden = (silu_val * up_piece).astype(jnp.bfloat16)
    partial_value = contract(hidden, cot_piece, 0, 0)
    down_grad = lax.psum_scatter(
        partial_value.astype(jnp.bfloat16), "dp", scatter_dimension=1, tiled=True
    ).astype(jnp.float32)
    d_hidden = contract(cot_piece, down_rows, 1, 1)
    d_up = (d_hidden * silu_val).astype(jnp.bfloat16)
    d_gate = (d_hidden * up_piece * sigma * (1.0 + gate_piece * (1.0 - sigma))).astype(jnp.bfloat16)
    term = contract(d_gate, gate_weight, 1, 1) + contract(d_up, up_weight, 1, 1)
    parts = lax.all_to_all(term.astype(jnp.bfloat16).reshape(n, rows, d), "tensor", 0, 0)
    input_grad = jnp.sum(parts.astype(jnp.float32), axis=0).astype(jnp.bfloat16)
    return (input_grad, down_grad)


def solution(mesh):
    placed = (
        P(("dp", "tensor"), None),
        P(("dp", "tensor"), None),
        P(None, "tensor"),
        P(None, "tensor"),
        P("tensor", "dp"),
    )
    return jax.shard_map(
        on_device,
        mesh=mesh,
        in_specs=placed,
        out_specs=(P(("dp", "tensor"), None), P("tensor", "dp")),
        check_vma=False,
    )
```

time: 1030 us -> 226 us (0.22)
  the two profiles are of different devices: /device:TPU:128 before, /device:TPU:1 now
where the time goes in v1:
time: 226 us; the launch traced here: 222 us
  waiting for transfers between devices  92.5 us (41%)
  blocking collectives  57.5 us (25%)
  local copies, waits for them, and re-layouts  22.9 us (10%)
  matrix products  15.9 us (7%)
  between operations  14.1 us (6%)
  starting transfers between devices  13.3 us (6%)
  other arithmetic  5.83 us (3%)
    all_to_all x1, waiting for transfers between devices, on_device(): got = lax.all_to_all(sent, 'tensor', 0, 0)  91.8 us
    all_to_all x1, blocking collectives, on_device(): lax.all_to_all(term.astype(jnp.bfloat16).reshape(n, rows, d), 'tensor', 0...  57.5 us
    dot_general x6, matrix products, contract(): lax.dot_general(a, b, (((ca,), (cb,)), ((), ())), preferred_element_type=...  15.9 us
    all_to_all x1, starting transfers between devices, on_device(): got = lax.all_to_all(sent, 'tensor', 0, 0)  13.2 us
    slice x1, local copies, waits for them, and re-layouts, on_device(): cot_piece = got[:, rows:].reshape(n * rows, d)  7.06 us
  transfers between devices with their start and end apart: 3, of which 1 were waited for; matrix products, arithmetic and copies ran while one was open for 15% of the time, Pallas kernels for 0%

profile of v1, /device:TPU:1, one launch (start us, length us, event | category | flops | bytes accessed | tf_op | source)
XLA Modules:
  0.0 221.9 jit_solution(420114902504590058)
XLA Ops:
  7.2 0.0 copy-start
  7.2 1.0 pad_maximum_fusion
  8.1 2.5 %broadcast_in_dim.2 = bf16[64,8,4096]{2,1,0:T(8,128)(2,1)} broadcast(bf16[8,4096]{1,0:T(8,128)(2,1)S(1)} %pad_maximum_fusion), dimensions={1,2} | broadcast | bytes 4259840 | tf_op jit(solution)/shard_map/broadcast_in_dim | solution.py:16
  10.6 13.2 %all-to-all-start = ((bf16[64,8,4096]{2,1,0:T(8,128)(2,1)}), bf16[64,8,4096]{2,1,0:T(8,128)(2,1)}, u32[]{:S(2)}, u32[]{:S(2)}) async-start(bf16[64,8,4096]{2,1,0:T(8,128)(2,1)} %broadcast_in_dim.2), calls=%async_computation | async-start | bytes 8388608 | tf_op jit(solution)/shard_map/all_to_all | solution.py:17
  23.8 0.0 all-gather.2.cloned.1.call-start
  23.9 0.7 all-gather.2.cloned.1.call-update
  24.6 0.0 reduce-scatter.2.cloned.1.call-start
  24.6 91.8 %all-to-all-done = bf16[64,8,4096]{2,1,0:T(8,128)(2,1)} async-done(((bf16[64,8,4096]{2,1,0:T(8,128)(2,1)}), bf16[64,8,4096]{2,1,0:T(8,128)(2,1)}, u32[]{:S(2)}, u32[]{:S(2)}) %all-to-all-start) | async-done | bytes 4194336 | tf_op jit(solution)/shard_map/all_to_all | solution.py:17
  116.4 7.1 %fusion.9 = (bf16[64,4,4096]{2,1,0:T(4,128)(2,1)}, bf16[64,4,4096]{2,1,0:T(4,128)(2,1)}) fusion(bf16[64,8,4096]{2,1,0:T(8,128)(2,1)} %all-to-all-done), kind=kLoop, calls=%fused_computation.14 | loop fusion | bytes 8388608 | tf_op jit(solution)/shard_map/slice | solution.py:19
  123.4 3.9 %reshape.15 = bf16[256,4096]{1,0:T(8,128)(2,1)} reshape(bf16[64,4,4096]{2,1,0:T(4,128)(2,1)} %get-tuple-element.3) | data formatting | bytes 4194304 | tf_op jit(solution)/shard_map/reshape | solution.py:18
  127.4 4.0 %reshape.14 = bf16[256,4096]{1,0:T(8,128)(2,1)} reshape(bf16[64,4,4096]{2,1,0:T(4,128)(2,1)} %get-tuple-element.2) | data formatting | bytes 4194304 | tf_op jit(solution)/shard_map/reshape | solution.py:19
  131.4 0.0 copy-done
  131.4 0.0 copy-start.2
  131.4 0.0 copy-start.3
  131.4 2.4 %fusion.12 = f32[256,256]{1,0:T(8,128)S(1)} fusion(bf16[256,4096]{1,0:T(8,128)(2,1)} %reshape.15, bf16[4096,256]{1,0:T(8,128)(2,1)S(1)} %copy-done), kind=kOutput, calls=%fused_computation.17 | convolution fusion | flops 536870912 | bytes 4456448 | tf_op jit(solution)/shard_map/dot_general | solution.py:8
  133.9 0.0 copy-done.2
  133.9 0.4 copy-done.3
  134.2 0.0 copy-start.1
  134.3 0.7 fusion.11
  135.0 0.9 copy-done.1
  135.8 2.1 convolution_convert_fusion
  137.9 0.0 all-gather.2.cloned.1.call-done
  137.9 3.0 %fusion.10 = f32[256,256]{1,0:T(8,128)S(1)} fusion(bf16[256,4096]{1,0:T(8,128)(2,1)} %reshape.14, bf16[256,4096]{1,0:T(8,128)(2,1)} %all-gather.2.cloned.1.call-done), kind=kOutput, calls=%fused_computation.15 | convolution fusion | flops 536870912 | bytes 4456448 | tf_op jit(solution)/shard_map/dot_general | solution.py:8
  140.9 2.7 %fusion.2 = f32[256,4096]{1,0:T(8,128)} fusion(bf16[4096,256]{1,0:T(8,128)(2,1)S(1)} %copy-done, f32[256,256]{1,0:T(8,128)S(1)} %fusion.12, f32[256,256]{1,0:T(8,128)S(1)} %fusion.10, f32[256,256]{1,0:T(8,128)S(1)} %fusion.11), kind=kOutput, calls=%fused_computation.8 | convolution fusion | flops 537526272 | bytes 7077888 | tf_op jit(solution)/shard_map/dot_general | solution.py:8
  143.6 0.0 reduce-scatter.2.cloned.1.call-update
  143.6 4.9 %fusion = bf16[256,4096]{1,0:T(8,128)(2,1)} fusion(f32[256,4096]{1,0:T(8,128)} %fusion.2, bf16[4096,256]{1,0:T(8,128)(2,1)} %param.8, f32[256,256]{1,0:T(8,128)S(1)} %fusion.10, f32[256,256]{1,0:T(8,128)S(1)} %fusion.12), kind=kOutput, calls=%fused_computation.1 | convolution fusion | flops 539361280 | bytes 8912896 | tf_op jit(solution)/shard_map/dot_general | solution.py:8
  148.6 4.1 %reshape.16 = bf16[64,4,4096]{2,1,0:T(4,128)(2,1)} reshape(bf16[256,4096]{1,0:T(8,128)(2,1)} %fusion) | data formatting | bytes 4194304 | tf_op jit(solution)/shard_map/reshape | solution.py:33
  152.7 57.5 %all_to_all.10 = bf16[64,4,4096]{2,1,0:T(4,128)(2,1)} all-to-all(bf16[64,4,4096]{2,1,0:T(4,128)(2,1)} %reshape.16), channel_id=1, replica_groups=mesh['dp'=8,'tensor'=64] {'tensor'}, dimensions={0} | all-to-all | bytes 4194304 | tf_op jit(solution)/shard_map/all_to_all | solution.py:33
  210.2 3.1 %reduce_sum.12 = bf16[4,4096]{1,0:T(4,128)(2,1)} reduce(bf16[64,4,4096]{2,1,0:T(4,128)(2,1)} %all_to_all.10, bf16[]{:T(256)} %constant.4.clone.1), dimensions={0}, to_apply=%region_0.0 | reduce | flops 1032192 | bytes 2129922 | tf_op jit(solution)/shard_map/reduce_sum | solution.py:34
  213.3 0.0 reduce-scatter.2.cloned.1.call-done
  213.3 1.8 convert_element_type.25
Async XLA Ops:
  7.2 124.2 %copy-start = (bf16[4096,256]{1,0:T(8,128)(2,1)S(1)}, bf16[4096,256]{1,0:T(8,128)(2,1)}, u32[]{:S(2)}) copy-start(bf16[4096,256]{1,0:T(8,128)(2,1)} %param.7) | copy-start | bytes 6291460
  10.6 105.7 %all-to-all-start = ((bf16[64,8,4096]{2,1,0:T(8,128)(2,1)}), bf16[64,8,4096]{2,1,0:T(8,128)(2,1)}, u32[]{:S(2)}, u32[]{:S(2)}) async-start(bf16[64,8,4096]{2,1,0:T(8,128)(2,1)} %broadcast_in_dim.2), calls=%async_computation | async-start | bytes 8388608 | tf_op jit(solution)/shard_map/all_to_all | solution.py:17
  23.8 114.1 %all-gather.2.cloned.1.call-start = ((), (), s32[]{:S(2)}) async-start(), calls=%async_computation.3 | async-start | bytes 2359296 | tf_op jit(solution)/shard_map/all_gather | solution.py:14
  24.6 188.7 %reduce-scatter.2.cloned.1.call-start = ((), (), s32[]{:S(2)}) async-start(), calls=%async_computation.4 | async-start | bytes 2359296 | tf_op jit(solution)/shard_map/reduce_scatter | solution.py:26
  131.4 2.5 %copy-start.2 = (bf16[256,4096]{1,0:T(8,128)(2,1)S(1)}, bf16[256,4096]{1,0:T(8,128)(2,1)}, u32[]{:S(2)}) copy-start(bf16[256,4096]{1,0:T(8,128)(2,1)} %reshape.15) | copy-start | bytes 6291460
  131.4 2.9 %copy-start.3 = (bf16[4096,256]{1,0:T(8,128)(2,1)S(1)}, bf16[4096,256]{1,0:T(8,128)(2,1)}, u32[]{:S(2)}) copy-start(bf16[4096,256]{1,0:T(8,128)(2,1)} %param.8) | copy-start | bytes 6291460
  134.2 1.6 copy-start.1
Sparse Core Ops, SparseCore 0:
  26.8 53.6 all-gather.1
  143.8 56.9 reduce-scatter.1

commit v2 on v1

v2 whole, which is shorter than its diff:
```python
import jax
import jax.numpy as jnp
from jax import lax
from jax.sharding import Mesh, PartitionSpec as P

BF16 = jnp.bfloat16
F32 = jnp.float32
DP = ("zh", "c")
PLANE = ("y", "x")
TENSOR = ("zl", "y", "x")


def contract(a, b, ca, cb):
    return lax.dot_general(a, b, (((ca,), (cb,)), ((), ())), preferred_element_type=F32)


def swap(value, axis):
    return lax.ppermute(value, axis, [(0, 1), (1, 0)])


def spread(block, axis):
    n = lax.axis_size(axis)
    return lax.all_to_all(jnp.broadcast_to(block[None], (n, *block.shape)), axis, 0, 0)


def on_device(tokens, cotangent, gate_weight, up_weight, down_weight):
    n_dp, n_plane = lax.axis_size(DP), lax.axis_size(PLANE)
    rows, d = tokens.shape
    feats = d // n_dp
    hid = gate_weight.shape[1]
    half = n_plane * rows
    first = lax.axis_index("c") == 0

    mine = swap(jnp.where(first, gate_weight, up_weight), "zl")
    other = swap(mine, "c")
    down_pair = jnp.concatenate([down_weight, swap(down_weight, "zl")], axis=0)

    cot = cotangent.reshape(rows, n_dp, feats).swapaxes(0, 1)
    cot = lax.all_to_all(cot, DP, 0, 0)
    cot = spread(cot.reshape(n_dp * rows, feats), PLANE)
    cot = cot.reshape(n_plane, n_dp, rows, feats).swapaxes(0, 1).reshape(n_dp * half, feats)

    part = contract(cot, down_pair, 1, 1).astype(BF16)
    part = part.reshape(lax.axis_size("zh"), 2, half, 2 * hid).swapaxes(0, 1)
    part = lax.all_to_all(part, "c", 0, 0)
    part = (part[0].astype(F32) + part[1].astype(F32)).astype(BF16)
    part = lax.all_to_all(part, "zh", 0, 0)
    d_hidden = jnp.sum(part.astype(F32), axis=0)

    tok = spread(tokens, PLANE).reshape(half, d)
    pre_mine = contract(tok, mine, 1, 0)
    pre_other = contract(tok, other, 1, 0)
    gate = jnp.concatenate(
        [contract(tok, gate_weight, 1, 0), jnp.where(first, pre_mine, pre_other)], axis=1
    )
    up = jnp.concatenate(
        [contract(tok, up_weight, 1, 0), jnp.where(first, pre_other, pre_mine)], axis=1
    )
    sigma = jax.nn.sigmoid(gate)
    silu = gate * sigma
    hidden = (silu * up).astype(BF16)
    d_up = (d_hidden * silu).astype(BF16)
    d_gate = (d_hidden * up * sigma * (1.0 + gate * (1.0 - sigma))).astype(BF16)

    hidden_all = spread(hidden, "zh")
    hidden_all = spread(hidden_all, "c").swapaxes(0, 1).reshape(n_dp * half, 2 * hid)

    dg, du = d_gate[:, hid:], d_up[:, hid:]
    term = (
        contract(d_gate[:, :hid], gate_weight, 1, 1)
        + contract(d_up[:, :hid], up_weight, 1, 1)
        + contract(jnp.where(first, dg, du), mine, 1, 1)
        + contract(jnp.where(first, du, dg), other, 1, 1)
    )
    parts = lax.all_to_all(term.astype(BF16).reshape(n_plane, rows, d), PLANE, 0, 0)
    input_grad = jnp.sum(parts.astype(F32), axis=0).astype(BF16)

    grads = contract(hidden_all, cot, 0, 0)
    down_grad = grads[:hid] + swap(grads[hid:].astype(BF16), "zl").astype(F32)
    return (input_grad, down_grad)


def solution(mesh):
    fine = Mesh(mesh.devices.reshape(4, 2, 2, 8, 4), ("zh", "c", "zl", "y", "x"))
    placed = (
        P((*DP, *TENSOR), None),
        P((*DP, *TENSOR), None),
        P(None, TENSOR),
        P(None, TENSOR),
        P(TENSOR, DP),
    )
    return jax.shard_map(
        on_device,
        mesh=fine,
        in_specs=placed,
        out_specs=(P((*DP, *TENSOR), None), P(TENSOR, DP)),
        check_vma=False,
    )
```

time: 226 us -> 201 us (0.89)
  starting transfers between devices: 13.3 us -> 47.7 us
  waiting for transfers between devices: 92.5 us -> 66 us
  blocking collectives: 57.5 us -> 38 us
  between operations: 14.1 us -> 0.87 us
  matrix products: 15.9 us -> 19.1 us
  local copies, waits for them, and re-layouts: 22.9 us -> 20.1 us
    all_to_all x1 -> x5, waiting for transfers between devices: 91.8 us -> 45.4 us  [the longest x3 23.8 us: spread(): lax.all_to_all(jnp.broadcast_to(block[None], (n, *block.shape)), axis, 0, 0)]
    ppermute x0 -> x4, waiting for transfers between devices: none -> 20.6 us  [swap(): return lax.ppermute(value, axis, [(0, 1), (1, 0)])]
    all_to_all x1 -> x3, blocking collectives: 57.5 us -> 38 us  [the longest x1 19.2 us: on_device(): cot = lax.all_to_all(cot, DP, 0, 0)]
    all_to_all x1 -> x5, starting transfers between devices: 13.2 us -> 32 us  [the longest x3 22.4 us: spread(): lax.all_to_all(jnp.broadcast_to(block[None], (n, *block.shape)), axis, 0, 0)]
    ppermute x0 -> x4, starting transfers between devices: none -> 15.7 us  [swap(): return lax.ppermute(value, axis, [(0, 1), (1, 0)])]
    slice x1, local copies, waits for them, and re-layouts: 7.06 us -> 0.03 us  [on_device(): down_grad = grads[:hid] + swap(grads[hid:].astype(BF16), 'zl').astype(F32)]
    dot_general x6 -> x10, matrix products: 15.9 us -> 19.1 us  [contract(): lax.dot_general(a, b, (((ca,), (cb,)), ((), ())), preferred_element_type=...]
    broadcast_in_dim x1 -> x5, local copies, waits for them, and re-layouts: 2.49 us -> 5.4 us  [spread(): jnp.broadcast_to(block[None], (n, *block.shape))]
  transfers between devices with their start and end apart: 3 -> 9, of which waited for: 1 -> 7; matrix products, arithmetic and copies ran while one was open for 15% -> 19% of each run, Pallas kernels for 0% -> 0%
where the time goes in v2:
time: 201 us; the launch traced here: 198 us
  waiting for transfers between devices  66 us (33%)
  starting transfers between devices  47.7 us (24%)
  blocking collectives  38 us (19%)
  local copies, waits for them, and re-layouts  20.1 us (10%)
  matrix products  19.1 us (10%)
  other arithmetic  5.75 us (3%)
    all_to_all x3, waiting for transfers between devices, spread(): lax.all_to_all(jnp.broadcast_to(block[None], (n, *block.shape)), axis, 0, 0)  23.8 us
    all_to_all x3, starting transfers between devices, spread(): lax.all_to_all(jnp.broadcast_to(block[None], (n, *block.shape)), axis, 0, 0)  22.4 us
    ppermute x4, waiting for transfers between devices, swap(): return lax.ppermute(value, axis, [(0, 1), (1, 0)])  20.6 us
    all_to_all x1, blocking collectives, on_device(): cot = lax.all_to_all(cot, DP, 0, 0)  19.2 us
    dot_general x10, matrix products, contract(): lax.dot_general(a, b, (((ca,), (cb,)), ((), ())), preferred_element_type=...  19.1 us
    ppermute x4, starting transfers between devices, swap(): return lax.ppermute(value, axis, [(0, 1), (1, 0)])  15.7 us
    all_to_all x1, waiting for transfers between devices, on_device(): lax.all_to_all(term.astype(BF16).reshape(n_plane, rows, d), PLANE, 0, 0)  14.3 us
    all_to_all x1, blocking collectives, spread(): lax.all_to_all(jnp.broadcast_to(block[None], (n, *block.shape)), axis, 0, 0)  9.65 us
  transfers between devices with their start and end apart: 9, of which 7 were waited for; matrix products, arithmetic and copies ran while one was open for 19% of the time, Pallas kernels for 0%

profile of v2, /device:TPU:1, one launch (start us, length us, event | category | flops | bytes accessed | tf_op | source)
XLA Modules:
  0.0 197.5 jit_solution(18394222988546511014)
XLA Ops:
  0.6 0.0 copy-start
  0.6 19.2 %all_to_all.40 = bf16[8,4,512]{2,1,0:T(4,128)(2,1)S(1)} all-to-all(bf16[8,4,512]{2,1,0:T(4,128)(2,1)} %bitcast.38), channel_id=1, replica_groups=mesh['zh'=4,'c'=2,'zl'=2,'y'=8,'x'=4] {'zh','c'}, dimensions={0} | all-to-all | bytes 65536 | tf_op jit(solution)/shard_map/all_to_all | solution.py:39
  19.9 2.2 %broadcast_in_dim.12 = bf16[32,4,4096]{2,1,0:T(4,128)(2,1)} broadcast(bf16[4,4096]{1,0:T(4,128)(2,1)} %param.5), dimensions={1,2} | broadcast | bytes 1081344 | tf_op jit(solution)/shard_map/broadcast_in_dim | solution.py:23
  22.1 9.7 %all-to-all-start.4 = ((bf16[32,4,4096]{2,1,0:T(4,128)(2,1)}), bf16[32,4,4096]{2,1,0:T(4,128)(2,1)S(1)}, u32[]{:S(2)}, u32[]{:S(2)}) async-start(bf16[32,4,4096]{2,1,0:T(4,128)(2,1)} %broadcast_in_dim.12), calls=%async_computation.4 | async-start | bytes 2097152 | tf_op jit(solution)/shard_map/all_to_all | solution.py:23
  31.8 0.0 copy-done
  31.8 1.5 broadcast_select_fusion
  33.3 0.0 copy-start.4
  33.3 3.1 %collective-permute-start.1 = (bf16[4096,256]{1,0:T(8,128)(2,1)}, bf16[4096,256]{1,0:T(8,128)(2,1)}, u32[]{:S(2)}, u32[]{:S(2)}) collective-permute-start(bf16[4096,256]{1,0:T(8,128)(2,1)} %broadcast_select_fusion), channel_id=1, source_target_pairs={{0,32},{32,0},{1,33},{33,1},{2,34},{34,2},{3,35},{35,3},{4,36},{36... | collective-permute-start | bytes 6291464 | tf_op jit(solution)/shard_map/ppermute | solution.py:18
  36.5 21.4 %all-to-all-done.4 = bf16[32,4,4096]{2,1,0:T(4,128)(2,1)S(1)} async-done(((bf16[32,4,4096]{2,1,0:T(4,128)(2,1)}), bf16[32,4,4096]{2,1,0:T(4,128)(2,1)S(1)}, u32[]{:S(2)}, u32[]{:S(2)}) %all-to-all-start.4) | async-done | bytes 1048608 | tf_op jit(solution)/shard_map/all_to_all | solution.py:23
  57.9 0.0 copy-start.1
  57.9 1.2 broadcast_in_dim.11
  59.2 6.4 %all-to-all-start.1 = ((bf16[32,32,512]{2,1,0:T(8,128)(2,1)}), bf16[32,32,512]{2,1,0:T(8,128)(2,1)}, u32[]{:S(2)}, u32[]{:S(2)}) async-start(bf16[32,32,512]{2,1,0:T(8,128)(2,1)} %broadcast_in_dim.11), calls=%async_computation.1 | async-start | bytes 2097152 | tf_op jit(solution)/shard_map/all_to_all | solution.py:23
  65.6 14.6 %collective-permute-done.1 = bf16[4096,256]{1,0:T(8,128)(2,1)} collective-permute-done((bf16[4096,256]{1,0:T(8,128)(2,1)}, bf16[4096,256]{1,0:T(8,128)(2,1)}, u32[]{:S(2)}, u32[]{:S(2)}) %collective-permute-start.1) | collective-permute-done | bytes 2097184 | tf_op jit(solution)/shard_map/ppermute | solution.py:18
  80.2 5.4 %collective-permute-start.2 = (bf16[4096,256]{1,0:T(8,128)(2,1)}, bf16[4096,256]{1,0:T(8,128)(2,1)}, u32[]{:S(2)}, u32[]{:S(2)}) collective-permute-start(bf16[4096,256]{1,0:T(8,128)(2,1)} %collective-permute-done.1), channel_id=1, source_target_pairs={{0,64},{64,0},{1,65},{65,1},{2,66},{66,2},{3,67},{67,3},{4,68},{68... | collective-permute-start | bytes 6291464 | tf_op jit(solution)/shard_map/ppermute | solution.py:18
  85.6 0.0 copy-done.1
  85.6 0.0 copy-done.4
  85.6 3.0 %collective-permute-start = (bf16[256,512]{1,0:T(8,128)(2,1)S(1)}, bf16[256,512]{1,0:T(8,128)(2,1)}, u32[]{:S(2)}, u32[]{:S(2)}) collective-permute-start(bf16[256,512]{1,0:T(8,128)(2,1)S(1)} %copy-done.4), channel_id=1, source_target_pairs={{0,32},{32,0},{1,33},{33,1},{2,34},{34,2},{3,35},{35,3},{4,36},{36... | collective-permute-start | bytes 786440 | tf_op jit(solution)/shard_map/ppermute | solution.py:18
  88.7 1.3 reshape.83
  90.0 0.8 all-to-all-done.1
  90.8 1.8 copy.25
  92.6 1.8 copy.26
  94.4 2.1 %reshape.81 = bf16[1024,512]{1,0:T(8,128)(2,1)} reshape(bf16[8,32,4,512]{3,2,1,0:T(4,128)(2,1)} %copy.26) | data formatting | bytes 2097152 | tf_op jit(solution)/shard_map/reshape | solution.py:41
  96.6 0.0 collective-permute-done
  96.6 3.1 %fusion.1 = bf16[1024,512]{0,1:T(8,128)(2,1)} fusion(bf16[1024,512]{1,0:T(8,128)(2,1)} %reshape.81, bf16[256,512]{1,0:T(8,128)(2,1)} %collective-permute-done, bf16[256,512]{1,0:T(8,128)(2,1)S(1)} %copy-done.4), kind=kOutput, calls=%fused_computation.6 | convolution fusion | flops 538443776 | bytes 2621440 | tf_op jit(solution)/shard_map/dot_general | solution.py:14
  99.6 2.6 %reshape.82 = bf16[4,2,128,512]{2,1,0,3:T(2,128)(2,1)} reshape(bf16[1024,512]{0,1:T(8,128)(2,1)} %fusion.1) | data formatting | bytes 2097152 | tf_op jit(solution)/shard_map/reshape | solution.py:44
  102.2 3.7 %copy.27 = bf16[4,2,128,512]{3,2,0,1:T(8,128)(2,1)} copy(bf16[4,2,128,512]{2,1,0,3:T(2,128)(2,1)} %reshape.82) | data formatting | bytes 2097152 | tf_op jit(solution)/shard_map/reshape | solution.py:44
  105.9 9.1 %all_to_all.41 = bf16[2,4,128,512]{3,2,1,0:T(8,128)(2,1)S(1)} all-to-all(bf16[2,4,128,512]{3,2,1,0:T(8,128)(2,1)} %bitcast.36), channel_id=1, replica_groups=mesh['zh'=4,'c'=2,'zl'=2,'y'=8,'x'=4] {'c'}, dimensions={0} | all-to-all | bytes 2097152 | tf_op jit(solution)/shard_map/all_to_all | solution.py:45
  115.0 0.9 fusion.2
  115.9 4.2 %all-to-all-start.3 = ((bf16[4,128,512]{2,1,0:T(8,128)(2,1)}), bf16[4,128,512]{2,1,0:T(8,128)(2,1)}, u32[]{:S(2)}, u32[]{:S(2)}) async-start(bf16[4,128,512]{2,1,0:T(8,128)(2,1)} %fusion.2), calls=%async_computation.3 | async-start | bytes 1048576 | tf_op jit(solution)/shard_map/all_to_all | solution.py:47
  120.1 2.0 %fusion.20 = f32[128,256]{1,0:T(8,128)S(1)} fusion(bf16[128,4096]{1,0:T(8,128)(2,1)S(1)} %reshape.83, bf16[4096,256]{1,0:T(8,128)(2,1)} %param.7), kind=kOutput, calls=%fused_computation.37 | convolution fusion | flops 268435456 | bytes 3276800 | tf_op jit(solution)/shard_map/dot_general | solution.py:14
  122.1 1.1 fusion.19
  123.2 2.0 %fusion.22 = f32[256,128]{0,1:T(8,128)S(1)} fusion(bf16[128,4096]{1,0:T(8,128)(2,1)S(1)} %reshape.83, bf16[4096,256]{1,0:T(8,128)(2,1)} %collective-permute-done.1), kind=kOutput, calls=%fused_computation.39 | convolution fusion | flops 268435456 | bytes 3276800 | tf_op jit(solution)/shard_map/dot_general | solution.py:14
  125.2 7.3 %all-to-all-done.3 = bf16[4,128,512]{2,1,0:T(8,128)(2,1)} async-done(((bf16[4,128,512]{2,1,0:T(8,128)(2,1)}), bf16[4,128,512]{2,1,0:T(8,128)(2,1)}, u32[]{:S(2)}, u32[]{:S(2)}) %all-to-all-start.3) | async-done | bytes 524320 | tf_op jit(solution)/shard_map/all_to_all | solution.py:47
  132.5 0.0 copy-start.3
  132.5 1.2 convert_reduce_fusion
  133.7 0.0 collective-permute-done.2
  133.7 2.0 %select_bitcast_fusion.1 = (f32[128,256]{1,0:T(8,128)S(1)}, f32[128,256]{1,0:T(8,128)S(1)}) fusion(f32[256,128]{0,1:T(8,128)S(1)} %fusion.22, pred[]{:T(512)S(6)} %eq.3, bf16[128,4096]{1,0:T(8,128)(2,1)S(1)} %reshape.83, bf16[4096,256]{1,0:T(8,128)(2,1)} %collective-permute-done.2), kind=kOutput, calls=%fused_computation.23 | convolution fusion | flops 268500992 | bytes 3538945 | tf_op jit(solution)/shard_map/dot_general | solution.py:14
  135.8 0.0 copy-done.3
  135.8 0.2 multiply_convert_fusion
  136.0 0.8 broadcast_in_dim.13
  136.8 6.3 %all-to-all-start.6 = ((bf16[4,128,512]{2,1,0:T(8,128)(2,1)}), bf16[4,128,512]{2,1,0:T(8,128)(2,1)}, u32[]{:S(2)}, u32[]{:S(2)}) async-start(bf16[4,128,512]{2,1,0:T(8,128)(2,1)} %broadcast_in_dim.13), calls=%async_computation.6 | async-start | bytes 1048576 | tf_op jit(solution)/shard_map/all_to_all | solution.py:23
  143.1 2.4 %fusion.8 = f32[128,4096]{1,0:T(8,128)S(1)} fusion(bf16[4096,256]{1,0:T(8,128)(2,1)} %param.7, bf16[128,512]{1,0:T(8,128)(2,1)S(1)} %get-tuple-element.3), kind=kOutput, calls=%fused_computation.25 | convolution fusion | flops 268435456 | bytes 4259840 | tf_op jit(solution)/shard_map/dot_general | solution.py:14
  145.5 0.8 convolution_add_fusion.2
  146.3 2.4 %convolution_add_fusion.1 = f32[128,4096]{1,0:T(8,128)S(1)} fusion(f32[128,4096]{1,0:T(8,128)S(1)} %convolution_add_fusion.2, bf16[4096,256]{1,0:T(8,128)(2,1)} %collective-permute-done.1, pred[]{:T(512)S(6)} %eq.3, bf16[128,512]{1,0:T(8,128)(2,1)S(1)} %get-tuple-element.4, bf16[128,512]{1,0:T(8,128)(2,1)S(1)} %get-tuple-element.3), kind=kOutput, calls=%fused_computation.1 | convolution fusion | flops 268992512 | bytes 6422529 | tf_op jit(solution)/shard_map/dot_general | solution.py:14
  148.8 2.4 %fusion = bf16[128,4096]{1,0:T(8,128)(2,1)S(1)} fusion(f32[128,4096]{1,0:T(8,128)S(1)} %convolution_add_fusion.1, bf16[4096,256]{1,0:T(8,128)(2,1)} %collective-permute-done.2, pred[]{:T(512)S(6)} %eq.3, bf16[128,512]{1,0:T(8,128)(2,1)S(1)} %get-tuple-element.4, bf16[128,512]{1,0:T(8,128)(2,1)S(1)} %get-tuple-element.3), kind=kOutput, calls=%fused_computation.3 | convolution fusion | flops 269516800 | bytes 5373953 | tf_op jit(solution)/shard_map/dot_general | solution.py:14
  151.2 1.2 reshape.84
  152.4 1.5 all-to-all-done.6
  153.9 1.1 broadcast_in_dim.14
  155.1 9.7 %all_to_all.42 = bf16[2,4,128,512]{3,2,1,0:T(8,128)(2,1)S(1)} all-to-all(bf16[2,4,128,512]{3,2,1,0:T(8,128)(2,1)S(1)} %broadcast_in_dim.14), channel_id=1, replica_groups=mesh['zh'=4,'c'=2,'zl'=2,'y'=8,'x'=4] {'c'}, dimensions={0} | all-to-all | bytes 2097152 | tf_op jit(solution)/shard_map/all_to_all | solution.py:23
  164.7 0.0 copy-start.2
  164.7 5.4 %all-to-all-start.5 = ((bf16[32,4,4096]{2,1,0:T(4,128)(2,1)}), bf16[32,4,4096]{2,1,0:T(4,128)(2,1)S(1)}, u32[]{:S(2)}, u32[]{:S(2)}) async-start(bf16[32,4,4096]{2,1,0:T(4,128)(2,1)} %reshape.84), calls=%async_computation.5 | async-start | bytes 2097152 | tf_op jit(solution)/shard_map/all_to_all | solution.py:75
  170.2 0.1 copy.32
  170.3 0.0 copy-done.2
  170.3 0.7 fusion.21
  171.1 4.2 %collective-permute-start.3 = (bf16[256,512]{1,0:T(8,128)(2,1)S(1)}, bf16[256,512]{1,0:T(8,128)(2,1)S(1)}, u32[]{:S(2)}, u32[]{:S(2)}) collective-permute-start(bf16[256,512]{1,0:T(8,128)(2,1)S(1)} %slice.65), channel_id=1, source_target_pairs={{0,32},{32,0},{1,33},{33,1},{2,34},{34,2},{3,35},{35,3},{4,36},{36... | collective-permute-start | bytes 786440 | tf_op jit(solution)/shard_map/ppermute | solution.py:18
  175.2 6.0 %collective-permute-done.3 = bf16[256,512]{1,0:T(8,128)(2,1)S(1)} collective-permute-done((bf16[256,512]{1,0:T(8,128)(2,1)S(1)}, bf16[256,512]{1,0:T(8,128)(2,1)S(1)}, u32[]{:S(2)}, u32[]{:S(2)}) %collective-permute-start.3) | collective-permute-done | bytes 262176 | tf_op jit(solution)/shard_map/ppermute | solution.py:18
  181.3 0.9 slice_add_fusion
  182.2 14.3 %all-to-all-done.5 = bf16[32,4,4096]{2,1,0:T(4,128)(2,1)S(1)} async-done(((bf16[32,4,4096]{2,1,0:T(4,128)(2,1)}), bf16[32,4,4096]{2,1,0:T(4,128)(2,1)S(1)}, u32[]{:S(2)}, u32[]{:S(2)}) %all-to-all-start.5) | async-done | bytes 1048608 | tf_op jit(solution)/shard_map/all_to_all | solution.py:75
  196.5 1.0 reduce_sum.22
  (2 shorter events, 0.0 us)
Async XLA Ops:
  0.6 31.1 %copy-start = (bf16[4096,256]{1,0:T(8,128)(2,1)S(1)}, bf16[4096,256]{1,0:T(8,128)(2,1)}, u32[]{:S(2)}) copy-start(bf16[4096,256]{1,0:T(8,128)(2,1)} %param.8) | copy-start | bytes 6291460
  22.1 35.9 %all-to-all-start.4 = ((bf16[32,4,4096]{2,1,0:T(4,128)(2,1)}), bf16[32,4,4096]{2,1,0:T(4,128)(2,1)S(1)}, u32[]{:S(2)}, u32[]{:S(2)}) async-start(bf16[32,4,4096]{2,1,0:T(4,128)(2,1)} %broadcast_in_dim.12), calls=%async_computation.4 | async-start | bytes 2097152 | tf_op jit(solution)/shard_map/all_to_all | solution.py:23
  33.3 52.3 %copy-start.4 = (bf16[256,512]{1,0:T(8,128)(2,1)S(1)}, bf16[256,512]{1,0:T(8,128)(2,1)}, u32[]{:S(2)}) copy-start(bf16[256,512]{1,0:T(8,128)(2,1)} %param.9) | copy-start | bytes 786436
  33.3 46.9 %collective-permute-start.1 = (bf16[4096,256]{1,0:T(8,128)(2,1)}, bf16[4096,256]{1,0:T(8,128)(2,1)}, u32[]{:S(2)}, u32[]{:S(2)}) collective-permute-start(bf16[4096,256]{1,0:T(8,128)(2,1)} %broadcast_select_fusion), channel_id=1, source_target_pairs={{0,32},{32,0},{1,33},{33,1},{2,34},{34,2},{3,35},{35,3},{4,36},{36... | collective-permute-start | bytes 6291464 | tf_op jit(solution)/shard_map/ppermute | solution.py:18
  57.9 27.7 %copy-start.1 = (bf16[32,4,4096]{2,1,0:T(4,128)(2,1)}, bf16[32,4,4096]{2,1,0:T(4,128)(2,1)S(1)}, u32[]{:S(2)}) copy-start(bf16[32,4,4096]{2,1,0:T(4,128)(2,1)S(1)} %all-to-all-done.4) | copy-start | bytes 3145732
  59.2 31.6 %all-to-all-start.1 = ((bf16[32,32,512]{2,1,0:T(8,128)(2,1)}), bf16[32,32,512]{2,1,0:T(8,128)(2,1)}, u32[]{:S(2)}, u32[]{:S(2)}) async-start(bf16[32,32,512]{2,1,0:T(8,128)(2,1)} %broadcast_in_dim.11), calls=%async_computation.1 | async-start | bytes 2097152 | tf_op jit(solution)/shard_map/all_to_all | solution.py:23
  80.2 53.5 %collective-permute-start.2 = (bf16[4096,256]{1,0:T(8,128)(2,1)}, bf16[4096,256]{1,0:T(8,128)(2,1)}, u32[]{:S(2)}, u32[]{:S(2)}) collective-permute-start(bf16[4096,256]{1,0:T(8,128)(2,1)} %collective-permute-done.1), channel_id=1, source_target_pairs={{0,64},{64,0},{1,65},{65,1},{2,66},{66,2},{3,67},{67,3},{4,68},{68... | collective-permute-start | bytes 6291464 | tf_op jit(solution)/shard_map/ppermute | solution.py:18
  85.6 10.9 %collective-permute-start = (bf16[256,512]{1,0:T(8,128)(2,1)S(1)}, bf16[256,512]{1,0:T(8,128)(2,1)}, u32[]{:S(2)}, u32[]{:S(2)}) collective-permute-start(bf16[256,512]{1,0:T(8,128)(2,1)S(1)} %copy-done.4), channel_id=1, source_target_pairs={{0,32},{32,0},{1,33},{33,1},{2,34},{34,2},{3,35},{35,3},{4,36},{36... | collective-permute-start | bytes 786440 | tf_op jit(solution)/shard_map/ppermute | solution.py:18
  115.9 16.6 %all-to-all-start.3 = ((bf16[4,128,512]{2,1,0:T(8,128)(2,1)}), bf16[4,128,512]{2,1,0:T(8,128)(2,1)}, u32[]{:S(2)}, u32[]{:S(2)}) async-start(bf16[4,128,512]{2,1,0:T(8,128)(2,1)} %fusion.2), calls=%async_computation.3 | async-start | bytes 1048576 | tf_op jit(solution)/shard_map/all_to_all | solution.py:47
  132.5 3.2 %copy-start.3 = (f32[128,256]{1,0:T(8,128)S(1)}, f32[128,256]{1,0:T(8,128)}, u32[]{:S(2)}) copy-start(f32[128,256]{1,0:T(8,128)} %fusion.19) | copy-start | bytes 393220
  136.8 17.1 %all-to-all-start.6 = ((bf16[4,128,512]{2,1,0:T(8,128)(2,1)}), bf16[4,128,512]{2,1,0:T(8,128)(2,1)}, u32[]{:S(2)}, u32[]{:S(2)}) async-start(bf16[4,128,512]{2,1,0:T(8,128)(2,1)} %broadcast_in_dim.13), calls=%async_computation.6 | async-start | bytes 1048576 | tf_op jit(solution)/shard_map/all_to_all | solution.py:23
  164.7 5.6 %copy-start.2 = (bf16[1024,512]{1,0:T(8,128)(2,1)S(1)}, bf16[1024,512]{1,0:T(8,128)(2,1)}, u32[]{:S(2)}) copy-start(bf16[1024,512]{1,0:T(8,128)(2,1)} %reshape.81) | copy-start | bytes 3145732
  164.7 31.8 %all-to-all-start.5 = ((bf16[32,4,4096]{2,1,0:T(4,128)(2,1)}), bf16[32,4,4096]{2,1,0:T(4,128)(2,1)S(1)}, u32[]{:S(2)}, u32[]{:S(2)}) async-start(bf16[32,4,4096]{2,1,0:T(4,128)(2,1)} %reshape.84), calls=%async_computation.5 | async-start | bytes 2097152 | tf_op jit(solution)/shard_map/all_to_all | solution.py:75
  171.1 10.2 %collective-permute-start.3 = (bf16[256,512]{1,0:T(8,128)(2,1)S(1)}, bf16[256,512]{1,0:T(8,128)(2,1)S(1)}, u32[]{:S(2)}, u32[]{:S(2)}) collective-permute-start(bf16[256,512]{1,0:T(8,128)(2,1)S(1)} %slice.65), channel_id=1, source_target_pairs={{0,32},{32,0},{1,33},{33,1},{2,34},{34,2},{3,35},{35,3},{4,36},{36... | collective-permute-start | bytes 786440 | tf_op jit(solution)/shard_map/ppermute | solution.py:18

commit v3 on v2

v3 whole, which is shorter than its diff:
```python
import jax
import jax.numpy as jnp
from jax import lax
from jax.sharding import Mesh, PartitionSpec as P

BF16 = jnp.bfloat16
F32 = jnp.float32
DP = ("zh", "c")
TENSOR = ("zl", "y", "x")


def contract(a, b, ca, cb):
    return lax.dot_general(a, b, (((ca,), (cb,)), ((), ())), preferred_element_type=F32)


def swap(value, axis):
    return lax.ppermute(value, axis, [(0, 1), (1, 0)])


def shift(value, axis, k):
    n = lax.axis_size(axis)
    return lax.ppermute(value, axis, [(i, (i + k) % n) for i in range(n)])


def spread(block, axis):
    n = lax.axis_size(axis)
    return lax.all_to_all(jnp.broadcast_to(block[None], (n, *block.shape)), axis, 0, 0)


def on_device(tokens, cotangent, gate_weight, up_weight, down_weight):
    nz, ny, nx = lax.axis_size("zh"), lax.axis_size("y"), lax.axis_size("x")
    rows, d = tokens.shape
    feats = d // (2 * nz)
    wide = d // 2
    hid = gate_weight.shape[1]
    half = nx * ny * rows
    first = lax.axis_index("c") == 0
    low = lax.axis_index("zl") == 0

    mine = swap(jnp.where(first, gate_weight, up_weight), "zl")
    down_rows = lax.all_gather(down_weight, ("zh", "zl"), axis=0).reshape(nz, 2 * hid, feats)

    cot = cotangent.reshape(rows, nz, 2, feats)
    cot_0, cot_1 = cot[:, :, 0].reshape(rows, wide), cot[:, :, 1].reshape(rows, wide)
    cot_own = jnp.where(first, cot_0, cot_1)
    cot_far = swap(jnp.where(first, cot_1, cot_0), "c")
    block = spread(jnp.concatenate([tokens, cot_own, cot_far], axis=1), "y")
    blocks = [block] + [shift(block, "x", k) for k in (1, 2, 3)]
    plane = jnp.stack(blocks).reshape(half, 2 * d)
    other = swap(mine, "c")
    tok, cot_own, cot_far = plane[:, :d], plane[:, d : d + wide], plane[:, d + wide :]

    def down(cot):
        return sum(contract(cot[:, z * feats : (z + 1) * feats], down_rows[z], 1, 1) for z in range(nz))

    d_hidden = down(cot_own) + swap(down(cot_far), "c")
    d_low, d_high = d_hidden[:, :hid], d_hidden[:, hid:]
    d_hidden = jnp.concatenate([jnp.where(low, d_low, d_high), jnp.where(low, d_high, d_low)], axis=1)

    pre_mine = contract(tok, mine, 1, 0)
    pre_other = contract(tok, other, 1, 0)
    gate = jnp.concatenate(
        [contract(tok, gate_weight, 1, 0), jnp.where(first, pre_mine, pre_other)], axis=1
    )
    up = jnp.concatenate(
        [contract(tok, up_weight, 1, 0), jnp.where(first, pre_other, pre_mine)], axis=1
    )
    sigma = jax.nn.sigmoid(gate)
    silu = gate * sigma
    hidden = (silu * up).astype(BF16)
    d_up = (d_hidden * silu).astype(BF16)
    d_gate = (d_hidden * up * sigma * (1.0 + gate * (1.0 - sigma))).astype(BF16)

    dg, du = d_gate[:, hid:], d_up[:, hid:]
    term = (
        contract(d_gate[:, :hid], gate_weight, 1, 1)
        + contract(d_up[:, :hid], up_weight, 1, 1)
        + contract(jnp.where(first, dg, du), mine, 1, 1)
        + contract(jnp.where(first, du, dg), other, 1, 1)
    ).astype(BF16)
    term = term.reshape(nx, ny * rows, d)
    total = term[0].astype(F32)
    for k in (1, 2, 3):
        total = total + shift(term[k], "x", -k).astype(F32)
    parts = lax.all_to_all(total.astype(BF16).reshape(ny, rows, d), "y", 0, 0)
    input_grad = jnp.sum(parts.astype(F32), axis=0).astype(BF16)

    both = jnp.stack([cot_own, cot_far]).reshape(2, half, nz, feats)
    both = lax.all_to_all(jnp.moveaxis(both, 2, 0), "zh", 0, 0)
    hid_own = spread(hidden, "zh")
    hid_far = swap(hid_own, "c")
    grads = contract(hid_own.reshape(nz * half, 2 * hid), both[:, 0].reshape(nz * half, feats), 0, 0)
    grads = grads + contract(
        hid_far.reshape(nz * half, 2 * hid), both[:, 1].reshape(nz * half, feats), 0, 0
    )
    down_grad = grads[:hid] + swap(grads[hid:].astype(BF16), "zl").astype(F32)
    return (input_grad, down_grad)


def solution(mesh):
    fine = Mesh(mesh.devices.reshape(4, 2, 2, 8, 4), ("zh", "c", "zl", "y", "x"))
    placed = (
        P((*DP, *TENSOR), None),
        P((*DP, *TENSOR), None),
        P(None, TENSOR),
        P(None, TENSOR),
        P(TENSOR, DP),
    )
    return jax.shard_map(
        on_device,
        mesh=fine,
        in_specs=placed,
        out_specs=(P((*DP, *TENSOR), None), P(TENSOR, DP)),
        check_vma=False,
    )
```

time: 201 us -> 197 us (0.980)
  blocking collectives: 38 us -> 0 us
  starting transfers between devices: 47.7 us -> 67 us
  between operations: 0.87 us -> 14.5 us
  other arithmetic: 5.75 us -> 10.5 us
  local copies, waits for them, and re-layouts: 20.1 us -> 15.7 us
    all_to_all x3 -> x0, blocking collectives: 38 us -> none  [the longest x1 19.2 us: on_device(): cot = lax.all_to_all(cot, DP, 0, 0)]
    ppermute x0 -> x6, waiting for transfers between devices: none -> 20.6 us  [shift(): return lax.ppermute(value, axis, [(i, (i + k) % n) for i in range(n)])]
    ppermute x0 -> x6, starting transfers between devices: none -> 17.1 us  [shift(): return lax.ppermute(value, axis, [(i, (i + k) % n) for i in range(n)])]
    all_to_all x2, waiting for transfers between devices: 21.6 us -> 4.72 us  [the longest x1 4.72 us: on_device(): parts = lax.all_to_all(total.astype(BF16).reshape(ny, rows, d), 'y', 0, 0)]
    all_to_all x3 -> x2, starting transfers between devices: 22.4 us -> 8.79 us  [spread(): lax.all_to_all(jnp.broadcast_to(block[None], (n, *block.shape)), axis, 0, 0)]
    ppermute x4 -> x6, starting transfers between devices: 15.7 us -> 25.3 us  [swap(): return lax.ppermute(value, axis, [(0, 1), (1, 0)])]
    reshape x5 -> x3, local copies, waits for them, and re-layouts: 10.9 us -> 4.29 us  [the longest x1 2.53 us: on_device(): plane = jnp.stack(blocks).reshape(half, 2 * d)]
    all_to_all x3 -> x2, waiting for transfers between devices: 23.8 us -> 17.2 us  [spread(): lax.all_to_all(jnp.broadcast_to(block[None], (n, *block.shape)), axis, 0, 0)]
  transfers between devices with their start and end apart: 9 -> 17, of which waited for: 7 -> 9; matrix products, arithmetic and copies ran while one was open for 19% -> 22% of each run, Pallas kernels for 0% -> 0%
where the time goes in v3:
time: 197 us; the launch traced here: 194 us
  starting transfers between devices  67 us (34%)
  waiting for transfers between devices  65.5 us (33%)
  matrix products  21 us (11%)
  local copies, waits for them, and re-layouts  15.7 us (8%)
  between operations  14.5 us (7%)
  other arithmetic  10.5 us (5%)
    ppermute x6, starting transfers between devices, swap(): return lax.ppermute(value, axis, [(0, 1), (1, 0)])  25.3 us
    ppermute x6, waiting for transfers between devices, swap(): return lax.ppermute(value, axis, [(0, 1), (1, 0)])  22.2 us
    dot_general x18, matrix products, contract(): lax.dot_general(a, b, (((ca,), (cb,)), ((), ())), preferred_element_type=...  21 us
    ppermute x6, waiting for transfers between devices, shift(): return lax.ppermute(value, axis, [(i, (i + k) % n) for i in range(n)])  20.6 us
    all_to_all x2, waiting for transfers between devices, spread(): lax.all_to_all(jnp.broadcast_to(block[None], (n, *block.shape)), axis, 0, 0)  17.2 us
    ppermute x6, starting transfers between devices, shift(): return lax.ppermute(value, axis, [(i, (i + k) % n) for i in range(n)])  17.1 us
    all_to_all x1, starting transfers between devices, on_device(): both = lax.all_to_all(jnp.moveaxis(both, 2, 0), 'zh', 0, 0)  10 us
    all_to_all x2, starting transfers between devices, spread(): lax.all_to_all(jnp.broadcast_to(block[None], (n, *block.shape)), axis, 0, 0)  8.79 us
  transfers between devices with their start and end apart: 17, of which 9 were waited for; matrix products, arithmetic and copies ran while one was open for 22% of the time, Pallas kernels for 0%

profile of v3, /device:TPU:1, one launch (start us, length us, event | category | flops | bytes accessed | tf_op | source)
XLA Modules:
  0.0 194.1 jit_solution(2675994413124556147)
XLA Ops:
  7.2 0.9 reshape.94
  8.2 8.8 %collective-permute-start = (bf16[4,2048]{1,0:T(4,128)(2,1)S(1)}, bf16[4,2048]{1,0:T(4,128)(2,1)S(1)}, u32[]{:S(2)}, u32[]{:S(2)}) collective-permute-start(bf16[4,2048]{1,0:T(4,128)(2,1)S(1)} %bitcast.42), channel_id=1, source_target_pairs={{0,64},{64,0},{1,65},{65,1},{2,66},{66,2},{3,67},{67,3},{4,68},{68... | collective-permute-start | bytes 49160 | tf_op jit(solution)/shard_map/ppermute | solution.py:17
  17.1 0.8 collective-permute-done
  17.9 0.8 pad_maximum_fusion.4
  18.6 0.9 broadcast_in_dim.4
  19.6 3.5 %all-to-all-start = ((bf16[8,4,8192]{2,1,0:T(4,128)(2,1)}), bf16[8,4,8192]{2,1,0:T(4,128)(2,1)S(1)}, u32[]{:S(2)}, u32[]{:S(2)}) async-start(bf16[8,4,8192]{2,1,0:T(4,128)(2,1)} %broadcast_in_dim.4), calls=%async_computation | async-start | bytes 1048576 | tf_op jit(solution)/shard_map/all_to_all | solution.py:27
  23.1 0.7 all-gather.3.cloned.1.call-update
  23.8 17.2 %all-to-all-done = bf16[8,4,8192]{2,1,0:T(4,128)(2,1)S(1)} async-done(((bf16[8,4,8192]{2,1,0:T(4,128)(2,1)}), bf16[8,4,8192]{2,1,0:T(4,128)(2,1)S(1)}, u32[]{:S(2)}, u32[]{:S(2)}) %all-to-all-start) | async-done | bytes 524320 | tf_op jit(solution)/shard_map/all_to_all | solution.py:27
  41.0 2.3 %collective-permute-start.3 = (bf16[8,4,8192]{2,1,0:T(4,128)(2,1)S(1)}, bf16[8,4,8192]{2,1,0:T(4,128)(2,1)S(1)}, u32[]{:S(2)}, u32[]{:S(2)}) collective-permute-start(bf16[8,4,8192]{2,1,0:T(4,128)(2,1)S(1)} %all-to-all-done), channel_id=1, source_target_pairs={{0,3},{1,0},{2,1},{3,2},{4,7},{5,4},{6,5},{7,6},{8,11},{9,8},{10,9... | collective-permute-start | bytes 1572872 | tf_op jit(solution)/shard_map/ppermute | solution.py:22
  43.4 2.4 %collective-permute-start.2 = (bf16[8,4,8192]{2,1,0:T(4,128)(2,1)S(1)}, bf16[8,4,8192]{2,1,0:T(4,128)(2,1)}, u32[]{:S(2)}, u32[]{:S(2)}) collective-permute-start(bf16[8,4,8192]{2,1,0:T(4,128)(2,1)S(1)} %all-to-all-done), channel_id=1, source_target_pairs={{0,2},{1,3},{2,0},{3,1},{4,6},{5,7},{6,4},{7,5},{8,10},{9,11},{10,... | collective-permute-start | bytes 1572872 | tf_op jit(solution)/shard_map/ppermute | solution.py:22
  45.8 2.5 %collective-permute-start.1 = (bf16[8,4,8192]{2,1,0:T(4,128)(2,1)S(1)}, bf16[8,4,8192]{2,1,0:T(4,128)(2,1)}, u32[]{:S(2)}, u32[]{:S(2)}) collective-permute-start(bf16[8,4,8192]{2,1,0:T(4,128)(2,1)S(1)} %all-to-all-done), channel_id=1, source_target_pairs={{0,1},{1,2},{2,3},{3,0},{4,5},{5,6},{6,7},{7,4},{8,9},{9,10},{10,1... | collective-permute-start | bytes 1572872 | tf_op jit(solution)/shard_map/ppermute | solution.py:22
  48.3 1.6 broadcast_select_fusion
  49.9 4.0 %collective-permute-start.5 = (bf16[4096,256]{1,0:T(8,128)(2,1)}, bf16[4096,256]{1,0:T(8,128)(2,1)}, u32[]{:S(2)}, u32[]{:S(2)}) collective-permute-start(bf16[4096,256]{1,0:T(8,128)(2,1)} %broadcast_select_fusion), channel_id=1, source_target_pairs={{0,32},{32,0},{1,33},{33,1},{2,34},{34,2},{3,35},{35,3},{4,36},{36... | collective-permute-start | bytes 6291464 | tf_op jit(solution)/shard_map/ppermute | solution.py:17
  53.9 2.1 %collective-permute-done.3 = bf16[8,4,8192]{2,1,0:T(4,128)(2,1)S(1)} collective-permute-done((bf16[8,4,8192]{2,1,0:T(4,128)(2,1)S(1)}, bf16[8,4,8192]{2,1,0:T(4,128)(2,1)S(1)}, u32[]{:S(2)}, u32[]{:S(2)}) %collective-permute-start.3) | collective-permute-done | bytes 524320 | tf_op jit(solution)/shard_map/ppermute | solution.py:22
  56.0 3.6 %collective-permute-done.2 = bf16[8,4,8192]{2,1,0:T(4,128)(2,1)} collective-permute-done((bf16[8,4,8192]{2,1,0:T(4,128)(2,1)S(1)}, bf16[8,4,8192]{2,1,0:T(4,128)(2,1)}, u32[]{:S(2)}, u32[]{:S(2)}) %collective-permute-start.2) | collective-permute-done | bytes 524320 | tf_op jit(solution)/shard_map/ppermute | solution.py:22
  59.6 12.4 %collective-permute-done.1 = bf16[8,4,8192]{2,1,0:T(4,128)(2,1)} collective-permute-done((bf16[8,4,8192]{2,1,0:T(4,128)(2,1)S(1)}, bf16[8,4,8192]{2,1,0:T(4,128)(2,1)}, u32[]{:S(2)}, u32[]{:S(2)}) %collective-permute-start.1) | collective-permute-done | bytes 524320 | tf_op jit(solution)/shard_map/ppermute | solution.py:22
  71.9 3.9 %pad_maximum_fusion = bf16[4,8,4,8192]{3,2,1,0:T(4,128)(2,1)} fusion(bf16[1,8,4,8192]{3,2,1,0:T(4,128)(2,1)S(1)} %bitcast.40, bf16[1,8,4,8192]{3,2,1,0:T(4,128)(2,1)} %bitcast.2, bf16[1,8,4,8192]{3,2,1,0:T(4,128)(2,1)} %bitcast.1, bf16[1,8,4,8192]{3,2,1,0:T(4,128)(2,1)S(1)} %bitcast.39), kind=kLoop, calls=%fused_computation.4 | loop fusion | flops 3145728 | bytes 4194304 | tf_op jit(solution)/shard_map/stack | solution.py:49
  75.9 2.5 %reshape.95 = bf16[128,8192]{1,0:T(8,128)(2,1)S(1)} reshape(bf16[4,8,4,8192]{3,2,1,0:T(4,128)(2,1)} %pad_maximum_fusion) | data formatting | bytes 4194304 | tf_op jit(solution)/shard_map/reshape | solution.py:49
  78.4 0.9 fusion.40
  79.3 1.3 copy.25
  80.6 1.0 copy.26
  81.6 1.1 maximum_bitcast_fusion
  82.8 1.0 copy.27
  83.8 10.0 %all-to-all-start.3 = ((bf16[4,2,128,512]{2,3,1,0:T(8,128)(2,1)}), bf16[4,2,128,512]{2,3,1,0:T(8,128)(2,1)S(1)}, u32[]{:S(2)}, u32[]{:S(2)}) async-start(bf16[4,2,128,512]{2,3,1,0:T(8,128)(2,1)} %copy.27), calls=%async_computation.3 | async-start | bytes 2097152 | tf_op jit(solution)/shard_map/all_to_all | solution.py:89
  93.8 2.2 %fusion.2 = f32[128,256]{1,0:T(8,128)S(1)} fusion(bf16[4096,256]{1,0:T(8,128)(2,1)} %param.7, bf16[128,8192]{1,0:T(8,128)(2,1)S(1)} %reshape.95), kind=kOutput, calls=%fused_computation.15 | convolution fusion | flops 268435456 | bytes 3276800 | tf_op jit(solution)/shard_map/dot_general | solution.py:13
  96.0 0.4 fusion.8
  96.5 20.9 %collective-permute-done.5 = bf16[4096,256]{1,0:T(8,128)(2,1)} collective-permute-done((bf16[4096,256]{1,0:T(8,128)(2,1)}, bf16[4096,256]{1,0:T(8,128)(2,1)}, u32[]{:S(2)}, u32[]{:S(2)}) %collective-permute-start.5) | collective-permute-done | bytes 2097184 | tf_op jit(solution)/shard_map/ppermute | solution.py:17
  117.3 4.5 %collective-permute-start.6 = (bf16[4096,256]{1,0:T(8,128)(2,1)}, bf16[4096,256]{1,0:T(8,128)(2,1)}, u32[]{:S(2)}, u32[]{:S(2)}) collective-permute-start(bf16[4096,256]{1,0:T(8,128)(2,1)} %collective-permute-done.5), channel_id=1, source_target_pairs={{0,64},{64,0},{1,65},{65,1},{2,66},{66,2},{3,67},{67,3},{4,68},{68... | collective-permute-start | bytes 6291464 | tf_op jit(solution)/shard_map/ppermute | solution.py:17
  121.8 2.0 %fusion.4 = f32[128,256]{1,0:T(8,128)S(1)} fusion(bf16[4096,256]{1,0:T(8,128)(2,1)} %collective-permute-done.5, bf16[128,8192]{1,0:T(8,128)(2,1)S(1)} %reshape.95), kind=kOutput, calls=%fused_computation.17 | convolution fusion | flops 268435456 | bytes 3276800 | tf_op jit(solution)/shard_map/dot_general | solution.py:13
  123.9 1.5 fusion.16
  125.4 1.3 convolution_add_fusion.6
  126.8 1.3 convolution_add_fusion.5
  128.1 0.3 convolution_add_fusion.4
  128.4 1.9 collective-permute-start.4
  130.7 0.3 convolution_add_fusion.9
  131.0 0.3 convolution_add_fusion.8
  131.3 0.6 collective-permute-done.4
  131.9 0.3 fusion.1
  132.2 2.2 %broadcast_select_fusion.2 = (f32[128,256]{1,0:T(8,128)S(1)}, f32[128,256]{1,0:T(8,128)S(1)}) fusion(f32[128,256]{1,0:T(8,128)S(1)} %fusion.4, pred[]{:T(512)S(6)} %eq.7, bf16[4096,256]{1,0:T(8,128)(2,1)} %collective-permute-done.6, bf16[128,8192]{1,0:T(8,128)(2,1)S(1)} %reshape.95), kind=kOutput, calls=%fused_computation.63 | convolution fusion | flops 268500992 | bytes 3538945 | tf_op jit(solution)/shard_map/dot_general | solution.py:13
  134.6 0.8 fusion.30
  135.4 0.8 copy-done.2
  136.2 0.8 convolution_add_fusion.2
  137.0 2.4 %convolution_add_fusion.1 = f32[128,4096]{1,0:T(8,128)S(1)} fusion(f32[128,4096]{1,0:T(8,128)S(1)} %convolution_add_fusion.2, bf16[4096,256]{1,0:T(8,128)(2,1)} %collective-permute-done.5, pred[]{:T(512)S(6)} %eq.7, bf16[128,512]{1,0:T(8,128)(2,1)S(1)} %get-tuple-element.11, bf16[128,512]{1,0:T(8,128)(2,1)S(1)} %get-tuple-element.10), kind=kOutput, calls=%fused_computation.1 | convolution fusion | flops 268992512 | bytes 6422529 | tf_op jit(solution)/shard_map/dot_general | solution.py:13
  139.5 2.4 %fusion = bf16[128,4096]{1,0:T(8,128)(2,1)S(1)} fusion(f32[128,4096]{1,0:T(8,128)S(1)} %convolution_add_fusion.1, bf16[4096,256]{1,0:T(8,128)(2,1)} %collective-permute-done.6, pred[]{:T(512)S(6)} %eq.7, bf16[128,512]{1,0:T(8,128)(2,1)S(1)} %get-tuple-element.11, bf16[128,512]{1,0:T(8,128)(2,1)S(1)} %get-tuple-element.10), kind=kOutput, calls=%fused_computation.3 | convolution fusion | flops 269516800 | bytes 5373953 | tf_op jit(solution)/shard_map/dot_general | solution.py:13
  141.9 0.8 broadcast_in_dim.5
  142.8 5.3 %all-to-all-start.2 = ((bf16[4,128,512]{2,1,0:T(8,128)(2,1)}), bf16[4,128,512]{2,1,0:T(8,128)(2,1)S(1)}, u32[]{:S(2)}, u32[]{:S(2)}) async-start(bf16[4,128,512]{2,1,0:T(8,128)(2,1)} %broadcast_in_dim.5), calls=%async_computation.2 | async-start | bytes 1048576 | tf_op jit(solution)/shard_map/all_to_all | solution.py:27
  148.0 0.9 fusion.42
  149.0 4.3 %collective-permute-start.7 = (bf16[32,4096]{1,0:T(8,128)(2,1)}, bf16[32,4096]{1,0:T(8,128)(2,1)S(1)}, u32[]{:S(2)}, u32[]{:S(2)}) collective-permute-start(bf16[32,4096]{1,0:T(8,128)(2,1)} %get-tuple-element.6), channel_id=1, source_target_pairs={{0,3},{1,0},{2,1},{3,2},{4,7},{5,4},{6,5},{7,6},{8,11},{9,8},{10,9... | collective-permute-start | bytes 786440 | tf_op jit(solution)/shard_map/ppermute | solution.py:22
  153.3 1.9 collective-permute-start.9
  155.2 3.6 %collective-permute-start.8 = (bf16[32,4096]{1,0:T(8,128)(2,1)}, bf16[32,4096]{1,0:T(8,128)(2,1)}, u32[]{:S(2)}, u32[]{:S(2)}) collective-permute-start(bf16[32,4096]{1,0:T(8,128)(2,1)} %get-tuple-element.8), channel_id=1, source_target_pairs={{0,2},{1,3},{2,0},{3,1},{4,6},{5,7},{6,4},{7,5},{8,10},{9,11},{10,... | collective-permute-start | bytes 786440 | tf_op jit(solution)/shard_map/ppermute | solution.py:22
  158.8 1.1 fusion.41
  159.9 1.2 copy.33
  161.1 1.2 copy.32
  162.4 3.5 %collective-permute-start.10 = (bf16[4,128,512]{2,1,0:T(8,128)(2,1)S(1)}, bf16[4,128,512]{2,1,0:T(8,128)(2,1)}, u32[]{:S(2)}, u32[]{:S(2)}) collective-permute-start(bf16[4,128,512]{2,1,0:T(8,128)(2,1)S(1)} %all-to-all-done.2), channel_id=1, source_target_pairs={{0,64},{64,0},{1,65},{65,1},{2,66},{66,2},{3,67},{67,3},{4,68},{68... | collective-permute-start | bytes 1572872 | tf_op jit(solution)/shard_map/ppermute | solution.py:17
  165.9 2.6 %collective-permute-done.8 = bf16[32,4096]{1,0:T(8,128)(2,1)} collective-permute-done((bf16[32,4096]{1,0:T(8,128)(2,1)}, bf16[32,4096]{1,0:T(8,128)(2,1)}, u32[]{:S(2)}, u32[]{:S(2)}) %collective-permute-start.8) | collective-permute-done | bytes 262176 | tf_op jit(solution)/shard_map/ppermute | solution.py:22
  168.5 1.2 add_convert_fusion
  169.7 0.8 reshape.96
  170.5 5.8 %all-to-all-start.1 = ((bf16[8,4,4096]{2,1,0:T(4,128)(2,1)}), bf16[8,4,4096]{2,1,0:T(4,128)(2,1)S(1)}, u32[]{:S(2)}, u32[]{:S(2)}) async-start(bf16[8,4,4096]{2,1,0:T(4,128)(2,1)} %reshape.96), calls=%async_computation.1 | async-start | bytes 524288 | tf_op jit(solution)/shard_map/all_to_all | solution.py:85
  176.2 0.5 fusion.44
  176.7 1.5 convolution_add_fusion.3
  178.3 2.6 %collective-permute-start.11 = (bf16[256,512]{1,0:T(8,128)(2,1)S(1)}, bf16[256,512]{1,0:T(8,128)(2,1)S(1)}, u32[]{:S(2)}, u32[]{:S(2)}) collective-permute-start(bf16[256,512]{1,0:T(8,128)(2,1)S(1)} %slice.247), channel_id=1, source_target_pairs={{0,32},{32,0},{1,33},{33,1},{2,34},{34,2},{3,35},{35,3},{4,36},{36... | collective-permute-start | bytes 786440 | tf_op jit(solution)/shard_map/ppermute | solution.py:17
  180.9 4.7 %all-to-all-done.1 = bf16[8,4,4096]{2,1,0:T(4,128)(2,1)S(1)} async-done(((bf16[8,4,4096]{2,1,0:T(4,128)(2,1)}), bf16[8,4,4096]{2,1,0:T(4,128)(2,1)S(1)}, u32[]{:S(2)}, u32[]{:S(2)}) %all-to-all-start.1) | async-done | bytes 262176 | tf_op jit(solution)/shard_map/all_to_all | solution.py:85
  185.6 0.7 reduce_sum.12
  186.4 0.9 slice_add_fusion
  (26 shorter events, 0.8 us)
Async XLA Ops:
  7.2 41.2 %copy-start = (bf16[4096,256]{1,0:T(8,128)(2,1)S(1)}, bf16[4096,256]{1,0:T(8,128)(2,1)}, u32[]{:S(2)}) copy-start(bf16[4096,256]{1,0:T(8,128)(2,1)} %param.8) | copy-start | bytes 6291460
  8.2 9.6 %collective-permute-start = (bf16[4,2048]{1,0:T(4,128)(2,1)S(1)}, bf16[4,2048]{1,0:T(4,128)(2,1)S(1)}, u32[]{:S(2)}, u32[]{:S(2)}) collective-permute-start(bf16[4,2048]{1,0:T(4,128)(2,1)S(1)} %bitcast.42), channel_id=1, source_target_pairs={{0,64},{64,0},{1,65},{65,1},{2,66},{66,2},{3,67},{67,3},{4,68},{68... | collective-permute-start | bytes 49160 | tf_op jit(solution)/shard_map/ppermute | solution.py:17
  19.6 21.4 %all-to-all-start = ((bf16[8,4,8192]{2,1,0:T(4,128)(2,1)}), bf16[8,4,8192]{2,1,0:T(4,128)(2,1)S(1)}, u32[]{:S(2)}, u32[]{:S(2)}) async-start(bf16[8,4,8192]{2,1,0:T(4,128)(2,1)} %broadcast_in_dim.4), calls=%async_computation | async-start | bytes 1048576 | tf_op jit(solution)/shard_map/all_to_all | solution.py:27
  23.1 100.8 %all-gather.3.cloned.1.call-start = ((), (), s32[]{:S(2)}) async-start(), calls=%async_computation.4 | async-start | bytes 2359296 | tf_op jit(solution)/shard_map/all_gather | solution.py:41
  41.0 15.0 %collective-permute-start.3 = (bf16[8,4,8192]{2,1,0:T(4,128)(2,1)S(1)}, bf16[8,4,8192]{2,1,0:T(4,128)(2,1)S(1)}, u32[]{:S(2)}, u32[]{:S(2)}) collective-permute-start(bf16[8,4,8192]{2,1,0:T(4,128)(2,1)S(1)} %all-to-all-done), channel_id=1, source_target_pairs={{0,3},{1,0},{2,1},{3,2},{4,7},{5,4},{6,5},{7,6},{8,11},{9,8},{10,9... | collective-permute-start | bytes 1572872 | tf_op jit(solution)/shard_map/ppermute | solution.py:22
  43.4 16.2 %collective-permute-start.2 = (bf16[8,4,8192]{2,1,0:T(4,128)(2,1)S(1)}, bf16[8,4,8192]{2,1,0:T(4,128)(2,1)}, u32[]{:S(2)}, u32[]{:S(2)}) collective-permute-start(bf16[8,4,8192]{2,1,0:T(4,128)(2,1)S(1)} %all-to-all-done), channel_id=1, source_target_pairs={{0,2},{1,3},{2,0},{3,1},{4,6},{5,7},{6,4},{7,5},{8,10},{9,11},{10,... | collective-permute-start | bytes 1572872 | tf_op jit(solution)/shard_map/ppermute | solution.py:22
  45.8 26.1 %collective-permute-start.1 = (bf16[8,4,8192]{2,1,0:T(4,128)(2,1)S(1)}, bf16[8,4,8192]{2,1,0:T(4,128)(2,1)}, u32[]{:S(2)}, u32[]{:S(2)}) collective-permute-start(bf16[8,4,8192]{2,1,0:T(4,128)(2,1)S(1)} %all-to-all-done), channel_id=1, source_target_pairs={{0,1},{1,2},{2,3},{3,0},{4,5},{5,6},{6,7},{7,4},{8,9},{9,10},{10,1... | collective-permute-start | bytes 1572872 | tf_op jit(solution)/shard_map/ppermute | solution.py:22
  49.9 67.4 %collective-permute-start.5 = (bf16[4096,256]{1,0:T(8,128)(2,1)}, bf16[4096,256]{1,0:T(8,128)(2,1)}, u32[]{:S(2)}, u32[]{:S(2)}) collective-permute-start(bf16[4096,256]{1,0:T(8,128)(2,1)} %broadcast_select_fusion), channel_id=1, source_target_pairs={{0,32},{32,0},{1,33},{33,1},{2,34},{34,2},{3,35},{35,3},{4,36},{36... | collective-permute-start | bytes 6291464 | tf_op jit(solution)/shard_map/ppermute | solution.py:17
  83.8 58.1 %all-to-all-start.3 = ((bf16[4,2,128,512]{2,3,1,0:T(8,128)(2,1)}), bf16[4,2,128,512]{2,3,1,0:T(8,128)(2,1)S(1)}, u32[]{:S(2)}, u32[]{:S(2)}) async-start(bf16[4,2,128,512]{2,3,1,0:T(8,128)(2,1)} %copy.27), calls=%async_computation.3 | async-start | bytes 2097152 | tf_op jit(solution)/shard_map/all_to_all | solution.py:89
  93.8 2.2 %copy-start.1 = (bf16[4096,256]{1,0:T(8,128)(2,1)S(1)}, bf16[4096,256]{1,0:T(8,128)(2,1)}, u32[]{:S(2)}) copy-start(bf16[4096,256]{1,0:T(8,128)(2,1)} %param.8) | copy-start | bytes 6291460
  117.3 14.9 %collective-permute-start.6 = (bf16[4096,256]{1,0:T(8,128)(2,1)}, bf16[4096,256]{1,0:T(8,128)(2,1)}, u32[]{:S(2)}, u32[]{:S(2)}) collective-permute-start(bf16[4096,256]{1,0:T(8,128)(2,1)} %collective-permute-done.5), channel_id=1, source_target_pairs={{0,64},{64,0},{1,65},{65,1},{2,66},{66,2},{3,67},{67,3},{4,68},{68... | collective-permute-start | bytes 6291464 | tf_op jit(solution)/shard_map/ppermute | solution.py:17
  123.9 4.2 %copy-start.4 = (bf16[2048,512]{1,0:T(8,128)(2,1)S(1)}, bf16[2048,512]{1,0:T(8,128)(2,1)}, u32[]{:S(2)}) copy-start(bf16[2048,512]{1,0:T(8,128)(2,1)} %all-gather.3.cloned.1.call-done) | copy-start | bytes 6291460
  128.4 3.4 %collective-permute-start.4 = (f32[128,512]{1,0:T(8,128)S(1)}, f32[128,512]{1,0:T(8,128)S(1)}, u32[]{:S(2)}, u32[]{:S(2)}) collective-permute-start(f32[128,512]{1,0:T(8,128)S(1)} %convolution_add_fusion.4), channel_id=1, source_target_pairs={{0,64},{64,0},{1,65},{65,1},{2,66},{66,2},{3,67},{67,3},{4,68},{68... | collective-permute-start | bytes 786440 | tf_op jit(solution)/shard_map/ppermute | solution.py:17
  132.2 2.4 %copy-start.3 = (bf16[4096,256]{1,0:T(8,128)(2,1)S(1)}, bf16[4096,256]{1,0:T(8,128)(2,1)}, u32[]{:S(2)}) copy-start(bf16[4096,256]{1,0:T(8,128)(2,1)} %param.7) | copy-start | bytes 6291460
  134.6 1.6 copy-start.2
  142.8 19.6 %all-to-all-start.2 = ((bf16[4,128,512]{2,1,0:T(8,128)(2,1)}), bf16[4,128,512]{2,1,0:T(8,128)(2,1)S(1)}, u32[]{:S(2)}, u32[]{:S(2)}) async-start(bf16[4,128,512]{2,1,0:T(8,128)(2,1)} %broadcast_in_dim.5), calls=%async_computation.2 | async-start | bytes 1048576 | tf_op jit(solution)/shard_map/all_to_all | solution.py:27
  149.0 16.9 %collective-permute-start.7 = (bf16[32,4096]{1,0:T(8,128)(2,1)}, bf16[32,4096]{1,0:T(8,128)(2,1)S(1)}, u32[]{:S(2)}, u32[]{:S(2)}) collective-permute-start(bf16[32,4096]{1,0:T(8,128)(2,1)} %get-tuple-element.6), channel_id=1, source_target_pairs={{0,3},{1,0},{2,1},{3,2},{4,7},{5,4},{6,5},{7,6},{8,11},{9,8},{10,9... | collective-permute-start | bytes 786440 | tf_op jit(solution)/shard_map/ppermute | solution.py:22
  153.3 12.6 %collective-permute-start.9 = (bf16[32,4096]{1,0:T(8,128)(2,1)}, bf16[32,4096]{1,0:T(8,128)(2,1)}, u32[]{:S(2)}, u32[]{:S(2)}) collective-permute-start(bf16[32,4096]{1,0:T(8,128)(2,1)} %get-tuple-element.7), channel_id=1, source_target_pairs={{0,1},{1,2},{2,3},{3,0},{4,5},{5,6},{6,7},{7,4},{8,9},{9,10},{10,1... | collective-permute-start | bytes 786440 | tf_op jit(solution)/shard_map/ppermute | solution.py:22
  155.2 13.3 %collective-permute-start.8 = (bf16[32,4096]{1,0:T(8,128)(2,1)}, bf16[32,4096]{1,0:T(8,128)(2,1)}, u32[]{:S(2)}, u32[]{:S(2)}) collective-permute-start(bf16[32,4096]{1,0:T(8,128)(2,1)} %get-tuple-element.8), channel_id=1, source_target_pairs={{0,2},{1,3},{2,0},{3,1},{4,6},{5,7},{6,4},{7,5},{8,10},{9,11},{10,... | collective-permute-start | bytes 786440 | tf_op jit(solution)/shard_map/ppermute | solution.py:22
  162.4 14.3 %collective-permute-start.10 = (bf16[4,128,512]{2,1,0:T(8,128)(2,1)S(1)}, bf16[4,128,512]{2,1,0:T(8,128)(2,1)}, u32[]{:S(2)}, u32[]{:S(2)}) collective-permute-start(bf16[4,128,512]{2,1,0:T(8,128)(2,1)S(1)} %all-to-all-done.2), channel_id=1, source_target_pairs={{0,64},{64,0},{1,65},{65,1},{2,66},{66,2},{3,67},{67,3},{4,68},{68... | collective-permute-start | bytes 1572872 | tf_op jit(solution)/shard_map/ppermute | solution.py:17
  170.5 15.2 %all-to-all-start.1 = ((bf16[8,4,4096]{2,1,0:T(4,128)(2,1)}), bf16[8,4,4096]{2,1,0:T(4,128)(2,1)S(1)}, u32[]{:S(2)}, u32[]{:S(2)}) async-start(bf16[8,4,4096]{2,1,0:T(4,128)(2,1)} %reshape.96), calls=%async_computation.1 | async-start | bytes 524288 | tf_op jit(solution)/shard_map/all_to_all | solution.py:85
  178.3 8.1 %collective-permute-start.11 = (bf16[256,512]{1,0:T(8,128)(2,1)S(1)}, bf16[256,512]{1,0:T(8,128)(2,1)S(1)}, u32[]{:S(2)}, u32[]{:S(2)}) collective-permute-start(bf16[256,512]{1,0:T(8,128)(2,1)S(1)} %slice.247), channel_id=1, source_target_pairs={{0,32},{32,0},{1,33},{33,1},{2,34},{34,2},{3,35},{35,3},{4,36},{36... | collective-permute-start | bytes 786440 | tf_op jit(solution)/shard_map/ppermute | solution.py:17
Sparse Core Ops, SparseCore 0:
  26.0 52.2 all-gather.2

commit v4 on v2

v4 whole, which is shorter than its diff:
```python
import functools

import jax
import jax.numpy as jnp
import numpy as np
from jax import lax
from jax.experimental import pallas as pl
from jax.experimental.pallas import tpu as pltpu
from jax.sharding import Mesh, PartitionSpec as P

BF16 = jnp.bfloat16
F32 = jnp.float32
DP = ("zh", "c")
TENSOR = ("zl", "y", "x")
NZ, NY, NX = 4, 8, 4
ROWS = 4
HALF = NX * NY * ROWS
D = 4096
HID = 256
FEATS = 512
STEPS = D // FEATS
PIECE = 2 * NY * ROWS


def contract(a, b, ca, cb):
    return lax.dot_general(a, b, (((ca,), (cb,)), ((), ())), preferred_element_type=F32)


def swap(value, axis):
    return lax.ppermute(value, axis, [(0, 1), (1, 0)])


def shift(value, axis, k):
    n = lax.axis_size(axis)
    return lax.ppermute(value, axis, [(i, (i + k) % n) for i in range(n)])


def forward_body(where, pick, r0, r1, r2, r3, gw, uw, mw, ow, dn, df, exch, dd, tok, cot, acc, dacc):
    step = pl.program_id(0)
    zh, far = step // 2, step % 2

    @pl.when(step == 0)
    def _():
        acc[...] = jnp.zeros_like(acc)
        dacc[...] = jnp.zeros_like(dacc)

    n = NY * ROWS
    for i, piece in enumerate((r0, r1, r2, r3)):
        rows = contract(pick[...], piece[...], 1, 0).astype(BF16)
        tok[i * n : (i + 1) * n] = rows[:n]
        cot[i * n : (i + 1) * n] = rows[n:]
    t = tok[...]
    for i, w in enumerate((gw, uw, mw, ow)):
        acc[:, i * HID : (i + 1) * HID] += contract(t, w[...], 1, 0)
    exch[zh, far] = cot[...]

    @pl.when(far == 0)
    def _():
        dacc[...] += contract(cot[...], dn[0], 1, 1)

    @pl.when(far == 1)
    def _():
        dacc[...] += contract(cot[...], df[0], 1, 1)

    @pl.when(step == STEPS - 1)
    def _():
        first, low = where[0] == 0, where[1] == 0
        pm, po = acc[:, 2 * HID : 3 * HID], acc[:, 3 * HID :]
        dl, dh = dacc[:, :HID], dacc[:, HID:]
        sides = (
            (acc[:, :HID], acc[:, HID : 2 * HID], jnp.where(low, dl, dh)),
            (jnp.where(first, pm, po), jnp.where(first, po, pm), jnp.where(low, dh, dl)),
        )
        for i, (gate, up, d_hidden) in enumerate(sides):
            sigma = jax.nn.sigmoid(gate)
            silu = gate * sigma
            hidden = (silu * up).astype(BF16)
            for z in range(NZ):
                exch[z, 2, :, i * HID : (i + 1) * HID] = hidden
            d_up = d_hidden * silu
            d_gate = d_hidden * up * sigma * (1.0 + gate * (1.0 - sigma))
            if i == 1:
                d_gate, d_up = jnp.where(first, d_gate, d_up), jnp.where(first, d_up, d_gate)
            dd[:, 2 * i * HID : (2 * i + 1) * HID] = d_gate.astype(BF16)
            dd[:, (2 * i + 1) * HID : (2 * i + 2) * HID] = d_up.astype(BF16)


def forward(where, pick, pieces, gw, uw, mw, ow, dn, df):
    def column(j, s):
        far = j % 2
        return (j // 2) * 2 + far + s[0] - 2 * far * s[0]

    whole = lambda *shape: pl.BlockSpec(shape, lambda j, s: (0,) * len(shape))
    piece = pl.BlockSpec((PIECE, FEATS), lambda j, s: (0, column(j, s)))
    weight = pl.BlockSpec((FEATS, HID), lambda j, s: (column(j, s), 0))
    down = pl.BlockSpec((1, 2 * HID, FEATS), lambda j, s: (j // 2, 0, 0))
    return pl.pallas_call(
        forward_body,
        grid_spec=pltpu.PrefetchScalarGridSpec(
            num_scalar_prefetch=1,
            grid=(STEPS,),
            in_specs=[whole(PIECE, PIECE)] + [piece] * 4 + [weight] * 4 + [down] * 2,
            out_specs=[whole(NZ, 3, HALF, FEATS), whole(HALF, 4 * HID)],
            scratch_shapes=[
                pltpu.VMEM((HALF, FEATS), BF16),
                pltpu.VMEM((HALF, FEATS), BF16),
                pltpu.VMEM((HALF, 4 * HID), F32),
                pltpu.VMEM((HALF, 2 * HID), F32),
            ],
        ),
        out_shape=[
            jax.ShapeDtypeStruct((NZ, 3, HALF, FEATS), BF16),
            jax.ShapeDtypeStruct((HALF, 4 * HID), BF16),
        ],
        compiler_params=pltpu.CompilerParams(vmem_limit_bytes=32 * 2**20),
        name="forward",
    )(where, pick, *pieces, gw, uw, mw, ow, dn, df)


def term_body(dd, gw, uw, mw, ow, o0, o1, o2, o3):
    total = contract(dd[:, :HID], gw[...], 1, 1)
    for i, w in ((1, uw), (2, mw), (3, ow)):
        total += contract(dd[:, i * HID : (i + 1) * HID], w[...], 1, 1)
    n = NY * ROWS
    for i, o in enumerate((o0, o1, o2, o3)):
        o[...] = total[i * n : (i + 1) * n].astype(BF16)


def term(dd, gw, uw, mw, ow):
    weight = pl.BlockSpec((FEATS, HID), lambda j: (j, 0))
    out = pl.BlockSpec((NY * ROWS, FEATS), lambda j: (0, j))
    return pl.pallas_call(
        term_body,
        grid=(STEPS,),
        in_specs=[pl.BlockSpec((HALF, 4 * HID), lambda j: (0, 0))] + [weight] * 4,
        out_specs=[out] * 4,
        out_shape=[jax.ShapeDtypeStruct((NY * ROWS, D), BF16)] * 4,
        compiler_params=pltpu.CompilerParams(vmem_limit_bytes=32 * 2**20),
        name="term",
    )(dd, gw, uw, mw, ow)


def grads_body(near, far, keep, send, acc):
    step = pl.program_id(0)

    @pl.when(step == 0)
    def _():
        acc[...] = jnp.zeros_like(acc)

    acc[...] += contract(near[0, 2], near[0, 0], 0, 0) + contract(far[0, 1], far[0, 0], 0, 0)

    @pl.when(step == NZ - 1)
    def _():
        keep[...] = acc[:HID]
        send[...] = acc[HID:].astype(BF16)


def grads(near, far):
    return pl.pallas_call(
        grads_body,
        grid=(NZ,),
        in_specs=[
            pl.BlockSpec((1, 3, HALF, FEATS), lambda j: (j, 0, 0, 0)),
            pl.BlockSpec((1, 2, HALF, FEATS), lambda j: (j, 0, 0, 0)),
        ],
        out_specs=[pl.BlockSpec((HID, FEATS), lambda j: (0, 0))] * 2,
        out_shape=[
            jax.ShapeDtypeStruct((HID, FEATS), F32),
            jax.ShapeDtypeStruct((HID, FEATS), BF16),
        ],
        scratch_shapes=[pltpu.VMEM((2 * HID, FEATS), F32)],
        compiler_params=pltpu.CompilerParams(vmem_limit_bytes=32 * 2**20),
        name="grads",
    )(near, far)


def pick_matrix():
    out = np.zeros((PIECE, PIECE), np.float32)
    for y in range(NY):
        for t in range(ROWS):
            out[y * ROWS + t, 2 * y * ROWS + t] = 1
            out[NY * ROWS + y * ROWS + t, (2 * y + 1) * ROWS + t] = 1
    return jnp.asarray(out, BF16)


def on_device(tokens, cotangent, gate_weight, up_weight, down_weight):
    core, zl = lax.axis_index("c"), lax.axis_index("zl")
    where = jnp.stack([core, zl]).astype(jnp.int32)

    picked = jnp.where(core == 0, gate_weight, up_weight)
    picked, tokens = lax.optimization_barrier((picked, tokens))
    mine = swap(picked, "zl")
    down_near = lax.all_gather(down_weight, ("zh", "zl"), axis=0).reshape(NZ, 2 * HID, FEATS)
    down_far = swap(down_near, "c")

    block = jnp.concatenate([tokens, cotangent], axis=0)
    block = jnp.broadcast_to(block[None], (NY, 2 * ROWS, D))
    block = lax.all_to_all(block, "y", 0, 0).reshape(PIECE, D)
    near_1, near_3 = shift(block, "x", 1), shift(block, "x", 3)
    late, mine = lax.optimization_barrier((block, mine))
    other = swap(mine, "c")
    pieces = (block, near_1, shift(late, "x", 2), near_3)

    exch, dd = forward(where, pick_matrix(), pieces, gate_weight, up_weight, mine, other, down_near, down_far)

    exch = lax.all_to_all(exch, "zh", 0, 0)
    parts = term(dd, gate_weight, up_weight, mine, other)
    total = parts[0].astype(F32)
    for k in (1, 2, 3):
        total = total + shift(parts[k], "x", -k).astype(F32)
    total = lax.all_to_all(total.astype(BF16).reshape(NY, ROWS, D), "y", 0, 0)
    input_grad = jnp.sum(total.astype(F32), axis=0).astype(BF16)

    keep, send = grads(exch, swap(exch[:, 1:], "c"))
    down_grad = keep + swap(send, "zl").astype(F32)
    return (input_grad, down_grad)


def solution(mesh):
    fine = Mesh(mesh.devices.reshape(NZ, 2, 2, NY, NX), ("zh", "c", "zl", "y", "x"))
    placed = (
        P((*DP, *TENSOR), None),
        P((*DP, *TENSOR), None),
        P(None, TENSOR),
        P(None, TENSOR),
        P(TENSOR, DP),
    )
    return jax.shard_map(
        on_device,
        mesh=fine,
        in_specs=placed,
        out_specs=(P((*DP, *TENSOR), None), P(TENSOR, DP)),
        check_vma=False,
    )
```

time: 201 us -> 216 us (1.075)
  starting transfers between devices: 47.7 us -> 69.7 us
  Pallas kernels: 0 us -> 20.3 us
  matrix products: 19.1 us -> 0 us
  blocking collectives: 38 us -> 22.2 us
  between operations: 0.87 us -> 14.3 us
  local copies, waits for them, and re-layouts: 20.1 us -> 11.3 us
  waiting for transfers between devices: 66 us -> 71.9 us
    all_to_all x5 -> x2, waiting for transfers between devices: 45.4 us -> 7.36 us  [the longest x1 7.36 us: on_device(): exch = lax.all_to_all(exch, 'zh', 0, 0)]
    ppermute x4 -> x5, waiting for transfers between devices: 20.6 us -> 43.3 us  [swap(): return lax.ppermute(value, axis, [(0, 1), (1, 0)])]
    ppermute x0 -> x6, waiting for transfers between devices: none -> 20.6 us  [shift(): return lax.ppermute(value, axis, [(i, (i + k) % n) for i in range(n)])]
    pallas_call x0 -> x3, Pallas kernels: none -> 20.3 us  [the longest x1 10 us: forward(): pl.pallas_call(forward_body, grid_spec=pltpu.PrefetchScalarGridSpec(num_s...]
    ppermute x4 -> x5, starting transfers between devices: 15.7 us -> 35.4 us  [swap(): return lax.ppermute(value, axis, [(0, 1), (1, 0)])]
    dot_general x10 -> x0, matrix products: 19.1 us -> none  [contract(): lax.dot_general(a, b, (((ca,), (cb,)), ((), ())), preferred_element_type=...]
    ppermute x0 -> x6, starting transfers between devices: none -> 18 us  [shift(): return lax.ppermute(value, axis, [(i, (i + k) % n) for i in range(n)])]
    all_to_all x5 -> x2, starting transfers between devices: 32 us -> 16.2 us  [the longest x1 9.38 us: on_device(): exch = lax.all_to_all(exch, 'zh', 0, 0)]
  transfers between devices with their start and end apart: 9 -> 14, of which waited for: 7 -> 6; matrix products, arithmetic and copies ran while one was open for 19% -> 3% of each run, Pallas kernels for 0% -> 5%
where the time goes in v4:
time: 216 us; the launch traced here: 215 us
  waiting for transfers between devices  71.9 us (33%)
  starting transfers between devices  69.7 us (32%)
  blocking collectives  22.2 us (10%)
  Pallas kernels  20.3 us (9%)
  between operations  14.3 us (7%)
  local copies, waits for them, and re-layouts  11.3 us (5%)
  other arithmetic  4.77 us (2%)
    ppermute x5, waiting for transfers between devices, swap(): return lax.ppermute(value, axis, [(0, 1), (1, 0)])  43.3 us
    ppermute x5, starting transfers between devices, swap(): return lax.ppermute(value, axis, [(0, 1), (1, 0)])  35.4 us
    all_to_all x1, blocking collectives, on_device(): block = lax.all_to_all(block, 'y', 0, 0).reshape(PIECE, D)  22.2 us
    ppermute x6, waiting for transfers between devices, shift(): return lax.ppermute(value, axis, [(i, (i + k) % n) for i in range(n)])  20.6 us
    ppermute x6, starting transfers between devices, shift(): return lax.ppermute(value, axis, [(i, (i + k) % n) for i in range(n)])  18 us
    pallas_call x1, Pallas kernels, forward(): pl.pallas_call(forward_body, grid_spec=pltpu.PrefetchScalarGridSpec(num_s...  10 us
    all_to_all x1, starting transfers between devices, on_device(): exch = lax.all_to_all(exch, 'zh', 0, 0)  9.38 us
    unnamed x20, local copies, waits for them, and re-layouts  8.15 us
  transfers between devices with their start and end apart: 14, of which 6 were waited for; matrix products, arithmetic and copies ran while one was open for 3% of the time, Pallas kernels for 5%

profile of v4, /device:TPU:1, one launch (start us, length us, event | category | flops | bytes accessed | tf_op | source)
XLA Modules:
  0.0 214.6 jit_solution(4868580811321331814)
XLA Ops:
  7.2 0.0 all-gather.3.cloned.1.call-start
  7.2 0.7 all-gather.3.cloned.1.call-update
  7.9 0.0 copy-start.8
  7.9 0.0 copy-start.9
  7.9 0.0 copy-start
  7.9 0.0 copy-start.7
  7.9 2.0 broadcast_select_fusion
  9.9 4.8 %collective-permute-start.1 = (bf16[4096,256]{1,0:T(8,128)(2,1)S(1)}, bf16[4096,256]{1,0:T(8,128)(2,1)}, u32[]{:S(2)}, u32[]{:S(2)}) collective-permute-start(bf16[4096,256]{1,0:T(8,128)(2,1)S(1)} %broadcast_select_fusion), channel_id=1, source_target_pairs={{0,32},{32,0},{1,33},{33,1},{2,34},{34,2},{3,35},{35,3},{4,36},{36... | collective-permute-start | bytes 6291464 | tf_op jit(solution)/shard_map/ppermute | solution.py:30
  14.8 0.0 copy-done.8
  14.8 0.0 copy-done.9
  14.9 22.2 %all_to_all.15 = bf16[8,8,4096]{2,1,0:T(8,128)(2,1)S(1)} all-to-all(bf16[8,8,4096]{2,1,0:T(8,128)(2,1)S(1)} %broadcast_in_dim.2), channel_id=1, replica_groups=mesh['zh'=4,'c'=2,'zl'=2,'y'=8,'x'=4] {'y'}, dimensions={0} | all-to-all | bytes 1048576 | tf_op jit(solution)/shard_map/all_to_all | solution.py:198
  37.1 38.5 %collective-permute-done.1.mw = bf16[4096,256]{1,0:T(8,128)(2,1)} collective-permute-done((bf16[4096,256]{1,0:T(8,128)(2,1)S(1)}, bf16[4096,256]{1,0:T(8,128)(2,1)}, u32[]{:S(2)}, u32[]{:S(2)}) %collective-permute-start.1) | collective-permute-done | bytes 2097184 | tf_op jit(solution)/shard_map/ppermute | solution.py:30
  75.6 7.4 %collective-permute-start.4 = (bf16[4096,256]{1,0:T(8,128)(2,1)}, bf16[4096,256]{1,0:T(8,128)(2,1)}, u32[]{:S(2)}, u32[]{:S(2)}) collective-permute-start(bf16[4096,256]{1,0:T(8,128)(2,1)} %collective-permute-done.1.mw), channel_id=1, source_target_pairs={{0,64},{64,0},{1,65},{65,1},{2,66},{66,2},{3,67},{67,3},{4,68},{68... | collective-permute-start | bytes 6291464 | tf_op jit(solution)/shard_map/ppermute | solution.py:30
  83.0 0.0 all-gather.3.cloned.1.call-done
  83.0 1.9 collective-permute-start.5
  85.0 4.4 %collective-permute-start.3 = (bf16[64,4096]{1,0:T(8,128)(2,1)S(1)}, bf16[64,4096]{1,0:T(8,128)(2,1)S(1)}, u32[]{:S(2)}, u32[]{:S(2)}) collective-permute-start(bf16[64,4096]{1,0:T(8,128)(2,1)S(1)} %bitcast.6), channel_id=1, source_target_pairs={{0,3},{1,0},{2,1},{3,2},{4,7},{5,4},{6,5},{7,6},{8,11},{9,8},{10,9... | collective-permute-start | bytes 1572872 | tf_op jit(solution)/shard_map/ppermute | solution.py:35
  89.4 1.9 collective-permute-start
  91.3 3.6 %collective-permute-start.2 = (bf16[64,4096]{1,0:T(8,128)(2,1)S(1)}, bf16[64,4096]{1,0:T(8,128)(2,1)}, u32[]{:S(2)}, u32[]{:S(2)}) collective-permute-start(bf16[64,4096]{1,0:T(8,128)(2,1)S(1)} %bitcast.8), channel_id=1, source_target_pairs={{0,2},{1,3},{2,0},{3,1},{4,6},{5,7},{6,4},{7,5},{8,10},{9,11},{10,... | collective-permute-start | bytes 1572872 | tf_op jit(solution)/shard_map/ppermute | solution.py:35
  94.9 0.1 pad_add_fusion.where
  95.0 5.9 %collective-permute-done.3.r3 = bf16[64,4096]{1,0:T(8,128)(2,1)S(1)} collective-permute-done((bf16[64,4096]{1,0:T(8,128)(2,1)S(1)}, bf16[64,4096]{1,0:T(8,128)(2,1)S(1)}, u32[]{:S(2)}, u32[]{:S(2)}) %collective-permute-start.3) | collective-permute-done | bytes 524320 | tf_op jit(solution)/shard_map/ppermute | solution.py:35
  100.9 5.3 %collective-permute-done.r1 = bf16[64,4096]{1,0:T(8,128)(2,1)} collective-permute-done((bf16[64,4096]{1,0:T(8,128)(2,1)S(1)}, bf16[64,4096]{1,0:T(8,128)(2,1)}, u32[]{:S(2)}, u32[]{:S(2)}) %collective-permute-start) | collective-permute-done | bytes 524320 | tf_op jit(solution)/shard_map/ppermute | solution.py:35
  106.2 9.4 %collective-permute-done.2.r2 = bf16[64,4096]{1,0:T(8,128)(2,1)} collective-permute-done((bf16[64,4096]{1,0:T(8,128)(2,1)S(1)}, bf16[64,4096]{1,0:T(8,128)(2,1)}, u32[]{:S(2)}, u32[]{:S(2)}) %collective-permute-start.2) | collective-permute-done | bytes 524320 | tf_op jit(solution)/shard_map/ppermute | solution.py:35
  115.6 0.0 collective-permute-done.4.ow
  115.6 0.0 collective-permute-done.5.df
  115.6 0.0 copy-done
  115.6 0.0 copy-done.7
  115.6 0.0 copy-start.1
  115.6 1.6 copy-done.1
  117.2 0.0 copy-start.3
  117.2 1.6 copy-done.3
  118.8 10.0 %forward.1 = (bf16[4,3,128,512]{3,2,1,0:T(8,128)(2,1)S(1)}, bf16[128,1024]{1,0:T(8,128)(2,1)S(1)}) custom-call(s32[2]{0:T(128)S(1)} %pad_add_fusion.where, bf16[64,64]{1,0:T(8,128)(2,1)S(1)} %copy-done.7, bf16[64,4096]{1,0:T(8,128)(2,1)S(1)} %bitcast.9, bf16[64,4096]{1,0:T(8,128)(2,1)} %collective-permute-done.r1, ...), custom_call_target="tpu_custom_call" | custom-call | tf_op jit(solution)/shard_map/forward/pallas_call | solution.py:97
  128.8 0.0 copy-start.4
  128.8 1.1 copy-done.4
  130.0 9.4 %all-to-all-start.2 = ((bf16[4,3,128,512]{3,2,1,0:T(8,128)(2,1)}), bf16[4,3,128,512]{3,2,1,0:T(8,128)(2,1)}, u32[]{:S(2)}, u32[]{:S(2)}) async-start(bf16[4,3,128,512]{3,2,1,0:T(8,128)(2,1)} %copy-done.4), calls=%async_computation.2 | async-start | bytes 3145728 | tf_op jit(solution)/shard_map/all_to_all | solution.py:206
  139.4 0.0 copy-start.2
  139.4 1.6 copy-done.2
  141.0 6.7 %term.1 = (bf16[32,4096]{1,0:T(8,128)(2,1)S(1)}, bf16[32,4096]{1,0:T(8,128)(2,1)S(1)}, bf16[32,4096]{1,0:T(8,128)(2,1)S(1)}, bf16[32,4096]{1,0:T(8,128)(2,1)S(1)}) custom-call(bf16[128,1024]{1,0:T(8,128)(2,1)S(1)} %get-tuple-element.18.dd, bf16[4096,256]{1,0:T(8,128)(2,1)S(1)} %copy-done, bf16[4096,256]{1,0:T(8,128)(2,1)S(1)} %copy-done.2, ...), custom_call_target="tpu_custom_call" | custom-call | tf_op jit(solution)/shard_map/term/pallas_call | solution.py:132
  147.7 1.9 collective-permute-start.6
  149.6 3.4 %collective-permute-start.7 = (bf16[32,4096]{1,0:T(8,128)(2,1)S(1)}, bf16[32,4096]{1,0:T(8,128)(2,1)S(1)}, u32[]{:S(2)}, u32[]{:S(2)}) collective-permute-start(bf16[32,4096]{1,0:T(8,128)(2,1)S(1)} %get-tuple-element.21), channel_id=1, source_target_pairs={{0,2},{1,3},{2,0},{3,1},{4,6},{5,7},{6,4},{7,5},{8,10},{9,11},{10,... | collective-permute-start | bytes 786440 | tf_op jit(solution)/shard_map/ppermute | solution.py:35
  153.1 2.8 %collective-permute-start.8 = (bf16[32,4096]{1,0:T(8,128)(2,1)S(1)}, bf16[32,4096]{1,0:T(8,128)(2,1)S(1)}, u32[]{:S(2)}, u32[]{:S(2)}) collective-permute-start(bf16[32,4096]{1,0:T(8,128)(2,1)S(1)} %get-tuple-element.22), channel_id=1, source_target_pairs={{0,1},{1,2},{2,3},{3,0},{4,5},{5,6},{6,7},{7,4},{8,9},{9,10},{10,1... | collective-permute-start | bytes 786440 | tf_op jit(solution)/shard_map/ppermute | solution.py:35
  155.8 7.4 %all-to-all-done.2.near = bf16[4,3,128,512]{3,2,1,0:T(8,128)(2,1)} async-done(((bf16[4,3,128,512]{3,2,1,0:T(8,128)(2,1)}), bf16[4,3,128,512]{3,2,1,0:T(8,128)(2,1)}, u32[]{:S(2)}, u32[]{:S(2)}) %all-to-all-start.2) | async-done | bytes 1572896 | tf_op jit(solution)/shard_map/all_to_all | solution.py:206
  163.2 2.3 %slice.4 = bf16[4,2,128,512]{3,2,1,0:T(8,128)(2,1)} slice(bf16[4,3,128,512]{3,2,1,0:T(8,128)(2,1)} %all-to-all-done.2.near), slice={[0:4], [1:3], [0:128], [0:512]} | slice | bytes 2097152 | tf_op jit(solution)/shard_map/slice | solution.py:214
  165.5 7.1 %collective-permute-start.9 = (bf16[4,2,128,512]{3,2,1,0:T(8,128)(2,1)}, bf16[4,2,128,512]{3,2,1,0:T(8,128)(2,1)S(1)}, u32[]{:S(2)}, u32[]{:S(2)}) collective-permute-start(bf16[4,2,128,512]{3,2,1,0:T(8,128)(2,1)} %slice.4), channel_id=1, source_target_pairs={{0,64},{64,0},{1,65},{65,1},{2,66},{66,2},{3,67},{67,3},{4,68},{68... | collective-permute-start | bytes 3145736 | tf_op jit(solution)/shard_map/ppermute | solution.py:30
  172.6 0.0 collective-permute-done.6
  172.6 0.0 collective-permute-done.7
  172.7 0.0 collective-permute-done.8
  172.7 0.1 add_convert_fusion
  172.8 0.8 reshape.16
  173.6 6.8 %all-to-all-start.1 = ((bf16[8,4,4096]{2,1,0:T(4,128)(2,1)}), bf16[8,4,4096]{2,1,0:T(4,128)(2,1)}, u32[]{:S(2)}, u32[]{:S(2)}) async-start(bf16[8,4,4096]{2,1,0:T(4,128)(2,1)} %reshape.16), calls=%async_computation.1 | async-start | bytes 524288 | tf_op jit(solution)/shard_map/all_to_all | solution.py:211
  180.5 0.0 collective-permute-done.9.far
  180.5 0.0 copy-start.5
  180.5 1.0 copy-done.5
  181.5 0.0 copy-start.6
  181.5 1.2 copy-done.6
  182.7 3.6 %grads.1 = (f32[256,512]{1,0:T(8,128)S(1)}, bf16[256,512]{1,0:T(8,128)(2,1)S(1)}) custom-call(bf16[4,3,128,512]{3,2,1,0:T(8,128)(2,1)} %all-to-all-done.2.near, bf16[4,2,128,512]{3,2,1,0:T(8,128)(2,1)S(1)} %copy-done.6), custom_call_target="tpu_custom_call" | custom-call | tf_op jit(solution)/shard_map/grads/pallas_call | solution.py:159
  186.3 14.1 %collective-permute-start.10 = (bf16[256,512]{1,0:T(8,128)(2,1)S(1)}, bf16[256,512]{1,0:T(8,128)(2,1)S(1)}, u32[]{:S(2)}, u32[]{:S(2)}) collective-permute-start(bf16[256,512]{1,0:T(8,128)(2,1)S(1)} %get-tuple-element.25), channel_id=1, source_target_pairs={{0,32},{32,0},{1,33},{33,1},{2,34},{34,2},{3,35},{35,3},{4,36},{36... | collective-permute-start | bytes 786440 | tf_op jit(solution)/shard_map/ppermute | solution.py:30
  200.4 0.0 all-to-all-done.1
  200.4 1.7 reduce_sum.12
  202.1 4.8 %collective-permute-done.10 = bf16[256,512]{1,0:T(8,128)(2,1)S(1)} collective-permute-done((bf16[256,512]{1,0:T(8,128)(2,1)S(1)}, bf16[256,512]{1,0:T(8,128)(2,1)S(1)}, u32[]{:S(2)}, u32[]{:S(2)}) %collective-permute-start.10) | collective-permute-done | bytes 262176 | tf_op jit(solution)/shard_map/ppermute | solution.py:30
  206.9 0.9 convert_add_fusion
  (2 shorter events, 0.1 us)
Async XLA Ops:
  7.2 75.9 %all-gather.3.cloned.1.call-start = ((), (), s32[]{:S(2)}) async-start(), calls=%async_computation.3 | async-start | bytes 2359296 | tf_op jit(solution)/shard_map/all_gather | solution.py:193
  7.9 6.9 %copy-start.8 = (bf16[4,4096]{1,0:T(4,128)(2,1)S(1)}, bf16[4,4096]{1,0:T(4,128)(2,1)}, u32[]{:S(2)}) copy-start(bf16[4,4096]{1,0:T(4,128)(2,1)} %param.7) | copy-start | bytes 98308
  7.9 6.9 %copy-start.9 = (bf16[4,4096]{1,0:T(4,128)(2,1)S(1)}, bf16[4,4096]{1,0:T(4,128)(2,1)}, u32[]{:S(2)}) copy-start(bf16[4,4096]{1,0:T(4,128)(2,1)} %param.6) | copy-start | bytes 98308
  7.9 107.7 %copy-start = (bf16[4096,256]{1,0:T(8,128)(2,1)S(1)}, bf16[4096,256]{1,0:T(8,128)(2,1)}, u32[]{:S(2)}) copy-start(bf16[4096,256]{1,0:T(8,128)(2,1)} %gw.3) | copy-start | bytes 6291460
  7.9 107.6 %copy-start.7 = (bf16[64,64]{1,0:T(8,128)(2,1)S(1)}, bf16[64,64]{1,0:T(8,128)(2,1)}, u32[]{:S(2)}) copy-start(bf16[64,64]{1,0:T(8,128)(2,1)} %constant.17.clone.pick) | copy-start | bytes 24580
  9.9 65.7 %collective-permute-start.1 = (bf16[4096,256]{1,0:T(8,128)(2,1)S(1)}, bf16[4096,256]{1,0:T(8,128)(2,1)}, u32[]{:S(2)}, u32[]{:S(2)}) collective-permute-start(bf16[4096,256]{1,0:T(8,128)(2,1)S(1)} %broadcast_select_fusion), channel_id=1, source_target_pairs={{0,32},{32,0},{1,33},{33,1},{2,34},{34,2},{3,35},{35,3},{4,36},{36... | collective-permute-start | bytes 6291464 | tf_op jit(solution)/shard_map/ppermute | solution.py:30
  75.6 39.9 %collective-permute-start.4 = (bf16[4096,256]{1,0:T(8,128)(2,1)}, bf16[4096,256]{1,0:T(8,128)(2,1)}, u32[]{:S(2)}, u32[]{:S(2)}) collective-permute-start(bf16[4096,256]{1,0:T(8,128)(2,1)} %collective-permute-done.1.mw), channel_id=1, source_target_pairs={{0,64},{64,0},{1,65},{65,1},{2,66},{66,2},{3,67},{67,3},{4,68},{68... | collective-permute-start | bytes 6291464 | tf_op jit(solution)/shard_map/ppermute | solution.py:30
  83.0 32.5 %collective-permute-start.5 = (bf16[4,512,512]{2,1,0:T(8,128)(2,1)}, bf16[4,512,512]{2,1,0:T(8,128)(2,1)}, u32[]{:S(2)}, u32[]{:S(2)}) collective-permute-start(bf16[4,512,512]{2,1,0:T(8,128)(2,1)} %bitcast.4), channel_id=1, source_target_pairs={{0,64},{64,0},{1,65},{65,1},{2,66},{66,2},{3,67},{67,3},{4,68},{68... | collective-permute-start | bytes 6291464 | tf_op jit(solution)/shard_map/ppermute | solution.py:30
  85.0 16.0 %collective-permute-start.3 = (bf16[64,4096]{1,0:T(8,128)(2,1)S(1)}, bf16[64,4096]{1,0:T(8,128)(2,1)S(1)}, u32[]{:S(2)}, u32[]{:S(2)}) collective-permute-start(bf16[64,4096]{1,0:T(8,128)(2,1)S(1)} %bitcast.6), channel_id=1, source_target_pairs={{0,3},{1,0},{2,1},{3,2},{4,7},{5,4},{6,5},{7,6},{8,11},{9,8},{10,9... | collective-permute-start | bytes 1572872 | tf_op jit(solution)/shard_map/ppermute | solution.py:35
  89.4 16.8 %collective-permute-start = (bf16[64,4096]{1,0:T(8,128)(2,1)S(1)}, bf16[64,4096]{1,0:T(8,128)(2,1)}, u32[]{:S(2)}, u32[]{:S(2)}) collective-permute-start(bf16[64,4096]{1,0:T(8,128)(2,1)S(1)} %bitcast.7), channel_id=1, source_target_pairs={{0,1},{1,2},{2,3},{3,0},{4,5},{5,6},{6,7},{7,4},{8,9},{9,10},{10,1... | collective-permute-start | bytes 1572872 | tf_op jit(solution)/shard_map/ppermute | solution.py:35
  91.3 24.3 %collective-permute-start.2 = (bf16[64,4096]{1,0:T(8,128)(2,1)S(1)}, bf16[64,4096]{1,0:T(8,128)(2,1)}, u32[]{:S(2)}, u32[]{:S(2)}) collective-permute-start(bf16[64,4096]{1,0:T(8,128)(2,1)S(1)} %bitcast.8), channel_id=1, source_target_pairs={{0,2},{1,3},{2,0},{3,1},{4,6},{5,7},{6,4},{7,5},{8,10},{9,11},{10,... | collective-permute-start | bytes 1572872 | tf_op jit(solution)/shard_map/ppermute | solution.py:35
  115.6 1.6 copy-start.1
  117.2 1.6 copy-start.3
  128.8 1.1 copy-start.4
  130.0 33.2 %all-to-all-start.2 = ((bf16[4,3,128,512]{3,2,1,0:T(8,128)(2,1)}), bf16[4,3,128,512]{3,2,1,0:T(8,128)(2,1)}, u32[]{:S(2)}, u32[]{:S(2)}) async-start(bf16[4,3,128,512]{3,2,1,0:T(8,128)(2,1)} %copy-done.4), calls=%async_computation.2 | async-start | bytes 3145728 | tf_op jit(solution)/shard_map/all_to_all | solution.py:206
  139.4 1.6 copy-start.2
  147.7 24.9 %collective-permute-start.6 = (bf16[32,4096]{1,0:T(8,128)(2,1)S(1)}, bf16[32,4096]{1,0:T(8,128)(2,1)S(1)}, u32[]{:S(2)}, u32[]{:S(2)}) collective-permute-start(bf16[32,4096]{1,0:T(8,128)(2,1)S(1)} %get-tuple-element.20), channel_id=1, source_target_pairs={{0,3},{1,0},{2,1},{3,2},{4,7},{5,4},{6,5},{7,6},{8,11},{9,8},{10,9... | collective-permute-start | bytes 786440 | tf_op jit(solution)/shard_map/ppermute | solution.py:35
  149.6 23.0 %collective-permute-start.7 = (bf16[32,4096]{1,0:T(8,128)(2,1)S(1)}, bf16[32,4096]{1,0:T(8,128)(2,1)S(1)}, u32[]{:S(2)}, u32[]{:S(2)}) collective-permute-start(bf16[32,4096]{1,0:T(8,128)(2,1)S(1)} %get-tuple-element.21), channel_id=1, source_target_pairs={{0,2},{1,3},{2,0},{3,1},{4,6},{5,7},{6,4},{7,5},{8,10},{9,11},{10,... | collective-permute-start | bytes 786440 | tf_op jit(solution)/shard_map/ppermute | solution.py:35
  153.1 19.6 %collective-permute-start.8 = (bf16[32,4096]{1,0:T(8,128)(2,1)S(1)}, bf16[32,4096]{1,0:T(8,128)(2,1)S(1)}, u32[]{:S(2)}, u32[]{:S(2)}) collective-permute-start(bf16[32,4096]{1,0:T(8,128)(2,1)S(1)} %get-tuple-element.22), channel_id=1, source_target_pairs={{0,1},{1,2},{2,3},{3,0},{4,5},{5,6},{6,7},{7,4},{8,9},{9,10},{10,1... | collective-permute-start | bytes 786440 | tf_op jit(solution)/shard_map/ppermute | solution.py:35
  165.5 15.0 %collective-permute-start.9 = (bf16[4,2,128,512]{3,2,1,0:T(8,128)(2,1)}, bf16[4,2,128,512]{3,2,1,0:T(8,128)(2,1)S(1)}, u32[]{:S(2)}, u32[]{:S(2)}) collective-permute-start(bf16[4,2,128,512]{3,2,1,0:T(8,128)(2,1)} %slice.4), channel_id=1, source_target_pairs={{0,64},{64,0},{1,65},{65,1},{2,66},{66,2},{3,67},{67,3},{4,68},{68... | collective-permute-start | bytes 3145736 | tf_op jit(solution)/shard_map/ppermute | solution.py:30
  173.6 26.8 %all-to-all-start.1 = ((bf16[8,4,4096]{2,1,0:T(4,128)(2,1)}), bf16[8,4,4096]{2,1,0:T(4,128)(2,1)}, u32[]{:S(2)}, u32[]{:S(2)}) async-start(bf16[8,4,4096]{2,1,0:T(4,128)(2,1)} %reshape.16), calls=%async_computation.1 | async-start | bytes 524288 | tf_op jit(solution)/shard_map/all_to_all | solution.py:211
  180.5 1.0 copy-start.5
  181.5 1.2 copy-start.6
  186.3 20.6 %collective-permute-start.10 = (bf16[256,512]{1,0:T(8,128)(2,1)S(1)}, bf16[256,512]{1,0:T(8,128)(2,1)S(1)}, u32[]{:S(2)}, u32[]{:S(2)}) collective-permute-start(bf16[256,512]{1,0:T(8,128)(2,1)S(1)} %get-tuple-element.25), channel_id=1, source_target_pairs={{0,32},{32,0},{1,33},{33,1},{2,34},{34,2},{3,35},{35,3},{4,36},{36... | collective-permute-start | bytes 786440 | tf_op jit(solution)/shard_map/ppermute | solution.py:30
Sparse Core Ops, SparseCore 0:
  10.1 61.7 all-gather.2

commit v5 on v4

--- a/solution.py
+++ b/solution.py
@@ -35,32 +35,70 @@
     return lax.ppermute(value, axis, [(i, (i + k) % n) for i in range(n)])
 
 
-def forward_body(where, pick, r0, r1, r2, r3, gw, uw, mw, ow, dn, df, exch, dd, tok, cot, acc, dacc):
+def neighbours(value):
+    at = lambda zh, c, zl: ((zh % NZ) * 2 + c) * 2 + zl
+    pairs = []
+    for zh in range(NZ):
+        pairs += [(at(zh, 0, 0), at(zh, 0, 1)), (at(zh, 0, 1), at(zh, 0, 0))]
+        pairs += [(at(zh, 1, 1), at(zh + 1, 1, 0)), (at(zh + 1, 1, 0), at(zh, 1, 1))]
+    return lax.ppermute(value, ("zh", "c", "zl"), pairs)
+
+
+def split_body(where, pick, r0, r1, r2, r3, tok, cot):
     step = pl.program_id(0)
-    zh, far = step // 2, step % 2
-
-    @pl.when(step == 0)
-    def _():
-        acc[...] = jnp.zeros_like(acc)
-        dacc[...] = jnp.zeros_like(dacc)
-
     n = NY * ROWS
     for i, piece in enumerate((r0, r1, r2, r3)):
         rows = contract(pick[...], piece[...], 1, 0).astype(BF16)
         tok[i * n : (i + 1) * n] = rows[:n]
-        cot[i * n : (i + 1) * n] = rows[n:]
+        cot[0, 0, i * n : (i + 1) * n] = rows[n:]
+
+
+def split(where, pick, pieces):
+    piece = pl.BlockSpec((PIECE, FEATS), lambda j, s: (0, j))
+    return pl.pallas_call(
+        split_body,
+        grid_spec=pltpu.PrefetchScalarGridSpec(
+            num_scalar_prefetch=1,
+            grid=(STEPS,),
+            in_specs=[pl.BlockSpec((PIECE, PIECE), lambda j, s: (0, 0))] + [piece] * 4,
+            out_specs=[
+                pl.BlockSpec((HALF, FEATS), lambda j, s: (0, j)),
+                pl.BlockSpec((1, 1, HALF, FEATS), lambda j, s: (j // 2, flip(j % 2, s[0]), 0, 0)),
+            ],
+        ),
+        out_shape=[
+            jax.ShapeDtypeStruct((HALF, D), BF16),
+            jax.ShapeDtypeStruct((NZ, 2, HALF, FEATS), BF16),
+        ],
+        compiler_params=pltpu.CompilerParams(vmem_limit_bytes=32 * 2**20),
+        name="split",
+    )(where, pick, *pieces)
+
+
+def flip(a, b):
+    return a + b - 2 * a * b
+
+
+def forward_body(where, tok, cot, gw, uw, mw, ow, dn, df, hid, dd, acc, dacc):
+    step = pl.program_id(0)
+    far = step % 2
+
+    @pl.when(step == 0)
+    def _():
+        acc[...] = jnp.zeros_like(acc)
+        dacc[...] = jnp.zeros_like(dacc)
+
     t = tok[...]
     for i, w in enumerate((gw, uw, mw, ow)):
         acc[:, i * HID : (i + 1) * HID] += contract(t, w[...], 1, 0)
-    exch[zh, far] = cot[...]
 
     @pl.when(far == 0)
     def _():
-        dacc[...] += contract(cot[...], dn[0], 1, 1)
+        dacc[...] += contract(cot[0, 0], dn[0], 1, 1)
 
     @pl.when(far == 1)
     def _():
-        dacc[...] += contract(cot[...], df[0], 1, 1)
+        dacc[...] += contract(cot[0, 0], df[0], 1, 1)
 
     @pl.when(step == STEPS - 1)
     def _():
@@ -74,9 +112,7 @@
         for i, (gate, up, d_hidden) in enumerate(sides):
             sigma = jax.nn.sigmoid(gate)
             silu = gate * sigma
-            hidden = (silu * up).astype(BF16)
-            for z in range(NZ):
-                exch[z, 2, :, i * HID : (i + 1) * HID] = hidden
+            hid[:, i * HID : (i + 1) * HID] = (silu * up).astype(BF16)
             d_up = d_hidden * silu
             d_gate = d_hidden * up * sigma * (1.0 + gate * (1.0 - sigma))
             if i == 1:
@@ -85,13 +121,10 @@
             dd[:, (2 * i + 1) * HID : (2 * i + 2) * HID] = d_up.astype(BF16)
 
 
-def forward(where, pick, pieces, gw, uw, mw, ow, dn, df):
+def forward(where, tok, cot, gw, uw, mw, ow, dn, df):
     def column(j, s):
-        far = j % 2
-        return (j // 2) * 2 + far + s[0] - 2 * far * s[0]
-
-    whole = lambda *shape: pl.BlockSpec(shape, lambda j, s: (0,) * len(shape))
-    piece = pl.BlockSpec((PIECE, FEATS), lambda j, s: (0, column(j, s)))
+        return (j // 2) * 2 + flip(j % 2, s[0])
+
     weight = pl.BlockSpec((FEATS, HID), lambda j, s: (column(j, s), 0))
     down = pl.BlockSpec((1, 2 * HID, FEATS), lambda j, s: (j // 2, 0, 0))
     return pl.pallas_call(
@@ -99,22 +132,28 @@
         grid_spec=pltpu.PrefetchScalarGridSpec(
             num_scalar_prefetch=1,
             grid=(STEPS,),
-            in_specs=[whole(PIECE, PIECE)] + [piece] * 4 + [weight] * 4 + [down] * 2,
-            out_specs=[whole(NZ, 3, HALF, FEATS), whole(HALF, 4 * HID)],
+            in_specs=[
+                pl.BlockSpec((HALF, FEATS), lambda j, s: (0, column(j, s))),
+                pl.BlockSpec((1, 1, HALF, FEATS), lambda j, s: (j // 2, j % 2, 0, 0)),
+            ]
+            + [weight] * 4
+            + [down] * 2,
+            out_specs=[
+                pl.BlockSpec((HALF, 2 * HID), lambda j, s: (0, 0)),
+                pl.BlockSpec((HALF, 4 * HID), lambda j, s: (0, 0)),
+            ],
             scratch_shapes=[
-                pltpu.VMEM((HALF, FEATS), BF16),
-                pltpu.VMEM((HALF, FEATS), BF16),
                 pltpu.VMEM((HALF, 4 * HID), F32),
                 pltpu.VMEM((HALF, 2 * HID), F32),
             ],
         ),
         out_shape=[
-            jax.ShapeDtypeStruct((NZ, 3, HALF, FEATS), BF16),
+            jax.ShapeDtypeStruct((HALF, 2 * HID), BF16),
             jax.ShapeDtypeStruct((HALF, 4 * HID), BF16),
         ],
         compiler_params=pltpu.CompilerParams(vmem_limit_bytes=32 * 2**20),
         name="forward",
-    )(where, pick, *pieces, gw, uw, mw, ow, dn, df)
+    )(where, tok, cot, gw, uw, mw, ow, dn, df)
 
 
 def term_body(dd, gw, uw, mw, ow, o0, o1, o2, o3):
@@ -140,14 +179,14 @@
     )(dd, gw, uw, mw, ow)
 
 
-def grads_body(near, far, keep, send, acc):
+def grads_body(hn, cn, hf, cf, keep, send, acc):
     step = pl.program_id(0)
 
     @pl.when(step == 0)
     def _():
         acc[...] = jnp.zeros_like(acc)
 
-    acc[...] += contract(near[0, 2], near[0, 0], 0, 0) + contract(far[0, 1], far[0, 0], 0, 0)
+    acc[...] += contract(hn[0], cn[0, 0], 0, 0) + contract(hf[0], cf[0], 0, 0)
 
     @pl.when(step == NZ - 1)
     def _():
@@ -155,14 +194,12 @@
         send[...] = acc[HID:].astype(BF16)
 
 
-def grads(near, far):
+def grads(hid_near, cot_near, hid_far, cot_far):
+    plain = pl.BlockSpec((1, HALF, FEATS), lambda j: (j, 0, 0))
     return pl.pallas_call(
         grads_body,
         grid=(NZ,),
-        in_specs=[
-            pl.BlockSpec((1, 3, HALF, FEATS), lambda j: (j, 0, 0, 0)),
-            pl.BlockSpec((1, 2, HALF, FEATS), lambda j: (j, 0, 0, 0)),
-        ],
+        in_specs=[plain, pl.BlockSpec((1, 1, HALF, FEATS), lambda j: (j, 0, 0, 0)), plain, plain],
         out_specs=[pl.BlockSpec((HID, FEATS), lambda j: (0, 0))] * 2,
         out_shape=[
             jax.ShapeDtypeStruct((HID, FEATS), F32),
@@ -171,7 +208,7 @@
         scratch_shapes=[pltpu.VMEM((2 * HID, FEATS), F32)],
         compiler_params=pltpu.CompilerParams(vmem_limit_bytes=32 * 2**20),
         name="grads",
-    )(near, far)
+    )(hid_near, cot_near, hid_far, cot_far)
 
 
 def pick_matrix():
@@ -189,7 +226,7 @@
 
     picked = jnp.where(core == 0, gate_weight, up_weight)
     picked, tokens = lax.optimization_barrier((picked, tokens))
-    mine = swap(picked, "zl")
+    mine = neighbours(picked)
     down_near = lax.all_gather(down_weight, ("zh", "zl"), axis=0).reshape(NZ, 2 * HID, FEATS)
     down_far = swap(down_near, "c")
 
@@ -201,9 +238,12 @@
     other = swap(mine, "c")
     pieces = (block, near_1, shift(late, "x", 2), near_3)
 
-    exch, dd = forward(where, pick_matrix(), pieces, gate_weight, up_weight, mine, other, down_near, down_far)
-
-    exch = lax.all_to_all(exch, "zh", 0, 0)
+    tok, cot = split(where, pick_matrix(), pieces)
+    cot_x = lax.all_to_all(cot, "zh", 0, 0)
+    cot_far = swap(cot_x[:, 1], "c")
+    hidden, dd = forward(where, tok, cot, gate_weight, up_weight, mine, other, down_near, down_far)
+
+    hid_near = lax.all_to_all(jnp.broadcast_to(hidden[None], (NZ, *hidden.shape)), "zh", 0, 0)
     parts = term(dd, gate_weight, up_weight, mine, other)
     total = parts[0].astype(F32)
     for k in (1, 2, 3):
@@ -211,7 +251,7 @@
     total = lax.all_to_all(total.astype(BF16).reshape(NY, ROWS, D), "y", 0, 0)
     input_grad = jnp.sum(total.astype(F32), axis=0).astype(BF16)
 
-    keep, send = grads(exch, swap(exch[:, 1:], "c"))
+    keep, send = grads(hid_near, cot_x, swap(hid_near, "c"), cot_far)
     down_grad = keep + swap(send, "zl").astype(F32)
     return (input_grad, down_grad)
 

time: 216 us -> 186 us (0.86)
  waiting for transfers between devices: 71.9 us -> 37.3 us
  Pallas kernels: 20.3 us -> 25.2 us
  blocking collectives: 22.2 us -> 19.4 us
    ppermute x5, waiting for transfers between devices: 43.3 us -> 4.52 us  [swap(): return lax.ppermute(value, axis, [(0, 1), (1, 0)])]
    ppermute x0 -> x1, waiting for transfers between devices: none -> 17.2 us  [neighbours(): return lax.ppermute(value, ('zh', 'c', 'zl'), pairs)]
    ppermute x6, waiting for transfers between devices: 20.6 us -> 8.07 us  [shift(): return lax.ppermute(value, axis, [(i, (i + k) % n) for i in range(n)])]
    ppermute x0 -> x1, starting transfers between devices: none -> 11.5 us  [neighbours(): return lax.ppermute(value, ('zh', 'c', 'zl'), pairs)]
    ppermute x5, starting transfers between devices: 35.4 us -> 24 us  [swap(): return lax.ppermute(value, axis, [(0, 1), (1, 0)])]
    pallas_call x1 -> x2, Pallas kernels: 3.56 us -> 8.64 us  [the longest x1 5.27 us: split(): pl.pallas_call(split_body, grid_spec=pltpu.PrefetchScalarGridSpec(num_sca...]
    all_to_all x1, blocking collectives: 22.2 us -> 19.4 us  [on_device(): block = lax.all_to_all(block, 'y', 0, 0).reshape(PIECE, D)]
    unnamed x20 -> x26, local copies, waits for them, and re-layouts: 8.15 us -> 10.9 us
  transfers between devices with their start and end apart: 14 -> 16, of which waited for: 6 -> 4; matrix products, arithmetic and copies ran while one was open for 3% -> 3% of each run, Pallas kernels for 5% -> 14%
where the time goes in v5:
time: 186 us; the launch traced here: 184 us
  starting transfers between devices  70.5 us (38%)
  waiting for transfers between devices  37.3 us (20%)
  Pallas kernels  25.2 us (14%)
  blocking collectives  19.4 us (10%)
  between operations  14.4 us (8%)
  local copies, waits for them, and re-layouts  12.6 us (7%)
  other arithmetic  4.7 us (3%)
    ppermute x5, starting transfers between devices, swap(): return lax.ppermute(value, axis, [(0, 1), (1, 0)])  24 us
    all_to_all x1, blocking collectives, on_device(): block = lax.all_to_all(block, 'y', 0, 0).reshape(PIECE, D)  19.4 us
    ppermute x6, starting transfers between devices, shift(): return lax.ppermute(value, axis, [(i, (i + k) % n) for i in range(n)])  18.3 us
    ppermute x1, waiting for transfers between devices, neighbours(): return lax.ppermute(value, ('zh', 'c', 'zl'), pairs)  17.2 us
    ppermute x1, starting transfers between devices, neighbours(): return lax.ppermute(value, ('zh', 'c', 'zl'), pairs)  11.5 us
    unnamed x26, local copies, waits for them, and re-layouts  10.9 us
    pallas_call x1, Pallas kernels, forward(): pl.pallas_call(forward_body, grid_spec=pltpu.PrefetchScalarGridSpec(num_s...  9.01 us
    ppermute x6, waiting for transfers between devices, shift(): return lax.ppermute(value, axis, [(i, (i + k) % n) for i in range(n)])  8.07 us
  transfers between devices with their start and end apart: 16, of which 4 were waited for; matrix products, arithmetic and copies ran while one was open for 3% of the time, Pallas kernels for 14%

profile of v5, /device:TPU:1, one launch (start us, length us, event | category | flops | bytes accessed | tf_op | source)
XLA Modules:
  0.0 184.1 jit_solution(18198231055402372404)
XLA Ops:
  7.2 0.0 all-gather.3.cloned.1.call-start
  7.2 0.7 all-gather.3.cloned.1.call-update
  7.9 0.0 copy-start.11
  7.9 0.0 copy-start.12
  7.9 0.0 copy-start.10
  7.9 1.8 broadcast_select_fusion
  9.8 11.5 %collective-permute-start.1 = (bf16[4096,256]{1,0:T(8,128)(2,1)S(1)}, bf16[4096,256]{1,0:T(8,128)(2,1)}, u32[]{:S(2)}, u32[]{:S(2)}) collective-permute-start(bf16[4096,256]{1,0:T(8,128)(2,1)S(1)} %broadcast_select_fusion), channel_id=1, source_target_pairs={{0,32},{32,0},{96,192},{192,96},{128,160},{160,128},{224,320},{320... | collective-permute-start | bytes 6291464 | tf_op jit(solution)/shard_map/ppermute | solution.py:44
  21.3 0.0 copy-done.11
  21.3 0.0 copy-done.12
  21.4 19.4 %all_to_all.20 = bf16[8,8,4096]{2,1,0:T(8,128)(2,1)S(1)} all-to-all(bf16[8,8,4096]{2,1,0:T(8,128)(2,1)S(1)} %broadcast_in_dim.4), channel_id=1, replica_groups=mesh['zh'=4,'c'=2,'zl'=2,'y'=8,'x'=4] {'y'}, dimensions={0} | all-to-all | bytes 1048576 | tf_op jit(solution)/shard_map/all_to_all | solution.py:235
  40.8 3.1 %collective-permute-start = (bf16[64,4096]{1,0:T(8,128)(2,1)S(1)}, bf16[64,4096]{1,0:T(8,128)(2,1)S(1)}, u32[]{:S(2)}, u32[]{:S(2)}) collective-permute-start(bf16[64,4096]{1,0:T(8,128)(2,1)S(1)} %bitcast.8), channel_id=1, source_target_pairs={{0,1},{1,2},{2,3},{3,0},{4,5},{5,6},{6,7},{7,4},{8,9},{9,10},{10,1... | collective-permute-start | bytes 1572872 | tf_op jit(solution)/shard_map/ppermute | solution.py:35
  43.9 3.4 %collective-permute-start.3 = (bf16[64,4096]{1,0:T(8,128)(2,1)S(1)}, bf16[64,4096]{1,0:T(8,128)(2,1)}, u32[]{:S(2)}, u32[]{:S(2)}) collective-permute-start(bf16[64,4096]{1,0:T(8,128)(2,1)S(1)} %bitcast.9), channel_id=1, source_target_pairs={{0,3},{1,0},{2,1},{3,2},{4,7},{5,4},{6,5},{7,6},{8,11},{9,8},{10,9... | collective-permute-start | bytes 1572872 | tf_op jit(solution)/shard_map/ppermute | solution.py:35
  47.3 17.2 %collective-permute-done.1.mw = bf16[4096,256]{1,0:T(8,128)(2,1)} collective-permute-done((bf16[4096,256]{1,0:T(8,128)(2,1)S(1)}, bf16[4096,256]{1,0:T(8,128)(2,1)}, u32[]{:S(2)}, u32[]{:S(2)}) %collective-permute-start.1) | collective-permute-done | bytes 2097184 | tf_op jit(solution)/shard_map/ppermute | solution.py:44
  64.4 4.6 %collective-permute-start.2 = (bf16[64,4096]{1,0:T(8,128)(2,1)S(1)}, bf16[64,4096]{1,0:T(8,128)(2,1)}, u32[]{:S(2)}, u32[]{:S(2)}) collective-permute-start(bf16[64,4096]{1,0:T(8,128)(2,1)S(1)} %bitcast.10), channel_id=1, source_target_pairs={{0,2},{1,3},{2,0},{3,1},{4,6},{5,7},{6,4},{7,5},{8,10},{9,11},{10,... | collective-permute-start | bytes 1572872 | tf_op jit(solution)/shard_map/ppermute | solution.py:35
  69.1 1.9 %collective-permute-start.4 = (bf16[4096,256]{1,0:T(8,128)(2,1)}, bf16[4096,256]{1,0:T(8,128)(2,1)}, u32[]{:S(2)}, u32[]{:S(2)}) collective-permute-start(bf16[4096,256]{1,0:T(8,128)(2,1)} %collective-permute-done.1.mw), channel_id=1, source_target_pairs={{0,64},{64,0},{1,65},{65,1},{2,66},{66,2},{3,67},{67,3},{4,68},{68... | collective-permute-start | bytes 6291464 | tf_op jit(solution)/shard_map/ppermute | solution.py:30
  71.0 0.0 all-gather.3.cloned.1.call-done
  71.1 2.4 %collective-permute-start.5 = (bf16[4,512,512]{2,1,0:T(8,128)(2,1)}, bf16[4,512,512]{2,1,0:T(8,128)(2,1)}, u32[]{:S(2)}, u32[]{:S(2)}) collective-permute-start(bf16[4,512,512]{2,1,0:T(8,128)(2,1)} %bitcast.12), channel_id=1, source_target_pairs={{0,64},{64,0},{1,65},{65,1},{2,66},{66,2},{3,67},{67,3},{4,68},{68... | collective-permute-start | bytes 6291464 | tf_op jit(solution)/shard_map/ppermute | solution.py:30
  73.5 0.1 pad_add_fusion.where
  73.6 0.0 collective-permute-done.r1
  73.6 0.0 collective-permute-done.3.r3
  73.6 8.1 %collective-permute-done.2.r2 = bf16[64,4096]{1,0:T(8,128)(2,1)} collective-permute-done((bf16[64,4096]{1,0:T(8,128)(2,1)S(1)}, bf16[64,4096]{1,0:T(8,128)(2,1)}, u32[]{:S(2)}, u32[]{:S(2)}) %collective-permute-start.2) | collective-permute-done | bytes 524320 | tf_op jit(solution)/shard_map/ppermute | solution.py:35
  81.6 0.0 copy-done.10
  81.6 5.3 %split.1 = (bf16[128,4096]{1,0:T(8,128)(2,1)S(1)}, bf16[4,2,128,512]{3,2,1,0:T(8,128)(2,1)S(1)}) custom-call(s32[2]{0:T(128)S(1)} %pad_add_fusion.where, bf16[64,64]{1,0:T(8,128)(2,1)S(1)} %copy-done.10, bf16[64,4096]{1,0:T(8,128)(2,1)S(1)} %bitcast.11, bf16[64,4096]{1,0:T(8,128)(2,1)S(1)} %collective-permute-done.r1, ...), custom_call_target="tpu_custom_call" | custom-call | tf_op jit(solution)/shard_map/split/pallas_call | solution.py:58
  86.9 0.0 copy-start.3
  86.9 1.0 copy-done.3
  87.9 1.0 copy-done.6
  88.9 3.5 %all-to-all-start.3 = ((bf16[4,2,128,512]{3,2,1,0:T(8,128)(2,1)}), bf16[4,2,128,512]{3,2,1,0:T(8,128)(2,1)S(1)}, u32[]{:S(2)}, u32[]{:S(2)}) async-start(bf16[4,2,128,512]{3,2,1,0:T(8,128)(2,1)} %copy-done.3), calls=%async_computation.3 | async-start | bytes 2097152 | tf_op jit(solution)/shard_map/all_to_all | solution.py:242
  92.5 0.0 collective-permute-done.4.ow
  92.5 0.0 collective-permute-done.5.df
  92.5 0.0 copy-done
  92.5 0.0 copy-start.1
  92.5 1.6 copy-done.1
  94.1 1.2 copy-done.4
  95.3 1.6 copy-done.5
  96.9 1.2 copy-done.7
  98.1 9.0 %forward.1 = (bf16[128,512]{1,0:T(8,128)(2,1)S(1)}, bf16[128,1024]{1,0:T(8,128)(2,1)S(1)}) custom-call(s32[2]{0:T(128)S(1)} %pad_add_fusion.where, bf16[128,4096]{1,0:T(8,128)(2,1)S(1)} %copy-done.7, bf16[4,2,128,512]{3,2,1,0:T(8,128)(2,1)S(1)} %copy-done.4, bf16[4096,256]{1,0:T(8,128)(2,1)S(1)} %copy-done, bf16[4096,256]{1,0:T(8,128)(2,1)S(1)} %copy-done.1, ...), custom_call_target="tpu_custom_call" | custom-call | tf_op jit(solution)/shard_map/forward/pallas_call | solution.py:130
  107.1 0.0 copy-start.8
  107.1 0.7 copy-done.8
  107.8 6.8 %all-to-all-done.3.cn = bf16[4,2,128,512]{3,2,1,0:T(8,128)(2,1)S(1)} async-done(((bf16[4,2,128,512]{3,2,1,0:T(8,128)(2,1)}), bf16[4,2,128,512]{3,2,1,0:T(8,128)(2,1)S(1)}, u32[]{:S(2)}, u32[]{:S(2)}) %all-to-all-start.3) | async-done | bytes 1048608 | tf_op jit(solution)/shard_map/all_to_all | solution.py:242
  114.6 0.8 broadcast_in_dim.5
  115.5 6.4 %all-to-all-start.2 = ((bf16[4,128,512]{2,1,0:T(8,128)(2,1)}), bf16[4,128,512]{2,1,0:T(8,128)(2,1)}, u32[]{:S(2)}, u32[]{:S(2)}) async-start(bf16[4,128,512]{2,1,0:T(8,128)(2,1)} %broadcast_in_dim.5), calls=%async_computation.2 | async-start | bytes 1048576 | tf_op jit(solution)/shard_map/all_to_all | solution.py:246
  121.8 1.6 copy-done.2
  123.4 0.9 copy-done.9
  124.4 7.6 %term.1 = (bf16[32,4096]{1,0:T(8,128)(2,1)S(1)}, bf16[32,4096]{1,0:T(8,128)(2,1)}, bf16[32,4096]{1,0:T(8,128)(2,1)}, bf16[32,4096]{1,0:T(8,128)(2,1)}) custom-call(bf16[128,1024]{1,0:T(8,128)(2,1)S(1)} %copy-done.9, bf16[4096,256]{1,0:T(8,128)(2,1)S(1)} %copy-done, bf16[4096,256]{1,0:T(8,128)(2,1)S(1)} %copy-done.2, ...), custom_call_target="tpu_custom_call" | custom-call | tf_op jit(solution)/shard_map/term/pallas_call | solution.py:171
  131.9 1.9 %collective-permute-start.6 = (bf16[32,4096]{1,0:T(8,128)(2,1)}, bf16[32,4096]{1,0:T(8,128)(2,1)S(1)}, u32[]{:S(2)}, u32[]{:S(2)}) collective-permute-start(bf16[32,4096]{1,0:T(8,128)(2,1)} %get-tuple-element.24), channel_id=1, source_target_pairs={{0,3},{1,0},{2,1},{3,2},{4,7},{5,4},{6,5},{7,6},{8,11},{9,8},{10,9... | collective-permute-start | bytes 786440 | tf_op jit(solution)/shard_map/ppermute | solution.py:35
  133.8 1.9 %collective-permute-start.7 = (bf16[32,4096]{1,0:T(8,128)(2,1)}, bf16[32,4096]{1,0:T(8,128)(2,1)}, u32[]{:S(2)}, u32[]{:S(2)}) collective-permute-start(bf16[32,4096]{1,0:T(8,128)(2,1)} %get-tuple-element.25), channel_id=1, source_target_pairs={{0,2},{1,3},{2,0},{3,1},{4,6},{5,7},{6,4},{7,5},{8,10},{9,11},{10,... | collective-permute-start | bytes 786440 | tf_op jit(solution)/shard_map/ppermute | solution.py:35
  135.8 3.4 %collective-permute-start.8 = (bf16[32,4096]{1,0:T(8,128)(2,1)}, bf16[32,4096]{1,0:T(8,128)(2,1)}, u32[]{:S(2)}, u32[]{:S(2)}) collective-permute-start(bf16[32,4096]{1,0:T(8,128)(2,1)} %get-tuple-element.26), channel_id=1, source_target_pairs={{0,1},{1,2},{2,3},{3,0},{4,5},{5,6},{6,7},{7,4},{8,9},{9,10},{10,1... | collective-permute-start | bytes 786440 | tf_op jit(solution)/shard_map/ppermute | solution.py:35
  139.2 7.4 %collective-permute-start.10 = (bf16[4,128,512]{2,1,0:T(8,128)(2,1)S(1)}, bf16[4,128,512]{2,1,0:T(8,128)(2,1)S(1)}, u32[]{:S(2)}, u32[]{:S(2)}) collective-permute-start(bf16[4,128,512]{2,1,0:T(8,128)(2,1)S(1)} %slice_bitcast_fusion), channel_id=1, source_target_pairs={{0,64},{64,0},{1,65},{65,1},{2,66},{66,2},{3,67},{67,3},{4,68},{68... | collective-permute-start | bytes 1572872 | tf_op jit(solution)/shard_map/ppermute | solution.py:30
  146.6 0.0 all-to-all-done.2.hn
  146.6 1.9 %collective-permute-start.9 = (bf16[4,128,512]{2,1,0:T(8,128)(2,1)}, bf16[4,128,512]{2,1,0:T(8,128)(2,1)S(1)}, u32[]{:S(2)}, u32[]{:S(2)}) collective-permute-start(bf16[4,128,512]{2,1,0:T(8,128)(2,1)} %all-to-all-done.2.hn), channel_id=1, source_target_pairs={{0,64},{64,0},{1,65},{65,1},{2,66},{66,2},{3,67},{67,3},{4,68},{68... | collective-permute-start | bytes 1572872 | tf_op jit(solution)/shard_map/ppermute | solution.py:30
  148.5 0.0 collective-permute-done.6
  148.5 0.0 collective-permute-done.7
  148.6 0.0 collective-permute-done.8
  148.6 1.2 add_convert_fusion
  149.7 0.8 reshape.17
  150.5 6.8 %all-to-all-start.1 = ((bf16[8,4,4096]{2,1,0:T(4,128)(2,1)}), bf16[8,4,4096]{2,1,0:T(4,128)(2,1)S(1)}, u32[]{:S(2)}, u32[]{:S(2)}) async-start(bf16[8,4,4096]{2,1,0:T(4,128)(2,1)} %reshape.17), calls=%async_computation.1 | async-start | bytes 524288 | tf_op jit(solution)/shard_map/all_to_all | solution.py:251
  157.4 0.0 collective-permute-done.10.cf
  157.4 0.0 collective-permute-done.9.hf
  157.4 3.4 %grads.1 = (f32[256,512]{1,0:T(8,128)S(1)}, bf16[256,512]{1,0:T(8,128)(2,1)S(1)}) custom-call(bf16[4,128,512]{2,1,0:T(8,128)(2,1)} %all-to-all-done.2.hn, bf16[4,2,128,512]{3,2,1,0:T(8,128)(2,1)S(1)} %all-to-all-done.3.cn, bf16[4,128,512]{2,1,0:T(8,128)(2,1)S(1)} %collective-permute-done.9.hf, bf16[4,128,512]{2,1,0:T(8,128)(2,1)S(1)} %collective-permute-done.10.cf), custom_call_target="tpu_custom_call" | custom-call | tf_op jit(solution)/shard_map/grads/pallas_call | solution.py:199
  160.8 10.3 %collective-permute-start.11 = (bf16[256,512]{1,0:T(8,128)(2,1)S(1)}, bf16[256,512]{1,0:T(8,128)(2,1)S(1)}, u32[]{:S(2)}, u32[]{:S(2)}) collective-permute-start(bf16[256,512]{1,0:T(8,128)(2,1)S(1)} %get-tuple-element.29), channel_id=1, source_target_pairs={{0,32},{32,0},{1,33},{33,1},{2,34},{34,2},{3,35},{35,3},{4,36},{36... | collective-permute-start | bytes 786440 | tf_op jit(solution)/shard_map/ppermute | solution.py:30
  171.1 0.0 all-to-all-done.1
  171.1 0.7 reduce_sum.12
  171.8 4.5 %collective-permute-done.11 = bf16[256,512]{1,0:T(8,128)(2,1)S(1)} collective-permute-done((bf16[256,512]{1,0:T(8,128)(2,1)S(1)}, bf16[256,512]{1,0:T(8,128)(2,1)S(1)}, u32[]{:S(2)}, u32[]{:S(2)}) %collective-permute-start.11) | collective-permute-done | bytes 262176 | tf_op jit(solution)/shard_map/ppermute | solution.py:30
  176.3 0.9 convert_add_fusion
  (10 shorter events, 0.1 us)
Async XLA Ops:
  7.2 63.9 %all-gather.3.cloned.1.call-start = ((), (), s32[]{:S(2)}) async-start(), calls=%async_computation.4 | async-start | bytes 2359296 | tf_op jit(solution)/shard_map/all_gather | solution.py:230
  7.9 13.4 %copy-start.11 = (bf16[4,4096]{1,0:T(4,128)(2,1)S(1)}, bf16[4,4096]{1,0:T(4,128)(2,1)}, u32[]{:S(2)}) copy-start(bf16[4,4096]{1,0:T(4,128)(2,1)} %param.7) | copy-start | bytes 98308
  7.9 13.4 %copy-start.12 = (bf16[4,4096]{1,0:T(4,128)(2,1)S(1)}, bf16[4,4096]{1,0:T(4,128)(2,1)}, u32[]{:S(2)}) copy-start(bf16[4,4096]{1,0:T(4,128)(2,1)} %param.6) | copy-start | bytes 98308
  7.9 73.7 %copy-start.10 = (bf16[64,64]{1,0:T(8,128)(2,1)S(1)}, bf16[64,64]{1,0:T(8,128)(2,1)}, u32[]{:S(2)}) copy-start(bf16[64,64]{1,0:T(8,128)(2,1)} %constant.17.clone.pick) | copy-start | bytes 24580
  9.8 54.7 %collective-permute-start.1 = (bf16[4096,256]{1,0:T(8,128)(2,1)S(1)}, bf16[4096,256]{1,0:T(8,128)(2,1)}, u32[]{:S(2)}, u32[]{:S(2)}) collective-permute-start(bf16[4096,256]{1,0:T(8,128)(2,1)S(1)} %broadcast_select_fusion), channel_id=1, source_target_pairs={{0,32},{32,0},{96,192},{192,96},{128,160},{160,128},{224,320},{320... | collective-permute-start | bytes 6291464 | tf_op jit(solution)/shard_map/ppermute | solution.py:44
  40.8 32.8 %collective-permute-start = (bf16[64,4096]{1,0:T(8,128)(2,1)S(1)}, bf16[64,4096]{1,0:T(8,128)(2,1)S(1)}, u32[]{:S(2)}, u32[]{:S(2)}) collective-permute-start(bf16[64,4096]{1,0:T(8,128)(2,1)S(1)} %bitcast.8), channel_id=1, source_target_pairs={{0,1},{1,2},{2,3},{3,0},{4,5},{5,6},{6,7},{7,4},{8,9},{9,10},{10,1... | collective-permute-start | bytes 1572872 | tf_op jit(solution)/shard_map/ppermute | solution.py:35
  43.9 29.7 %collective-permute-start.3 = (bf16[64,4096]{1,0:T(8,128)(2,1)S(1)}, bf16[64,4096]{1,0:T(8,128)(2,1)}, u32[]{:S(2)}, u32[]{:S(2)}) collective-permute-start(bf16[64,4096]{1,0:T(8,128)(2,1)S(1)} %bitcast.9), channel_id=1, source_target_pairs={{0,3},{1,0},{2,1},{3,2},{4,7},{5,4},{6,5},{7,6},{8,11},{9,8},{10,9... | collective-permute-start | bytes 1572872 | tf_op jit(solution)/shard_map/ppermute | solution.py:35
  64.4 17.2 %collective-permute-start.2 = (bf16[64,4096]{1,0:T(8,128)(2,1)S(1)}, bf16[64,4096]{1,0:T(8,128)(2,1)}, u32[]{:S(2)}, u32[]{:S(2)}) collective-permute-start(bf16[64,4096]{1,0:T(8,128)(2,1)S(1)} %bitcast.10), channel_id=1, source_target_pairs={{0,2},{1,3},{2,0},{3,1},{4,6},{5,7},{6,4},{7,5},{8,10},{9,11},{10,... | collective-permute-start | bytes 1572872 | tf_op jit(solution)/shard_map/ppermute | solution.py:35
  69.1 23.4 %collective-permute-start.4 = (bf16[4096,256]{1,0:T(8,128)(2,1)}, bf16[4096,256]{1,0:T(8,128)(2,1)}, u32[]{:S(2)}, u32[]{:S(2)}) collective-permute-start(bf16[4096,256]{1,0:T(8,128)(2,1)} %collective-permute-done.1.mw), channel_id=1, source_target_pairs={{0,64},{64,0},{1,65},{65,1},{2,66},{66,2},{3,67},{67,3},{4,68},{68... | collective-permute-start | bytes 6291464 | tf_op jit(solution)/shard_map/ppermute | solution.py:30
  71.1 21.4 %collective-permute-start.5 = (bf16[4,512,512]{2,1,0:T(8,128)(2,1)}, bf16[4,512,512]{2,1,0:T(8,128)(2,1)}, u32[]{:S(2)}, u32[]{:S(2)}) collective-permute-start(bf16[4,512,512]{2,1,0:T(8,128)(2,1)} %bitcast.12), channel_id=1, source_target_pairs={{0,64},{64,0},{1,65},{65,1},{2,66},{66,2},{3,67},{67,3},{4,68},{68... | collective-permute-start | bytes 6291464 | tf_op jit(solution)/shard_map/ppermute | solution.py:30
  73.5 18.9 %copy-start = (bf16[4096,256]{1,0:T(8,128)(2,1)S(1)}, bf16[4096,256]{1,0:T(8,128)(2,1)}, u32[]{:S(2)}) copy-start(bf16[4096,256]{1,0:T(8,128)(2,1)} %gw.3) | copy-start | bytes 6291460
  86.9 1.0 copy-start.3
  87.9 1.0 copy-start.6
  88.9 25.7 %all-to-all-start.3 = ((bf16[4,2,128,512]{3,2,1,0:T(8,128)(2,1)}), bf16[4,2,128,512]{3,2,1,0:T(8,128)(2,1)S(1)}, u32[]{:S(2)}, u32[]{:S(2)}) async-start(bf16[4,2,128,512]{3,2,1,0:T(8,128)(2,1)} %copy-done.3), calls=%async_computation.3 | async-start | bytes 2097152 | tf_op jit(solution)/shard_map/all_to_all | solution.py:242
  92.5 1.6 copy-start.1
  94.1 1.2 copy-start.4
  95.3 1.6 copy-start.5
  96.9 1.2 copy-start.7
  107.1 0.7 copy-start.8
  115.5 31.1 %all-to-all-start.2 = ((bf16[4,128,512]{2,1,0:T(8,128)(2,1)}), bf16[4,128,512]{2,1,0:T(8,128)(2,1)}, u32[]{:S(2)}, u32[]{:S(2)}) async-start(bf16[4,128,512]{2,1,0:T(8,128)(2,1)} %broadcast_in_dim.5), calls=%async_computation.2 | async-start | bytes 1048576 | tf_op jit(solution)/shard_map/all_to_all | solution.py:246
  121.8 1.6 copy-start.2
  123.4 0.9 copy-start.9
  131.9 16.6 %collective-permute-start.6 = (bf16[32,4096]{1,0:T(8,128)(2,1)}, bf16[32,4096]{1,0:T(8,128)(2,1)S(1)}, u32[]{:S(2)}, u32[]{:S(2)}) collective-permute-start(bf16[32,4096]{1,0:T(8,128)(2,1)} %get-tuple-element.24), channel_id=1, source_target_pairs={{0,3},{1,0},{2,1},{3,2},{4,7},{5,4},{6,5},{7,6},{8,11},{9,8},{10,9... | collective-permute-start | bytes 786440 | tf_op jit(solution)/shard_map/ppermute | solution.py:35
  133.8 14.7 %collective-permute-start.7 = (bf16[32,4096]{1,0:T(8,128)(2,1)}, bf16[32,4096]{1,0:T(8,128)(2,1)}, u32[]{:S(2)}, u32[]{:S(2)}) collective-permute-start(bf16[32,4096]{1,0:T(8,128)(2,1)} %get-tuple-element.25), channel_id=1, source_target_pairs={{0,2},{1,3},{2,0},{3,1},{4,6},{5,7},{6,4},{7,5},{8,10},{9,11},{10,... | collective-permute-start | bytes 786440 | tf_op jit(solution)/shard_map/ppermute | solution.py:35
  135.8 12.8 %collective-permute-start.8 = (bf16[32,4096]{1,0:T(8,128)(2,1)}, bf16[32,4096]{1,0:T(8,128)(2,1)}, u32[]{:S(2)}, u32[]{:S(2)}) collective-permute-start(bf16[32,4096]{1,0:T(8,128)(2,1)} %get-tuple-element.26), channel_id=1, source_target_pairs={{0,1},{1,2},{2,3},{3,0},{4,5},{5,6},{6,7},{7,4},{8,9},{9,10},{10,1... | collective-permute-start | bytes 786440 | tf_op jit(solution)/shard_map/ppermute | solution.py:35
  139.2 18.2 %collective-permute-start.10 = (bf16[4,128,512]{2,1,0:T(8,128)(2,1)S(1)}, bf16[4,128,512]{2,1,0:T(8,128)(2,1)S(1)}, u32[]{:S(2)}, u32[]{:S(2)}) collective-permute-start(bf16[4,128,512]{2,1,0:T(8,128)(2,1)S(1)} %slice_bitcast_fusion), channel_id=1, source_target_pairs={{0,64},{64,0},{1,65},{65,1},{2,66},{66,2},{3,67},{67,3},{4,68},{68... | collective-permute-start | bytes 1572872 | tf_op jit(solution)/shard_map/ppermute | solution.py:30
  146.6 10.8 %collective-permute-start.9 = (bf16[4,128,512]{2,1,0:T(8,128)(2,1)}, bf16[4,128,512]{2,1,0:T(8,128)(2,1)S(1)}, u32[]{:S(2)}, u32[]{:S(2)}) collective-permute-start(bf16[4,128,512]{2,1,0:T(8,128)(2,1)} %all-to-all-done.2.hn), channel_id=1, source_target_pairs={{0,64},{64,0},{1,65},{65,1},{2,66},{66,2},{3,67},{67,3},{4,68},{68... | collective-permute-start | bytes 1572872 | tf_op jit(solution)/shard_map/ppermute | solution.py:30
  150.5 20.6 %all-to-all-start.1 = ((bf16[8,4,4096]{2,1,0:T(4,128)(2,1)}), bf16[8,4,4096]{2,1,0:T(4,128)(2,1)S(1)}, u32[]{:S(2)}, u32[]{:S(2)}) async-start(bf16[8,4,4096]{2,1,0:T(4,128)(2,1)} %reshape.17), calls=%async_computation.1 | async-start | bytes 524288 | tf_op jit(solution)/shard_map/all_to_all | solution.py:251
  160.8 15.6 %collective-permute-start.11 = (bf16[256,512]{1,0:T(8,128)(2,1)S(1)}, bf16[256,512]{1,0:T(8,128)(2,1)S(1)}, u32[]{:S(2)}, u32[]{:S(2)}) collective-permute-start(bf16[256,512]{1,0:T(8,128)(2,1)S(1)} %get-tuple-element.29), channel_id=1, source_target_pairs={{0,32},{32,0},{1,33},{33,1},{2,34},{34,2},{3,35},{35,3},{4,36},{36... | collective-permute-start | bytes 786440 | tf_op jit(solution)/shard_map/ppermute | solution.py:30
Sparse Core Ops, SparseCore 0:
  10.1 54.1 all-gather.2

commit v6 on v5

--- a/solution.py
+++ b/solution.py
@@ -67,12 +67,20 @@
             ],
         ),
         out_shape=[
-            jax.ShapeDtypeStruct((HALF, D), BF16),
-            jax.ShapeDtypeStruct((NZ, 2, HALF, FEATS), BF16),
+            hbm((HALF, D), BF16),
+            hbm((NZ, 2, HALF, FEATS), BF16),
         ],
         compiler_params=pltpu.CompilerParams(vmem_limit_bytes=32 * 2**20),
         name="split",
     )(where, pick, *pieces)
+
+
+def hbm(shape, dtype):
+    return pltpu.MemorySpace.HBM(shape, dtype)
+
+
+def pinned(*values):
+    return [pltpu.with_memory_space_constraint(v, pltpu.MemorySpace.HBM) for v in values]
 
 
 def flip(a, b):
@@ -153,40 +161,42 @@
         ],
         compiler_params=pltpu.CompilerParams(vmem_limit_bytes=32 * 2**20),
         name="forward",
-    )(where, tok, cot, gw, uw, mw, ow, dn, df)
-
-
-def term_body(dd, gw, uw, mw, ow, o0, o1, o2, o3):
+    )(where, *pinned(tok, cot, gw, uw, mw), ow, *pinned(dn), df)
+
+
+def term_body(where, dd, gw, uw, mw, ow, out):
     total = contract(dd[:, :HID], gw[...], 1, 1)
     for i, w in ((1, uw), (2, mw), (3, ow)):
         total += contract(dd[:, i * HID : (i + 1) * HID], w[...], 1, 1)
     n = NY * ROWS
-    for i, o in enumerate((o0, o1, o2, o3)):
-        o[...] = total[i * n : (i + 1) * n].astype(BF16)
-
-
-def term(dd, gw, uw, mw, ow):
-    weight = pl.BlockSpec((FEATS, HID), lambda j: (j, 0))
-    out = pl.BlockSpec((NY * ROWS, FEATS), lambda j: (0, j))
+    for i in range(NX):
+        out[(where[2] + NX - i) % NX] = total[i * n : (i + 1) * n].astype(BF16)
+
+
+def term(where, dd, gw, uw, mw, ow):
+    weight = pl.BlockSpec((FEATS, HID), lambda j, s: (j, 0))
     return pl.pallas_call(
         term_body,
-        grid=(STEPS,),
-        in_specs=[pl.BlockSpec((HALF, 4 * HID), lambda j: (0, 0))] + [weight] * 4,
-        out_specs=[out] * 4,
-        out_shape=[jax.ShapeDtypeStruct((NY * ROWS, D), BF16)] * 4,
+        grid_spec=pltpu.PrefetchScalarGridSpec(
+            num_scalar_prefetch=1,
+            grid=(STEPS,),
+            in_specs=[pl.BlockSpec((HALF, 4 * HID), lambda j, s: (0, 0))] + [weight] * 4,
+            out_specs=pl.BlockSpec((NX, NY * ROWS, FEATS), lambda j, s: (0, 0, j)),
+        ),
+        out_shape=jax.ShapeDtypeStruct((NX, NY * ROWS, D), BF16),
         compiler_params=pltpu.CompilerParams(vmem_limit_bytes=32 * 2**20),
         name="term",
-    )(dd, gw, uw, mw, ow)
-
-
-def grads_body(hn, cn, hf, cf, keep, send, acc):
+    )(where, dd, *pinned(gw, uw, mw), ow)
+
+
+def grads_body(h, cn, cf, keep, send, acc):
     step = pl.program_id(0)
 
     @pl.when(step == 0)
     def _():
         acc[...] = jnp.zeros_like(acc)
 
-    acc[...] += contract(hn[0], cn[0, 0], 0, 0) + contract(hf[0], cf[0], 0, 0)
+    acc[...] += contract(h[0, 0], cn[0, 0], 0, 0) + contract(h[0, 1], cf[0], 0, 0)
 
     @pl.when(step == NZ - 1)
     def _():
@@ -194,12 +204,15 @@
         send[...] = acc[HID:].astype(BF16)
 
 
-def grads(hid_near, cot_near, hid_far, cot_far):
-    plain = pl.BlockSpec((1, HALF, FEATS), lambda j: (j, 0, 0))
+def grads(hidden, cot_near, cot_far):
     return pl.pallas_call(
         grads_body,
         grid=(NZ,),
-        in_specs=[plain, pl.BlockSpec((1, 1, HALF, FEATS), lambda j: (j, 0, 0, 0)), plain, plain],
+        in_specs=[
+            pl.BlockSpec((1, 2, HALF, 2 * HID), lambda j: (j, 0, 0, 0)),
+            pl.BlockSpec((1, 1, HALF, FEATS), lambda j: (j, 0, 0, 0)),
+            pl.BlockSpec((1, HALF, FEATS), lambda j: (j, 0, 0)),
+        ],
         out_specs=[pl.BlockSpec((HID, FEATS), lambda j: (0, 0))] * 2,
         out_shape=[
             jax.ShapeDtypeStruct((HID, FEATS), F32),
@@ -208,7 +221,7 @@
         scratch_shapes=[pltpu.VMEM((2 * HID, FEATS), F32)],
         compiler_params=pltpu.CompilerParams(vmem_limit_bytes=32 * 2**20),
         name="grads",
-    )(hid_near, cot_near, hid_far, cot_far)
+    )(hidden, cot_near, cot_far)
 
 
 def pick_matrix():
@@ -221,37 +234,31 @@
 
 
 def on_device(tokens, cotangent, gate_weight, up_weight, down_weight):
-    core, zl = lax.axis_index("c"), lax.axis_index("zl")
-    where = jnp.stack([core, zl]).astype(jnp.int32)
+    core = lax.axis_index("c")
+    where = jnp.stack([core, lax.axis_index("zl"), lax.axis_index("x")]).astype(jnp.int32)
 
     picked = jnp.where(core == 0, gate_weight, up_weight)
     picked, tokens = lax.optimization_barrier((picked, tokens))
     mine = neighbours(picked)
     down_near = lax.all_gather(down_weight, ("zh", "zl"), axis=0).reshape(NZ, 2 * HID, FEATS)
-    down_far = swap(down_near, "c")
 
     block = jnp.concatenate([tokens, cotangent], axis=0)
     block = jnp.broadcast_to(block[None], (NY, 2 * ROWS, D))
     block = lax.all_to_all(block, "y", 0, 0).reshape(PIECE, D)
-    near_1, near_3 = shift(block, "x", 1), shift(block, "x", 3)
-    late, mine = lax.optimization_barrier((block, mine))
-    other = swap(mine, "c")
-    pieces = (block, near_1, shift(late, "x", 2), near_3)
-
+    pieces = [block] + [shift(block, "x", k) for k in (1, 2, 3)]
     tok, cot = split(where, pick_matrix(), pieces)
     cot_x = lax.all_to_all(cot, "zh", 0, 0)
+    tok, mine, down_near = lax.optimization_barrier((tok, mine, down_near))
+    other, down_far = swap(mine, "c"), swap(down_near, "c")
     cot_far = swap(cot_x[:, 1], "c")
     hidden, dd = forward(where, tok, cot, gate_weight, up_weight, mine, other, down_near, down_far)
 
-    hid_near = lax.all_to_all(jnp.broadcast_to(hidden[None], (NZ, *hidden.shape)), "zh", 0, 0)
-    parts = term(dd, gate_weight, up_weight, mine, other)
-    total = parts[0].astype(F32)
-    for k in (1, 2, 3):
-        total = total + shift(parts[k], "x", -k).astype(F32)
-    total = lax.all_to_all(total.astype(BF16).reshape(NY, ROWS, D), "y", 0, 0)
-    input_grad = jnp.sum(total.astype(F32), axis=0).astype(BF16)
-
-    keep, send = grads(hid_near, cot_x, swap(hid_near, "c"), cot_far)
+    hidden = lax.all_gather(jnp.stack([hidden, swap(hidden, "c")]), "zh", axis=0)
+    parts = term(where, dd, gate_weight, up_weight, mine, other)
+    parts = lax.all_to_all(parts.reshape(NX * NY, ROWS, D), ("x", "y"), 0, 0)
+    input_grad = jnp.sum(parts.astype(F32), axis=0).astype(BF16)
+
+    keep, send = grads(hidden, cot_x, cot_far)
     down_grad = keep + swap(send, "zl").astype(F32)
     return (input_grad, down_grad)
 

time: 186 us -> 160 us (0.86)
  starting transfers between devices: 70.5 us -> 48.9 us
  local copies, waits for them, and re-layouts: 12.6 us -> 4.53 us
  waiting for transfers between devices: 37.3 us -> 39.3 us
    ppermute x1, waiting for transfers between devices: 17.2 us -> 0.01 us  [neighbours(): return lax.ppermute(value, ('zh', 'c', 'zl'), pairs)]
    all_gather x0 -> x1, waiting for transfers between devices: none -> 16 us  [on_device(): lax.all_gather(jnp.stack([hidden, swap(hidden, 'c')]), 'zh', axis=0)]
    ppermute x5, starting transfers between devices: 24 us -> 13.3 us  [swap(): return lax.ppermute(value, axis, [(0, 1), (1, 0)])]
    unnamed x26 -> x10, local copies, waits for them, and re-layouts: 10.9 us -> 2.2 us
    ppermute x6 -> x3, waiting for transfers between devices: 8.07 us -> 16.1 us  [shift(): return lax.ppermute(value, axis, [(i, (i + k) % n) for i in range(n)])]
    ppermute x6 -> x3, starting transfers between devices: 18.3 us -> 10.5 us  [shift(): return lax.ppermute(value, axis, [(i, (i + k) % n) for i in range(n)])]
    all_to_all x2 -> x1, starting transfers between devices: 13.2 us -> 6.28 us  [on_device(): parts = lax.all_to_all(parts.reshape(NX * NY, ROWS, D), ('x', 'y'), 0, 0)]
    all_to_all x1, waiting for transfers between devices: 6.8 us -> 0.01 us  [on_device(): cot_x = lax.all_to_all(cot, 'zh', 0, 0)]
  transfers between devices with their start and end apart: 16 -> 13, of which waited for: 4 -> 7; matrix products, arithmetic and copies ran while one was open for 3% -> 5% of each run, Pallas kernels for 14% -> 16%
where the time goes in v6:
time: 160 us; the launch traced here: 157 us
  starting transfers between devices  48.9 us (31%)
  waiting for transfers between devices  39.3 us (25%)
  Pallas kernels  24.7 us (15%)
  blocking collectives  19.4 us (12%)
  between operations  14.2 us (9%)
  other arithmetic  5.92 us (4%)
  local copies, waits for them, and re-layouts  4.53 us (3%)
    all_to_all x1, blocking collectives, on_device(): block = lax.all_to_all(block, 'y', 0, 0).reshape(PIECE, D)  19.4 us
    ppermute x3, waiting for transfers between devices, shift(): return lax.ppermute(value, axis, [(i, (i + k) % n) for i in range(n)])  16.1 us
    all_gather x1, waiting for transfers between devices, on_device(): lax.all_gather(jnp.stack([hidden, swap(hidden, 'c')]), 'zh', axis=0)  16 us
    ppermute x5, starting transfers between devices, swap(): return lax.ppermute(value, axis, [(0, 1), (1, 0)])  13.3 us
    ppermute x1, starting transfers between devices, neighbours(): return lax.ppermute(value, ('zh', 'c', 'zl'), pairs)  11.5 us
    ppermute x3, starting transfers between devices, shift(): return lax.ppermute(value, axis, [(i, (i + k) % n) for i in range(n)])  10.5 us
    pallas_call x1, Pallas kernels, forward(): pl.pallas_call(forward_body, grid_spec=pltpu.PrefetchScalarGridSpec(num_s...  10.3 us
    pallas_call x1, Pallas kernels, term(): pl.pallas_call(term_body, grid_spec=pltpu.PrefetchScalarGridSpec(num_scal...  7.65 us
  transfers between devices with their start and end apart: 13, of which 7 were waited for; matrix products, arithmetic and copies ran while one was open for 5% of the time, Pallas kernels for 16%

profile of v6, /device:TPU:1, one launch (start us, length us, event | category | flops | bytes accessed | tf_op | source)
XLA Modules:
  0.0 157.1 jit_solution(8943917155013723217)
XLA Ops:
  7.2 0.0 all-gather.5.cloned.1.call-start
  7.2 0.7 all-gather.5.cloned.1.call-update
  7.9 0.0 copy-start.3
  7.9 0.0 copy-start.4
  7.9 0.0 copy-start.2
  7.9 3.2 %broadcast_select_fusion = bf16[4096,256]{1,0:T(8,128)(2,1)} fusion(bf16[4096,256]{1,0:T(8,128)(2,1)} %gw.3, bf16[4096,256]{1,0:T(8,128)(2,1)} %uw.3, pred[]{:T(512)S(6)} %eq.3), kind=kLoop, calls=%fused_computation | loop fusion | flops 1048576 | bytes 6291457 | tf_op jit(solution)/shard_map/jit(_where)/select_n | solution.py:240
  11.1 11.5 %collective-permute-start.3 = (bf16[4096,256]{1,0:T(8,128)(2,1)}, bf16[4096,256]{1,0:T(8,128)(2,1)}, u32[]{:S(2)}, u32[]{:S(2)}) collective-permute-start(bf16[4096,256]{1,0:T(8,128)(2,1)} %broadcast_select_fusion), channel_id=1, source_target_pairs={{0,32},{32,0},{96,192},{192,96},{128,160},{160,128},{224,320},{320... | collective-permute-start | bytes 6291464 | tf_op jit(solution)/shard_map/ppermute | solution.py:44
  22.6 0.0 copy-done.3
  22.6 0.0 copy-done.4
  22.7 19.4 %all_to_all.15 = bf16[8,8,4096]{2,1,0:T(8,128)(2,1)S(1)} all-to-all(bf16[8,8,4096]{2,1,0:T(8,128)(2,1)S(1)} %broadcast_in_dim.2), channel_id=1, replica_groups=mesh['zh'=4,'c'=2,'zl'=2,'y'=8,'x'=4] {'y'}, dimensions={0} | all-to-all | bytes 1048576 | tf_op jit(solution)/shard_map/all_to_all | solution.py:247
  42.1 3.1 %collective-permute-start = (bf16[64,4096]{1,0:T(8,128)(2,1)S(1)}, bf16[64,4096]{1,0:T(8,128)(2,1)S(1)}, u32[]{:S(2)}, u32[]{:S(2)}) collective-permute-start(bf16[64,4096]{1,0:T(8,128)(2,1)S(1)} %bitcast.12), channel_id=1, source_target_pairs={{0,1},{1,2},{2,3},{3,0},{4,5},{5,6},{6,7},{7,4},{8,9},{9,10},{10,1... | collective-permute-start | bytes 1572872 | tf_op jit(solution)/shard_map/ppermute | solution.py:35
  45.2 4.4 %collective-permute-start.1 = (bf16[64,4096]{1,0:T(8,128)(2,1)S(1)}, bf16[64,4096]{1,0:T(8,128)(2,1)S(1)}, u32[]{:S(2)}, u32[]{:S(2)}) collective-permute-start(bf16[64,4096]{1,0:T(8,128)(2,1)S(1)} %bitcast.13), channel_id=1, source_target_pairs={{0,2},{1,3},{2,0},{3,1},{4,6},{5,7},{6,4},{7,5},{8,10},{9,11},{10,... | collective-permute-start | bytes 1572872 | tf_op jit(solution)/shard_map/ppermute | solution.py:35
  49.6 3.1 %collective-permute-start.2 = (bf16[64,4096]{1,0:T(8,128)(2,1)S(1)}, bf16[64,4096]{1,0:T(8,128)(2,1)S(1)}, u32[]{:S(2)}, u32[]{:S(2)}) collective-permute-start(bf16[64,4096]{1,0:T(8,128)(2,1)S(1)} %bitcast.14), channel_id=1, source_target_pairs={{0,3},{1,0},{2,1},{3,2},{4,7},{5,4},{6,5},{7,6},{8,11},{9,8},{10,9... | collective-permute-start | bytes 1572872 | tf_op jit(solution)/shard_map/ppermute | solution.py:35
  52.7 0.1 pad_add_fusion.where
  52.7 5.6 %collective-permute-done.r1 = bf16[64,4096]{1,0:T(8,128)(2,1)S(1)} collective-permute-done((bf16[64,4096]{1,0:T(8,128)(2,1)S(1)}, bf16[64,4096]{1,0:T(8,128)(2,1)S(1)}, u32[]{:S(2)}, u32[]{:S(2)}) %collective-permute-start) | collective-permute-done | bytes 524320 | tf_op jit(solution)/shard_map/ppermute | solution.py:35
  58.3 8.7 %collective-permute-done.1.r2 = bf16[64,4096]{1,0:T(8,128)(2,1)S(1)} collective-permute-done((bf16[64,4096]{1,0:T(8,128)(2,1)S(1)}, bf16[64,4096]{1,0:T(8,128)(2,1)S(1)}, u32[]{:S(2)}, u32[]{:S(2)}) %collective-permute-start.1) | collective-permute-done | bytes 524320 | tf_op jit(solution)/shard_map/ppermute | solution.py:35
  67.0 1.8 %collective-permute-done.2.r3 = bf16[64,4096]{1,0:T(8,128)(2,1)S(1)} collective-permute-done((bf16[64,4096]{1,0:T(8,128)(2,1)S(1)}, bf16[64,4096]{1,0:T(8,128)(2,1)S(1)}, u32[]{:S(2)}, u32[]{:S(2)}) %collective-permute-start.2) | collective-permute-done | bytes 524320 | tf_op jit(solution)/shard_map/ppermute | solution.py:35
  68.8 0.0 copy-done.2
  68.8 4.7 %split.1 = (bf16[128,4096]{1,0:T(8,128)(2,1)}, bf16[4,2,128,512]{3,2,1,0:T(8,128)(2,1)}) custom-call(s32[3]{0:T(128)S(1)} %pad_add_fusion.where, bf16[64,64]{1,0:T(8,128)(2,1)S(1)} %copy-done.2, bf16[64,4096]{1,0:T(8,128)(2,1)S(1)} %bitcast.15, bf16[64,4096]{1,0:T(8,128)(2,1)S(1)} %collective-permute-done.r1, ...), custom_call_target="tpu_custom_call" | custom-call | tf_op jit(solution)/shard_map/split/pallas_call | solution.py:58
  73.5 0.0 collective-permute-done.3.mw
  73.6 0.0 all-gather.5.cloned.1.call-done
  73.6 1.9 %collective-permute-start.4 = (bf16[4096,256]{1,0:T(8,128)(2,1)}, bf16[4096,256]{1,0:T(8,128)(2,1)S(1)}, u32[]{:S(2)}, u32[]{:S(2)}) collective-permute-start(bf16[4096,256]{1,0:T(8,128)(2,1)} %collective-permute-done.3.mw), channel_id=1, source_target_pairs={{0,64},{64,0},{1,65},{65,1},{2,66},{66,2},{3,67},{67,3},{4,68},{68... | collective-permute-start | bytes 6291464 | tf_op jit(solution)/shard_map/ppermute | solution.py:30
  75.5 2.4 %collective-permute-start.5 = (bf16[4,512,512]{2,1,0:T(8,128)(2,1)}, bf16[4,512,512]{2,1,0:T(8,128)(2,1)}, u32[]{:S(2)}, u32[]{:S(2)}) collective-permute-start(bf16[4,512,512]{2,1,0:T(8,128)(2,1)} %bitcast.18), channel_id=1, source_target_pairs={{0,64},{64,0},{1,65},{65,1},{2,66},{66,2},{3,67},{67,3},{4,68},{68... | collective-permute-start | bytes 6291464 | tf_op jit(solution)/shard_map/ppermute | solution.py:30
  77.9 7.3 %all-to-all-start.2 = ((bf16[4,2,128,512]{3,2,1,0:T(8,128)(2,1)}), bf16[4,2,128,512]{3,2,1,0:T(8,128)(2,1)S(1)}, u32[]{:S(2)}, u32[]{:S(2)}) async-start(bf16[4,2,128,512]{3,2,1,0:T(8,128)(2,1)} %get-tuple-element.17.cot), calls=%async_computation.2 | async-start | bytes 2097152 | tf_op jit(solution)/shard_map/all_to_all | solution.py:250
  85.2 0.0 all-gather.7.cloned.1.call-start
  85.2 0.0 collective-permute-done.4.ow
  85.2 0.0 collective-permute-done.5.df
  85.2 10.3 %forward.1 = (bf16[128,512]{1,0:T(8,128)(2,1)S(1)}, bf16[128,1024]{1,0:T(8,128)(2,1)S(1)}) custom-call(s32[3]{0:T(128)S(1)} %pad_add_fusion.where, bf16[128,4096]{1,0:T(8,128)(2,1)} %get-tuple-element.16.tok, bf16[4,2,128,512]{3,2,1,0:T(8,128)(2,1)} %get-tuple-element.17.cot, bf16[4096,256]{1,0:T(8,128)(2,1)} %gw.3, bf16[4096,256]{1,0:T(8,128)(2,1)} %uw.3, ...), custom_call_target="tpu_custom_call" | custom-call | tf_op jit(solution)/shard_map/forward/pallas_call | solution.py:138
  95.6 2.7 %collective-permute-start.6 = (bf16[128,512]{1,0:T(8,128)(2,1)S(1)}, bf16[128,512]{1,0:T(8,128)(2,1)S(1)}, u32[]{:S(2)}, u32[]{:S(2)}) collective-permute-start(bf16[128,512]{1,0:T(8,128)(2,1)S(1)} %get-tuple-element.21), channel_id=1, source_target_pairs={{0,64},{64,0},{1,65},{65,1},{2,66},{66,2},{3,67},{67,3},{4,68},{68... | collective-permute-start | bytes 393224 | tf_op jit(solution)/shard_map/ppermute | solution.py:30
  98.3 1.0 collective-permute-done.6
  99.2 0.7 pad_maximum_fusion
  100.0 0.0 all-gather.7.cloned.1.call-update
  100.0 7.6 %term.1 = bf16[4,32,4096]{2,1,0:T(8,128)(2,1)S(1)} custom-call(s32[3]{0:T(128)S(1)} %pad_add_fusion.where, bf16[128,1024]{1,0:T(8,128)(2,1)S(1)} %get-tuple-element.20.dd, bf16[4096,256]{1,0:T(8,128)(2,1)} %gw.3, bf16[4096,256]{1,0:T(8,128)(2,1)} %uw.3, bf16[4096,256]{1,0:T(8,128)(2,1)} %collective-permute-done.3.mw, ...), custom_call_target="tpu_custom_call" | custom-call | tf_op jit(solution)/shard_map/term/pallas_call | solution.py:178
  107.6 0.0 copy-start
  107.6 1.0 copy-done
  108.6 2.3 %reshape.16 = bf16[32,4,4096]{2,1,0:T(4,128)(2,1)} reshape(bf16[4,32,4096]{2,1,0:T(8,128)(2,1)} %copy-done) | data formatting | bytes 2097152 | tf_op jit(solution)/shard_map/reshape | solution.py:258
  110.9 0.0 all-to-all-done.2.cn
  110.9 6.3 %all-to-all-start.1 = ((bf16[32,4,4096]{2,1,0:T(4,128)(2,1)}), bf16[32,4,4096]{2,1,0:T(4,128)(2,1)S(1)}, u32[]{:S(2)}, u32[]{:S(2)}) async-start(bf16[32,4,4096]{2,1,0:T(4,128)(2,1)} %reshape.16), calls=%async_computation.1 | async-start | bytes 2097152 | tf_op jit(solution)/shard_map/all_to_all | solution.py:258
  117.2 2.6 %collective-permute-start.7 = (bf16[4,128,512]{2,1,0:T(8,128)(2,1)S(1)}, bf16[4,128,512]{2,1,0:T(8,128)(2,1)S(1)}, u32[]{:S(2)}, u32[]{:S(2)}) collective-permute-start(bf16[4,128,512]{2,1,0:T(8,128)(2,1)S(1)} %slice_bitcast_fusion), channel_id=1, source_target_pairs={{0,64},{64,0},{1,65},{65,1},{2,66},{66,2},{3,67},{67,3},{4,68},{68... | collective-permute-start | bytes 1572872 | tf_op jit(solution)/shard_map/ppermute | solution.py:30
  119.8 1.5 collective-permute-done.7.cf
  121.3 16.0 %all-gather.7.cloned.1.call-done = bf16[8,128,512]{2,1,0:T(8,128)(2,1)} async-done(((bf16[2,128,512]{2,1,0:T(8,128)(2,1)}), bf16[8,128,512]{2,1,0:T(8,128)(2,1)}) %all-gather.7.cloned.1.call-update) | async-done | bytes 1048592 | tf_op jit(solution)/shard_map/all_gather | solution.py:256
  137.3 0.0 copy-start.1
  137.3 1.2 copy-done.1
  138.5 2.0 %grads.1 = (f32[256,512]{1,0:T(8,128)S(1)}, bf16[256,512]{1,0:T(8,128)(2,1)S(1)}) custom-call(bf16[4,2,128,512]{3,2,1,0:T(8,128)(2,1)S(1)} %bitcast.16, bf16[4,2,128,512]{3,2,1,0:T(8,128)(2,1)S(1)} %all-to-all-done.2.cn, bf16[4,128,512]{2,1,0:T(8,128)(2,1)S(1)} %collective-permute-done.7.cf), custom_call_target="tpu_custom_call" | custom-call | tf_op jit(solution)/shard_map/grads/pallas_call | solution.py:208
  140.5 3.7 %collective-permute-start.8 = (bf16[256,512]{1,0:T(8,128)(2,1)S(1)}, bf16[256,512]{1,0:T(8,128)(2,1)S(1)}, u32[]{:S(2)}, u32[]{:S(2)}) collective-permute-start(bf16[256,512]{1,0:T(8,128)(2,1)S(1)} %get-tuple-element.23), channel_id=1, source_target_pairs={{0,32},{32,0},{1,33},{33,1},{2,34},{34,2},{3,35},{35,3},{4,36},{36... | collective-permute-start | bytes 786440 | tf_op jit(solution)/shard_map/ppermute | solution.py:30
  144.3 4.0 %collective-permute-done.8 = bf16[256,512]{1,0:T(8,128)(2,1)S(1)} collective-permute-done((bf16[256,512]{1,0:T(8,128)(2,1)S(1)}, bf16[256,512]{1,0:T(8,128)(2,1)S(1)}, u32[]{:S(2)}, u32[]{:S(2)}) %collective-permute-start.8) | collective-permute-done | bytes 262176 | tf_op jit(solution)/shard_map/ppermute | solution.py:30
  148.3 0.9 convert_add_fusion
  149.2 0.0 all-to-all-done.1
  149.2 1.1 reduce_sum.12
  (3 shorter events, 0.1 us)
Async XLA Ops:
  7.2 66.4 %all-gather.5.cloned.1.call-start = ((), (), s32[]{:S(2)}) async-start(), calls=%async_computation.3 | async-start | bytes 2359296 | tf_op jit(solution)/shard_map/all_gather | solution.py:243
  7.9 14.7 %copy-start.3 = (bf16[4,4096]{1,0:T(4,128)(2,1)S(1)}, bf16[4,4096]{1,0:T(4,128)(2,1)}, u32[]{:S(2)}) copy-start(bf16[4,4096]{1,0:T(4,128)(2,1)} %param.7) | copy-start | bytes 98308
  7.9 14.7 %copy-start.4 = (bf16[4,4096]{1,0:T(4,128)(2,1)S(1)}, bf16[4,4096]{1,0:T(4,128)(2,1)}, u32[]{:S(2)}) copy-start(bf16[4,4096]{1,0:T(4,128)(2,1)} %param.6) | copy-start | bytes 98308
  7.9 60.9 %copy-start.2 = (bf16[64,64]{1,0:T(8,128)(2,1)S(1)}, bf16[64,64]{1,0:T(8,128)(2,1)}, u32[]{:S(2)}) copy-start(bf16[64,64]{1,0:T(8,128)(2,1)} %constant.21.clone.pick) | copy-start | bytes 24580
  11.1 62.5 %collective-permute-start.3 = (bf16[4096,256]{1,0:T(8,128)(2,1)}, bf16[4096,256]{1,0:T(8,128)(2,1)}, u32[]{:S(2)}, u32[]{:S(2)}) collective-permute-start(bf16[4096,256]{1,0:T(8,128)(2,1)} %broadcast_select_fusion), channel_id=1, source_target_pairs={{0,32},{32,0},{96,192},{192,96},{128,160},{160,128},{224,320},{320... | collective-permute-start | bytes 6291464 | tf_op jit(solution)/shard_map/ppermute | solution.py:44
  42.1 16.2 %collective-permute-start = (bf16[64,4096]{1,0:T(8,128)(2,1)S(1)}, bf16[64,4096]{1,0:T(8,128)(2,1)S(1)}, u32[]{:S(2)}, u32[]{:S(2)}) collective-permute-start(bf16[64,4096]{1,0:T(8,128)(2,1)S(1)} %bitcast.12), channel_id=1, source_target_pairs={{0,1},{1,2},{2,3},{3,0},{4,5},{5,6},{6,7},{7,4},{8,9},{9,10},{10,1... | collective-permute-start | bytes 1572872 | tf_op jit(solution)/shard_map/ppermute | solution.py:35
  45.2 21.8 %collective-permute-start.1 = (bf16[64,4096]{1,0:T(8,128)(2,1)S(1)}, bf16[64,4096]{1,0:T(8,128)(2,1)S(1)}, u32[]{:S(2)}, u32[]{:S(2)}) collective-permute-start(bf16[64,4096]{1,0:T(8,128)(2,1)S(1)} %bitcast.13), channel_id=1, source_target_pairs={{0,2},{1,3},{2,0},{3,1},{4,6},{5,7},{6,4},{7,5},{8,10},{9,11},{10,... | collective-permute-start | bytes 1572872 | tf_op jit(solution)/shard_map/ppermute | solution.py:35
  49.6 19.2 %collective-permute-start.2 = (bf16[64,4096]{1,0:T(8,128)(2,1)S(1)}, bf16[64,4096]{1,0:T(8,128)(2,1)S(1)}, u32[]{:S(2)}, u32[]{:S(2)}) collective-permute-start(bf16[64,4096]{1,0:T(8,128)(2,1)S(1)} %bitcast.14), channel_id=1, source_target_pairs={{0,3},{1,0},{2,1},{3,2},{4,7},{5,4},{6,5},{7,6},{8,11},{9,8},{10,9... | collective-permute-start | bytes 1572872 | tf_op jit(solution)/shard_map/ppermute | solution.py:35
  73.6 11.7 %collective-permute-start.4 = (bf16[4096,256]{1,0:T(8,128)(2,1)}, bf16[4096,256]{1,0:T(8,128)(2,1)S(1)}, u32[]{:S(2)}, u32[]{:S(2)}) collective-permute-start(bf16[4096,256]{1,0:T(8,128)(2,1)} %collective-permute-done.3.mw), channel_id=1, source_target_pairs={{0,64},{64,0},{1,65},{65,1},{2,66},{66,2},{3,67},{67,3},{4,68},{68... | collective-permute-start | bytes 6291464 | tf_op jit(solution)/shard_map/ppermute | solution.py:30
  75.5 9.7 %collective-permute-start.5 = (bf16[4,512,512]{2,1,0:T(8,128)(2,1)}, bf16[4,512,512]{2,1,0:T(8,128)(2,1)}, u32[]{:S(2)}, u32[]{:S(2)}) collective-permute-start(bf16[4,512,512]{2,1,0:T(8,128)(2,1)} %bitcast.18), channel_id=1, source_target_pairs={{0,64},{64,0},{1,65},{65,1},{2,66},{66,2},{3,67},{67,3},{4,68},{68... | collective-permute-start | bytes 6291464 | tf_op jit(solution)/shard_map/ppermute | solution.py:30
  77.9 33.0 %all-to-all-start.2 = ((bf16[4,2,128,512]{3,2,1,0:T(8,128)(2,1)}), bf16[4,2,128,512]{3,2,1,0:T(8,128)(2,1)S(1)}, u32[]{:S(2)}, u32[]{:S(2)}) async-start(bf16[4,2,128,512]{3,2,1,0:T(8,128)(2,1)} %get-tuple-element.17.cot), calls=%async_computation.2 | async-start | bytes 2097152 | tf_op jit(solution)/shard_map/all_to_all | solution.py:250
  85.2 52.1 %all-gather.7.cloned.1.call-start = ((), (), s32[]{:S(2)}) async-start(), calls=%async_computation.4 | async-start | bytes 1310720 | tf_op jit(solution)/shard_map/all_gather | solution.py:256
  95.6 3.7 %collective-permute-start.6 = (bf16[128,512]{1,0:T(8,128)(2,1)S(1)}, bf16[128,512]{1,0:T(8,128)(2,1)S(1)}, u32[]{:S(2)}, u32[]{:S(2)}) collective-permute-start(bf16[128,512]{1,0:T(8,128)(2,1)S(1)} %get-tuple-element.21), channel_id=1, source_target_pairs={{0,64},{64,0},{1,65},{65,1},{2,66},{66,2},{3,67},{67,3},{4,68},{68... | collective-permute-start | bytes 393224 | tf_op jit(solution)/shard_map/ppermute | solution.py:30
  107.6 1.0 copy-start
  110.9 38.4 %all-to-all-start.1 = ((bf16[32,4,4096]{2,1,0:T(4,128)(2,1)}), bf16[32,4,4096]{2,1,0:T(4,128)(2,1)S(1)}, u32[]{:S(2)}, u32[]{:S(2)}) async-start(bf16[32,4,4096]{2,1,0:T(4,128)(2,1)} %reshape.16), calls=%async_computation.1 | async-start | bytes 2097152 | tf_op jit(solution)/shard_map/all_to_all | solution.py:258
  117.2 4.1 %collective-permute-start.7 = (bf16[4,128,512]{2,1,0:T(8,128)(2,1)S(1)}, bf16[4,128,512]{2,1,0:T(8,128)(2,1)S(1)}, u32[]{:S(2)}, u32[]{:S(2)}) collective-permute-start(bf16[4,128,512]{2,1,0:T(8,128)(2,1)S(1)} %slice_bitcast_fusion), channel_id=1, source_target_pairs={{0,64},{64,0},{1,65},{65,1},{2,66},{66,2},{3,67},{67,3},{4,68},{68... | collective-permute-start | bytes 1572872 | tf_op jit(solution)/shard_map/ppermute | solution.py:30
  137.3 1.2 copy-start.1
  140.5 7.8 %collective-permute-start.8 = (bf16[256,512]{1,0:T(8,128)(2,1)S(1)}, bf16[256,512]{1,0:T(8,128)(2,1)S(1)}, u32[]{:S(2)}, u32[]{:S(2)}) collective-permute-start(bf16[256,512]{1,0:T(8,128)(2,1)S(1)} %get-tuple-element.23), channel_id=1, source_target_pairs={{0,32},{32,0},{1,33},{33,1},{2,34},{34,2},{3,35},{35,3},{4,36},{36... | collective-permute-start | bytes 786440 | tf_op jit(solution)/shard_map/ppermute | solution.py:30
Sparse Core Ops, SparseCore 0:
  10.1 54.1 all-gather.4
  100.1 37.1 all-gather.6

commit v7 on v6

v7 whole, which is shorter than its diff:
```python
import functools

import jax
import jax.numpy as jnp
import numpy as np
from jax import lax
from jax.experimental import pallas as pl
from jax.experimental.pallas import tpu as pltpu
from jax.sharding import Mesh, PartitionSpec as P

BF16 = jnp.bfloat16
F32 = jnp.float32
DP = ("zh", "c")
TENSOR = ("zl", "y", "x")
NZ, NY, NX = 4, 8, 4
ROWS = 4
HALF = NX * NY * ROWS
D = 4096
HID = 256
FEATS = 512
STEPS = D // FEATS
PIECE = 2 * NY * ROWS


def contract(a, b, ca, cb):
    return lax.dot_general(a, b, (((ca,), (cb,)), ((), ())), preferred_element_type=F32)


def swap(value, axis):
    return lax.ppermute(value, axis, [(0, 1), (1, 0)])


def shift(value, axis, k):
    n = lax.axis_size(axis)
    return lax.ppermute(value, axis, [(i, (i + k) % n) for i in range(n)])


def neighbours(value):
    at = lambda zh, c, zl: ((zh % NZ) * 2 + c) * 2 + zl
    pairs = []
    for zh in range(NZ):
        pairs += [(at(zh, 0, 0), at(zh, 0, 1)), (at(zh, 0, 1), at(zh, 0, 0))]
        pairs += [(at(zh, 1, 1), at(zh + 1, 1, 0)), (at(zh + 1, 1, 0), at(zh, 1, 1))]
    return lax.ppermute(value, ("zh", "c", "zl"), pairs)


def split_body(where, pick_tok, pick_cot, t0, t1, t2, t3, c, tok, cot):
    n = NY * ROWS
    for i, piece in enumerate((t0, t1, t2, t3)):
        rows = contract(pick_tok[...], piece[...], 1, 0).astype(BF16)
        tok[0, i * n : (i + 1) * n] = rows[:n]
        tok[1, i * n : (i + 1) * n] = rows[n:]
    rows = contract(pick_cot[...], c[...], 1, 0).astype(BF16)
    cot[0, 0, 0] = rows[:HALF]
    cot[1, 0, 0] = rows[HALF:]


def split(where, pieces, cot):
    whole = lambda n: pl.BlockSpec((n, n), lambda j, s: (0, 0))
    return pl.pallas_call(
        split_body,
        grid_spec=pltpu.PrefetchScalarGridSpec(
            num_scalar_prefetch=1,
            grid=(STEPS // 2,),
            in_specs=[whole(PIECE), whole(2 * HALF)]
            + [pl.BlockSpec((PIECE, FEATS), lambda j, s: (0, j))] * 4
            + [pl.BlockSpec((2 * HALF, FEATS), lambda j, s: (0, j))],
            out_specs=[
                pl.BlockSpec((2, HALF, FEATS), lambda j, s: (0, 0, j)),
                pl.BlockSpec((2, 1, 1, HALF, FEATS), lambda j, s: (0, j // 2, flip(j % 2, s[0]), 0, 0)),
            ],
        ),
        out_shape=[
            hbm((2, HALF, D // 2), BF16),
            hbm((2, NZ // 2, 2, HALF, FEATS), BF16),
        ],
        compiler_params=pltpu.CompilerParams(vmem_limit_bytes=32 * 2**20),
        name="split",
    )(where, *picks(), *pieces, cot)


def hbm(shape, dtype):
    return pltpu.MemorySpace.HBM(shape, dtype)


def pinned(*values):
    return [pltpu.with_memory_space_constraint(v, pltpu.MemorySpace.HBM) for v in values]


def flip(a, b):
    return a + b - 2 * a * b


def gates_body(where, tok, gw, uw, mw, ow, hid, fac, acc):
    step = pl.program_id(0)

    @pl.when(step == 0)
    def _():
        acc[...] = jnp.zeros_like(acc)

    t = tok[0]
    for i, w in enumerate((gw, uw, mw, ow)):
        acc[:, i * HID : (i + 1) * HID] += contract(t, w[...], 1, 0)

    @pl.when(step == STEPS - 1)
    def _():
        first = where[0] == 0
        pm, po = acc[:, 2 * HID : 3 * HID], acc[:, 3 * HID :]
        sides = (
            (acc[:, :HID], acc[:, HID : 2 * HID]),
            (jnp.where(first, pm, po), jnp.where(first, po, pm)),
        )
        for i, (gate, up) in enumerate(sides):
            sigma = jax.nn.sigmoid(gate)
            silu = gate * sigma
            hid[:, i * HID : (i + 1) * HID] = (silu * up).astype(BF16)
            slope = up * sigma * (1.0 + gate * (1.0 - sigma))
            if i == 1:
                slope, silu = jnp.where(first, slope, silu), jnp.where(first, silu, slope)
            fac[:, 2 * i * HID : (2 * i + 1) * HID] = slope
            fac[:, (2 * i + 1) * HID : (2 * i + 2) * HID] = silu


def gates(where, tok, gw, uw, mw, ow):
    weight = pl.BlockSpec((FEATS, HID), lambda j, s: (j, 0))
    return pl.pallas_call(
        gates_body,
        grid_spec=pltpu.PrefetchScalarGridSpec(
            num_scalar_prefetch=1,
            grid=(STEPS,),
            in_specs=[pl.BlockSpec((1, HALF, FEATS), lambda j, s: (j // NZ, 0, j % NZ))] + [weight] * 4,
            out_specs=[
                pl.BlockSpec((HALF, 2 * HID), lambda j, s: (0, 0)),
                pl.BlockSpec((HALF, 4 * HID), lambda j, s: (0, 0)),
            ],
            scratch_shapes=[pltpu.VMEM((HALF, 4 * HID), F32)],
        ),
        out_shape=[
            jax.ShapeDtypeStruct((HALF, 2 * HID), BF16),
            jax.ShapeDtypeStruct((HALF, 4 * HID), F32),
        ],
        compiler_params=pltpu.CompilerParams(vmem_limit_bytes=32 * 2**20),
        name="gates",
    )(where, *pinned(tok, gw, uw, mw), ow)


def down_body(where, cot, dn, df, fac, dd, acc):
    step = pl.program_id(0)

    @pl.when(step == 0)
    def _():
        acc[...] = jnp.zeros_like(acc)

    acc[...] += contract(cot[0, 0], dn[0], 1, 1) + contract(cot[0, 1], df[0], 1, 1)

    @pl.when(step == NZ - 1)
    def _():
        low = where[1] == 0
        dl, dh = acc[:, :HID], acc[:, HID:]
        for i, d_hidden in enumerate((jnp.where(low, dl, dh), jnp.where(low, dh, dl))):
            for k in (2 * i, 2 * i + 1):
                dd[:, k * HID : (k + 1) * HID] = (d_hidden * fac[:, k * HID : (k + 1) * HID]).astype(BF16)


def down(where, cot, dn, df, fac):
    plane = pl.BlockSpec((1, 2 * HID, FEATS), lambda j, s: (j, 0, 0))
    block = pl.BlockSpec((HALF, 4 * HID), lambda j, s: (0, 0))
    return pl.pallas_call(
        down_body,
        grid_spec=pltpu.PrefetchScalarGridSpec(
            num_scalar_prefetch=1,
            grid=(NZ,),
            in_specs=[pl.BlockSpec((1, 2, HALF, FEATS), lambda j, s: (j, 0, 0, 0)), plane, plane, block],
            out_specs=block,
            scratch_shapes=[pltpu.VMEM((HALF, 2 * HID), F32)],
        ),
        out_shape=jax.ShapeDtypeStruct((HALF, 4 * HID), BF16),
        compiler_params=pltpu.CompilerParams(vmem_limit_bytes=32 * 2**20),
        name="down",
    )(where, *pinned(cot, dn), df, fac)


def term_body(where, pick, dd, *refs):
    weights, out = refs[:-1], refs[-1]
    halves = []
    for h in range(2):
        total = None
        for i, w in enumerate(weights[h::2]):
            part = contract(dd[:, i * HID : (i + 1) * HID], w[...], 1, 1)
            total = part if total is None else total + part
        halves.append(total.astype(BF16))
    rows = contract(pick[...], jnp.concatenate(halves, axis=0), 1, 0).astype(BF16)
    for i in range(NX):
        out[(where[2] + NX - i) % NX] = rows[i * PIECE : (i + 1) * PIECE]


def term(where, dd, gw, uw, mw, ow):
    low = pl.BlockSpec((FEATS, HID), lambda j, s: (j, 0))
    high = pl.BlockSpec((FEATS, HID), lambda j, s: (j + NZ, 0))
    gw, uw, mw = pinned(gw, uw, mw)
    return pl.pallas_call(
        term_body,
        grid_spec=pltpu.PrefetchScalarGridSpec(
            num_scalar_prefetch=1,
            grid=(STEPS // 2,),
            in_specs=[
                pl.BlockSpec((2 * HALF, 2 * HALF), lambda j, s: (0, 0)),
                pl.BlockSpec((HALF, 4 * HID), lambda j, s: (0, 0)),
            ]
            + [low, high] * 4,
            out_specs=pl.BlockSpec((NX, PIECE, FEATS), lambda j, s: (0, 0, j)),
        ),
        out_shape=hbm((NX, PIECE, D // 2), BF16),
        compiler_params=pltpu.CompilerParams(vmem_limit_bytes=32 * 2**20),
        name="term",
    )(where, merge(), dd, gw, gw, uw, uw, mw, mw, ow, ow)


def grads_body(h, cn, cf, keep, send, acc):
    step = pl.program_id(0)

    @pl.when(step == 0)
    def _():
        acc[...] = jnp.zeros_like(acc)

    acc[...] += contract(h[0, 0], cn[0, 0], 0, 0) + contract(h[0, 1], cf[0], 0, 0)

    @pl.when(step == NZ - 1)
    def _():
        keep[...] = acc[:HID]
        send[...] = acc[HID:].astype(BF16)


def grads(hidden, cot_near, cot_far):
    return pl.pallas_call(
        grads_body,
        grid=(NZ,),
        in_specs=[
            pl.BlockSpec((1, 2, HALF, 2 * HID), lambda j: (j, 0, 0, 0)),
            pl.BlockSpec((1, 1, HALF, FEATS), lambda j: (j, 0, 0, 0)),
            pl.BlockSpec((1, HALF, FEATS), lambda j: (j, 0, 0)),
        ],
        out_specs=[pl.BlockSpec((HID, FEATS), lambda j: (0, 0))] * 2,
        out_shape=[
            jax.ShapeDtypeStruct((HID, FEATS), F32),
            jax.ShapeDtypeStruct((HID, FEATS), BF16),
        ],
        scratch_shapes=[pltpu.VMEM((2 * HID, FEATS), F32)],
        compiler_params=pltpu.CompilerParams(vmem_limit_bytes=32 * 2**20),
        name="grads",
    )(hidden, cot_near, cot_far)


def selection(shape, order):
    source = np.arange(np.prod(shape)).reshape(shape).transpose(order).reshape(-1)
    return jnp.asarray(np.eye(source.size, dtype=np.float32)[source], BF16)


def picks():
    return selection((NY, 2, ROWS), (1, 0, 2)), selection((NY, NX, 2, ROWS), (2, 1, 0, 3))


def merge():
    return selection((2, NX, NY, ROWS), (1, 2, 0, 3))


def folded(rows):
    return jnp.concatenate([rows[:, : D // 2], rows[:, D // 2 :]], axis=0)


def spread(block, axis):
    n = lax.axis_size(axis)
    return lax.all_to_all(jnp.broadcast_to(block[None], (n, *block.shape)), axis, 0, 0)


def on_device(tokens, cotangent, gate_weight, up_weight, down_weight):
    core = lax.axis_index("c")
    where = jnp.stack([core, lax.axis_index("zl"), lax.axis_index("x")]).astype(jnp.int32)

    picked = jnp.where(core == 0, gate_weight, up_weight)
    picked, tokens = lax.optimization_barrier((picked, tokens))
    mine = neighbours(picked)
    down_near = lax.all_gather(down_weight, ("zh", "zl"), axis=0).reshape(NZ, 2 * HID, FEATS)

    tok = spread(folded(tokens), "y").reshape(PIECE, D // 2)
    cot = folded(cotangent)
    cot = jnp.concatenate([cot] + [shift(cot, "x", k) for k in (1, 2, 3)], axis=0)
    cot = spread(cot, "y").reshape(2 * HALF, D // 2)
    tok = [tok] + [shift(tok, "x", k) for k in (1, 2, 3)]

    tok, cot = split(where, tok, cot)
    cot = cot.reshape(NZ, 2, HALF, FEATS)
    cot_x = lax.all_to_all(cot, "zh", 0, 0)
    cot_far = swap(cot_x[:, 1], "c")
    tok, mine, down_near = lax.optimization_barrier((tok, mine, down_near))
    other, down_far = swap(mine, "c"), swap(down_near, "c")
    hidden, factors = gates(where, tok, gate_weight, up_weight, mine, other)
    hidden = lax.all_gather(jnp.stack([hidden, swap(hidden, "c")]), "zh", axis=0)
    dd = down(where, cot, down_near, down_far, factors)

    parts = term(where, dd, gate_weight, up_weight, mine, other)
    parts = lax.all_to_all(parts.reshape(NX * NY, 2 * ROWS, D // 2), ("x", "y"), 0, 0)
    total = jnp.sum(parts.astype(F32), axis=0).astype(BF16)
    input_grad = jnp.concatenate([total[:ROWS], total[ROWS:]], axis=1)

    keep, send = grads(hidden, cot_x, cot_far)
    down_grad = keep + swap(send, "zl").astype(F32)
    return (input_grad, down_grad)


def solution(mesh):
    fine = Mesh(mesh.devices.reshape(NZ, 2, 2, NY, NX), ("zh", "c", "zl", "y", "x"))
    placed = (
        P((*DP, *TENSOR), None),
        P((*DP, *TENSOR), None),
        P(None, TENSOR),
        P(None, TENSOR),
        P(TENSOR, DP),
    )
    return jax.shard_map(
        on_device,
        mesh=fine,
        in_specs=placed,
        out_specs=(P((*DP, *TENSOR), None), P(TENSOR, DP)),
        check_vma=False,
    )
```

time: 160 us -> 160 us (level)
  blocking collectives: 19.4 us -> 0 us
  starting transfers between devices: 48.9 us -> 65.6 us
  waiting for transfers between devices: 39.3 us -> 41.8 us
    all_to_all x1 -> x0, blocking collectives: 19.4 us -> none  [on_device(): block = lax.all_to_all(block, 'y', 0, 0).reshape(PIECE, D)]
    all_to_all x1 -> x3, starting transfers between devices: 6.28 us -> 19.1 us  [the longest x2 14.4 us: spread(): lax.all_to_all(jnp.broadcast_to(block[None], (n, *block.shape)), axis, 0, 0)]
    ppermute x3 -> x6, starting transfers between devices: 10.5 us -> 19.8 us  [shift(): return lax.ppermute(value, axis, [(i, (i + k) % n) for i in range(n)])]
    all_to_all x1 -> x3, waiting for transfers between devices: 0.01 us -> 9.08 us  [the longest x2 9.07 us: spread(): lax.all_to_all(jnp.broadcast_to(block[None], (n, *block.shape)), axis, 0, 0)]
    ppermute x3 -> x6, waiting for transfers between devices: 16.1 us -> 9.42 us  [shift(): return lax.ppermute(value, axis, [(i, (i + k) % n) for i in range(n)])]
    ppermute x5, waiting for transfers between devices: 6.53 us -> 9.6 us  [swap(): return lax.ppermute(value, axis, [(0, 1), (1, 0)])]
    all_gather x1, waiting for transfers between devices: 16 us -> 13 us  [on_device(): lax.all_gather(jnp.stack([hidden, swap(hidden, 'c')]), 'zh', axis=0)]
    all_to_all x1, starting transfers between devices: 7.32 us -> 4.86 us  [on_device(): cot_x = lax.all_to_all(cot, 'zh', 0, 0)]
  transfers between devices with their start and end apart: 13 -> 18, of which waited for: 7 -> 9; matrix products, arithmetic and copies ran while one was open for 5% -> 4% of each run, Pallas kernels for 16% -> 16%
where the time goes in v7:
time: 160 us; the launch traced here: 158 us
  starting transfers between devices  65.6 us (41%)
  waiting for transfers between devices  41.8 us (26%)
  Pallas kernels  24.5 us (15%)
  between operations  14.3 us (9%)
  other arithmetic  6.95 us (4%)
  local copies, waits for them, and re-layouts  4.98 us (3%)
    ppermute x6, starting transfers between devices, shift(): return lax.ppermute(value, axis, [(i, (i + k) % n) for i in range(n)])  19.8 us
    all_to_all x2, starting transfers between devices, spread(): lax.all_to_all(jnp.broadcast_to(block[None], (n, *block.shape)), axis, 0, 0)  14.4 us
    all_gather x1, waiting for transfers between devices, on_device(): lax.all_gather(jnp.stack([hidden, swap(hidden, 'c')]), 'zh', axis=0)  13 us
    ppermute x5, starting transfers between devices, swap(): return lax.ppermute(value, axis, [(0, 1), (1, 0)])  11.1 us
    ppermute x1, starting transfers between devices, neighbours(): return lax.ppermute(value, ('zh', 'c', 'zl'), pairs)  10.7 us
    ppermute x5, waiting for transfers between devices, swap(): return lax.ppermute(value, axis, [(0, 1), (1, 0)])  9.6 us
    ppermute x6, waiting for transfers between devices, shift(): return lax.ppermute(value, axis, [(i, (i + k) % n) for i in range(n)])  9.42 us
    all_to_all x2, waiting for transfers between devices, spread(): lax.all_to_all(jnp.broadcast_to(block[None], (n, *block.shape)), axis, 0, 0)  9.07 us
  transfers between devices with their start and end apart: 18, of which 9 were waited for; matrix products, arithmetic and copies ran while one was open for 4% of the time, Pallas kernels for 16%

profile of v7, /device:TPU:1, one launch (start us, length us, event | category | flops | bytes accessed | tf_op | source)
XLA Modules:
  0.0 158.1 jit_solution(14563132053141535158)
XLA Ops:
  7.2 0.0 all-gather.5.cloned.1.call-start
  7.2 0.7 all-gather.5.cloned.1.call-update
  7.9 0.0 copy-start.6
  7.9 0.0 copy-start.7
  7.9 3.2 %broadcast_select_fusion = bf16[4096,256]{1,0:T(8,128)(2,1)} fusion(bf16[4096,256]{1,0:T(8,128)(2,1)} %refs_1_.1, bf16[4096,256]{1,0:T(8,128)(2,1)} %refs_3_.1, pred[]{:T(512)S(6)} %eq.3), kind=kLoop, calls=%fused_computation | loop fusion | flops 1048576 | bytes 6291457 | tf_op jit(solution)/shard_map/jit(_where)/select_n | solution.py:280
  11.1 0.0 copy-done.6
  11.2 0.7 broadcast_in_dim.4
  11.9 0.0 copy-start.4
  11.9 0.0 copy-start.5
  11.9 7.8 %all-to-all-start = ((bf16[8,8,2048]{2,1,0:T(8,128)(2,1)}), bf16[8,8,2048]{2,1,0:T(8,128)(2,1)S(1)}, u32[]{:S(2)}, u32[]{:S(2)}) async-start(bf16[8,8,2048]{2,1,0:T(8,128)(2,1)} %broadcast_in_dim.4), calls=%async_computation | async-start | bytes 524288 | tf_op jit(solution)/shard_map/all_to_all | solution.py:273
  19.7 10.7 %collective-permute-start.6 = (bf16[4096,256]{1,0:T(8,128)(2,1)}, bf16[4096,256]{1,0:T(8,128)(2,1)}, u32[]{:S(2)}, u32[]{:S(2)}) collective-permute-start(bf16[4096,256]{1,0:T(8,128)(2,1)} %broadcast_select_fusion), channel_id=1, source_target_pairs={{0,32},{32,0},{96,192},{192,96},{128,160},{160,128},{224,320},{320... | collective-permute-start | bytes 6291464 | tf_op jit(solution)/shard_map/ppermute | solution.py:44
  30.3 0.0 copy-done.7
  30.4 3.1 %collective-permute-start.3 = (bf16[8,2048]{1,0:T(8,128)(2,1)S(1)}, bf16[8,2048]{1,0:T(8,128)(2,1)S(1)}, u32[]{:S(2)}, u32[]{:S(2)}) collective-permute-start(bf16[8,2048]{1,0:T(8,128)(2,1)S(1)} %pad_maximum_fusion.2), channel_id=1, source_target_pairs={{0,1},{1,2},{2,3},{3,0},{4,5},{5,6},{6,7},{7,4},{8,9},{9,10},{10,1... | collective-permute-start | bytes 98312 | tf_op jit(solution)/shard_map/ppermute | solution.py:35
  33.5 4.4 %collective-permute-start.4 = (bf16[8,2048]{1,0:T(8,128)(2,1)S(1)}, bf16[8,2048]{1,0:T(8,128)(2,1)S(1)}, u32[]{:S(2)}, u32[]{:S(2)}) collective-permute-start(bf16[8,2048]{1,0:T(8,128)(2,1)S(1)} %pad_maximum_fusion.2), channel_id=1, source_target_pairs={{0,2},{1,3},{2,0},{3,1},{4,6},{5,7},{6,4},{7,5},{8,10},{9,11},{10,... | collective-permute-start | bytes 98312 | tf_op jit(solution)/shard_map/ppermute | solution.py:35
  37.9 3.1 %collective-permute-start.5 = (bf16[8,2048]{1,0:T(8,128)(2,1)S(1)}, bf16[8,2048]{1,0:T(8,128)(2,1)S(1)}, u32[]{:S(2)}, u32[]{:S(2)}) collective-permute-start(bf16[8,2048]{1,0:T(8,128)(2,1)S(1)} %pad_maximum_fusion.2), channel_id=1, source_target_pairs={{0,3},{1,0},{2,1},{3,2},{4,7},{5,4},{6,5},{7,6},{8,11},{9,8},{10,9... | collective-permute-start | bytes 98312 | tf_op jit(solution)/shard_map/ppermute | solution.py:35
  41.0 0.0 collective-permute-done.3
  41.0 0.0 collective-permute-done.4
  41.0 2.0 %collective-permute-done.5 = bf16[8,2048]{1,0:T(8,128)(2,1)S(1)} collective-permute-done((bf16[8,2048]{1,0:T(8,128)(2,1)S(1)}, bf16[8,2048]{1,0:T(8,128)(2,1)S(1)}, u32[]{:S(2)}, u32[]{:S(2)}) %collective-permute-start.5) | collective-permute-done | bytes 32800 | tf_op jit(solution)/shard_map/ppermute | solution.py:35
  43.0 0.0 all-to-all-done
  43.0 1.1 broadcast_in_dim.5
  44.1 6.6 %all-to-all-start.1 = ((bf16[8,32,2048]{2,1,0:T(8,128)(2,1)}), bf16[8,32,2048]{2,1,0:T(8,128)(2,1)S(1)}, u32[]{:S(2)}, u32[]{:S(2)}) async-start(bf16[8,32,2048]{2,1,0:T(8,128)(2,1)} %broadcast_in_dim.5), calls=%async_computation.1 | async-start | bytes 2097152 | tf_op jit(solution)/shard_map/all_to_all | solution.py:273
  50.7 1.9 %collective-permute-start = (bf16[64,2048]{1,0:T(8,128)(2,1)S(1)}, bf16[64,2048]{1,0:T(8,128)(2,1)S(1)}, u32[]{:S(2)}, u32[]{:S(2)}) collective-permute-start(bf16[64,2048]{1,0:T(8,128)(2,1)S(1)} %bitcast.16), channel_id=1, source_target_pairs={{0,1},{1,2},{2,3},{3,0},{4,5},{5,6},{6,7},{7,4},{8,9},{9,10},{10,1... | collective-permute-start | bytes 786440 | tf_op jit(solution)/shard_map/ppermute | solution.py:35
  52.7 5.4 %collective-permute-start.1 = (bf16[64,2048]{1,0:T(8,128)(2,1)S(1)}, bf16[64,2048]{1,0:T(8,128)(2,1)S(1)}, u32[]{:S(2)}, u32[]{:S(2)}) collective-permute-start(bf16[64,2048]{1,0:T(8,128)(2,1)S(1)} %bitcast.17), channel_id=1, source_target_pairs={{0,2},{1,3},{2,0},{3,1},{4,6},{5,7},{6,4},{7,5},{8,10},{9,11},{10,... | collective-permute-start | bytes 786440 | tf_op jit(solution)/shard_map/ppermute | solution.py:35
  58.1 1.9 %collective-permute-start.2 = (bf16[64,2048]{1,0:T(8,128)(2,1)S(1)}, bf16[64,2048]{1,0:T(8,128)(2,1)S(1)}, u32[]{:S(2)}, u32[]{:S(2)}) collective-permute-start(bf16[64,2048]{1,0:T(8,128)(2,1)S(1)} %bitcast.18), channel_id=1, source_target_pairs={{0,3},{1,0},{2,1},{3,2},{4,7},{5,4},{6,5},{7,6},{8,11},{9,8},{10,9... | collective-permute-start | bytes 786440 | tf_op jit(solution)/shard_map/ppermute | solution.py:35
  60.0 0.1 pad_add_fusion.where
  60.1 1.9 %collective-permute-done.t1 = bf16[64,2048]{1,0:T(8,128)(2,1)S(1)} collective-permute-done((bf16[64,2048]{1,0:T(8,128)(2,1)S(1)}, bf16[64,2048]{1,0:T(8,128)(2,1)S(1)}, u32[]{:S(2)}, u32[]{:S(2)}) %collective-permute-start) | collective-permute-done | bytes 262176 | tf_op jit(solution)/shard_map/ppermute | solution.py:35
  62.0 3.2 %collective-permute-done.1.t2 = bf16[64,2048]{1,0:T(8,128)(2,1)S(1)} collective-permute-done((bf16[64,2048]{1,0:T(8,128)(2,1)S(1)}, bf16[64,2048]{1,0:T(8,128)(2,1)S(1)}, u32[]{:S(2)}, u32[]{:S(2)}) %collective-permute-start.1) | collective-permute-done | bytes 262176 | tf_op jit(solution)/shard_map/ppermute | solution.py:35
  65.2 2.3 %collective-permute-done.2.t3 = bf16[64,2048]{1,0:T(8,128)(2,1)S(1)} collective-permute-done((bf16[64,2048]{1,0:T(8,128)(2,1)S(1)}, bf16[64,2048]{1,0:T(8,128)(2,1)S(1)}, u32[]{:S(2)}, u32[]{:S(2)}) %collective-permute-start.2) | collective-permute-done | bytes 262176 | tf_op jit(solution)/shard_map/ppermute | solution.py:35
  67.6 9.1 %all-to-all-done.1 = bf16[8,32,2048]{2,1,0:T(8,128)(2,1)S(1)} async-done(((bf16[8,32,2048]{2,1,0:T(8,128)(2,1)}), bf16[8,32,2048]{2,1,0:T(8,128)(2,1)S(1)}, u32[]{:S(2)}, u32[]{:S(2)}) %all-to-all-start.1) | async-done | bytes 1048608 | tf_op jit(solution)/shard_map/all_to_all | solution.py:273
  76.6 0.0 copy-done.4
  76.6 0.0 copy-done.5
  76.6 3.2 %split.1 = (bf16[2,128,2048]{2,1,0:T(8,128)(2,1)}, bf16[2,2,2,128,512]{4,3,2,1,0:T(8,128)(2,1)}) custom-call(s32[3]{0:T(128)S(1)} %pad_add_fusion.where, bf16[64,64]{1,0:T(8,128)(2,1)S(1)} %copy-done.5, bf16[256,256]{1,0:T(8,128)(2,1)S(1)} %copy-done.4, bf16[64,2048]{1,0:T(8,128)(2,1)S(1)} %bitcast.19, bf16[64,2048]{1,0:T(8,128)(2,1)S(1)} %collective-permute-done.t1, ...), custom_call_target="tpu_custom_call" | custom-call | tf_op jit(solution)/shard_map/split/pallas_call | solution.py:60
  79.9 0.0 collective-permute-done.6.mw.refs_4_.refs_5_
  79.9 1.9 %collective-permute-start.8 = (bf16[4096,256]{1,0:T(8,128)(2,1)}, bf16[4096,256]{1,0:T(8,128)(2,1)S(1)}, u32[]{:S(2)}, u32[]{:S(2)}) collective-permute-start(bf16[4096,256]{1,0:T(8,128)(2,1)} %collective-permute-done.6.mw.refs_4_.refs_5_), channel_id=1, source_target_pairs={{0,64},{64,0},{1,65},{65,1},{2,66},{66,2},{3,67},{67,3},{4,68},{68... | collective-permute-start | bytes 6291464 | tf_op jit(solution)/shard_map/ppermute | solution.py:30
  81.8 2.4 %collective-permute-start.7 = (bf16[4,512,512]{2,1,0:T(8,128)(2,1)}, bf16[4,512,512]{2,1,0:T(8,128)(2,1)}, u32[]{:S(2)}, u32[]{:S(2)}) collective-permute-start(bf16[4,512,512]{2,1,0:T(8,128)(2,1)} %bitcast.25), channel_id=1, source_target_pairs={{0,64},{64,0},{1,65},{65,1},{2,66},{66,2},{3,67},{67,3},{4,68},{68... | collective-permute-start | bytes 6291464 | tf_op jit(solution)/shard_map/ppermute | solution.py:30
  84.2 4.9 %all-to-all-start.3 = ((bf16[4,2,128,512]{3,2,1,0:T(8,128)(2,1)}), bf16[4,2,128,512]{3,2,1,0:T(8,128)(2,1)S(1)}, u32[]{:S(2)}, u32[]{:S(2)}) async-start(bf16[4,2,128,512]{3,2,1,0:T(8,128)(2,1)} %bitcast.22), calls=%async_computation.3 | async-start | bytes 2097152 | tf_op jit(solution)/shard_map/all_to_all | solution.py:293
  89.1 0.0 all-gather.7.cloned.1.call-start
  89.1 0.0 collective-permute-done.8.ow.refs_6_.refs_7_
  89.1 7.2 %gates.1 = (bf16[128,512]{1,0:T(8,128)(2,1)S(1)}, f32[128,1024]{1,0:T(8,128)S(1)}) custom-call(s32[3]{0:T(128)S(1)} %pad_add_fusion.where, bf16[2,128,2048]{2,1,0:T(8,128)(2,1)} %get-tuple-element.18.tok, bf16[4096,256]{1,0:T(8,128)(2,1)} %refs_1_.1, bf16[4096,256]{1,0:T(8,128)(2,1)} %refs_3_.1, bf16[4096,256]{1,0:T(8,128)(2,1)} %collective-permute-done.6.mw.refs_4_.refs_5_, ...), custom_call_target="tpu_custom_call" | custom-call | tf_op jit(solution)/shard_map/gates/pallas_call | solution.py:126
  96.3 0.0 copy-start.1
  96.4 0.8 copy-done.1
  97.1 2.7 %collective-permute-start.9 = (bf16[128,512]{1,0:T(8,128)(2,1)S(1)}, bf16[128,512]{1,0:T(8,128)(2,1)S(1)}, u32[]{:S(2)}, u32[]{:S(2)}) collective-permute-start(bf16[128,512]{1,0:T(8,128)(2,1)S(1)} %get-tuple-element.21), channel_id=1, source_target_pairs={{0,64},{64,0},{1,65},{65,1},{2,66},{66,2},{3,67},{67,3},{4,68},{68... | collective-permute-start | bytes 393224 | tf_op jit(solution)/shard_map/ppermute | solution.py:30
  99.8 1.0 collective-permute-done.9
  100.8 0.7 pad_maximum_fusion
  101.5 0.0 all-gather.7.cloned.1.call-update
  101.6 0.0 collective-permute-done.7.df
  101.6 0.0 copy-start.2
  101.6 1.0 copy-done.2
  102.6 4.8 %down.1.dd = bf16[128,1024]{1,0:T(8,128)(2,1)S(1)} custom-call(s32[3]{0:T(128)S(1)} %pad_add_fusion.where, bf16[4,2,128,512]{3,2,1,0:T(8,128)(2,1)} %bitcast.23, bf16[4,512,512]{2,1,0:T(8,128)(2,1)} %bitcast.26, bf16[4,512,512]{2,1,0:T(8,128)(2,1)} %collective-permute-done.7.df, f32[128,1024]{1,0:T(8,128)S(1)} %copy-done.2), custom_call_target="tpu_custom_call" | custom-call | tf_op jit(solution)/shard_map/down/pallas_call | solution.py:168
  107.4 0.0 copy-done.3
  107.4 7.3 %term.1 = bf16[4,64,2048]{2,1,0:T(8,128)(2,1)} custom-call(s32[3]{0:T(128)S(1)} %pad_add_fusion.where, bf16[256,256]{1,0:T(8,128)(2,1)S(1)} %copy-done.3, bf16[128,1024]{1,0:T(8,128)(2,1)S(1)} %down.1.dd, bf16[4096,256]{1,0:T(8,128)(2,1)} %refs_1_.1, bf16[4096,256]{1,0:T(8,128)(2,1)} %refs_1_.1, bf16[4096,256]{1,0:T(8,128)(2,1)} %refs_3_.1, ...), custom_call_target="tpu_custom_call" | custom-call | tf_op jit(solution)/shard_map/term/pallas_call | solution.py:201
  114.7 0.0 all-to-all-done.3.cn
  114.7 4.7 %all-to-all-start.2 = ((bf16[32,8,2048]{2,1,0:T(8,128)(2,1)}), bf16[32,8,2048]{2,1,0:T(8,128)(2,1)}, u32[]{:S(2)}, u32[]{:S(2)}) async-start(bf16[32,8,2048]{2,1,0:T(8,128)(2,1)} %bitcast.24), calls=%async_computation.2 | async-start | bytes 2097152 | tf_op jit(solution)/shard_map/all_to_all | solution.py:302
  119.4 2.2 %collective-permute-start.10 = (bf16[4,128,512]{2,1,0:T(8,128)(2,1)S(1)}, bf16[4,128,512]{2,1,0:T(8,128)(2,1)S(1)}, u32[]{:S(2)}, u32[]{:S(2)}) collective-permute-start(bf16[4,128,512]{2,1,0:T(8,128)(2,1)S(1)} %slice_bitcast_fusion), channel_id=1, source_target_pairs={{0,64},{64,0},{1,65},{65,1},{2,66},{66,2},{3,67},{67,3},{4,68},{68... | collective-permute-start | bytes 1572872 | tf_op jit(solution)/shard_map/ppermute | solution.py:30
  121.6 1.6 collective-permute-done.10.cf
  123.2 13.0 %all-gather.7.cloned.1.call-done = bf16[8,128,512]{2,1,0:T(8,128)(2,1)} async-done(((bf16[2,128,512]{2,1,0:T(8,128)(2,1)}), bf16[8,128,512]{2,1,0:T(8,128)(2,1)}) %all-gather.7.cloned.1.call-update) | async-done | bytes 1048592 | tf_op jit(solution)/shard_map/all_gather | solution.py:298
  136.2 1.2 copy-done
  137.4 2.0 %grads.1 = (f32[256,512]{1,0:T(8,128)S(1)}, bf16[256,512]{1,0:T(8,128)(2,1)S(1)}) custom-call(bf16[4,2,128,512]{3,2,1,0:T(8,128)(2,1)S(1)} %bitcast.20, bf16[4,2,128,512]{3,2,1,0:T(8,128)(2,1)S(1)} %all-to-all-done.3.cn, bf16[4,128,512]{2,1,0:T(8,128)(2,1)S(1)} %collective-permute-done.10.cf), custom_call_target="tpu_custom_call" | custom-call | tf_op jit(solution)/shard_map/grads/pallas_call | solution.py:235
  139.4 1.9 %collective-permute-start.11 = (bf16[256,512]{1,0:T(8,128)(2,1)S(1)}, bf16[256,512]{1,0:T(8,128)(2,1)S(1)}, u32[]{:S(2)}, u32[]{:S(2)}) collective-permute-start(bf16[256,512]{1,0:T(8,128)(2,1)S(1)} %get-tuple-element.23), channel_id=1, source_target_pairs={{0,32},{32,0},{1,33},{33,1},{2,34},{34,2},{3,35},{35,3},{4,36},{36... | collective-permute-start | bytes 786440 | tf_op jit(solution)/shard_map/ppermute | solution.py:30
  141.3 7.1 %collective-permute-done.11 = bf16[256,512]{1,0:T(8,128)(2,1)S(1)} collective-permute-done((bf16[256,512]{1,0:T(8,128)(2,1)S(1)}, bf16[256,512]{1,0:T(8,128)(2,1)S(1)}, u32[]{:S(2)}, u32[]{:S(2)}) %collective-permute-start.11) | collective-permute-done | bytes 262176 | tf_op jit(solution)/shard_map/ppermute | solution.py:30
  148.4 0.9 convert_add_fusion
  149.2 0.0 all-to-all-done.2
  149.2 1.4 reduce_sum.12
  150.6 0.6 pad_maximum_fusion.3
  (10 shorter events, 0.2 us)
Async XLA Ops:
  7.2 72.7 %all-gather.5.cloned.1.call-start = ((), (), s32[]{:S(2)}) async-start(), calls=%async_computation.4 | async-start | bytes 2359296 | tf_op jit(solution)/shard_map/all_gather | solution.py:283
  7.9 3.2 %copy-start.6 = (bf16[4,4096]{1,0:T(4,128)(2,1)S(1)}, bf16[4,4096]{1,0:T(4,128)(2,1)}, u32[]{:S(2)}) copy-start(bf16[4,4096]{1,0:T(4,128)(2,1)} %param.8) | copy-start | bytes 98308
  7.9 22.4 %copy-start.7 = (bf16[4,4096]{1,0:T(4,128)(2,1)S(1)}, bf16[4,4096]{1,0:T(4,128)(2,1)}, u32[]{:S(2)}) copy-start(bf16[4,4096]{1,0:T(4,128)(2,1)} %param.9) | copy-start | bytes 98308
  11.9 64.7 %copy-start.4 = (bf16[256,256]{1,0:T(8,128)(2,1)S(1)}, bf16[256,256]{1,0:T(8,128)(2,1)}, u32[]{:S(2)}) copy-start(bf16[256,256]{1,0:T(8,128)(2,1)} %constant.26.clone.pick_cot) | copy-start | bytes 393220
  11.9 64.7 %copy-start.5 = (bf16[64,64]{1,0:T(8,128)(2,1)S(1)}, bf16[64,64]{1,0:T(8,128)(2,1)}, u32[]{:S(2)}) copy-start(bf16[64,64]{1,0:T(8,128)(2,1)} %constant.25.clone.pick_tok) | copy-start | bytes 24580
  11.9 31.1 %all-to-all-start = ((bf16[8,8,2048]{2,1,0:T(8,128)(2,1)}), bf16[8,8,2048]{2,1,0:T(8,128)(2,1)S(1)}, u32[]{:S(2)}, u32[]{:S(2)}) async-start(bf16[8,8,2048]{2,1,0:T(8,128)(2,1)} %broadcast_in_dim.4), calls=%async_computation | async-start | bytes 524288 | tf_op jit(solution)/shard_map/all_to_all | solution.py:273
  19.7 60.2 %collective-permute-start.6 = (bf16[4096,256]{1,0:T(8,128)(2,1)}, bf16[4096,256]{1,0:T(8,128)(2,1)}, u32[]{:S(2)}, u32[]{:S(2)}) collective-permute-start(bf16[4096,256]{1,0:T(8,128)(2,1)} %broadcast_select_fusion), channel_id=1, source_target_pairs={{0,32},{32,0},{96,192},{192,96},{128,160},{160,128},{224,320},{320... | collective-permute-start | bytes 6291464 | tf_op jit(solution)/shard_map/ppermute | solution.py:44
  30.4 10.6 %collective-permute-start.3 = (bf16[8,2048]{1,0:T(8,128)(2,1)S(1)}, bf16[8,2048]{1,0:T(8,128)(2,1)S(1)}, u32[]{:S(2)}, u32[]{:S(2)}) collective-permute-start(bf16[8,2048]{1,0:T(8,128)(2,1)S(1)} %pad_maximum_fusion.2), channel_id=1, source_target_pairs={{0,1},{1,2},{2,3},{3,0},{4,5},{5,6},{6,7},{7,4},{8,9},{9,10},{10,1... | collective-permute-start | bytes 98312 | tf_op jit(solution)/shard_map/ppermute | solution.py:35
  33.5 7.4 %collective-permute-start.4 = (bf16[8,2048]{1,0:T(8,128)(2,1)S(1)}, bf16[8,2048]{1,0:T(8,128)(2,1)S(1)}, u32[]{:S(2)}, u32[]{:S(2)}) collective-permute-start(bf16[8,2048]{1,0:T(8,128)(2,1)S(1)} %pad_maximum_fusion.2), channel_id=1, source_target_pairs={{0,2},{1,3},{2,0},{3,1},{4,6},{5,7},{6,4},{7,5},{8,10},{9,11},{10,... | collective-permute-start | bytes 98312 | tf_op jit(solution)/shard_map/ppermute | solution.py:35
  37.9 5.1 %collective-permute-start.5 = (bf16[8,2048]{1,0:T(8,128)(2,1)S(1)}, bf16[8,2048]{1,0:T(8,128)(2,1)S(1)}, u32[]{:S(2)}, u32[]{:S(2)}) collective-permute-start(bf16[8,2048]{1,0:T(8,128)(2,1)S(1)} %pad_maximum_fusion.2), channel_id=1, source_target_pairs={{0,3},{1,0},{2,1},{3,2},{4,7},{5,4},{6,5},{7,6},{8,11},{9,8},{10,9... | collective-permute-start | bytes 98312 | tf_op jit(solution)/shard_map/ppermute | solution.py:35
  44.1 32.5 %all-to-all-start.1 = ((bf16[8,32,2048]{2,1,0:T(8,128)(2,1)}), bf16[8,32,2048]{2,1,0:T(8,128)(2,1)S(1)}, u32[]{:S(2)}, u32[]{:S(2)}) async-start(bf16[8,32,2048]{2,1,0:T(8,128)(2,1)} %broadcast_in_dim.5), calls=%async_computation.1 | async-start | bytes 2097152 | tf_op jit(solution)/shard_map/all_to_all | solution.py:273
  50.7 11.3 %collective-permute-start = (bf16[64,2048]{1,0:T(8,128)(2,1)S(1)}, bf16[64,2048]{1,0:T(8,128)(2,1)S(1)}, u32[]{:S(2)}, u32[]{:S(2)}) collective-permute-start(bf16[64,2048]{1,0:T(8,128)(2,1)S(1)} %bitcast.16), channel_id=1, source_target_pairs={{0,1},{1,2},{2,3},{3,0},{4,5},{5,6},{6,7},{7,4},{8,9},{9,10},{10,1... | collective-permute-start | bytes 786440 | tf_op jit(solution)/shard_map/ppermute | solution.py:35
  52.7 12.6 %collective-permute-start.1 = (bf16[64,2048]{1,0:T(8,128)(2,1)S(1)}, bf16[64,2048]{1,0:T(8,128)(2,1)S(1)}, u32[]{:S(2)}, u32[]{:S(2)}) collective-permute-start(bf16[64,2048]{1,0:T(8,128)(2,1)S(1)} %bitcast.17), channel_id=1, source_target_pairs={{0,2},{1,3},{2,0},{3,1},{4,6},{5,7},{6,4},{7,5},{8,10},{9,11},{10,... | collective-permute-start | bytes 786440 | tf_op jit(solution)/shard_map/ppermute | solution.py:35
  58.1 9.5 %collective-permute-start.2 = (bf16[64,2048]{1,0:T(8,128)(2,1)S(1)}, bf16[64,2048]{1,0:T(8,128)(2,1)S(1)}, u32[]{:S(2)}, u32[]{:S(2)}) collective-permute-start(bf16[64,2048]{1,0:T(8,128)(2,1)S(1)} %bitcast.18), channel_id=1, source_target_pairs={{0,3},{1,0},{2,1},{3,2},{4,7},{5,4},{6,5},{7,6},{8,11},{9,8},{10,9... | collective-permute-start | bytes 786440 | tf_op jit(solution)/shard_map/ppermute | solution.py:35
  79.9 9.2 %collective-permute-start.8 = (bf16[4096,256]{1,0:T(8,128)(2,1)}, bf16[4096,256]{1,0:T(8,128)(2,1)S(1)}, u32[]{:S(2)}, u32[]{:S(2)}) collective-permute-start(bf16[4096,256]{1,0:T(8,128)(2,1)} %collective-permute-done.6.mw.refs_4_.refs_5_), channel_id=1, source_target_pairs={{0,64},{64,0},{1,65},{65,1},{2,66},{66,2},{3,67},{67,3},{4,68},{68... | collective-permute-start | bytes 6291464 | tf_op jit(solution)/shard_map/ppermute | solution.py:30
  81.8 19.8 %collective-permute-start.7 = (bf16[4,512,512]{2,1,0:T(8,128)(2,1)}, bf16[4,512,512]{2,1,0:T(8,128)(2,1)}, u32[]{:S(2)}, u32[]{:S(2)}) collective-permute-start(bf16[4,512,512]{2,1,0:T(8,128)(2,1)} %bitcast.25), channel_id=1, source_target_pairs={{0,64},{64,0},{1,65},{65,1},{2,66},{66,2},{3,67},{67,3},{4,68},{68... | collective-permute-start | bytes 6291464 | tf_op jit(solution)/shard_map/ppermute | solution.py:30
  84.2 30.5 %all-to-all-start.3 = ((bf16[4,2,128,512]{3,2,1,0:T(8,128)(2,1)}), bf16[4,2,128,512]{3,2,1,0:T(8,128)(2,1)S(1)}, u32[]{:S(2)}, u32[]{:S(2)}) async-start(bf16[4,2,128,512]{3,2,1,0:T(8,128)(2,1)} %bitcast.22), calls=%async_computation.3 | async-start | bytes 2097152 | tf_op jit(solution)/shard_map/all_to_all | solution.py:293
  89.1 47.1 %all-gather.7.cloned.1.call-start = ((), (), s32[]{:S(2)}) async-start(), calls=%async_computation.5 | async-start | bytes 1310720 | tf_op jit(solution)/shard_map/all_gather | solution.py:298
  96.3 0.8 copy-start.1
  97.1 3.6 %collective-permute-start.9 = (bf16[128,512]{1,0:T(8,128)(2,1)S(1)}, bf16[128,512]{1,0:T(8,128)(2,1)S(1)}, u32[]{:S(2)}, u32[]{:S(2)}) collective-permute-start(bf16[128,512]{1,0:T(8,128)(2,1)S(1)} %get-tuple-element.21), channel_id=1, source_target_pairs={{0,64},{64,0},{1,65},{65,1},{2,66},{66,2},{3,67},{67,3},{4,68},{68... | collective-permute-start | bytes 393224 | tf_op jit(solution)/shard_map/ppermute | solution.py:30
  101.6 1.0 copy-start.2
  102.6 4.8 %copy-start.3 = (bf16[256,256]{1,0:T(8,128)(2,1)S(1)}, bf16[256,256]{1,0:T(8,128)(2,1)}, u32[]{:S(2)}) copy-start(bf16[256,256]{1,0:T(8,128)(2,1)} %constant.27.clone.pick) | copy-start | bytes 393220
  114.7 34.6 %all-to-all-start.2 = ((bf16[32,8,2048]{2,1,0:T(8,128)(2,1)}), bf16[32,8,2048]{2,1,0:T(8,128)(2,1)}, u32[]{:S(2)}, u32[]{:S(2)}) async-start(bf16[32,8,2048]{2,1,0:T(8,128)(2,1)} %bitcast.24), calls=%async_computation.2 | async-start | bytes 2097152 | tf_op jit(solution)/shard_map/all_to_all | solution.py:302
  119.4 3.8 %collective-permute-start.10 = (bf16[4,128,512]{2,1,0:T(8,128)(2,1)S(1)}, bf16[4,128,512]{2,1,0:T(8,128)(2,1)S(1)}, u32[]{:S(2)}, u32[]{:S(2)}) collective-permute-start(bf16[4,128,512]{2,1,0:T(8,128)(2,1)S(1)} %slice_bitcast_fusion), channel_id=1, source_target_pairs={{0,64},{64,0},{1,65},{65,1},{2,66},{66,2},{3,67},{67,3},{4,68},{68... | collective-permute-start | bytes 1572872 | tf_op jit(solution)/shard_map/ppermute | solution.py:30
  136.2 1.2 copy-start
  139.4 9.0 %collective-permute-start.11 = (bf16[256,512]{1,0:T(8,128)(2,1)S(1)}, bf16[256,512]{1,0:T(8,128)(2,1)S(1)}, u32[]{:S(2)}, u32[]{:S(2)}) collective-permute-start(bf16[256,512]{1,0:T(8,128)(2,1)S(1)} %get-tuple-element.23), channel_id=1, source_target_pairs={{0,32},{32,0},{1,33},{33,1},{2,34},{34,2},{3,35},{35,3},{4,36},{36... | collective-permute-start | bytes 786440 | tf_op jit(solution)/shard_map/ppermute | solution.py:30
Sparse Core Ops, SparseCore 0:
  10.1 54.1 all-gather.4
  101.7 34.4 all-gather.6

commit v8 on v7

--- a/solution.py
+++ b/solution.py
@@ -44,39 +44,34 @@
     return lax.ppermute(value, ("zh", "c", "zl"), pairs)
 
 
-def split_body(where, pick_tok, pick_cot, t0, t1, t2, t3, c, tok, cot):
+def split_body(where, pick, r0, r1, r2, r3, tok, cot):
     n = NY * ROWS
-    for i, piece in enumerate((t0, t1, t2, t3)):
-        rows = contract(pick_tok[...], piece[...], 1, 0).astype(BF16)
-        tok[0, i * n : (i + 1) * n] = rows[:n]
-        tok[1, i * n : (i + 1) * n] = rows[n:]
-    rows = contract(pick_cot[...], c[...], 1, 0).astype(BF16)
-    cot[0, 0, 0] = rows[:HALF]
-    cot[1, 0, 0] = rows[HALF:]
-
-
-def split(where, pieces, cot):
-    whole = lambda n: pl.BlockSpec((n, n), lambda j, s: (0, 0))
+    for i, piece in enumerate((r0, r1, r2, r3)):
+        rows = contract(pick[...], piece[...], 1, 0).astype(BF16)
+        tok[i * n : (i + 1) * n] = rows[:n]
+        cot[0, 0, i * n : (i + 1) * n] = rows[n:]
+
+
+def split(where, pieces):
+    piece = pl.BlockSpec((PIECE, FEATS), lambda j, s: (0, j))
     return pl.pallas_call(
         split_body,
         grid_spec=pltpu.PrefetchScalarGridSpec(
             num_scalar_prefetch=1,
-            grid=(STEPS // 2,),
-            in_specs=[whole(PIECE), whole(2 * HALF)]
-            + [pl.BlockSpec((PIECE, FEATS), lambda j, s: (0, j))] * 4
-            + [pl.BlockSpec((2 * HALF, FEATS), lambda j, s: (0, j))],
+            grid=(STEPS,),
+            in_specs=[pl.BlockSpec((PIECE, PIECE), lambda j, s: (0, 0))] + [piece] * 4,
             out_specs=[
-                pl.BlockSpec((2, HALF, FEATS), lambda j, s: (0, 0, j)),
-                pl.BlockSpec((2, 1, 1, HALF, FEATS), lambda j, s: (0, j // 2, flip(j % 2, s[0]), 0, 0)),
+                pl.BlockSpec((HALF, FEATS), lambda j, s: (0, j)),
+                pl.BlockSpec((1, 1, HALF, FEATS), lambda j, s: (j // 2, flip(j % 2, s[0]), 0, 0)),
             ],
         ),
         out_shape=[
-            hbm((2, HALF, D // 2), BF16),
-            hbm((2, NZ // 2, 2, HALF, FEATS), BF16),
+            hbm((HALF, D), BF16),
+            hbm((NZ, 2, HALF, FEATS), BF16),
         ],
         compiler_params=pltpu.CompilerParams(vmem_limit_bytes=32 * 2**20),
         name="split",
-    )(where, *picks(), *pieces, cot)
+    )(where, selection((NY, 2, ROWS), (1, 0, 2)), *pieces)
 
 
 def hbm(shape, dtype):
@@ -98,7 +93,7 @@
     def _():
         acc[...] = jnp.zeros_like(acc)
 
-    t = tok[0]
+    t = tok[...]
     for i, w in enumerate((gw, uw, mw, ow)):
         acc[:, i * HID : (i + 1) * HID] += contract(t, w[...], 1, 0)
 
@@ -128,7 +123,7 @@
         grid_spec=pltpu.PrefetchScalarGridSpec(
             num_scalar_prefetch=1,
             grid=(STEPS,),
-            in_specs=[pl.BlockSpec((1, HALF, FEATS), lambda j, s: (j // NZ, 0, j % NZ))] + [weight] * 4,
+            in_specs=[pl.BlockSpec((HALF, FEATS), lambda j, s: (0, j))] + [weight] * 4,
             out_specs=[
                 pl.BlockSpec((HALF, 2 * HID), lambda j, s: (0, 0)),
                 pl.BlockSpec((HALF, 4 * HID), lambda j, s: (0, 0)),
@@ -216,39 +211,29 @@
     )(where, merge(), dd, gw, gw, uw, uw, mw, mw, ow, ow)
 
 
-def grads_body(h, cn, cf, keep, send, acc):
-    step = pl.program_id(0)
-
-    @pl.when(step == 0)
-    def _():
-        acc[...] = jnp.zeros_like(acc)
-
-    acc[...] += contract(h[0, 0], cn[0, 0], 0, 0) + contract(h[0, 1], cf[0], 0, 0)
-
-    @pl.when(step == NZ - 1)
-    def _():
-        keep[...] = acc[:HID]
-        send[...] = acc[HID:].astype(BF16)
-
-
-def grads(hidden, cot_near, cot_far):
+def grads_body(where, h, n0, n1, n2, n3, far, keep, send):
+    total = None
+    for j, near in enumerate((n0, n1, n2, n3)):
+        z = (where[3] + NZ - j) % NZ
+        part = contract(h[z, 0], near[0], 0, 0) + contract(h[z, 1], far[j], 0, 0)
+        total = part if total is None else total + part
+    keep[...] = total[:HID]
+    send[...] = total[HID:].astype(BF16)
+
+
+def grads(where, hidden, near, far):
+    vmem = pl.BlockSpec(memory_space=pltpu.MemorySpace.VMEM)
     return pl.pallas_call(
         grads_body,
-        grid=(NZ,),
-        in_specs=[
-            pl.BlockSpec((1, 2, HALF, 2 * HID), lambda j: (j, 0, 0, 0)),
-            pl.BlockSpec((1, 1, HALF, FEATS), lambda j: (j, 0, 0, 0)),
-            pl.BlockSpec((1, HALF, FEATS), lambda j: (j, 0, 0)),
-        ],
-        out_specs=[pl.BlockSpec((HID, FEATS), lambda j: (0, 0))] * 2,
+        in_specs=[pl.BlockSpec(memory_space=pltpu.MemorySpace.SMEM)] + [vmem] * 6,
+        out_specs=[vmem] * 2,
         out_shape=[
             jax.ShapeDtypeStruct((HID, FEATS), F32),
             jax.ShapeDtypeStruct((HID, FEATS), BF16),
         ],
-        scratch_shapes=[pltpu.VMEM((2 * HID, FEATS), F32)],
         compiler_params=pltpu.CompilerParams(vmem_limit_bytes=32 * 2**20),
         name="grads",
-    )(hidden, cot_near, cot_far)
+    )(where, hidden.reshape(NZ, 2, HALF, 2 * HID), *near, far)
 
 
 def selection(shape, order):
@@ -256,16 +241,8 @@
     return jnp.asarray(np.eye(source.size, dtype=np.float32)[source], BF16)
 
 
-def picks():
-    return selection((NY, 2, ROWS), (1, 0, 2)), selection((NY, NX, 2, ROWS), (2, 1, 0, 3))
-
-
 def merge():
     return selection((2, NX, NY, ROWS), (1, 2, 0, 3))
-
-
-def folded(rows):
-    return jnp.concatenate([rows[:, : D // 2], rows[:, D // 2 :]], axis=0)
 
 
 def spread(block, axis):
@@ -275,23 +252,18 @@
 
 def on_device(tokens, cotangent, gate_weight, up_weight, down_weight):
     core = lax.axis_index("c")
-    where = jnp.stack([core, lax.axis_index("zl"), lax.axis_index("x")]).astype(jnp.int32)
+    where = [core, lax.axis_index("zl"), lax.axis_index("x"), lax.axis_index("zh")]
+    where = jnp.stack(where).astype(jnp.int32)
 
     picked = jnp.where(core == 0, gate_weight, up_weight)
     picked, tokens = lax.optimization_barrier((picked, tokens))
     mine = neighbours(picked)
     down_near = lax.all_gather(down_weight, ("zh", "zl"), axis=0).reshape(NZ, 2 * HID, FEATS)
 
-    tok = spread(folded(tokens), "y").reshape(PIECE, D // 2)
-    cot = folded(cotangent)
-    cot = jnp.concatenate([cot] + [shift(cot, "x", k) for k in (1, 2, 3)], axis=0)
-    cot = spread(cot, "y").reshape(2 * HALF, D // 2)
-    tok = [tok] + [shift(tok, "x", k) for k in (1, 2, 3)]
-
-    tok, cot = split(where, tok, cot)
-    cot = cot.reshape(NZ, 2, HALF, FEATS)
-    cot_x = lax.all_to_all(cot, "zh", 0, 0)
-    cot_far = swap(cot_x[:, 1], "c")
+    block = spread(jnp.concatenate([tokens, cotangent], axis=0), "y").reshape(PIECE, D)
+    pieces = [block] + [shift(block, "x", k) for k in (1, 2, 3)]
+
+    tok, cot = split(where, pieces)
     tok, mine, down_near = lax.optimization_barrier((tok, mine, down_near))
     other, down_far = swap(mine, "c"), swap(down_near, "c")
     hidden, factors = gates(where, tok, gate_weight, up_weight, mine, other)
@@ -299,11 +271,15 @@
     dd = down(where, cot, down_near, down_far, factors)
 
     parts = term(where, dd, gate_weight, up_weight, mine, other)
+    parts, cot = lax.optimization_barrier((parts, cot))
     parts = lax.all_to_all(parts.reshape(NX * NY, 2 * ROWS, D // 2), ("x", "y"), 0, 0)
     total = jnp.sum(parts.astype(F32), axis=0).astype(BF16)
     input_grad = jnp.concatenate([total[:ROWS], total[ROWS:]], axis=1)
 
-    keep, send = grads(hidden, cot_x, cot_far)
+    at = lambda k: lax.dynamic_index_in_dim(cot, (lax.axis_index("zh") + k) % NZ, 0, keepdims=False)
+    near = [at(0)] + [shift(at(k), "zh", k) for k in (1, 2, 3)]
+    far = swap(jnp.stack([n[1] for n in near]), "c")
+    keep, send = grads(where, hidden, near, far)
     down_grad = keep + swap(send, "zl").astype(F32)
     return (input_grad, down_grad)
 

time: 160 us -> 180 us (1.12)
  blocking collectives: 0 us -> 19.4 us
  waiting for transfers between devices: 41.8 us -> 56.5 us
  starting transfers between devices: 65.6 us -> 54.4 us
  local copies, waits for them, and re-layouts: 4.98 us -> 1.43 us
    ppermute x6, waiting for transfers between devices: 9.42 us -> 43.7 us  [shift(): return lax.ppermute(value, axis, [(i, (i + k) % n) for i in range(n)])]
    all_to_all x0 -> x1, blocking collectives: none -> 19.4 us  [spread(): lax.all_to_all(jnp.broadcast_to(block[None], (n, *block.shape)), axis, 0, 0)]
    all_to_all x3 -> x0, starting transfers between devices: 19.3 us -> none  [the longest x2 14.4 us: spread(): lax.all_to_all(jnp.broadcast_to(block[None], (n, *block.shape)), axis, 0, 0)]
    all_gather x1, waiting for transfers between devices: 13 us -> 0.01 us  [on_device(): lax.all_gather(jnp.stack([hidden, swap(hidden, 'c')]), 'zh', axis=0)]
    all_to_all x3 -> x0, waiting for transfers between devices: 9.08 us -> none  [the longest x2 9.07 us: spread(): lax.all_to_all(jnp.broadcast_to(block[None], (n, *block.shape)), axis, 0, 0)]
    ppermute x6, starting transfers between devices: 19.8 us -> 27 us  [shift(): return lax.ppermute(value, axis, [(i, (i + k) % n) for i in range(n)])]
    ppermute x5, waiting for transfers between devices: 9.6 us -> 12.1 us  [swap(): return lax.ppermute(value, axis, [(0, 1), (1, 0)])]
    unnamed x16 -> x12, local copies, waits for them, and re-layouts: 3.07 us -> 1.25 us
  transfers between devices with their start and end apart: 18 -> 15, of which waited for: 9 -> 10; matrix products, arithmetic and copies ran while one was open for 4% -> 3% of each run, Pallas kernels for 16% -> 14%
where the time goes in v8:
time: 180 us; the launch traced here: 179 us
  waiting for transfers between devices  56.5 us (31%)
  starting transfers between devices  54.4 us (30%)
  Pallas kernels  25.7 us (14%)
  blocking collectives  19.4 us (11%)
  between operations  14.4 us (8%)
  other arithmetic  6.97 us (4%)
    ppermute x6, waiting for transfers between devices, shift(): return lax.ppermute(value, axis, [(i, (i + k) % n) for i in range(n)])  43.7 us
    ppermute x6, starting transfers between devices, shift(): return lax.ppermute(value, axis, [(i, (i + k) % n) for i in range(n)])  27 us
    all_to_all x1, blocking collectives, spread(): lax.all_to_all(jnp.broadcast_to(block[None], (n, *block.shape)), axis, 0, 0)  19.4 us
    ppermute x5, waiting for transfers between devices, swap(): return lax.ppermute(value, axis, [(0, 1), (1, 0)])  12.1 us
    ppermute x1, starting transfers between devices, neighbours(): return lax.ppermute(value, ('zh', 'c', 'zl'), pairs)  11.5 us
    ppermute x5, starting transfers between devices, swap(): return lax.ppermute(value, axis, [(0, 1), (1, 0)])  10.7 us
    pallas_call x1, Pallas kernels, term(): pl.pallas_call(term_body, grid_spec=pltpu.PrefetchScalarGridSpec(num_scal...  7.25 us
    pallas_call x1, Pallas kernels, gates(): pl.pallas_call(gates_body, grid_spec=pltpu.PrefetchScalarGridSpec(num_sca...  7.16 us
  transfers between devices with their start and end apart: 15, of which 10 were waited for; matrix products, arithmetic and copies ran while one was open for 3% of the time, Pallas kernels for 14%

profile of v8, /device:TPU:1, one launch (start us, length us, event | category | flops | bytes accessed | tf_op | source)
XLA Modules:
  0.0 178.9 jit_solution(17315471218870552636)
XLA Ops:
  7.2 0.0 all-gather.5.cloned.1.call-start
  7.2 0.7 all-gather.5.cloned.1.call-update
  7.9 0.0 all-gather.7.cloned.1.call-start
  8.0 0.0 copy-start.4
  8.0 0.0 copy-start.5
  8.0 0.0 copy-start.2
  8.0 3.2 %broadcast_select_fusion = bf16[4096,256]{1,0:T(8,128)(2,1)} fusion(bf16[4096,256]{1,0:T(8,128)(2,1)} %refs_1_.1, bf16[4096,256]{1,0:T(8,128)(2,1)} %refs_3_.1, pred[]{:T(512)S(6)} %eq.8), kind=kLoop, calls=%fused_computation | loop fusion | flops 1048576 | bytes 6291457 | tf_op jit(solution)/shard_map/jit(_where)/select_n | solution.py:258
  11.2 11.5 %collective-permute-start.3 = (bf16[4096,256]{1,0:T(8,128)(2,1)}, bf16[4096,256]{1,0:T(8,128)(2,1)}, u32[]{:S(2)}, u32[]{:S(2)}) collective-permute-start(bf16[4096,256]{1,0:T(8,128)(2,1)} %broadcast_select_fusion), channel_id=1, source_target_pairs={{0,32},{32,0},{96,192},{192,96},{128,160},{160,128},{224,320},{320... | collective-permute-start | bytes 6291464 | tf_op jit(solution)/shard_map/ppermute | solution.py:44
  22.7 0.0 copy-done.4
  22.7 0.0 copy-done.5
  22.8 19.4 %all_to_all.10 = bf16[8,8,4096]{2,1,0:T(8,128)(2,1)S(1)} all-to-all(bf16[8,8,4096]{2,1,0:T(8,128)(2,1)S(1)} %broadcast_in_dim.2), channel_id=1, replica_groups=mesh['zh'=4,'c'=2,'zl'=2,'y'=8,'x'=4] {'y'}, dimensions={0} | all-to-all | bytes 1048576 | tf_op jit(solution)/shard_map/all_to_all | solution.py:250
  42.2 3.1 %collective-permute-start = (bf16[64,4096]{1,0:T(8,128)(2,1)S(1)}, bf16[64,4096]{1,0:T(8,128)(2,1)S(1)}, u32[]{:S(2)}, u32[]{:S(2)}) collective-permute-start(bf16[64,4096]{1,0:T(8,128)(2,1)S(1)} %bitcast.20), channel_id=1, source_target_pairs={{0,1},{1,2},{2,3},{3,0},{4,5},{5,6},{6,7},{7,4},{8,9},{9,10},{10,1... | collective-permute-start | bytes 1572872 | tf_op jit(solution)/shard_map/ppermute | solution.py:35
  45.3 4.4 %collective-permute-start.1 = (bf16[64,4096]{1,0:T(8,128)(2,1)S(1)}, bf16[64,4096]{1,0:T(8,128)(2,1)S(1)}, u32[]{:S(2)}, u32[]{:S(2)}) collective-permute-start(bf16[64,4096]{1,0:T(8,128)(2,1)S(1)} %bitcast.21), channel_id=1, source_target_pairs={{0,2},{1,3},{2,0},{3,1},{4,6},{5,7},{6,4},{7,5},{8,10},{9,11},{10,... | collective-permute-start | bytes 1572872 | tf_op jit(solution)/shard_map/ppermute | solution.py:35
  49.7 3.1 %collective-permute-start.2 = (bf16[64,4096]{1,0:T(8,128)(2,1)S(1)}, bf16[64,4096]{1,0:T(8,128)(2,1)S(1)}, u32[]{:S(2)}, u32[]{:S(2)}) collective-permute-start(bf16[64,4096]{1,0:T(8,128)(2,1)S(1)} %bitcast.22), channel_id=1, source_target_pairs={{0,3},{1,0},{2,1},{3,2},{4,7},{5,4},{6,5},{7,6},{8,11},{9,8},{10,9... | collective-permute-start | bytes 1572872 | tf_op jit(solution)/shard_map/ppermute | solution.py:35
  52.7 0.1 pad_add_fusion.where
  52.8 5.6 %collective-permute-done.r1 = bf16[64,4096]{1,0:T(8,128)(2,1)S(1)} collective-permute-done((bf16[64,4096]{1,0:T(8,128)(2,1)S(1)}, bf16[64,4096]{1,0:T(8,128)(2,1)S(1)}, u32[]{:S(2)}, u32[]{:S(2)}) %collective-permute-start) | collective-permute-done | bytes 524320 | tf_op jit(solution)/shard_map/ppermute | solution.py:35
  58.4 8.7 %collective-permute-done.1.r2 = bf16[64,4096]{1,0:T(8,128)(2,1)S(1)} collective-permute-done((bf16[64,4096]{1,0:T(8,128)(2,1)S(1)}, bf16[64,4096]{1,0:T(8,128)(2,1)S(1)}, u32[]{:S(2)}, u32[]{:S(2)}) %collective-permute-start.1) | collective-permute-done | bytes 524320 | tf_op jit(solution)/shard_map/ppermute | solution.py:35
  67.1 1.8 %collective-permute-done.2.r3 = bf16[64,4096]{1,0:T(8,128)(2,1)S(1)} collective-permute-done((bf16[64,4096]{1,0:T(8,128)(2,1)S(1)}, bf16[64,4096]{1,0:T(8,128)(2,1)S(1)}, u32[]{:S(2)}, u32[]{:S(2)}) %collective-permute-start.2) | collective-permute-done | bytes 524320 | tf_op jit(solution)/shard_map/ppermute | solution.py:35
  68.9 0.0 copy-done.2
  68.9 4.8 %split.1 = (bf16[128,4096]{1,0:T(8,128)(2,1)}, bf16[4,2,128,512]{3,2,1,0:T(8,128)(2,1)}) custom-call(s32[4]{0:T(128)S(1)} %pad_add_fusion.where, bf16[64,64]{1,0:T(8,128)(2,1)S(1)} %copy-done.2, bf16[64,4096]{1,0:T(8,128)(2,1)S(1)} %bitcast.23, bf16[64,4096]{1,0:T(8,128)(2,1)S(1)} %collective-permute-done.r1, ...), custom_call_target="tpu_custom_call" | custom-call | tf_op jit(solution)/shard_map/split/pallas_call | solution.py:57
  73.7 0.0 collective-permute-done.3.mw.refs_4_.refs_5_
  73.7 0.0 all-gather.5.cloned.1.call-done
  73.7 1.9 %collective-permute-start.5 = (bf16[4096,256]{1,0:T(8,128)(2,1)}, bf16[4096,256]{1,0:T(8,128)(2,1)S(1)}, u32[]{:S(2)}, u32[]{:S(2)}) collective-permute-start(bf16[4096,256]{1,0:T(8,128)(2,1)} %collective-permute-done.3.mw.refs_4_.refs_5_), channel_id=1, source_target_pairs={{0,64},{64,0},{1,65},{65,1},{2,66},{66,2},{3,67},{67,3},{4,68},{68... | collective-permute-start | bytes 6291464 | tf_op jit(solution)/shard_map/ppermute | solution.py:30
  75.6 2.4 %collective-permute-start.4 = (bf16[4,512,512]{2,1,0:T(8,128)(2,1)}, bf16[4,512,512]{2,1,0:T(8,128)(2,1)}, u32[]{:S(2)}, u32[]{:S(2)}) collective-permute-start(bf16[4,512,512]{2,1,0:T(8,128)(2,1)} %bitcast.27), channel_id=1, source_target_pairs={{0,64},{64,0},{1,65},{65,1},{2,66},{66,2},{3,67},{67,3},{4,68},{68... | collective-permute-start | bytes 6291464 | tf_op jit(solution)/shard_map/ppermute | solution.py:30
  78.0 1.9 %collective-permute-done.5.ow.refs_6_.refs_7_ = bf16[4096,256]{1,0:T(8,128)(2,1)S(1)} collective-permute-done((bf16[4096,256]{1,0:T(8,128)(2,1)}, bf16[4096,256]{1,0:T(8,128)(2,1)S(1)}, u32[]{:S(2)}, u32[]{:S(2)}) %collective-permute-start.5) | collective-permute-done | bytes 2097184 | tf_op jit(solution)/shard_map/ppermute | solution.py:30
  79.9 7.2 %gates.1 = (bf16[128,512]{1,0:T(8,128)(2,1)S(1)}, f32[128,1024]{1,0:T(8,128)S(1)}) custom-call(s32[4]{0:T(128)S(1)} %pad_add_fusion.where, bf16[128,4096]{1,0:T(8,128)(2,1)} %get-tuple-element.20.tok, bf16[4096,256]{1,0:T(8,128)(2,1)} %refs_1_.1, bf16[4096,256]{1,0:T(8,128)(2,1)} %refs_3_.1, bf16[4096,256]{1,0:T(8,128)(2,1)} %collective-permute-done.3.mw.refs_4_.refs_5_, ...), custom_call_target="tpu_custom_call" | custom-call | tf_op jit(solution)/shard_map/gates/pallas_call | solution.py:121
  87.1 2.0 %collective-permute-start.6 = (bf16[128,512]{1,0:T(8,128)(2,1)S(1)}, bf16[128,512]{1,0:T(8,128)(2,1)S(1)}, u32[]{:S(2)}, u32[]{:S(2)}) collective-permute-start(bf16[128,512]{1,0:T(8,128)(2,1)S(1)} %get-tuple-element.24), channel_id=1, source_target_pairs={{0,64},{64,0},{1,65},{65,1},{2,66},{66,2},{3,67},{67,3},{4,68},{68... | collective-permute-start | bytes 393224 | tf_op jit(solution)/shard_map/ppermute | solution.py:30
  89.1 1.2 collective-permute-done.6
  90.3 0.7 pad_maximum_fusion.1
  91.1 0.0 all-gather.7.cloned.1.call-update
  91.1 0.0 collective-permute-done.4.df
  91.1 0.0 copy-start.1
  91.1 4.8 %down.1.dd = bf16[128,1024]{1,0:T(8,128)(2,1)S(1)} custom-call(s32[4]{0:T(128)S(1)} %pad_add_fusion.where, bf16[4,2,128,512]{3,2,1,0:T(8,128)(2,1)} %get-tuple-element.25.cot, bf16[4,512,512]{2,1,0:T(8,128)(2,1)} %bitcast.28, bf16[4,512,512]{2,1,0:T(8,128)(2,1)} %collective-permute-done.4.df, f32[128,1024]{1,0:T(8,128)S(1)} %get-tuple-element.22.fac), custom_call_target="tpu_custom_call" | custom-call | tf_op jit(solution)/shard_map/down/pallas_call | solution.py:163
  95.9 0.0 copy-done.1
  95.9 7.2 %term.1 = bf16[4,64,2048]{2,1,0:T(8,128)(2,1)} custom-call(s32[4]{0:T(128)S(1)} %pad_add_fusion.where, bf16[256,256]{1,0:T(8,128)(2,1)S(1)} %copy-done.1, bf16[128,1024]{1,0:T(8,128)(2,1)S(1)} %down.1.dd, bf16[4096,256]{1,0:T(8,128)(2,1)} %refs_1_.1, bf16[4096,256]{1,0:T(8,128)(2,1)} %refs_1_.1, bf16[4096,256]{1,0:T(8,128)(2,1)} %refs_3_.1, ...), custom_call_target="tpu_custom_call" | custom-call | tf_op jit(solution)/shard_map/term/pallas_call | solution.py:196
  103.1 0.0 copy-start.3
  103.1 5.2 %all-to-all-start.1 = ((bf16[32,8,2048]{2,1,0:T(8,128)(2,1)}), bf16[32,8,2048]{2,1,0:T(8,128)(2,1)}, u32[]{:S(2)}, u32[]{:S(2)}) async-start(bf16[32,8,2048]{2,1,0:T(8,128)(2,1)} %bitcast.26), calls=%async_computation.1 | async-start | bytes 2097152 | tf_op jit(solution)/shard_map/all_to_all | solution.py:275
  108.4 0.0 copy-done.3
  108.4 0.1 dynamic-slice_bitcast_fusion
  108.5 3.5 %collective-permute-start.7 = (bf16[2,128,512]{2,1,0:T(8,128)(2,1)S(1)}, bf16[2,128,512]{2,1,0:T(8,128)(2,1)S(1)}, u32[]{:S(2)}, u32[]{:S(2)}) collective-permute-start(bf16[2,128,512]{2,1,0:T(8,128)(2,1)S(1)} %get-tuple-element.30), channel_id=1, source_target_pairs={{0,128},{128,256},{256,384},{384,0},{1,129},{129,257},{257,385},{3... | collective-permute-start | bytes 786440 | tf_op jit(solution)/shard_map/ppermute | solution.py:35
  112.0 9.9 %collective-permute-start.8 = (bf16[2,128,512]{2,1,0:T(8,128)(2,1)S(1)}, bf16[2,128,512]{2,1,0:T(8,128)(2,1)S(1)}, u32[]{:S(2)}, u32[]{:S(2)}) collective-permute-start(bf16[2,128,512]{2,1,0:T(8,128)(2,1)S(1)} %get-tuple-element.29), channel_id=1, source_target_pairs={{0,256},{128,384},{256,0},{384,128},{1,257},{129,385},{257,1},{385... | collective-permute-start | bytes 786440 | tf_op jit(solution)/shard_map/ppermute | solution.py:35
  121.8 3.1 %collective-permute-start.9 = (bf16[2,128,512]{2,1,0:T(8,128)(2,1)S(1)}, bf16[2,128,512]{2,1,0:T(8,128)(2,1)S(1)}, u32[]{:S(2)}, u32[]{:S(2)}) collective-permute-start(bf16[2,128,512]{2,1,0:T(8,128)(2,1)S(1)} %get-tuple-element.28), channel_id=1, source_target_pairs={{0,384},{128,0},{256,128},{384,256},{1,385},{129,1},{257,129},{385... | collective-permute-start | bytes 786440 | tf_op jit(solution)/shard_map/ppermute | solution.py:35
  125.0 16.0 %collective-permute-done.7.n1 = bf16[2,128,512]{2,1,0:T(8,128)(2,1)S(1)} collective-permute-done((bf16[2,128,512]{2,1,0:T(8,128)(2,1)S(1)}, bf16[2,128,512]{2,1,0:T(8,128)(2,1)S(1)}, u32[]{:S(2)}, u32[]{:S(2)}) %collective-permute-start.7) | collective-permute-done | bytes 262176 | tf_op jit(solution)/shard_map/ppermute | solution.py:35
  140.9 8.4 %collective-permute-done.8.n2 = bf16[2,128,512]{2,1,0:T(8,128)(2,1)S(1)} collective-permute-done((bf16[2,128,512]{2,1,0:T(8,128)(2,1)S(1)}, bf16[2,128,512]{2,1,0:T(8,128)(2,1)S(1)}, u32[]{:S(2)}, u32[]{:S(2)}) %collective-permute-start.8) | collective-permute-done | bytes 262176 | tf_op jit(solution)/shard_map/ppermute | solution.py:35
  149.4 3.3 %collective-permute-done.9.n3 = bf16[2,128,512]{2,1,0:T(8,128)(2,1)S(1)} collective-permute-done((bf16[2,128,512]{2,1,0:T(8,128)(2,1)S(1)}, bf16[2,128,512]{2,1,0:T(8,128)(2,1)S(1)}, u32[]{:S(2)}, u32[]{:S(2)}) %collective-permute-start.9) | collective-permute-done | bytes 262176 | tf_op jit(solution)/shard_map/ppermute | solution.py:35
  152.7 0.1 pad_maximum_fusion
  152.7 2.4 %collective-permute-start.10 = (bf16[4,128,512]{2,1,0:T(8,128)(2,1)S(1)}, bf16[4,128,512]{2,1,0:T(8,128)(2,1)S(1)}, u32[]{:S(2)}, u32[]{:S(2)}) collective-permute-start(bf16[4,128,512]{2,1,0:T(8,128)(2,1)S(1)} %pad_maximum_fusion), channel_id=1, source_target_pairs={{0,64},{64,0},{1,65},{65,1},{2,66},{66,2},{3,67},{67,3},{4,68},{68... | collective-permute-start | bytes 1572872 | tf_op jit(solution)/shard_map/ppermute | solution.py:30
  155.2 1.5 collective-permute-done.10.far
  156.7 0.0 all-gather.7.cloned.1.call-done
  156.7 0.0 copy-start
  156.7 1.2 copy-done
  157.9 1.8 %grads.1 = (f32[256,512]{1,0:T(8,128)S(1)}, bf16[256,512]{1,0:T(8,128)(2,1)S(1)}) custom-call(s32[4]{0:T(128)S(1)} %pad_add_fusion.where, bf16[4,2,128,512]{3,2,1,0:T(8,128)(2,1)S(1)} %bitcast.24, bf16[2,128,512]{2,1,0:T(8,128)(2,1)S(1)} %get-tuple-element.31.n0, bf16[2,128,512]{2,1,0:T(8,128)(2,1)S(1)} %collective-permute-done.7.n1, ...), custom_call_target="tpu_custom_call" | custom-call | tf_op jit(solution)/shard_map/grads/pallas_call | solution.py:226
  159.7 1.9 %collective-permute-start.11 = (bf16[256,512]{1,0:T(8,128)(2,1)S(1)}, bf16[256,512]{1,0:T(8,128)(2,1)S(1)}, u32[]{:S(2)}, u32[]{:S(2)}) collective-permute-start(bf16[256,512]{1,0:T(8,128)(2,1)S(1)} %get-tuple-element.27), channel_id=1, source_target_pairs={{0,32},{32,0},{1,33},{33,1},{2,34},{34,2},{3,35},{35,3},{4,36},{36... | collective-permute-start | bytes 786440 | tf_op jit(solution)/shard_map/ppermute | solution.py:30
  161.7 7.5 %collective-permute-done.11 = bf16[256,512]{1,0:T(8,128)(2,1)S(1)} collective-permute-done((bf16[256,512]{1,0:T(8,128)(2,1)S(1)}, bf16[256,512]{1,0:T(8,128)(2,1)S(1)}, u32[]{:S(2)}, u32[]{:S(2)}) %collective-permute-start.11) | collective-permute-done | bytes 262176 | tf_op jit(solution)/shard_map/ppermute | solution.py:30
  169.1 0.9 convert_add_fusion
  170.0 0.0 all-to-all-done.1
  170.0 1.4 reduce_sum.12
  171.4 0.6 pad_maximum_fusion.3
  (7 shorter events, 0.1 us)
Async XLA Ops:
  7.2 66.5 %all-gather.5.cloned.1.call-start = ((), (), s32[]{:S(2)}) async-start(), calls=%async_computation.2 | async-start | bytes 2359296 | tf_op jit(solution)/shard_map/all_gather | solution.py:261
  7.9 148.8 %all-gather.7.cloned.1.call-start = ((), (), s32[]{:S(2)}) async-start(), calls=%async_computation.3 | async-start | bytes 1310720 | tf_op jit(solution)/shard_map/all_gather | solution.py:270
  8.0 14.7 %copy-start.4 = (bf16[4,4096]{1,0:T(4,128)(2,1)S(1)}, bf16[4,4096]{1,0:T(4,128)(2,1)}, u32[]{:S(2)}) copy-start(bf16[4,4096]{1,0:T(4,128)(2,1)} %param.8) | copy-start | bytes 98308
  8.0 14.7 %copy-start.5 = (bf16[4,4096]{1,0:T(4,128)(2,1)S(1)}, bf16[4,4096]{1,0:T(4,128)(2,1)}, u32[]{:S(2)}) copy-start(bf16[4,4096]{1,0:T(4,128)(2,1)} %param.7) | copy-start | bytes 98308
  8.0 60.9 %copy-start.2 = (bf16[64,64]{1,0:T(8,128)(2,1)S(1)}, bf16[64,64]{1,0:T(8,128)(2,1)}, u32[]{:S(2)}) copy-start(bf16[64,64]{1,0:T(8,128)(2,1)} %constant.66.clone.pick) | copy-start | bytes 24580
  11.2 62.5 %collective-permute-start.3 = (bf16[4096,256]{1,0:T(8,128)(2,1)}, bf16[4096,256]{1,0:T(8,128)(2,1)}, u32[]{:S(2)}, u32[]{:S(2)}) collective-permute-start(bf16[4096,256]{1,0:T(8,128)(2,1)} %broadcast_select_fusion), channel_id=1, source_target_pairs={{0,32},{32,0},{96,192},{192,96},{128,160},{160,128},{224,320},{320... | collective-permute-start | bytes 6291464 | tf_op jit(solution)/shard_map/ppermute | solution.py:44
  42.2 16.2 %collective-permute-start = (bf16[64,4096]{1,0:T(8,128)(2,1)S(1)}, bf16[64,4096]{1,0:T(8,128)(2,1)S(1)}, u32[]{:S(2)}, u32[]{:S(2)}) collective-permute-start(bf16[64,4096]{1,0:T(8,128)(2,1)S(1)} %bitcast.20), channel_id=1, source_target_pairs={{0,1},{1,2},{2,3},{3,0},{4,5},{5,6},{6,7},{7,4},{8,9},{9,10},{10,1... | collective-permute-start | bytes 1572872 | tf_op jit(solution)/shard_map/ppermute | solution.py:35
  45.3 21.8 %collective-permute-start.1 = (bf16[64,4096]{1,0:T(8,128)(2,1)S(1)}, bf16[64,4096]{1,0:T(8,128)(2,1)S(1)}, u32[]{:S(2)}, u32[]{:S(2)}) collective-permute-start(bf16[64,4096]{1,0:T(8,128)(2,1)S(1)} %bitcast.21), channel_id=1, source_target_pairs={{0,2},{1,3},{2,0},{3,1},{4,6},{5,7},{6,4},{7,5},{8,10},{9,11},{10,... | collective-permute-start | bytes 1572872 | tf_op jit(solution)/shard_map/ppermute | solution.py:35
  49.7 19.2 %collective-permute-start.2 = (bf16[64,4096]{1,0:T(8,128)(2,1)S(1)}, bf16[64,4096]{1,0:T(8,128)(2,1)S(1)}, u32[]{:S(2)}, u32[]{:S(2)}) collective-permute-start(bf16[64,4096]{1,0:T(8,128)(2,1)S(1)} %bitcast.22), channel_id=1, source_target_pairs={{0,3},{1,0},{2,1},{3,2},{4,7},{5,4},{6,5},{7,6},{8,11},{9,8},{10,9... | collective-permute-start | bytes 1572872 | tf_op jit(solution)/shard_map/ppermute | solution.py:35
  73.7 6.3 %collective-permute-start.5 = (bf16[4096,256]{1,0:T(8,128)(2,1)}, bf16[4096,256]{1,0:T(8,128)(2,1)S(1)}, u32[]{:S(2)}, u32[]{:S(2)}) collective-permute-start(bf16[4096,256]{1,0:T(8,128)(2,1)} %collective-permute-done.3.mw.refs_4_.refs_5_), channel_id=1, source_target_pairs={{0,64},{64,0},{1,65},{65,1},{2,66},{66,2},{3,67},{67,3},{4,68},{68... | collective-permute-start | bytes 6291464 | tf_op jit(solution)/shard_map/ppermute | solution.py:30
  75.6 15.5 %collective-permute-start.4 = (bf16[4,512,512]{2,1,0:T(8,128)(2,1)}, bf16[4,512,512]{2,1,0:T(8,128)(2,1)}, u32[]{:S(2)}, u32[]{:S(2)}) collective-permute-start(bf16[4,512,512]{2,1,0:T(8,128)(2,1)} %bitcast.27), channel_id=1, source_target_pairs={{0,64},{64,0},{1,65},{65,1},{2,66},{66,2},{3,67},{67,3},{4,68},{68... | collective-permute-start | bytes 6291464 | tf_op jit(solution)/shard_map/ppermute | solution.py:30
  87.1 3.2 %collective-permute-start.6 = (bf16[128,512]{1,0:T(8,128)(2,1)S(1)}, bf16[128,512]{1,0:T(8,128)(2,1)S(1)}, u32[]{:S(2)}, u32[]{:S(2)}) collective-permute-start(bf16[128,512]{1,0:T(8,128)(2,1)S(1)} %get-tuple-element.24), channel_id=1, source_target_pairs={{0,64},{64,0},{1,65},{65,1},{2,66},{66,2},{3,67},{67,3},{4,68},{68... | collective-permute-start | bytes 393224 | tf_op jit(solution)/shard_map/ppermute | solution.py:30
  91.1 4.8 %copy-start.1 = (bf16[256,256]{1,0:T(8,128)(2,1)S(1)}, bf16[256,256]{1,0:T(8,128)(2,1)}, u32[]{:S(2)}) copy-start(bf16[256,256]{1,0:T(8,128)(2,1)} %constant.67.clone.pick) | copy-start | bytes 393220
  103.1 5.3 %copy-start.3 = (bf16[4,2,128,512]{3,2,1,0:T(8,128)(2,1)S(1)}, bf16[4,2,128,512]{3,2,1,0:T(8,128)(2,1)}, u32[]{:S(2)}) copy-start(bf16[4,2,128,512]{3,2,1,0:T(8,128)(2,1)} %get-tuple-element.25.cot) | copy-start | bytes 3145732
  103.1 66.9 %all-to-all-start.1 = ((bf16[32,8,2048]{2,1,0:T(8,128)(2,1)}), bf16[32,8,2048]{2,1,0:T(8,128)(2,1)}, u32[]{:S(2)}, u32[]{:S(2)}) async-start(bf16[32,8,2048]{2,1,0:T(8,128)(2,1)} %bitcast.26), calls=%async_computation.1 | async-start | bytes 2097152 | tf_op jit(solution)/shard_map/all_to_all | solution.py:275
  108.5 32.4 %collective-permute-start.7 = (bf16[2,128,512]{2,1,0:T(8,128)(2,1)S(1)}, bf16[2,128,512]{2,1,0:T(8,128)(2,1)S(1)}, u32[]{:S(2)}, u32[]{:S(2)}) collective-permute-start(bf16[2,128,512]{2,1,0:T(8,128)(2,1)S(1)} %get-tuple-element.30), channel_id=1, source_target_pairs={{0,128},{128,256},{256,384},{384,0},{1,129},{129,257},{257,385},{3... | collective-permute-start | bytes 786440 | tf_op jit(solution)/shard_map/ppermute | solution.py:35
  112.0 37.4 %collective-permute-start.8 = (bf16[2,128,512]{2,1,0:T(8,128)(2,1)S(1)}, bf16[2,128,512]{2,1,0:T(8,128)(2,1)S(1)}, u32[]{:S(2)}, u32[]{:S(2)}) collective-permute-start(bf16[2,128,512]{2,1,0:T(8,128)(2,1)S(1)} %get-tuple-element.29), channel_id=1, source_target_pairs={{0,256},{128,384},{256,0},{384,128},{1,257},{129,385},{257,1},{385... | collective-permute-start | bytes 786440 | tf_op jit(solution)/shard_map/ppermute | solution.py:35
  121.8 30.8 %collective-permute-start.9 = (bf16[2,128,512]{2,1,0:T(8,128)(2,1)S(1)}, bf16[2,128,512]{2,1,0:T(8,128)(2,1)S(1)}, u32[]{:S(2)}, u32[]{:S(2)}) collective-permute-start(bf16[2,128,512]{2,1,0:T(8,128)(2,1)S(1)} %get-tuple-element.28), channel_id=1, source_target_pairs={{0,384},{128,0},{256,128},{384,256},{1,385},{129,1},{257,129},{385... | collective-permute-start | bytes 786440 | tf_op jit(solution)/shard_map/ppermute | solution.py:35
  152.7 4.0 %collective-permute-start.10 = (bf16[4,128,512]{2,1,0:T(8,128)(2,1)S(1)}, bf16[4,128,512]{2,1,0:T(8,128)(2,1)S(1)}, u32[]{:S(2)}, u32[]{:S(2)}) collective-permute-start(bf16[4,128,512]{2,1,0:T(8,128)(2,1)S(1)} %pad_maximum_fusion), channel_id=1, source_target_pairs={{0,64},{64,0},{1,65},{65,1},{2,66},{66,2},{3,67},{67,3},{4,68},{68... | collective-permute-start | bytes 1572872 | tf_op jit(solution)/shard_map/ppermute | solution.py:30
  156.7 1.2 copy-start
  159.7 9.4 %collective-permute-start.11 = (bf16[256,512]{1,0:T(8,128)(2,1)S(1)}, bf16[256,512]{1,0:T(8,128)(2,1)S(1)}, u32[]{:S(2)}, u32[]{:S(2)}) collective-permute-start(bf16[256,512]{1,0:T(8,128)(2,1)S(1)} %get-tuple-element.27), channel_id=1, source_target_pairs={{0,32},{32,0},{1,33},{33,1},{2,34},{34,2},{3,35},{35,3},{4,36},{36... | collective-permute-start | bytes 786440 | tf_op jit(solution)/shard_map/ppermute | solution.py:30
Sparse Core Ops, SparseCore 0:
  10.1 54.1 all-gather.4
  91.2 57.3 all-gather.6

commit v9 on v8

--- a/solution.py
+++ b/solution.py
@@ -44,22 +44,24 @@
     return lax.ppermute(value, ("zh", "c", "zl"), pairs)
 
 
-def split_body(where, pick, r0, r1, r2, r3, tok, cot):
+def split_body(where, pick, r0, r1, r2a, r2b, r3, tok, cot):
     n = NY * ROWS
-    for i, piece in enumerate((r0, r1, r2, r3)):
-        rows = contract(pick[...], piece[...], 1, 0).astype(BF16)
+    r2 = jnp.concatenate([r2a[...], r2b[...]], axis=0)
+    for i, piece in enumerate((r0[...], r1[...], r2, r3[...])):
+        rows = contract(pick[...], piece, 1, 0).astype(BF16)
         tok[i * n : (i + 1) * n] = rows[:n]
         cot[0, 0, i * n : (i + 1) * n] = rows[n:]
 
 
 def split(where, pieces):
     piece = pl.BlockSpec((PIECE, FEATS), lambda j, s: (0, j))
+    part = pl.BlockSpec((PIECE // 2, FEATS), lambda j, s: (0, j))
     return pl.pallas_call(
         split_body,
         grid_spec=pltpu.PrefetchScalarGridSpec(
             num_scalar_prefetch=1,
             grid=(STEPS,),
-            in_specs=[pl.BlockSpec((PIECE, PIECE), lambda j, s: (0, 0))] + [piece] * 4,
+            in_specs=[pl.BlockSpec((PIECE, PIECE), lambda j, s: (0, 0)), piece, piece, part, part, piece],
             out_specs=[
                 pl.BlockSpec((HALF, FEATS), lambda j, s: (0, j)),
                 pl.BlockSpec((1, 1, HALF, FEATS), lambda j, s: (j // 2, flip(j % 2, s[0]), 0, 0)),
@@ -211,21 +213,20 @@
     )(where, merge(), dd, gw, gw, uw, uw, mw, mw, ow, ow)
 
 
-def grads_body(where, h, n0, n1, n2, n3, far, keep, send):
+def grads_body(hn, hf, cn, cf, keep, send):
     total = None
-    for j, near in enumerate((n0, n1, n2, n3)):
-        z = (where[3] + NZ - j) % NZ
-        part = contract(h[z, 0], near[0], 0, 0) + contract(h[z, 1], far[j], 0, 0)
+    for z in range(NZ):
+        part = contract(hn[z], cn[z, 0], 0, 0) + contract(hf[z], cf[z], 0, 0)
         total = part if total is None else total + part
     keep[...] = total[:HID]
     send[...] = total[HID:].astype(BF16)
 
 
-def grads(where, hidden, near, far):
+def grads(hid_near, hid_far, cot_near, cot_far):
     vmem = pl.BlockSpec(memory_space=pltpu.MemorySpace.VMEM)
     return pl.pallas_call(
         grads_body,
-        in_specs=[pl.BlockSpec(memory_space=pltpu.MemorySpace.SMEM)] + [vmem] * 6,
+        in_specs=[vmem] * 4,
         out_specs=[vmem] * 2,
         out_shape=[
             jax.ShapeDtypeStruct((HID, FEATS), F32),
@@ -233,7 +234,7 @@
         ],
         compiler_params=pltpu.CompilerParams(vmem_limit_bytes=32 * 2**20),
         name="grads",
-    )(where, hidden.reshape(NZ, 2, HALF, 2 * HID), *near, far)
+    )(hid_near, hid_far, cot_near, cot_far)
 
 
 def selection(shape, order):
@@ -252,8 +253,7 @@
 
 def on_device(tokens, cotangent, gate_weight, up_weight, down_weight):
     core = lax.axis_index("c")
-    where = [core, lax.axis_index("zl"), lax.axis_index("x"), lax.axis_index("zh")]
-    where = jnp.stack(where).astype(jnp.int32)
+    where = jnp.stack([core, lax.axis_index("zl"), lax.axis_index("x")]).astype(jnp.int32)
 
     picked = jnp.where(core == 0, gate_weight, up_weight)
     picked, tokens = lax.optimization_barrier((picked, tokens))
@@ -261,25 +261,26 @@
     down_near = lax.all_gather(down_weight, ("zh", "zl"), axis=0).reshape(NZ, 2 * HID, FEATS)
 
     block = spread(jnp.concatenate([tokens, cotangent], axis=0), "y").reshape(PIECE, D)
-    pieces = [block] + [shift(block, "x", k) for k in (1, 2, 3)]
+    left, right = shift(block, "x", 1), shift(block, "x", -1)
+    n = PIECE // 2
+    pieces = (block, left, shift(left[:n], "x", 1), shift(right[n:], "x", -1), right)
 
     tok, cot = split(where, pieces)
+    cot_near = lax.all_to_all(cot, "zh", 0, 0)
+    cot_far = swap(cot_near[:, 1], "c")
     tok, mine, down_near = lax.optimization_barrier((tok, mine, down_near))
     other, down_far = swap(mine, "c"), swap(down_near, "c")
     hidden, factors = gates(where, tok, gate_weight, up_weight, mine, other)
-    hidden = lax.all_gather(jnp.stack([hidden, swap(hidden, "c")]), "zh", axis=0)
     dd = down(where, cot, down_near, down_far, factors)
 
     parts = term(where, dd, gate_weight, up_weight, mine, other)
-    parts, cot = lax.optimization_barrier((parts, cot))
+    parts, hidden = lax.optimization_barrier((parts, hidden))
     parts = lax.all_to_all(parts.reshape(NX * NY, 2 * ROWS, D // 2), ("x", "y"), 0, 0)
     total = jnp.sum(parts.astype(F32), axis=0).astype(BF16)
     input_grad = jnp.concatenate([total[:ROWS], total[ROWS:]], axis=1)
 
-    at = lambda k: lax.dynamic_index_in_dim(cot, (lax.axis_index("zh") + k) % NZ, 0, keepdims=False)
-    near = [at(0)] + [shift(at(k), "zh", k) for k in (1, 2, 3)]
-    far = swap(jnp.stack([n[1] for n in near]), "c")
-    keep, send = grads(where, hidden, near, far)
+    hid_near = lax.all_gather(hidden, "zh", axis=0)
+    keep, send = grads(hid_near, swap(hid_near, "c"), cot_near, cot_far)
     down_grad = keep + swap(send, "zl").astype(F32)
     return (input_grad, down_grad)
 

time: 180 us -> 160 us (0.89)
  waiting for transfers between devices: 56.5 us -> 18.6 us
  blocking collectives: 19.4 us -> 39.7 us
  other arithmetic: 6.97 us -> 4.93 us
  starting transfers between devices: 54.4 us -> 56.3 us
    ppermute x6 -> x4, waiting for transfers between devices: 43.7 us -> 10 us  [shift(): return lax.ppermute(value, axis, [(i, (i + k) % n) for i in range(n)])]
    all_gather x0 -> x1, blocking collectives: none -> 20.3 us  [on_device(): hid_near = lax.all_gather(hidden, 'zh', axis=0)]
    ppermute x6 -> x4, starting transfers between devices: 27 us -> 13 us  [shift(): return lax.ppermute(value, axis, [(i, (i + k) % n) for i in range(n)])]
    all_to_all x0 -> x1, starting transfers between devices: none -> 8.05 us  [on_device(): cot_near = lax.all_to_all(cot, 'zh', 0, 0)]
    ppermute x5, starting transfers between devices: 10.7 us -> 16.7 us  [swap(): return lax.ppermute(value, axis, [(0, 1), (1, 0)])]
    ppermute x5, waiting for transfers between devices: 12.1 us -> 7.87 us  [swap(): return lax.ppermute(value, axis, [(0, 1), (1, 0)])]
  transfers between devices with their start and end apart: 15 -> 13, of which waited for: 10 -> 6; matrix products, arithmetic and copies ran while one was open for 3% -> 3% of each run, Pallas kernels for 14% -> 16%
where the time goes in v9:
time: 160 us; the launch traced here: 159 us
  starting transfers between devices  56.3 us (35%)
  blocking collectives  39.7 us (25%)
  Pallas kernels  25.1 us (16%)
  waiting for transfers between devices  18.6 us (12%)
  between operations  14.3 us (9%)
  other arithmetic  4.93 us (3%)
    all_gather x1, blocking collectives, on_device(): hid_near = lax.all_gather(hidden, 'zh', axis=0)  20.3 us
    all_to_all x1, blocking collectives, spread(): lax.all_to_all(jnp.broadcast_to(block[None], (n, *block.shape)), axis, 0, 0)  19.4 us
    ppermute x5, starting transfers between devices, swap(): return lax.ppermute(value, axis, [(0, 1), (1, 0)])  16.7 us
    ppermute x4, starting transfers between devices, shift(): return lax.ppermute(value, axis, [(i, (i + k) % n) for i in range(n)])  13 us
    ppermute x1, starting transfers between devices, neighbours(): return lax.ppermute(value, ('zh', 'c', 'zl'), pairs)  11.6 us
    ppermute x4, waiting for transfers between devices, shift(): return lax.ppermute(value, axis, [(i, (i + k) % n) for i in range(n)])  10 us
    all_to_all x1, starting transfers between devices, on_device(): cot_near = lax.all_to_all(cot, 'zh', 0, 0)  8.05 us
    ppermute x5, waiting for transfers between devices, swap(): return lax.ppermute(value, axis, [(0, 1), (1, 0)])  7.87 us
  transfers between devices with their start and end apart: 13, of which 6 were waited for; matrix products, arithmetic and copies ran while one was open for 3% of the time, Pallas kernels for 16%

profile of v9, /device:TPU:1, one launch (start us, length us, event | category | flops | bytes accessed | tf_op | source)
XLA Modules:
  0.0 159.1 jit_solution(16604076261808749076)
XLA Ops:
  7.2 0.0 all-gather.4.cloned.1.call-start
  7.2 0.7 all-gather.4.cloned.1.call-update
  7.9 0.0 copy-start.2
  7.9 0.0 copy-start.3
  7.9 3.2 %broadcast_select_fusion = bf16[4096,256]{1,0:T(8,128)(2,1)} fusion(bf16[4096,256]{1,0:T(8,128)(2,1)} %refs_1_.1, bf16[4096,256]{1,0:T(8,128)(2,1)} %refs_3_.1, pred[]{:T(512)S(6)} %eq.3), kind=kLoop, calls=%fused_computation | loop fusion | flops 1048576 | bytes 6291457 | tf_op jit(solution)/shard_map/jit(_where)/select_n | solution.py:258
  11.1 0.0 copy-start.1
  11.1 11.6 %collective-permute-start.4 = (bf16[4096,256]{1,0:T(8,128)(2,1)}, bf16[4096,256]{1,0:T(8,128)(2,1)}, u32[]{:S(2)}, u32[]{:S(2)}) collective-permute-start(bf16[4096,256]{1,0:T(8,128)(2,1)} %broadcast_select_fusion), channel_id=1, source_target_pairs={{0,32},{32,0},{96,192},{192,96},{128,160},{160,128},{224,320},{320... | collective-permute-start | bytes 6291464 | tf_op jit(solution)/shard_map/ppermute | solution.py:44
  22.7 0.0 copy-done.2
  22.7 0.0 copy-done.3
  22.8 19.4 %all_to_all.15 = bf16[8,8,4096]{2,1,0:T(8,128)(2,1)S(1)} all-to-all(bf16[8,8,4096]{2,1,0:T(8,128)(2,1)S(1)} %broadcast_in_dim.2), channel_id=1, replica_groups=mesh['zh'=4,'c'=2,'zl'=2,'y'=8,'x'=4] {'y'}, dimensions={0} | all-to-all | bytes 1048576 | tf_op jit(solution)/shard_map/all_to_all | solution.py:251
  42.2 3.1 %collective-permute-start = (bf16[64,4096]{1,0:T(8,128)(2,1)S(1)}, bf16[64,4096]{1,0:T(8,128)(2,1)S(1)}, u32[]{:S(2)}, u32[]{:S(2)}) collective-permute-start(bf16[64,4096]{1,0:T(8,128)(2,1)S(1)} %bitcast.13), channel_id=1, source_target_pairs={{0,1},{1,2},{2,3},{3,0},{4,5},{5,6},{6,7},{7,4},{8,9},{9,10},{10,1... | collective-permute-start | bytes 1572872 | tf_op jit(solution)/shard_map/ppermute | solution.py:35
  45.4 3.4 %collective-permute-start.2 = (bf16[64,4096]{1,0:T(8,128)(2,1)S(1)}, bf16[64,4096]{1,0:T(8,128)(2,1)S(1)}, u32[]{:S(2)}, u32[]{:S(2)}) collective-permute-start(bf16[64,4096]{1,0:T(8,128)(2,1)S(1)} %bitcast.14), channel_id=1, source_target_pairs={{0,3},{1,0},{2,1},{3,2},{4,7},{5,4},{6,5},{7,6},{8,11},{9,8},{10,9... | collective-permute-start | bytes 1572872 | tf_op jit(solution)/shard_map/ppermute | solution.py:35
  48.7 6.6 %collective-permute-done.r1 = bf16[64,4096]{1,0:T(8,128)(2,1)S(1)} collective-permute-done((bf16[64,4096]{1,0:T(8,128)(2,1)S(1)}, bf16[64,4096]{1,0:T(8,128)(2,1)S(1)}, u32[]{:S(2)}, u32[]{:S(2)}) %collective-permute-start) | collective-permute-done | bytes 524320 | tf_op jit(solution)/shard_map/ppermute | solution.py:35
  55.3 1.9 %collective-permute-start.1 = (bf16[32,4096]{1,0:T(8,128)(2,1)S(1)}, bf16[32,4096]{1,0:T(8,128)(2,1)S(1)}, u32[]{:S(2)}, u32[]{:S(2)}) collective-permute-start(bf16[32,4096]{1,0:T(8,128)(2,1)S(1)} %slice.20), channel_id=1, source_target_pairs={{0,1},{1,2},{2,3},{3,0},{4,5},{5,6},{6,7},{7,4},{8,9},{9,10},{10,1... | collective-permute-start | bytes 786440 | tf_op jit(solution)/shard_map/ppermute | solution.py:35
  57.3 0.2 collective-permute-done.2.r3
  57.5 4.6 %collective-permute-start.3 = (bf16[32,4096]{1,0:T(8,128)(2,1)S(1)}, bf16[32,4096]{1,0:T(8,128)(2,1)S(1)}, u32[]{:S(2)}, u32[]{:S(2)}) collective-permute-start(bf16[32,4096]{1,0:T(8,128)(2,1)S(1)} %slice.21), channel_id=1, source_target_pairs={{0,3},{1,0},{2,1},{3,2},{4,7},{5,4},{6,5},{7,6},{8,11},{9,8},{10,9... | collective-permute-start | bytes 786440 | tf_op jit(solution)/shard_map/ppermute | solution.py:35
  62.1 0.1 pad_add_fusion.where
  62.2 1.7 %collective-permute-done.1.r2a = bf16[32,4096]{1,0:T(8,128)(2,1)S(1)} collective-permute-done((bf16[32,4096]{1,0:T(8,128)(2,1)S(1)}, bf16[32,4096]{1,0:T(8,128)(2,1)S(1)}, u32[]{:S(2)}, u32[]{:S(2)}) %collective-permute-start.1) | collective-permute-done | bytes 262176 | tf_op jit(solution)/shard_map/ppermute | solution.py:35
  63.9 1.5 collective-permute-done.3.r2b
  65.4 0.0 copy-done.1
  65.4 4.7 %split.1 = (bf16[128,4096]{1,0:T(8,128)(2,1)}, bf16[4,2,128,512]{3,2,1,0:T(8,128)(2,1)}) custom-call(s32[3]{0:T(128)S(1)} %pad_add_fusion.where, bf16[64,64]{1,0:T(8,128)(2,1)S(1)} %copy-done.1, bf16[64,4096]{1,0:T(8,128)(2,1)S(1)} %bitcast.15, bf16[64,4096]{1,0:T(8,128)(2,1)S(1)} %collective-permute-done.r1, ...), custom_call_target="tpu_custom_call" | custom-call | tf_op jit(solution)/shard_map/split/pallas_call | solution.py:59
  70.2 0.0 collective-permute-done.4.mw.refs_4_.refs_5_
  70.2 0.0 all-gather.4.cloned.1.call-done
  70.2 1.9 %collective-permute-start.6 = (bf16[4096,256]{1,0:T(8,128)(2,1)}, bf16[4096,256]{1,0:T(8,128)(2,1)S(1)}, u32[]{:S(2)}, u32[]{:S(2)}) collective-permute-start(bf16[4096,256]{1,0:T(8,128)(2,1)} %collective-permute-done.4.mw.refs_4_.refs_5_), channel_id=1, source_target_pairs={{0,64},{64,0},{1,65},{65,1},{2,66},{66,2},{3,67},{67,3},{4,68},{68... | collective-permute-start | bytes 6291464 | tf_op jit(solution)/shard_map/ppermute | solution.py:30
  72.1 2.4 %collective-permute-start.5 = (bf16[4,512,512]{2,1,0:T(8,128)(2,1)}, bf16[4,512,512]{2,1,0:T(8,128)(2,1)}, u32[]{:S(2)}, u32[]{:S(2)}) collective-permute-start(bf16[4,512,512]{2,1,0:T(8,128)(2,1)} %bitcast.17), channel_id=1, source_target_pairs={{0,64},{64,0},{1,65},{65,1},{2,66},{66,2},{3,67},{67,3},{4,68},{68... | collective-permute-start | bytes 6291464 | tf_op jit(solution)/shard_map/ppermute | solution.py:30
  74.5 8.1 %all-to-all-start.2 = ((bf16[4,2,128,512]{3,2,1,0:T(8,128)(2,1)}), bf16[4,2,128,512]{3,2,1,0:T(8,128)(2,1)S(1)}, u32[]{:S(2)}, u32[]{:S(2)}) async-start(bf16[4,2,128,512]{3,2,1,0:T(8,128)(2,1)} %get-tuple-element.16.cot), calls=%async_computation.2 | async-start | bytes 2097152 | tf_op jit(solution)/shard_map/all_to_all | solution.py:269
  82.5 0.0 collective-permute-done.6.ow.refs_6_.refs_7_
  82.5 7.2 %gates.1 = (bf16[128,512]{1,0:T(8,128)(2,1)S(1)}, f32[128,1024]{1,0:T(8,128)S(1)}) custom-call(s32[3]{0:T(128)S(1)} %pad_add_fusion.where, bf16[128,4096]{1,0:T(8,128)(2,1)} %get-tuple-element.20.tok, bf16[4096,256]{1,0:T(8,128)(2,1)} %refs_1_.1, bf16[4096,256]{1,0:T(8,128)(2,1)} %refs_3_.1, bf16[4096,256]{1,0:T(8,128)(2,1)} %collective-permute-done.4.mw.refs_4_.refs_5_, ...), custom_call_target="tpu_custom_call" | custom-call | tf_op jit(solution)/shard_map/gates/pallas_call | solution.py:123
  89.7 0.0 collective-permute-done.5.df
  89.7 0.0 copy-start
  89.7 4.8 %down.1.dd = bf16[128,1024]{1,0:T(8,128)(2,1)S(1)} custom-call(s32[3]{0:T(128)S(1)} %pad_add_fusion.where, bf16[4,2,128,512]{3,2,1,0:T(8,128)(2,1)} %get-tuple-element.16.cot, bf16[4,512,512]{2,1,0:T(8,128)(2,1)} %bitcast.18, bf16[4,512,512]{2,1,0:T(8,128)(2,1)} %collective-permute-done.5.df, f32[128,1024]{1,0:T(8,128)S(1)} %get-tuple-element.22.fac), custom_call_target="tpu_custom_call" | custom-call | tf_op jit(solution)/shard_map/down/pallas_call | solution.py:165
  94.5 0.0 copy-done
  94.5 7.3 %term.1 = bf16[4,64,2048]{2,1,0:T(8,128)(2,1)} custom-call(s32[3]{0:T(128)S(1)} %pad_add_fusion.where, bf16[256,256]{1,0:T(8,128)(2,1)S(1)} %copy-done, bf16[128,1024]{1,0:T(8,128)(2,1)S(1)} %down.1.dd, bf16[4096,256]{1,0:T(8,128)(2,1)} %refs_1_.1, bf16[4096,256]{1,0:T(8,128)(2,1)} %refs_1_.1, bf16[4096,256]{1,0:T(8,128)(2,1)} %refs_3_.1, ...), custom_call_target="tpu_custom_call" | custom-call | tf_op jit(solution)/shard_map/term/pallas_call | solution.py:198
  101.8 0.0 all-to-all-done.2.cn
  101.8 6.9 %all-to-all-start.1 = ((bf16[32,8,2048]{2,1,0:T(8,128)(2,1)}), bf16[32,8,2048]{2,1,0:T(8,128)(2,1)S(1)}, u32[]{:S(2)}, u32[]{:S(2)}) async-start(bf16[32,8,2048]{2,1,0:T(8,128)(2,1)} %bitcast.16), calls=%async_computation.1 | async-start | bytes 2097152 | tf_op jit(solution)/shard_map/all_to_all | solution.py:278
  108.8 4.0 %collective-permute-start.8 = (bf16[4,128,512]{2,1,0:T(8,128)(2,1)S(1)}, bf16[4,128,512]{2,1,0:T(8,128)(2,1)S(1)}, u32[]{:S(2)}, u32[]{:S(2)}) collective-permute-start(bf16[4,128,512]{2,1,0:T(8,128)(2,1)S(1)} %slice_bitcast_fusion), channel_id=1, source_target_pairs={{0,64},{64,0},{1,65},{65,1},{2,66},{66,2},{3,67},{67,3},{4,68},{68... | collective-permute-start | bytes 1572872 | tf_op jit(solution)/shard_map/ppermute | solution.py:30
  112.8 20.3 %all-gather.1 = bf16[512,512]{1,0:T(8,128)(2,1)S(1)} all-gather(bf16[128,512]{1,0:T(8,128)(2,1)S(1)} %get-tuple-element.25), channel_id=3, replica_groups=mesh['zh'=4,'c'=2,'zl'=2,'y'=8,'x'=4] {'zh'}, dimensions={0}, use_global_device_ids=true | all-gather | bytes 655360 | tf_op jit(solution)/shard_map/all_gather | solution.py:282
  133.1 4.1 %collective-permute-start.7 = (bf16[4,128,512]{2,1,0:T(8,128)(2,1)S(1)}, bf16[4,128,512]{2,1,0:T(8,128)(2,1)S(1)}, u32[]{:S(2)}, u32[]{:S(2)}) collective-permute-start(bf16[4,128,512]{2,1,0:T(8,128)(2,1)S(1)} %bitcast.11), channel_id=1, source_target_pairs={{0,64},{64,0},{1,65},{65,1},{2,66},{66,2},{3,67},{67,3},{4,68},{68... | collective-permute-start | bytes 1572872 | tf_op jit(solution)/shard_map/ppermute | solution.py:30
  137.1 0.0 collective-permute-done.8.cf
  137.2 1.5 collective-permute-done.7.hf
  138.7 1.3 grads.1
  139.9 4.3 %collective-permute-start.9 = (bf16[256,512]{1,0:T(8,128)(2,1)S(1)}, bf16[256,512]{1,0:T(8,128)(2,1)S(1)}, u32[]{:S(2)}, u32[]{:S(2)}) collective-permute-start(bf16[256,512]{1,0:T(8,128)(2,1)S(1)} %get-tuple-element.27), channel_id=1, source_target_pairs={{0,32},{32,0},{1,33},{33,1},{2,34},{34,2},{3,35},{35,3},{4,36},{36... | collective-permute-start | bytes 786440 | tf_op jit(solution)/shard_map/ppermute | solution.py:30
  144.2 6.4 %collective-permute-done.9 = bf16[256,512]{1,0:T(8,128)(2,1)S(1)} collective-permute-done((bf16[256,512]{1,0:T(8,128)(2,1)S(1)}, bf16[256,512]{1,0:T(8,128)(2,1)S(1)}, u32[]{:S(2)}, u32[]{:S(2)}) %collective-permute-start.9) | collective-permute-done | bytes 262176 | tf_op jit(solution)/shard_map/ppermute | solution.py:30
  150.6 0.9 convert_add_fusion
  151.5 0.0 all-to-all-done.1
  151.5 0.2 reduce_sum.12
  151.6 0.6 pad_maximum_fusion.1
  (6 shorter events, 0.2 us)
Async XLA Ops:
  7.2 63.0 %all-gather.4.cloned.1.call-start = ((), (), s32[]{:S(2)}) async-start(), calls=%async_computation.3 | async-start | bytes 2359296 | tf_op jit(solution)/shard_map/all_gather | solution.py:261
  7.9 14.8 %copy-start.2 = (bf16[4,4096]{1,0:T(4,128)(2,1)S(1)}, bf16[4,4096]{1,0:T(4,128)(2,1)}, u32[]{:S(2)}) copy-start(bf16[4,4096]{1,0:T(4,128)(2,1)} %param.8) | copy-start | bytes 98308
  7.9 14.8 %copy-start.3 = (bf16[4,4096]{1,0:T(4,128)(2,1)S(1)}, bf16[4,4096]{1,0:T(4,128)(2,1)}, u32[]{:S(2)}) copy-start(bf16[4,4096]{1,0:T(4,128)(2,1)} %param.7) | copy-start | bytes 98308
  11.1 54.3 %copy-start.1 = (bf16[64,64]{1,0:T(8,128)(2,1)S(1)}, bf16[64,64]{1,0:T(8,128)(2,1)}, u32[]{:S(2)}) copy-start(bf16[64,64]{1,0:T(8,128)(2,1)} %constant.23.clone.pick) | copy-start | bytes 24580
  11.1 59.1 %collective-permute-start.4 = (bf16[4096,256]{1,0:T(8,128)(2,1)}, bf16[4096,256]{1,0:T(8,128)(2,1)}, u32[]{:S(2)}, u32[]{:S(2)}) collective-permute-start(bf16[4096,256]{1,0:T(8,128)(2,1)} %broadcast_select_fusion), channel_id=1, source_target_pairs={{0,32},{32,0},{96,192},{192,96},{128,160},{160,128},{224,320},{320... | collective-permute-start | bytes 6291464 | tf_op jit(solution)/shard_map/ppermute | solution.py:44
  42.2 13.1 %collective-permute-start = (bf16[64,4096]{1,0:T(8,128)(2,1)S(1)}, bf16[64,4096]{1,0:T(8,128)(2,1)S(1)}, u32[]{:S(2)}, u32[]{:S(2)}) collective-permute-start(bf16[64,4096]{1,0:T(8,128)(2,1)S(1)} %bitcast.13), channel_id=1, source_target_pairs={{0,1},{1,2},{2,3},{3,0},{4,5},{5,6},{6,7},{7,4},{8,9},{9,10},{10,1... | collective-permute-start | bytes 1572872 | tf_op jit(solution)/shard_map/ppermute | solution.py:35
  45.4 12.2 %collective-permute-start.2 = (bf16[64,4096]{1,0:T(8,128)(2,1)S(1)}, bf16[64,4096]{1,0:T(8,128)(2,1)S(1)}, u32[]{:S(2)}, u32[]{:S(2)}) collective-permute-start(bf16[64,4096]{1,0:T(8,128)(2,1)S(1)} %bitcast.14), channel_id=1, source_target_pairs={{0,3},{1,0},{2,1},{3,2},{4,7},{5,4},{6,5},{7,6},{8,11},{9,8},{10,9... | collective-permute-start | bytes 1572872 | tf_op jit(solution)/shard_map/ppermute | solution.py:35
  55.3 8.6 %collective-permute-start.1 = (bf16[32,4096]{1,0:T(8,128)(2,1)S(1)}, bf16[32,4096]{1,0:T(8,128)(2,1)S(1)}, u32[]{:S(2)}, u32[]{:S(2)}) collective-permute-start(bf16[32,4096]{1,0:T(8,128)(2,1)S(1)} %slice.20), channel_id=1, source_target_pairs={{0,1},{1,2},{2,3},{3,0},{4,5},{5,6},{6,7},{7,4},{8,9},{9,10},{10,1... | collective-permute-start | bytes 786440 | tf_op jit(solution)/shard_map/ppermute | solution.py:35
  57.5 7.9 %collective-permute-start.3 = (bf16[32,4096]{1,0:T(8,128)(2,1)S(1)}, bf16[32,4096]{1,0:T(8,128)(2,1)S(1)}, u32[]{:S(2)}, u32[]{:S(2)}) collective-permute-start(bf16[32,4096]{1,0:T(8,128)(2,1)S(1)} %slice.21), channel_id=1, source_target_pairs={{0,3},{1,0},{2,1},{3,2},{4,7},{5,4},{6,5},{7,6},{8,11},{9,8},{10,9... | collective-permute-start | bytes 786440 | tf_op jit(solution)/shard_map/ppermute | solution.py:35
  70.2 12.4 %collective-permute-start.6 = (bf16[4096,256]{1,0:T(8,128)(2,1)}, bf16[4096,256]{1,0:T(8,128)(2,1)S(1)}, u32[]{:S(2)}, u32[]{:S(2)}) collective-permute-start(bf16[4096,256]{1,0:T(8,128)(2,1)} %collective-permute-done.4.mw.refs_4_.refs_5_), channel_id=1, source_target_pairs={{0,64},{64,0},{1,65},{65,1},{2,66},{66,2},{3,67},{67,3},{4,68},{68... | collective-permute-start | bytes 6291464 | tf_op jit(solution)/shard_map/ppermute | solution.py:30
  72.1 17.6 %collective-permute-start.5 = (bf16[4,512,512]{2,1,0:T(8,128)(2,1)}, bf16[4,512,512]{2,1,0:T(8,128)(2,1)}, u32[]{:S(2)}, u32[]{:S(2)}) collective-permute-start(bf16[4,512,512]{2,1,0:T(8,128)(2,1)} %bitcast.17), channel_id=1, source_target_pairs={{0,64},{64,0},{1,65},{65,1},{2,66},{66,2},{3,67},{67,3},{4,68},{68... | collective-permute-start | bytes 6291464 | tf_op jit(solution)/shard_map/ppermute | solution.py:30
  74.5 27.3 %all-to-all-start.2 = ((bf16[4,2,128,512]{3,2,1,0:T(8,128)(2,1)}), bf16[4,2,128,512]{3,2,1,0:T(8,128)(2,1)S(1)}, u32[]{:S(2)}, u32[]{:S(2)}) async-start(bf16[4,2,128,512]{3,2,1,0:T(8,128)(2,1)} %get-tuple-element.16.cot), calls=%async_computation.2 | async-start | bytes 2097152 | tf_op jit(solution)/shard_map/all_to_all | solution.py:269
  89.7 4.8 %copy-start = (bf16[256,256]{1,0:T(8,128)(2,1)S(1)}, bf16[256,256]{1,0:T(8,128)(2,1)}, u32[]{:S(2)}) copy-start(bf16[256,256]{1,0:T(8,128)(2,1)} %constant.24.clone.pick) | copy-start | bytes 393220
  101.8 49.7 %all-to-all-start.1 = ((bf16[32,8,2048]{2,1,0:T(8,128)(2,1)}), bf16[32,8,2048]{2,1,0:T(8,128)(2,1)S(1)}, u32[]{:S(2)}, u32[]{:S(2)}) async-start(bf16[32,8,2048]{2,1,0:T(8,128)(2,1)} %bitcast.16), calls=%async_computation.1 | async-start | bytes 2097152 | tf_op jit(solution)/shard_map/all_to_all | solution.py:278
  108.8 28.4 %collective-permute-start.8 = (bf16[4,128,512]{2,1,0:T(8,128)(2,1)S(1)}, bf16[4,128,512]{2,1,0:T(8,128)(2,1)S(1)}, u32[]{:S(2)}, u32[]{:S(2)}) collective-permute-start(bf16[4,128,512]{2,1,0:T(8,128)(2,1)S(1)} %slice_bitcast_fusion), channel_id=1, source_target_pairs={{0,64},{64,0},{1,65},{65,1},{2,66},{66,2},{3,67},{67,3},{4,68},{68... | collective-permute-start | bytes 1572872 | tf_op jit(solution)/shard_map/ppermute | solution.py:30
  133.1 5.6 %collective-permute-start.7 = (bf16[4,128,512]{2,1,0:T(8,128)(2,1)S(1)}, bf16[4,128,512]{2,1,0:T(8,128)(2,1)S(1)}, u32[]{:S(2)}, u32[]{:S(2)}) collective-permute-start(bf16[4,128,512]{2,1,0:T(8,128)(2,1)S(1)} %bitcast.11), channel_id=1, source_target_pairs={{0,64},{64,0},{1,65},{65,1},{2,66},{66,2},{3,67},{67,3},{4,68},{68... | collective-permute-start | bytes 1572872 | tf_op jit(solution)/shard_map/ppermute | solution.py:30
  139.9 10.7 %collective-permute-start.9 = (bf16[256,512]{1,0:T(8,128)(2,1)S(1)}, bf16[256,512]{1,0:T(8,128)(2,1)S(1)}, u32[]{:S(2)}, u32[]{:S(2)}) collective-permute-start(bf16[256,512]{1,0:T(8,128)(2,1)S(1)} %get-tuple-element.27), channel_id=1, source_target_pairs={{0,32},{32,0},{1,33},{33,1},{2,34},{34,2},{3,35},{35,3},{4,36},{36... | collective-permute-start | bytes 786440 | tf_op jit(solution)/shard_map/ppermute | solution.py:30
Sparse Core Ops, SparseCore 0:
  10.1 54.1 all-gather.3

commit v10 on v9

--- a/solution.py
+++ b/solution.py
@@ -213,28 +213,26 @@
     )(where, merge(), dd, gw, gw, uw, uw, mw, mw, ow, ow)
 
 
-def grads_body(hn, hf, cn, cf, keep, send):
-    total = None
-    for z in range(NZ):
-        part = contract(hn[z], cn[z, 0], 0, 0) + contract(hf[z], cf[z], 0, 0)
-        total = part if total is None else total + part
-    keep[...] = total[:HID]
-    send[...] = total[HID:].astype(BF16)
-
-
-def grads(hid_near, hid_far, cot_near, cot_far):
+def grads_body(where, h0, h1, h2, h3, cot, *outs):
+    for far in range(2):
+        total = None
+        for j, h in enumerate((h0, h1, h2, h3)):
+            part = contract(h[...], cot[(where[3] + NZ - j) % NZ, far], 0, 0)
+            total = part if total is None else total + part
+        for side, out in enumerate(outs[far::2]):
+            out[...] = total[side * HID : (side + 1) * HID].astype(out.dtype)
+
+
+def grads(where, hid, cot):
     vmem = pl.BlockSpec(memory_space=pltpu.MemorySpace.VMEM)
     return pl.pallas_call(
         grads_body,
-        in_specs=[vmem] * 4,
-        out_specs=[vmem] * 2,
-        out_shape=[
-            jax.ShapeDtypeStruct((HID, FEATS), F32),
-            jax.ShapeDtypeStruct((HID, FEATS), BF16),
-        ],
+        in_specs=[pl.BlockSpec(memory_space=pltpu.MemorySpace.SMEM)] + [vmem] * 5,
+        out_specs=[vmem] * 4,
+        out_shape=[jax.ShapeDtypeStruct((HID, FEATS), F32)] + [jax.ShapeDtypeStruct((HID, FEATS), BF16)] * 3,
         compiler_params=pltpu.CompilerParams(vmem_limit_bytes=32 * 2**20),
         name="grads",
-    )(hid_near, hid_far, cot_near, cot_far)
+    )(where, *hid, cot)
 
 
 def selection(shape, order):
@@ -253,7 +251,8 @@
 
 def on_device(tokens, cotangent, gate_weight, up_weight, down_weight):
     core = lax.axis_index("c")
-    where = jnp.stack([core, lax.axis_index("zl"), lax.axis_index("x")]).astype(jnp.int32)
+    where = [core, lax.axis_index("zl"), lax.axis_index("x"), lax.axis_index("zh")]
+    where = jnp.stack(where).astype(jnp.int32)
 
     picked = jnp.where(core == 0, gate_weight, up_weight)
     picked, tokens = lax.optimization_barrier((picked, tokens))
@@ -267,7 +266,6 @@
 
     tok, cot = split(where, pieces)
     cot_near = lax.all_to_all(cot, "zh", 0, 0)
-    cot_far = swap(cot_near[:, 1], "c")
     tok, mine, down_near = lax.optimization_barrier((tok, mine, down_near))
     other, down_far = swap(mine, "c"), swap(down_near, "c")
     hidden, factors = gates(where, tok, gate_weight, up_weight, mine, other)
@@ -279,9 +277,14 @@
     total = jnp.sum(parts.astype(F32), axis=0).astype(BF16)
     input_grad = jnp.concatenate([total[:ROWS], total[ROWS:]], axis=1)
 
-    hid_near = lax.all_gather(hidden, "zh", axis=0)
-    keep, send = grads(hid_near, swap(hid_near, "c"), cot_near, cot_far)
-    down_grad = keep + swap(send, "zl").astype(F32)
+    hid = [hidden] + [shift(hidden, "zh", k) for k in (1, 2, 3)]
+    keep, core_part, zl_part, both_part = grads(where, hid, cot_near)
+    down_grad = (
+        keep
+        + swap(core_part, "c").astype(F32)
+        + swap(zl_part, "zl").astype(F32)
+        + lax.ppermute(both_part, ("c", "zl"), [(0, 3), (3, 0), (1, 2), (2, 1)]).astype(F32)
+    )
     return (input_grad, down_grad)
 
 

time: 160 us -> 169 us (1.056)
  blocking collectives: 39.7 us -> 19.4 us
  waiting for transfers between devices: 18.6 us -> 34.8 us
  starting transfers between devices: 56.3 us -> 69.1 us
    all_gather x1 -> x0, blocking collectives: 20.3 us -> none  [on_device(): hid_near = lax.all_gather(hidden, 'zh', axis=0)]
    ppermute x4 -> x7, starting transfers between devices: 13 us -> 29.4 us  [shift(): return lax.ppermute(value, axis, [(i, (i + k) % n) for i in range(n)])]
    ppermute x4 -> x7, waiting for transfers between devices: 10 us -> 24 us  [shift(): return lax.ppermute(value, axis, [(i, (i + k) % n) for i in range(n)])]
    ppermute x5 -> x4, starting transfers between devices: 16.7 us -> 9.38 us  [swap(): return lax.ppermute(value, axis, [(0, 1), (1, 0)])]
    ppermute x0 -> x1, waiting for transfers between devices: none -> 5.72 us  [on_device(): lax.ppermute(both_part, ('c', 'zl'), [(0, 3), (3, 0), (1, 2), (2, 1)])]
    ppermute x0 -> x1, starting transfers between devices: none -> 3.54 us  [on_device(): lax.ppermute(both_part, ('c', 'zl'), [(0, 3), (3, 0), (1, 2), (2, 1)])]
    ppermute x5 -> x4, waiting for transfers between devices: 7.87 us -> 4.34 us  [swap(): return lax.ppermute(value, axis, [(0, 1), (1, 0)])]
  transfers between devices with their start and end apart: 13 -> 16, of which waited for: 6 -> 8; matrix products, arithmetic and copies ran while one was open for 3% -> 3% of each run, Pallas kernels for 16% -> 15%
where the time goes in v10:
time: 169 us; the launch traced here: 168 us
  starting transfers between devices  69.1 us (41%)
  waiting for transfers between devices  34.8 us (21%)
  Pallas kernels  25.6 us (15%)
  blocking collectives  19.4 us (11%)
  between operations  14.3 us (8%)
  other arithmetic  5.03 us (3%)
    ppermute x7, starting transfers between devices, shift(): return lax.ppermute(value, axis, [(i, (i + k) % n) for i in range(n)])  29.4 us
    ppermute x7, waiting for transfers between devices, shift(): return lax.ppermute(value, axis, [(i, (i + k) % n) for i in range(n)])  24 us
    all_to_all x1, blocking collectives, spread(): lax.all_to_all(jnp.broadcast_to(block[None], (n, *block.shape)), axis, 0, 0)  19.4 us
    ppermute x1, starting transfers between devices, neighbours(): return lax.ppermute(value, ('zh', 'c', 'zl'), pairs)  11.6 us
    ppermute x4, starting transfers between devices, swap(): return lax.ppermute(value, axis, [(0, 1), (1, 0)])  9.38 us
    all_to_all x1, starting transfers between devices, on_device(): cot_near = lax.all_to_all(cot, 'zh', 0, 0)  8.1 us
    pallas_call x1, Pallas kernels, term(): pl.pallas_call(term_body, grid_spec=pltpu.PrefetchScalarGridSpec(num_scal...  7.23 us
    pallas_call x1, Pallas kernels, gates(): pl.pallas_call(gates_body, grid_spec=pltpu.PrefetchScalarGridSpec(num_sca...  7.15 us
  transfers between devices with their start and end apart: 16, of which 8 were waited for; matrix products, arithmetic and copies ran while one was open for 3% of the time, Pallas kernels for 15%

profile of v10, /device:TPU:1, one launch (start us, length us, event | category | flops | bytes accessed | tf_op | source)
XLA Modules:
  0.0 168.3 jit_solution(18411779683866365831)
XLA Ops:
  7.2 0.0 all-gather.3.cloned.1.call-start
  7.2 0.7 all-gather.3.cloned.1.call-update
  7.9 0.0 copy-start.2
  7.9 0.0 copy-start.3
  7.9 3.2 %broadcast_select_fusion = bf16[4096,256]{1,0:T(8,128)(2,1)} fusion(bf16[4096,256]{1,0:T(8,128)(2,1)} %refs_1_.1, bf16[4096,256]{1,0:T(8,128)(2,1)} %refs_3_.1, pred[]{:T(512)S(6)} %eq.3), kind=kLoop, calls=%fused_computation | loop fusion | flops 1048576 | bytes 6291457 | tf_op jit(solution)/shard_map/jit(_where)/select_n | solution.py:257
  11.1 0.0 copy-start.1
  11.1 11.6 %collective-permute-start.4 = (bf16[4096,256]{1,0:T(8,128)(2,1)}, bf16[4096,256]{1,0:T(8,128)(2,1)}, u32[]{:S(2)}, u32[]{:S(2)}) collective-permute-start(bf16[4096,256]{1,0:T(8,128)(2,1)} %broadcast_select_fusion), channel_id=1, source_target_pairs={{0,32},{32,0},{96,192},{192,96},{128,160},{160,128},{224,320},{320... | collective-permute-start | bytes 6291464 | tf_op jit(solution)/shard_map/ppermute | solution.py:44
  22.7 0.0 copy-done.2
  22.7 0.0 copy-done.3
  22.8 19.4 %all_to_all.15 = bf16[8,8,4096]{2,1,0:T(8,128)(2,1)S(1)} all-to-all(bf16[8,8,4096]{2,1,0:T(8,128)(2,1)S(1)} %broadcast_in_dim.2), channel_id=1, replica_groups=mesh['zh'=4,'c'=2,'zl'=2,'y'=8,'x'=4] {'y'}, dimensions={0} | all-to-all | bytes 1048576 | tf_op jit(solution)/shard_map/all_to_all | solution.py:249
  42.2 3.1 %collective-permute-start = (bf16[64,4096]{1,0:T(8,128)(2,1)S(1)}, bf16[64,4096]{1,0:T(8,128)(2,1)S(1)}, u32[]{:S(2)}, u32[]{:S(2)}) collective-permute-start(bf16[64,4096]{1,0:T(8,128)(2,1)S(1)} %bitcast.7), channel_id=1, source_target_pairs={{0,1},{1,2},{2,3},{3,0},{4,5},{5,6},{6,7},{7,4},{8,9},{9,10},{10,1... | collective-permute-start | bytes 1572872 | tf_op jit(solution)/shard_map/ppermute | solution.py:35
  45.4 3.4 %collective-permute-start.2 = (bf16[64,4096]{1,0:T(8,128)(2,1)S(1)}, bf16[64,4096]{1,0:T(8,128)(2,1)S(1)}, u32[]{:S(2)}, u32[]{:S(2)}) collective-permute-start(bf16[64,4096]{1,0:T(8,128)(2,1)S(1)} %bitcast.8), channel_id=1, source_target_pairs={{0,3},{1,0},{2,1},{3,2},{4,7},{5,4},{6,5},{7,6},{8,11},{9,8},{10,9... | collective-permute-start | bytes 1572872 | tf_op jit(solution)/shard_map/ppermute | solution.py:35
  48.7 6.6 %collective-permute-done.r1 = bf16[64,4096]{1,0:T(8,128)(2,1)S(1)} collective-permute-done((bf16[64,4096]{1,0:T(8,128)(2,1)S(1)}, bf16[64,4096]{1,0:T(8,128)(2,1)S(1)}, u32[]{:S(2)}, u32[]{:S(2)}) %collective-permute-start) | collective-permute-done | bytes 524320 | tf_op jit(solution)/shard_map/ppermute | solution.py:35
  55.3 1.9 %collective-permute-start.1 = (bf16[32,4096]{1,0:T(8,128)(2,1)S(1)}, bf16[32,4096]{1,0:T(8,128)(2,1)S(1)}, u32[]{:S(2)}, u32[]{:S(2)}) collective-permute-start(bf16[32,4096]{1,0:T(8,128)(2,1)S(1)} %slice.16), channel_id=1, source_target_pairs={{0,1},{1,2},{2,3},{3,0},{4,5},{5,6},{6,7},{7,4},{8,9},{9,10},{10,1... | collective-permute-start | bytes 786440 | tf_op jit(solution)/shard_map/ppermute | solution.py:35
  57.3 0.2 collective-permute-done.2.r3
  57.5 4.6 %collective-permute-start.3 = (bf16[32,4096]{1,0:T(8,128)(2,1)S(1)}, bf16[32,4096]{1,0:T(8,128)(2,1)S(1)}, u32[]{:S(2)}, u32[]{:S(2)}) collective-permute-start(bf16[32,4096]{1,0:T(8,128)(2,1)S(1)} %slice.17), channel_id=1, source_target_pairs={{0,3},{1,0},{2,1},{3,2},{4,7},{5,4},{6,5},{7,6},{8,11},{9,8},{10,9... | collective-permute-start | bytes 786440 | tf_op jit(solution)/shard_map/ppermute | solution.py:35
  62.1 0.1 pad_add_fusion.where
  62.2 1.7 %collective-permute-done.1.r2a = bf16[32,4096]{1,0:T(8,128)(2,1)S(1)} collective-permute-done((bf16[32,4096]{1,0:T(8,128)(2,1)S(1)}, bf16[32,4096]{1,0:T(8,128)(2,1)S(1)}, u32[]{:S(2)}, u32[]{:S(2)}) %collective-permute-start.1) | collective-permute-done | bytes 262176 | tf_op jit(solution)/shard_map/ppermute | solution.py:35
  63.9 1.5 collective-permute-done.3.r2b
  65.4 0.0 copy-done.1
  65.4 4.7 %split.1 = (bf16[128,4096]{1,0:T(8,128)(2,1)}, bf16[4,2,128,512]{3,2,1,0:T(8,128)(2,1)}) custom-call(s32[4]{0:T(128)S(1)} %pad_add_fusion.where, bf16[64,64]{1,0:T(8,128)(2,1)S(1)} %copy-done.1, bf16[64,4096]{1,0:T(8,128)(2,1)S(1)} %bitcast.9, bf16[64,4096]{1,0:T(8,128)(2,1)S(1)} %collective-permute-done.r1, ...), custom_call_target="tpu_custom_call" | custom-call | tf_op jit(solution)/shard_map/split/pallas_call | solution.py:59
  70.1 0.0 collective-permute-done.4.mw.refs_4_.refs_5_
  70.1 0.0 all-gather.3.cloned.1.call-done
  70.1 1.9 %collective-permute-start.6 = (bf16[4096,256]{1,0:T(8,128)(2,1)}, bf16[4096,256]{1,0:T(8,128)(2,1)S(1)}, u32[]{:S(2)}, u32[]{:S(2)}) collective-permute-start(bf16[4096,256]{1,0:T(8,128)(2,1)} %collective-permute-done.4.mw.refs_4_.refs_5_), channel_id=1, source_target_pairs={{0,64},{64,0},{1,65},{65,1},{2,66},{66,2},{3,67},{67,3},{4,68},{68... | collective-permute-start | bytes 6291464 | tf_op jit(solution)/shard_map/ppermute | solution.py:30
  72.1 2.4 %collective-permute-start.5 = (bf16[4,512,512]{2,1,0:T(8,128)(2,1)}, bf16[4,512,512]{2,1,0:T(8,128)(2,1)}, u32[]{:S(2)}, u32[]{:S(2)}) collective-permute-start(bf16[4,512,512]{2,1,0:T(8,128)(2,1)} %bitcast.11), channel_id=1, source_target_pairs={{0,64},{64,0},{1,65},{65,1},{2,66},{66,2},{3,67},{67,3},{4,68},{68... | collective-permute-start | bytes 6291464 | tf_op jit(solution)/shard_map/ppermute | solution.py:30
  74.5 8.1 %all-to-all-start.2 = ((bf16[4,2,128,512]{3,2,1,0:T(8,128)(2,1)}), bf16[4,2,128,512]{3,2,1,0:T(8,128)(2,1)S(1)}, u32[]{:S(2)}, u32[]{:S(2)}) async-start(bf16[4,2,128,512]{3,2,1,0:T(8,128)(2,1)} %get-tuple-element.18.cot), calls=%async_computation.2 | async-start | bytes 2097152 | tf_op jit(solution)/shard_map/all_to_all | solution.py:268
  82.6 0.0 collective-permute-done.6.ow.refs_6_.refs_7_
  82.6 7.2 %gates.1 = (bf16[128,512]{1,0:T(8,128)(2,1)S(1)}, f32[128,1024]{1,0:T(8,128)S(1)}) custom-call(s32[4]{0:T(128)S(1)} %pad_add_fusion.where, bf16[128,4096]{1,0:T(8,128)(2,1)} %get-tuple-element.22.tok, bf16[4096,256]{1,0:T(8,128)(2,1)} %refs_1_.1, bf16[4096,256]{1,0:T(8,128)(2,1)} %refs_3_.1, bf16[4096,256]{1,0:T(8,128)(2,1)} %collective-permute-done.4.mw.refs_4_.refs_5_, ...), custom_call_target="tpu_custom_call" | custom-call | tf_op jit(solution)/shard_map/gates/pallas_call | solution.py:123
  89.7 0.0 collective-permute-done.5.df
  89.7 0.0 copy-start
  89.8 4.8 %down.1.dd = bf16[128,1024]{1,0:T(8,128)(2,1)S(1)} custom-call(s32[4]{0:T(128)S(1)} %pad_add_fusion.where, bf16[4,2,128,512]{3,2,1,0:T(8,128)(2,1)} %get-tuple-element.18.cot, bf16[4,512,512]{2,1,0:T(8,128)(2,1)} %bitcast.12, bf16[4,512,512]{2,1,0:T(8,128)(2,1)} %collective-permute-done.5.df, f32[128,1024]{1,0:T(8,128)S(1)} %get-tuple-element.24.fac), custom_call_target="tpu_custom_call" | custom-call | tf_op jit(solution)/shard_map/down/pallas_call | solution.py:165
  94.5 0.0 copy-done
  94.5 7.2 %term.1 = bf16[4,64,2048]{2,1,0:T(8,128)(2,1)} custom-call(s32[4]{0:T(128)S(1)} %pad_add_fusion.where, bf16[256,256]{1,0:T(8,128)(2,1)S(1)} %copy-done, bf16[128,1024]{1,0:T(8,128)(2,1)S(1)} %down.1.dd, bf16[4096,256]{1,0:T(8,128)(2,1)} %refs_1_.1, bf16[4096,256]{1,0:T(8,128)(2,1)} %refs_1_.1, bf16[4096,256]{1,0:T(8,128)(2,1)} %refs_3_.1, ...), custom_call_target="tpu_custom_call" | custom-call | tf_op jit(solution)/shard_map/term/pallas_call | solution.py:198
  101.8 0.0 all-to-all-done.2.cot
  101.8 6.9 %all-to-all-start.1 = ((bf16[32,8,2048]{2,1,0:T(8,128)(2,1)}), bf16[32,8,2048]{2,1,0:T(8,128)(2,1)S(1)}, u32[]{:S(2)}, u32[]{:S(2)}) async-start(bf16[32,8,2048]{2,1,0:T(8,128)(2,1)} %bitcast.10), calls=%async_computation.1 | async-start | bytes 2097152 | tf_op jit(solution)/shard_map/all_to_all | solution.py:276
  108.7 6.7 %collective-permute-start.7 = (bf16[128,512]{1,0:T(8,128)(2,1)S(1)}, bf16[128,512]{1,0:T(8,128)(2,1)S(1)}, u32[]{:S(2)}, u32[]{:S(2)}) collective-permute-start(bf16[128,512]{1,0:T(8,128)(2,1)S(1)} %get-tuple-element.27.h0), channel_id=1, source_target_pairs={{0,128},{128,256},{256,384},{384,0},{1,129},{129,257},{257,385},{3... | collective-permute-start | bytes 393224 | tf_op jit(solution)/shard_map/ppermute | solution.py:35
  115.4 7.9 %collective-permute-start.8 = (bf16[128,512]{1,0:T(8,128)(2,1)S(1)}, bf16[128,512]{1,0:T(8,128)(2,1)S(1)}, u32[]{:S(2)}, u32[]{:S(2)}) collective-permute-start(bf16[128,512]{1,0:T(8,128)(2,1)S(1)} %get-tuple-element.27.h0), channel_id=1, source_target_pairs={{0,256},{128,384},{256,0},{384,128},{1,257},{129,385},{257,1},{385... | collective-permute-start | bytes 393224 | tf_op jit(solution)/shard_map/ppermute | solution.py:35
  123.3 1.9 %collective-permute-start.9 = (bf16[128,512]{1,0:T(8,128)(2,1)S(1)}, bf16[128,512]{1,0:T(8,128)(2,1)S(1)}, u32[]{:S(2)}, u32[]{:S(2)}) collective-permute-start(bf16[128,512]{1,0:T(8,128)(2,1)S(1)} %get-tuple-element.27.h0), channel_id=1, source_target_pairs={{0,384},{128,0},{256,128},{384,256},{1,385},{129,1},{257,129},{385... | collective-permute-start | bytes 393224 | tf_op jit(solution)/shard_map/ppermute | solution.py:35
  125.2 0.0 collective-permute-done.7.h1
  125.2 5.5 %collective-permute-done.8.h2 = bf16[128,512]{1,0:T(8,128)(2,1)S(1)} collective-permute-done((bf16[128,512]{1,0:T(8,128)(2,1)S(1)}, bf16[128,512]{1,0:T(8,128)(2,1)S(1)}, u32[]{:S(2)}, u32[]{:S(2)}) %collective-permute-start.8) | collective-permute-done | bytes 131104 | tf_op jit(solution)/shard_map/ppermute | solution.py:35
  130.7 8.5 %collective-permute-done.9.h3 = bf16[128,512]{1,0:T(8,128)(2,1)S(1)} collective-permute-done((bf16[128,512]{1,0:T(8,128)(2,1)S(1)}, bf16[128,512]{1,0:T(8,128)(2,1)S(1)}, u32[]{:S(2)}, u32[]{:S(2)}) %collective-permute-start.9) | collective-permute-done | bytes 131104 | tf_op jit(solution)/shard_map/ppermute | solution.py:35
  139.2 1.8 %grads.1 = (f32[256,512]{1,0:T(8,128)S(1)}, bf16[256,512]{1,0:T(8,128)(2,1)S(1)}, bf16[256,512]{1,0:T(8,128)(2,1)S(1)}, bf16[256,512]{1,0:T(8,128)(2,1)S(1)}) custom-call(s32[4]{0:T(128)S(1)} %pad_add_fusion.where, bf16[128,512]{1,0:T(8,128)(2,1)S(1)} %get-tuple-element.27.h0, bf16[128,512]{1,0:T(8,128)(2,1)S(1)} %collective-permute-done.7.h1, ...), custom_call_target="tpu_custom_call" | custom-call | tf_op jit(solution)/shard_map/grads/pallas_call | solution.py:228
  141.0 3.1 %collective-permute-start.10 = (bf16[256,512]{1,0:T(8,128)(2,1)S(1)}, bf16[256,512]{1,0:T(8,128)(2,1)S(1)}, u32[]{:S(2)}, u32[]{:S(2)}) collective-permute-start(bf16[256,512]{1,0:T(8,128)(2,1)S(1)} %get-tuple-element.29), channel_id=1, source_target_pairs={{0,64},{64,0},{1,65},{65,1},{2,66},{66,2},{3,67},{67,3},{4,68},{68... | collective-permute-start | bytes 786440 | tf_op jit(solution)/shard_map/ppermute | solution.py:30
  144.2 1.9 %collective-permute-start.11 = (bf16[256,512]{1,0:T(8,128)(2,1)S(1)}, bf16[256,512]{1,0:T(8,128)(2,1)S(1)}, u32[]{:S(2)}, u32[]{:S(2)}) collective-permute-start(bf16[256,512]{1,0:T(8,128)(2,1)S(1)} %get-tuple-element.30), channel_id=1, source_target_pairs={{0,32},{32,0},{1,33},{33,1},{2,34},{34,2},{3,35},{35,3},{4,36},{36... | collective-permute-start | bytes 786440 | tf_op jit(solution)/shard_map/ppermute | solution.py:30
  146.1 3.5 %collective-permute-start.12 = (bf16[256,512]{1,0:T(8,128)(2,1)S(1)}, bf16[256,512]{1,0:T(8,128)(2,1)S(1)}, u32[]{:S(2)}, u32[]{:S(2)}) collective-permute-start(bf16[256,512]{1,0:T(8,128)(2,1)S(1)} %get-tuple-element.31), channel_id=1, source_target_pairs={{0,96},{96,0},{32,64},{64,32},{1,97},{97,1},{33,65},{65,33},{2,98}... | collective-permute-start | bytes 786440 | tf_op jit(solution)/shard_map/ppermute | solution.py:286
  149.6 0.0 collective-permute-done.10
  149.7 4.3 %collective-permute-done.11 = bf16[256,512]{1,0:T(8,128)(2,1)S(1)} collective-permute-done((bf16[256,512]{1,0:T(8,128)(2,1)S(1)}, bf16[256,512]{1,0:T(8,128)(2,1)S(1)}, u32[]{:S(2)}, u32[]{:S(2)}) %collective-permute-start.11) | collective-permute-done | bytes 262176 | tf_op jit(solution)/shard_map/ppermute | solution.py:30
  154.0 5.7 %collective-permute-done.12 = bf16[256,512]{1,0:T(8,128)(2,1)S(1)} collective-permute-done((bf16[256,512]{1,0:T(8,128)(2,1)S(1)}, bf16[256,512]{1,0:T(8,128)(2,1)S(1)}, u32[]{:S(2)}, u32[]{:S(2)}) %collective-permute-start.12) | collective-permute-done | bytes 262176 | tf_op jit(solution)/shard_map/ppermute | solution.py:286
  159.7 1.0 convert_add_fusion
  160.7 0.0 all-to-all-done.1
  160.7 0.2 reduce_sum.12
  160.8 0.6 pad_maximum_fusion.1
  (5 shorter events, 0.1 us)
Async XLA Ops:
  7.2 63.0 %all-gather.3.cloned.1.call-start = ((), (), s32[]{:S(2)}) async-start(), calls=%async_computation.3 | async-start | bytes 2359296 | tf_op jit(solution)/shard_map/all_gather | solution.py:260
  7.9 14.8 %copy-start.2 = (bf16[4,4096]{1,0:T(4,128)(2,1)S(1)}, bf16[4,4096]{1,0:T(4,128)(2,1)}, u32[]{:S(2)}) copy-start(bf16[4,4096]{1,0:T(4,128)(2,1)} %param.8) | copy-start | bytes 98308
  7.9 14.8 %copy-start.3 = (bf16[4,4096]{1,0:T(4,128)(2,1)S(1)}, bf16[4,4096]{1,0:T(4,128)(2,1)}, u32[]{:S(2)}) copy-start(bf16[4,4096]{1,0:T(4,128)(2,1)} %param.7) | copy-start | bytes 98308
  11.1 54.3 %copy-start.1 = (bf16[64,64]{1,0:T(8,128)(2,1)S(1)}, bf16[64,64]{1,0:T(8,128)(2,1)}, u32[]{:S(2)}) copy-start(bf16[64,64]{1,0:T(8,128)(2,1)} %constant.27.clone.pick) | copy-start | bytes 24580
  11.1 59.0 %collective-permute-start.4 = (bf16[4096,256]{1,0:T(8,128)(2,1)}, bf16[4096,256]{1,0:T(8,128)(2,1)}, u32[]{:S(2)}, u32[]{:S(2)}) collective-permute-start(bf16[4096,256]{1,0:T(8,128)(2,1)} %broadcast_select_fusion), channel_id=1, source_target_pairs={{0,32},{32,0},{96,192},{192,96},{128,160},{160,128},{224,320},{320... | collective-permute-start | bytes 6291464 | tf_op jit(solution)/shard_map/ppermute | solution.py:44
  42.2 13.1 %collective-permute-start = (bf16[64,4096]{1,0:T(8,128)(2,1)S(1)}, bf16[64,4096]{1,0:T(8,128)(2,1)S(1)}, u32[]{:S(2)}, u32[]{:S(2)}) collective-permute-start(bf16[64,4096]{1,0:T(8,128)(2,1)S(1)} %bitcast.7), channel_id=1, source_target_pairs={{0,1},{1,2},{2,3},{3,0},{4,5},{5,6},{6,7},{7,4},{8,9},{9,10},{10,1... | collective-permute-start | bytes 1572872 | tf_op jit(solution)/shard_map/ppermute | solution.py:35
  45.4 12.2 %collective-permute-start.2 = (bf16[64,4096]{1,0:T(8,128)(2,1)S(1)}, bf16[64,4096]{1,0:T(8,128)(2,1)S(1)}, u32[]{:S(2)}, u32[]{:S(2)}) collective-permute-start(bf16[64,4096]{1,0:T(8,128)(2,1)S(1)} %bitcast.8), channel_id=1, source_target_pairs={{0,3},{1,0},{2,1},{3,2},{4,7},{5,4},{6,5},{7,6},{8,11},{9,8},{10,9... | collective-permute-start | bytes 1572872 | tf_op jit(solution)/shard_map/ppermute | solution.py:35
  55.3 8.6 %collective-permute-start.1 = (bf16[32,4096]{1,0:T(8,128)(2,1)S(1)}, bf16[32,4096]{1,0:T(8,128)(2,1)S(1)}, u32[]{:S(2)}, u32[]{:S(2)}) collective-permute-start(bf16[32,4096]{1,0:T(8,128)(2,1)S(1)} %slice.16), channel_id=1, source_target_pairs={{0,1},{1,2},{2,3},{3,0},{4,5},{5,6},{6,7},{7,4},{8,9},{9,10},{10,1... | collective-permute-start | bytes 786440 | tf_op jit(solution)/shard_map/ppermute | solution.py:35
  57.5 7.9 %collective-permute-start.3 = (bf16[32,4096]{1,0:T(8,128)(2,1)S(1)}, bf16[32,4096]{1,0:T(8,128)(2,1)S(1)}, u32[]{:S(2)}, u32[]{:S(2)}) collective-permute-start(bf16[32,4096]{1,0:T(8,128)(2,1)S(1)} %slice.17), channel_id=1, source_target_pairs={{0,3},{1,0},{2,1},{3,2},{4,7},{5,4},{6,5},{7,6},{8,11},{9,8},{10,9... | collective-permute-start | bytes 786440 | tf_op jit(solution)/shard_map/ppermute | solution.py:35
  70.1 12.4 %collective-permute-start.6 = (bf16[4096,256]{1,0:T(8,128)(2,1)}, bf16[4096,256]{1,0:T(8,128)(2,1)S(1)}, u32[]{:S(2)}, u32[]{:S(2)}) collective-permute-start(bf16[4096,256]{1,0:T(8,128)(2,1)} %collective-permute-done.4.mw.refs_4_.refs_5_), channel_id=1, source_target_pairs={{0,64},{64,0},{1,65},{65,1},{2,66},{66,2},{3,67},{67,3},{4,68},{68... | collective-permute-start | bytes 6291464 | tf_op jit(solution)/shard_map/ppermute | solution.py:30
  72.1 17.7 %collective-permute-start.5 = (bf16[4,512,512]{2,1,0:T(8,128)(2,1)}, bf16[4,512,512]{2,1,0:T(8,128)(2,1)}, u32[]{:S(2)}, u32[]{:S(2)}) collective-permute-start(bf16[4,512,512]{2,1,0:T(8,128)(2,1)} %bitcast.11), channel_id=1, source_target_pairs={{0,64},{64,0},{1,65},{65,1},{2,66},{66,2},{3,67},{67,3},{4,68},{68... | collective-permute-start | bytes 6291464 | tf_op jit(solution)/shard_map/ppermute | solution.py:30
  74.5 27.3 %all-to-all-start.2 = ((bf16[4,2,128,512]{3,2,1,0:T(8,128)(2,1)}), bf16[4,2,128,512]{3,2,1,0:T(8,128)(2,1)S(1)}, u32[]{:S(2)}, u32[]{:S(2)}) async-start(bf16[4,2,128,512]{3,2,1,0:T(8,128)(2,1)} %get-tuple-element.18.cot), calls=%async_computation.2 | async-start | bytes 2097152 | tf_op jit(solution)/shard_map/all_to_all | solution.py:268
  89.7 4.8 %copy-start = (bf16[256,256]{1,0:T(8,128)(2,1)S(1)}, bf16[256,256]{1,0:T(8,128)(2,1)}, u32[]{:S(2)}) copy-start(bf16[256,256]{1,0:T(8,128)(2,1)} %constant.28.clone.pick) | copy-start | bytes 393220
  101.8 58.9 %all-to-all-start.1 = ((bf16[32,8,2048]{2,1,0:T(8,128)(2,1)}), bf16[32,8,2048]{2,1,0:T(8,128)(2,1)S(1)}, u32[]{:S(2)}, u32[]{:S(2)}) async-start(bf16[32,8,2048]{2,1,0:T(8,128)(2,1)} %bitcast.10), calls=%async_computation.1 | async-start | bytes 2097152 | tf_op jit(solution)/shard_map/all_to_all | solution.py:276
  108.7 16.5 %collective-permute-start.7 = (bf16[128,512]{1,0:T(8,128)(2,1)S(1)}, bf16[128,512]{1,0:T(8,128)(2,1)S(1)}, u32[]{:S(2)}, u32[]{:S(2)}) collective-permute-start(bf16[128,512]{1,0:T(8,128)(2,1)S(1)} %get-tuple-element.27.h0), channel_id=1, source_target_pairs={{0,128},{128,256},{256,384},{384,0},{1,129},{129,257},{257,385},{3... | collective-permute-start | bytes 393224 | tf_op jit(solution)/shard_map/ppermute | solution.py:35
  115.4 15.3 %collective-permute-start.8 = (bf16[128,512]{1,0:T(8,128)(2,1)S(1)}, bf16[128,512]{1,0:T(8,128)(2,1)S(1)}, u32[]{:S(2)}, u32[]{:S(2)}) collective-permute-start(bf16[128,512]{1,0:T(8,128)(2,1)S(1)} %get-tuple-element.27.h0), channel_id=1, source_target_pairs={{0,256},{128,384},{256,0},{384,128},{1,257},{129,385},{257,1},{385... | collective-permute-start | bytes 393224 | tf_op jit(solution)/shard_map/ppermute | solution.py:35
  123.3 15.9 %collective-permute-start.9 = (bf16[128,512]{1,0:T(8,128)(2,1)S(1)}, bf16[128,512]{1,0:T(8,128)(2,1)S(1)}, u32[]{:S(2)}, u32[]{:S(2)}) collective-permute-start(bf16[128,512]{1,0:T(8,128)(2,1)S(1)} %get-tuple-element.27.h0), channel_id=1, source_target_pairs={{0,384},{128,0},{256,128},{384,256},{1,385},{129,1},{257,129},{385... | collective-permute-start | bytes 393224 | tf_op jit(solution)/shard_map/ppermute | solution.py:35
  141.0 8.6 %collective-permute-start.10 = (bf16[256,512]{1,0:T(8,128)(2,1)S(1)}, bf16[256,512]{1,0:T(8,128)(2,1)S(1)}, u32[]{:S(2)}, u32[]{:S(2)}) collective-permute-start(bf16[256,512]{1,0:T(8,128)(2,1)S(1)} %get-tuple-element.29), channel_id=1, source_target_pairs={{0,64},{64,0},{1,65},{65,1},{2,66},{66,2},{3,67},{67,3},{4,68},{68... | collective-permute-start | bytes 786440 | tf_op jit(solution)/shard_map/ppermute | solution.py:30
  144.2 9.8 %collective-permute-start.11 = (bf16[256,512]{1,0:T(8,128)(2,1)S(1)}, bf16[256,512]{1,0:T(8,128)(2,1)S(1)}, u32[]{:S(2)}, u32[]{:S(2)}) collective-permute-start(bf16[256,512]{1,0:T(8,128)(2,1)S(1)} %get-tuple-element.30), channel_id=1, source_target_pairs={{0,32},{32,0},{1,33},{33,1},{2,34},{34,2},{3,35},{35,3},{4,36},{36... | collective-permute-start | bytes 786440 | tf_op jit(solution)/shard_map/ppermute | solution.py:30
  146.1 13.6 %collective-permute-start.12 = (bf16[256,512]{1,0:T(8,128)(2,1)S(1)}, bf16[256,512]{1,0:T(8,128)(2,1)S(1)}, u32[]{:S(2)}, u32[]{:S(2)}) collective-permute-start(bf16[256,512]{1,0:T(8,128)(2,1)S(1)} %get-tuple-element.31), channel_id=1, source_target_pairs={{0,96},{96,0},{32,64},{64,32},{1,97},{97,1},{33,65},{65,33},{2,98}... | collective-permute-start | bytes 786440 | tf_op jit(solution)/shard_map/ppermute | solution.py:286
Sparse Core Ops, SparseCore 0:
  10.1 54.1 all-gather.2

commit v11 on v4

v11 whole, which is shorter than its diff:
```python
import functools

import jax
import jax.numpy as jnp
import numpy as np
from jax import lax
from jax.experimental import pallas as pl
from jax.experimental.pallas import tpu as pltpu
from jax.sharding import Mesh, PartitionSpec as P

BF16 = jnp.bfloat16
F32 = jnp.float32
DP = ("zh", "c")
TENSOR = ("zl", "y", "x")
NZ, NY, NX = 4, 8, 4
ROWS = 4
HALF = NX * NY * ROWS
D = 4096
HID = 256
FEATS = 512
STEPS = D // FEATS
PIECE = 2 * NY * ROWS


def contract(a, b, ca, cb):
    return lax.dot_general(a, b, (((ca,), (cb,)), ((), ())), preferred_element_type=F32)


def swap(value, axis):
    return lax.ppermute(value, axis, [(0, 1), (1, 0)])


def shift(value, axis, k):
    n = lax.axis_size(axis)
    return lax.ppermute(value, axis, [(i, (i + k) % n) for i in range(n)])


def neighbours(value):
    at = lambda zh, c, zl: ((zh % NZ) * 2 + c) * 2 + zl
    pairs = []
    for zh in range(NZ):
        pairs += [(at(zh, 0, 0), at(zh, 0, 1)), (at(zh, 0, 1), at(zh, 0, 0))]
        pairs += [(at(zh, 1, 1), at(zh + 1, 1, 0)), (at(zh + 1, 1, 0), at(zh, 1, 1))]
    return lax.ppermute(value, ("zh", "c", "zl"), pairs)


def pinned(*values):
    return [pltpu.with_memory_space_constraint(v, pltpu.MemorySpace.HBM) for v in values]


def flip(a, b):
    return a + b - 2 * a * b


def forward_body(where, pick, r0, r1, r2a, r2b, r3, gw, uw, mw, ow, dn, df, exch, dd, tok, cot, acc, dacc):
    step = pl.program_id(0)
    zh, far = step // 2, step % 2

    @pl.when(step == 0)
    def _():
        acc[...] = jnp.zeros_like(acc)
        dacc[...] = jnp.zeros_like(dacc)

    n = NY * ROWS
    r2 = jnp.concatenate([r2a[...], r2b[...]], axis=0)
    for i, piece in enumerate((r0[...], r1[...], r2, r3[...])):
        rows = contract(pick[...], piece, 1, 0).astype(BF16)
        tok[i * n : (i + 1) * n] = rows[:n]
        cot[i * n : (i + 1) * n] = rows[n:]
    t = tok[...]
    for i, w in enumerate((gw, uw, mw, ow)):
        acc[:, i * HID : (i + 1) * HID] += contract(t, w[...], 1, 0)
    exch[zh, far] = cot[...]

    @pl.when(far == 0)
    def _():
        dacc[...] += contract(cot[...], dn[0], 1, 1)

    @pl.when(far == 1)
    def _():
        dacc[...] += contract(cot[...], df[0], 1, 1)

    @pl.when(step == STEPS - 1)
    def _():
        first, low = where[0] == 0, where[1] == 0
        pm, po = acc[:, 2 * HID : 3 * HID], acc[:, 3 * HID :]
        dl, dh = dacc[:, :HID], dacc[:, HID:]
        sides = (
            (acc[:, :HID], acc[:, HID : 2 * HID], jnp.where(low, dl, dh)),
            (jnp.where(first, pm, po), jnp.where(first, po, pm), jnp.where(low, dh, dl)),
        )
        for i, (gate, up, d_hidden) in enumerate(sides):
            sigma = jax.nn.sigmoid(gate)
            silu = gate * sigma
            hidden = (silu * up).astype(BF16)
            for z in range(NZ):
                exch[z, 2, :, i * HID : (i + 1) * HID] = hidden
            d_up = d_hidden * silu
            d_gate = d_hidden * up * sigma * (1.0 + gate * (1.0 - sigma))
            if i == 1:
                d_gate, d_up = jnp.where(first, d_gate, d_up), jnp.where(first, d_up, d_gate)
            dd[:, 2 * i * HID : (2 * i + 1) * HID] = d_gate.astype(BF16)
            dd[:, (2 * i + 1) * HID : (2 * i + 2) * HID] = d_up.astype(BF16)


def forward(where, pieces, gw, uw, mw, ow, dn, df):
    def column(j, s):
        return (j // 2) * 2 + flip(j % 2, s[0])

    whole = lambda *shape: pl.BlockSpec(shape, lambda j, s: (0,) * len(shape))
    piece = pl.BlockSpec((PIECE, FEATS), lambda j, s: (0, column(j, s)))
    part = pl.BlockSpec((PIECE // 2, FEATS), lambda j, s: (0, column(j, s)))
    weight = pl.BlockSpec((FEATS, HID), lambda j, s: (column(j, s), 0))
    plane = pl.BlockSpec((1, 2 * HID, FEATS), lambda j, s: (j // 2, 0, 0))
    return pl.pallas_call(
        forward_body,
        grid_spec=pltpu.PrefetchScalarGridSpec(
            num_scalar_prefetch=1,
            grid=(STEPS,),
            in_specs=[whole(PIECE, PIECE), piece, piece, part, part, piece] + [weight] * 4 + [plane] * 2,
            out_specs=[whole(NZ, 3, HALF, FEATS), whole(HALF, 4 * HID)],
            scratch_shapes=[
                pltpu.VMEM((HALF, FEATS), BF16),
                pltpu.VMEM((HALF, FEATS), BF16),
                pltpu.VMEM((HALF, 4 * HID), F32),
                pltpu.VMEM((HALF, 2 * HID), F32),
            ],
        ),
        out_shape=[
            jax.ShapeDtypeStruct((NZ, 3, HALF, FEATS), BF16),
            jax.ShapeDtypeStruct((HALF, 4 * HID), BF16),
        ],
        compiler_params=pltpu.CompilerParams(vmem_limit_bytes=32 * 2**20),
        name="forward",
    )(where, selection((NY, 2, ROWS), (1, 0, 2)), *pieces, *pinned(gw, uw, mw), ow, *pinned(dn), df)


def term_body(pick, dd, *refs):
    weights, outs = refs[:-NX], refs[-NX:]
    halves = []
    for h in range(2):
        total = None
        for i, w in enumerate(weights[h::2]):
            part = contract(dd[:, i * HID : (i + 1) * HID], w[...], 1, 1)
            total = part if total is None else total + part
        halves.append(total.astype(BF16))
    rows = contract(pick[...], jnp.concatenate(halves, axis=0), 1, 0).astype(BF16)
    for i, out in enumerate(outs):
        out[...] = rows[i * PIECE : (i + 1) * PIECE]


def term(dd, gw, uw, mw, ow):
    low = pl.BlockSpec((FEATS, HID), lambda j: (j, 0))
    high = pl.BlockSpec((FEATS, HID), lambda j: (j + NZ, 0))
    gw, uw, mw = pinned(gw, uw, mw)
    return pl.pallas_call(
        term_body,
        grid=(STEPS // 2,),
        in_specs=[
            pl.BlockSpec((2 * HALF, 2 * HALF), lambda j: (0, 0)),
            pl.BlockSpec((HALF, 4 * HID), lambda j: (0, 0)),
        ]
        + [low, high] * 4,
        out_specs=[pl.BlockSpec((PIECE, FEATS), lambda j: (0, j))] * NX,
        out_shape=[jax.ShapeDtypeStruct((PIECE, D // 2), BF16)] * NX,
        compiler_params=pltpu.CompilerParams(vmem_limit_bytes=32 * 2**20),
        name="term",
    )(merge(), dd, gw, gw, uw, uw, mw, mw, ow, ow)


def grads_body(exch, *outs):
    for far in range(2):
        total = None
        for z in range(NZ):
            part = contract(exch[z, 2], exch[z, far], 0, 0)
            total = part if total is None else total + part
        for side, out in enumerate(outs[far::2]):
            out[...] = total[side * HID : (side + 1) * HID].astype(out.dtype)


def grads(exch):
    vmem = pl.BlockSpec(memory_space=pltpu.MemorySpace.VMEM)
    return pl.pallas_call(
        grads_body,
        in_specs=[vmem],
        out_specs=[vmem] * 4,
        out_shape=[jax.ShapeDtypeStruct((HID, FEATS), F32)] + [jax.ShapeDtypeStruct((HID, FEATS), BF16)] * 3,
        compiler_params=pltpu.CompilerParams(vmem_limit_bytes=32 * 2**20),
        name="grads",
    )(exch)


def selection(shape, order):
    source = np.arange(np.prod(shape)).reshape(shape).transpose(order).reshape(-1)
    return jnp.asarray(np.eye(source.size, dtype=np.float32)[source], BF16)


def merge():
    return selection((2, NX, NY, ROWS), (1, 2, 0, 3))


def spread(block, axis):
    n = lax.axis_size(axis)
    return lax.all_to_all(jnp.broadcast_to(block[None], (n, *block.shape)), axis, 0, 0)


def on_device(tokens, cotangent, gate_weight, up_weight, down_weight):
    core = lax.axis_index("c")
    where = jnp.stack([core, lax.axis_index("zl")]).astype(jnp.int32)

    picked = jnp.where(core == 0, gate_weight, up_weight)
    picked, tokens = lax.optimization_barrier((picked, tokens))
    mine = neighbours(picked)
    down_near = lax.all_gather(down_weight, ("zh", "zl"), axis=0).reshape(NZ, 2 * HID, FEATS)

    block = spread(jnp.concatenate([tokens, cotangent], axis=0), "y").reshape(PIECE, D)
    left, right = shift(block, "x", 1), shift(block, "x", -1)
    n = PIECE // 2
    far = shift(left[:n], "x", 1), shift(right[n:], "x", -1)
    far, mine, down_near = lax.optimization_barrier((far, mine, down_near))
    other, down_far = swap(mine, "c"), swap(down_near, "c")
    pieces = (block, left, *far, right)
    exch, dd = forward(where, pieces, gate_weight, up_weight, mine, other, down_near, down_far)

    exch = lax.all_to_all(exch, "zh", 0, 0)
    parts = term(dd, gate_weight, up_weight, mine, other)
    total = parts[0].astype(F32)
    for k in (1, 2, 3):
        total = total + shift(parts[k], "x", -k).astype(F32)
    total, exch = lax.optimization_barrier((total.astype(BF16), exch))
    parts = lax.all_to_all(total.reshape(NY, 2 * ROWS, D // 2), "y", 0, 0)
    total = jnp.sum(parts.astype(F32), axis=0).astype(BF16)
    input_grad = jnp.concatenate([total[:ROWS], total[ROWS:]], axis=1)

    keep, core_part, zl_part, both_part = grads(exch)
    down_grad = (
        keep
        + swap(core_part, "c").astype(F32)
        + swap(zl_part, "zl").astype(F32)
        + lax.ppermute(both_part, ("c", "zl"), [(0, 3), (3, 0), (1, 2), (2, 1)]).astype(F32)
    )
    return (input_grad, down_grad)


def solution(mesh):
    fine = Mesh(mesh.devices.reshape(NZ, 2, 2, NY, NX), ("zh", "c", "zl", "y", "x"))
    placed = (
        P((*DP, *TENSOR), None),
        P((*DP, *TENSOR), None),
        P(None, TENSOR),
        P(None, TENSOR),
        P(TENSOR, DP),
    )
    return jax.shard_map(
        on_device,
        mesh=fine,
        in_specs=placed,
        out_specs=(P((*DP, *TENSOR), None), P(TENSOR, DP)),
        check_vma=False,
    )
```

time: 216 us -> 173 us (0.80)
  waiting for transfers between devices: 71.9 us -> 40 us
  local copies, waits for them, and re-layouts: 11.3 us -> 4.7 us
  blocking collectives: 22.2 us -> 19.4 us
    ppermute x5 -> x4, waiting for transfers between devices: 43.3 us -> 5.49 us  [swap(): return lax.ppermute(value, axis, [(0, 1), (1, 0)])]
    ppermute x0 -> x2, starting transfers between devices: none -> 13.4 us  [the longest x1 11.5 us: neighbours(): return lax.ppermute(value, ('zh', 'c', 'zl'), pairs)]
    ppermute x5 -> x4, starting transfers between devices: 35.4 us -> 22.5 us  [swap(): return lax.ppermute(value, axis, [(0, 1), (1, 0)])]
    all_to_all x1, waiting for transfers between devices: 7.36 us -> 0.01 us  [on_device(): exch = lax.all_to_all(exch, 'zh', 0, 0)]
    ppermute x0 -> x2, waiting for transfers between devices: none -> 5.82 us  [the longest x1 5.82 us: on_device(): lax.ppermute(both_part, ('c', 'zl'), [(0, 3), (3, 0), (1, 2), (2, 1)])]
    ppermute x6 -> x7, waiting for transfers between devices: 20.6 us -> 24.4 us  [shift(): return lax.ppermute(value, axis, [(i, (i + k) % n) for i in range(n)])]
    all_to_all x1, waiting for transfers between devices: 0.01 us -> 3.58 us  [on_device(): parts = lax.all_to_all(total.reshape(NY, 2 * ROWS, D // 2), 'y', 0, 0)]
    unnamed x20 -> x22, local copies, waits for them, and re-layouts: 8.15 us -> 4.61 us
  transfers between devices with their start and end apart: 14 -> 16, of which waited for: 6 -> 12; matrix products, arithmetic and copies ran while one was open for 3% -> 2% of each run, Pallas kernels for 5% -> 3%
where the time goes in v11:
time: 173 us; the launch traced here: 172 us
  starting transfers between devices  69.5 us (40%)
  waiting for transfers between devices  40 us (23%)
  Pallas kernels  19.6 us (11%)
  blocking collectives  19.4 us (11%)
  between operations  14.3 us (8%)
  local copies, waits for them, and re-layouts  4.7 us (3%)
  other arithmetic  4.36 us (3%)
    ppermute x7, waiting for transfers between devices, shift(): return lax.ppermute(value, axis, [(i, (i + k) % n) for i in range(n)])  24.4 us
    ppermute x4, starting transfers between devices, swap(): return lax.ppermute(value, axis, [(0, 1), (1, 0)])  22.5 us
    ppermute x7, starting transfers between devices, shift(): return lax.ppermute(value, axis, [(i, (i + k) % n) for i in range(n)])  20.8 us
    all_to_all x1, blocking collectives, spread(): lax.all_to_all(jnp.broadcast_to(block[None], (n, *block.shape)), axis, 0, 0)  19.4 us
    ppermute x1, starting transfers between devices, neighbours(): return lax.ppermute(value, ('zh', 'c', 'zl'), pairs)  11.5 us
    pallas_call x1, Pallas kernels, forward(): pl.pallas_call(forward_body, grid_spec=pltpu.PrefetchScalarGridSpec(num_s...  10.9 us
    all_to_all x1, starting transfers between devices, on_device(): exch = lax.all_to_all(exch, 'zh', 0, 0)  8.63 us
    pallas_call x1, Pallas kernels, term(): pl.pallas_call(term_body, grid=(STEPS // 2,), in_specs=[pl.BlockSpec((2 *...  5.97 us
  transfers between devices with their start and end apart: 16, of which 12 were waited for; matrix products, arithmetic and copies ran while one was open for 2% of the time, Pallas kernels for 3%

profile of v11, /device:TPU:1, one launch (start us, length us, event | category | flops | bytes accessed | tf_op | source)
XLA Modules:
  0.0 171.8 jit_solution(4806242251262690162)
XLA Ops:
  7.2 0.0 all-gather.3.cloned.1.call-start
  7.2 0.7 all-gather.3.cloned.1.call-update
  7.9 0.0 copy-start.9
  7.9 0.0 copy-start.10
  7.9 1.8 %broadcast_select_fusion = bf16[4096,256]{1,0:T(8,128)(2,1)S(1)} fusion(bf16[4096,256]{1,0:T(8,128)(2,1)} %refs_1_.1, bf16[4096,256]{1,0:T(8,128)(2,1)} %refs_3_.1, pred[]{:T(512)S(6)} %eq.3), kind=kLoop, calls=%fused_computation | loop fusion | flops 1048576 | bytes 6291457 | tf_op jit(solution)/shard_map/jit(_where)/select_n | solution.py:211
  9.8 0.0 copy-start.8
  9.8 11.5 %collective-permute-start.4 = (bf16[4096,256]{1,0:T(8,128)(2,1)S(1)}, bf16[4096,256]{1,0:T(8,128)(2,1)}, u32[]{:S(2)}, u32[]{:S(2)}) collective-permute-start(bf16[4096,256]{1,0:T(8,128)(2,1)S(1)} %broadcast_select_fusion), channel_id=1, source_target_pairs={{0,32},{32,0},{96,192},{192,96},{128,160},{160,128},{224,320},{320... | collective-permute-start | bytes 6291464 | tf_op jit(solution)/shard_map/ppermute | solution.py:44
  21.3 0.0 copy-done.9
  21.3 0.0 copy-done.10
  21.4 19.4 %all_to_all.15 = bf16[8,8,4096]{2,1,0:T(8,128)(2,1)S(1)} all-to-all(bf16[8,8,4096]{2,1,0:T(8,128)(2,1)S(1)} %broadcast_in_dim.2), channel_id=1, replica_groups=mesh['zh'=4,'c'=2,'zl'=2,'y'=8,'x'=4] {'y'}, dimensions={0} | all-to-all | bytes 1048576 | tf_op jit(solution)/shard_map/all_to_all | solution.py:204
  40.8 4.4 %collective-permute-start.2 = (bf16[64,4096]{1,0:T(8,128)(2,1)S(1)}, bf16[64,4096]{1,0:T(8,128)(2,1)S(1)}, u32[]{:S(2)}, u32[]{:S(2)}) collective-permute-start(bf16[64,4096]{1,0:T(8,128)(2,1)S(1)} %bitcast.5), channel_id=1, source_target_pairs={{0,3},{1,0},{2,1},{3,2},{4,7},{5,4},{6,5},{7,6},{8,11},{9,8},{10,9... | collective-permute-start | bytes 1572872 | tf_op jit(solution)/shard_map/ppermute | solution.py:35
  45.2 1.9 %collective-permute-start = (bf16[64,4096]{1,0:T(8,128)(2,1)S(1)}, bf16[64,4096]{1,0:T(8,128)(2,1)S(1)}, u32[]{:S(2)}, u32[]{:S(2)}) collective-permute-start(bf16[64,4096]{1,0:T(8,128)(2,1)S(1)} %bitcast.6), channel_id=1, source_target_pairs={{0,1},{1,2},{2,3},{3,0},{4,5},{5,6},{6,7},{7,4},{8,9},{9,10},{10,1... | collective-permute-start | bytes 1572872 | tf_op jit(solution)/shard_map/ppermute | solution.py:35
  47.1 5.7 %collective-permute-done.2.r3 = bf16[64,4096]{1,0:T(8,128)(2,1)S(1)} collective-permute-done((bf16[64,4096]{1,0:T(8,128)(2,1)S(1)}, bf16[64,4096]{1,0:T(8,128)(2,1)S(1)}, u32[]{:S(2)}, u32[]{:S(2)}) %collective-permute-start.2) | collective-permute-done | bytes 524320 | tf_op jit(solution)/shard_map/ppermute | solution.py:35
  52.8 5.4 %collective-permute-start.3 = (bf16[32,4096]{1,0:T(8,128)(2,1)S(1)}, bf16[32,4096]{1,0:T(8,128)(2,1)S(1)}, u32[]{:S(2)}, u32[]{:S(2)}) collective-permute-start(bf16[32,4096]{1,0:T(8,128)(2,1)S(1)} %slice.17), channel_id=1, source_target_pairs={{0,3},{1,0},{2,1},{3,2},{4,7},{5,4},{6,5},{7,6},{8,11},{9,8},{10,9... | collective-permute-start | bytes 786440 | tf_op jit(solution)/shard_map/ppermute | solution.py:35
  58.3 0.3 collective-permute-done.r1
  58.5 0.0 copy-start.1
  58.6 1.9 %collective-permute-start.1 = (bf16[32,4096]{1,0:T(8,128)(2,1)S(1)}, bf16[32,4096]{1,0:T(8,128)(2,1)S(1)}, u32[]{:S(2)}, u32[]{:S(2)}) collective-permute-start(bf16[32,4096]{1,0:T(8,128)(2,1)S(1)} %slice.16), channel_id=1, source_target_pairs={{0,1},{1,2},{2,3},{3,0},{4,5},{5,6},{6,7},{7,4},{8,9},{9,10},{10,1... | collective-permute-start | bytes 786440 | tf_op jit(solution)/shard_map/ppermute | solution.py:35
  60.5 1.1 collective-permute-done.3.r2b
  61.6 5.3 %collective-permute-done.1.r2a = bf16[32,4096]{1,0:T(8,128)(2,1)S(1)} collective-permute-done((bf16[32,4096]{1,0:T(8,128)(2,1)S(1)}, bf16[32,4096]{1,0:T(8,128)(2,1)S(1)}, u32[]{:S(2)}, u32[]{:S(2)}) %collective-permute-start.1) | collective-permute-done | bytes 262176 | tf_op jit(solution)/shard_map/ppermute | solution.py:35
  66.9 0.0 copy-start.3
  66.9 0.7 copy-done.3
  67.6 0.0 collective-permute-done.4.mw.refs_4_.refs_5_
  67.6 0.0 all-gather.3.cloned.1.call-done
  67.6 0.0 copy-done.1
  67.6 1.9 %collective-permute-start.6 = (bf16[4,512,512]{2,1,0:T(8,128)(2,1)}, bf16[4,512,512]{2,1,0:T(8,128)(2,1)}, u32[]{:S(2)}, u32[]{:S(2)}) collective-permute-start(bf16[4,512,512]{2,1,0:T(8,128)(2,1)} %bitcast.8), channel_id=1, source_target_pairs={{0,64},{64,0},{1,65},{65,1},{2,66},{66,2},{3,67},{67,3},{4,68},{68... | collective-permute-start | bytes 6291464 | tf_op jit(solution)/shard_map/ppermute | solution.py:30
  69.6 2.4 %collective-permute-start.5 = (bf16[4096,256]{1,0:T(8,128)(2,1)}, bf16[4096,256]{1,0:T(8,128)(2,1)S(1)}, u32[]{:S(2)}, u32[]{:S(2)}) collective-permute-start(bf16[4096,256]{1,0:T(8,128)(2,1)} %collective-permute-done.4.mw.refs_4_.refs_5_), channel_id=1, source_target_pairs={{0,64},{64,0},{1,65},{65,1},{2,66},{66,2},{3,67},{67,3},{4,68},{68... | collective-permute-start | bytes 6291464 | tf_op jit(solution)/shard_map/ppermute | solution.py:30
  72.0 0.1 pad_add_fusion.where
  72.0 2.0 %collective-permute-done.6.df = bf16[4,512,512]{2,1,0:T(8,128)(2,1)} collective-permute-done((bf16[4,512,512]{2,1,0:T(8,128)(2,1)}, bf16[4,512,512]{2,1,0:T(8,128)(2,1)}, u32[]{:S(2)}, u32[]{:S(2)}) %collective-permute-start.6) | collective-permute-done | bytes 2097184 | tf_op jit(solution)/shard_map/ppermute | solution.py:30
  74.0 2.9 %collective-permute-done.5.ow.refs_6_.refs_7_ = bf16[4096,256]{1,0:T(8,128)(2,1)S(1)} collective-permute-done((bf16[4096,256]{1,0:T(8,128)(2,1)}, bf16[4096,256]{1,0:T(8,128)(2,1)S(1)}, u32[]{:S(2)}, u32[]{:S(2)}) %collective-permute-start.5) | collective-permute-done | bytes 2097184 | tf_op jit(solution)/shard_map/ppermute | solution.py:30
  76.9 0.0 copy-done.8
  76.9 0.0 copy-start.2
  76.9 1.0 copy-done.2
  77.9 0.0 copy-start.4
  77.9 0.9 copy-done.4
  78.9 10.9 %forward.1 = (bf16[4,3,128,512]{3,2,1,0:T(8,128)(2,1)S(1)}, bf16[128,1024]{1,0:T(8,128)(2,1)S(1)}) custom-call(s32[2]{0:T(128)S(1)} %pad_add_fusion.where, bf16[64,64]{1,0:T(8,128)(2,1)S(1)} %copy-done.8, bf16[64,4096]{1,0:T(8,128)(2,1)S(1)} %bitcast.7, bf16[64,4096]{1,0:T(8,128)(2,1)S(1)} %copy-done.2, bf16[32,4096]{1,0:T(8,128)(2,1)S(1)} %copy-done.4, ...), custom_call_target="tpu_custom_call" | custom-call | tf_op jit(solution)/shard_map/forward/pallas_call | solution.py:115
  89.8 0.0 copy-start
  89.8 1.2 copy-done
  91.0 0.0 copy-start.5
  91.0 0.7 copy-done.5
  91.7 0.0 copy-start.7
  91.7 0.0 copy-start.6
  91.7 8.6 %all-to-all-start.1 = ((bf16[4,3,128,512]{3,2,1,0:T(8,128)(2,1)}), bf16[4,3,128,512]{3,2,1,0:T(8,128)(2,1)}, u32[]{:S(2)}, u32[]{:S(2)}) async-start(bf16[4,3,128,512]{3,2,1,0:T(8,128)(2,1)} %copy-done), calls=%async_computation.1 | async-start | bytes 3145728 | tf_op jit(solution)/shard_map/all_to_all | solution.py:225
  100.3 0.0 copy-done.7
  100.3 0.0 copy-done.6
  100.3 6.0 %term.1 = (bf16[64,2048]{1,0:T(8,128)(2,1)S(1)}, bf16[64,2048]{1,0:T(8,128)(2,1)S(1)}, bf16[64,2048]{1,0:T(8,128)(2,1)S(1)}, bf16[64,2048]{1,0:T(8,128)(2,1)S(1)}) custom-call(bf16[256,256]{1,0:T(8,128)(2,1)S(1)} %copy-done.7, bf16[128,1024]{1,0:T(8,128)(2,1)S(1)} %copy-done.6, bf16[4096,256]{1,0:T(8,128)(2,1)} %refs_1_.1, bf16[4096,256]{1,0:T(8,128)(2,1)} %refs_1_.1, ...), custom_call_target="tpu_custom_call" | custom-call | tf_op jit(solution)/shard_map/term/pallas_call | solution.py:156
  106.3 1.9 %collective-permute-start.7 = (bf16[64,2048]{1,0:T(8,128)(2,1)S(1)}, bf16[64,2048]{1,0:T(8,128)(2,1)S(1)}, u32[]{:S(2)}, u32[]{:S(2)}) collective-permute-start(bf16[64,2048]{1,0:T(8,128)(2,1)S(1)} %get-tuple-element.28), channel_id=1, source_target_pairs={{0,3},{1,0},{2,1},{3,2},{4,7},{5,4},{6,5},{7,6},{8,11},{9,8},{10,9... | collective-permute-start | bytes 786440 | tf_op jit(solution)/shard_map/ppermute | solution.py:35
  108.2 2.2 %collective-permute-start.8 = (bf16[64,2048]{1,0:T(8,128)(2,1)S(1)}, bf16[64,2048]{1,0:T(8,128)(2,1)S(1)}, u32[]{:S(2)}, u32[]{:S(2)}) collective-permute-start(bf16[64,2048]{1,0:T(8,128)(2,1)S(1)} %get-tuple-element.29), channel_id=1, source_target_pairs={{0,2},{1,3},{2,0},{3,1},{4,6},{5,7},{6,4},{7,5},{8,10},{9,11},{10,... | collective-permute-start | bytes 786440 | tf_op jit(solution)/shard_map/ppermute | solution.py:35
  110.5 3.1 %collective-permute-start.9 = (bf16[64,2048]{1,0:T(8,128)(2,1)S(1)}, bf16[64,2048]{1,0:T(8,128)(2,1)S(1)}, u32[]{:S(2)}, u32[]{:S(2)}) collective-permute-start(bf16[64,2048]{1,0:T(8,128)(2,1)S(1)} %get-tuple-element.30), channel_id=1, source_target_pairs={{0,1},{1,2},{2,3},{3,0},{4,5},{5,6},{6,7},{7,4},{8,9},{9,10},{10,1... | collective-permute-start | bytes 786440 | tf_op jit(solution)/shard_map/ppermute | solution.py:35
  113.5 1.9 %collective-permute-done.7 = bf16[64,2048]{1,0:T(8,128)(2,1)S(1)} collective-permute-done((bf16[64,2048]{1,0:T(8,128)(2,1)S(1)}, bf16[64,2048]{1,0:T(8,128)(2,1)S(1)}, u32[]{:S(2)}, u32[]{:S(2)}) %collective-permute-start.7) | collective-permute-done | bytes 262176 | tf_op jit(solution)/shard_map/ppermute | solution.py:35
  115.5 3.5 %collective-permute-done.8 = bf16[64,2048]{1,0:T(8,128)(2,1)S(1)} collective-permute-done((bf16[64,2048]{1,0:T(8,128)(2,1)S(1)}, bf16[64,2048]{1,0:T(8,128)(2,1)S(1)}, u32[]{:S(2)}, u32[]{:S(2)}) %collective-permute-start.8) | collective-permute-done | bytes 262176 | tf_op jit(solution)/shard_map/ppermute | solution.py:35
  119.0 6.6 %collective-permute-done.9 = bf16[64,2048]{1,0:T(8,128)(2,1)S(1)} collective-permute-done((bf16[64,2048]{1,0:T(8,128)(2,1)S(1)}, bf16[64,2048]{1,0:T(8,128)(2,1)S(1)}, u32[]{:S(2)}, u32[]{:S(2)}) %collective-permute-start.9) | collective-permute-done | bytes 262176 | tf_op jit(solution)/shard_map/ppermute | solution.py:35
  125.6 0.8 add_convert_fusion
  126.4 0.0 all-to-all-done.1.exch
  126.4 2.7 %grads.1 = (f32[256,512]{1,0:T(8,128)S(1)}, bf16[256,512]{1,0:T(8,128)(2,1)S(1)}, bf16[256,512]{1,0:T(8,128)(2,1)S(1)}, bf16[256,512]{1,0:T(8,128)(2,1)S(1)}) custom-call(bf16[4,3,128,512]{3,2,1,0:T(8,128)(2,1)} %all-to-all-done.1.exch), custom_call_target="tpu_custom_call" | custom-call | tf_op jit(solution)/shard_map/grads/pallas_call | solution.py:183
  129.1 3.8 %collective-permute-start.10 = (bf16[256,512]{1,0:T(8,128)(2,1)S(1)}, bf16[256,512]{1,0:T(8,128)(2,1)S(1)}, u32[]{:S(2)}, u32[]{:S(2)}) collective-permute-start(bf16[256,512]{1,0:T(8,128)(2,1)S(1)} %get-tuple-element.35), channel_id=1, source_target_pairs={{0,64},{64,0},{1,65},{65,1},{2,66},{66,2},{3,67},{67,3},{4,68},{68... | collective-permute-start | bytes 786440 | tf_op jit(solution)/shard_map/ppermute | solution.py:30
  132.9 14.3 %collective-permute-start.11 = (bf16[256,512]{1,0:T(8,128)(2,1)S(1)}, bf16[256,512]{1,0:T(8,128)(2,1)S(1)}, u32[]{:S(2)}, u32[]{:S(2)}) collective-permute-start(bf16[256,512]{1,0:T(8,128)(2,1)S(1)} %get-tuple-element.36), channel_id=1, source_target_pairs={{0,32},{32,0},{1,33},{33,1},{2,34},{34,2},{3,35},{35,3},{4,36},{36... | collective-permute-start | bytes 786440 | tf_op jit(solution)/shard_map/ppermute | solution.py:30
  147.3 1.9 %collective-permute-start.12 = (bf16[256,512]{1,0:T(8,128)(2,1)S(1)}, bf16[256,512]{1,0:T(8,128)(2,1)S(1)}, u32[]{:S(2)}, u32[]{:S(2)}) collective-permute-start(bf16[256,512]{1,0:T(8,128)(2,1)S(1)} %get-tuple-element.37), channel_id=1, source_target_pairs={{0,96},{96,0},{32,64},{64,32},{1,97},{97,1},{33,65},{65,33},{2,98}... | collective-permute-start | bytes 786440 | tf_op jit(solution)/shard_map/ppermute | solution.py:240
  149.2 4.1 %all-to-all-start.2 = ((bf16[8,8,2048]{2,1,0:T(8,128)(2,1)}), bf16[8,8,2048]{2,1,0:T(8,128)(2,1)S(1)}, u32[]{:S(2)}, u32[]{:S(2)}) async-start(bf16[8,8,2048]{2,1,0:T(8,128)(2,1)} %bitcast.4), calls=%async_computation.2 | async-start | bytes 524288 | tf_op jit(solution)/shard_map/all_to_all | solution.py:231
  153.3 0.0 collective-permute-done.10
  153.3 0.6 collective-permute-done.11
  153.9 5.8 %collective-permute-done.12 = bf16[256,512]{1,0:T(8,128)(2,1)S(1)} collective-permute-done((bf16[256,512]{1,0:T(8,128)(2,1)S(1)}, bf16[256,512]{1,0:T(8,128)(2,1)S(1)}, u32[]{:S(2)}, u32[]{:S(2)}) %collective-permute-start.12) | collective-permute-done | bytes 262176 | tf_op jit(solution)/shard_map/ppermute | solution.py:240
  159.7 0.9 convert_add_fusion
  160.7 3.6 %all-to-all-done.2 = bf16[8,8,2048]{2,1,0:T(8,128)(2,1)S(1)} async-done(((bf16[8,8,2048]{2,1,0:T(8,128)(2,1)}), bf16[8,8,2048]{2,1,0:T(8,128)(2,1)S(1)}, u32[]{:S(2)}, u32[]{:S(2)}) %all-to-all-start.2) | async-done | bytes 262176 | tf_op jit(solution)/shard_map/all_to_all | solution.py:231
  164.3 0.6 pad_maximum_fusion.1
  (6 shorter events, 0.2 us)
Async XLA Ops:
  7.2 60.5 %all-gather.3.cloned.1.call-start = ((), (), s32[]{:S(2)}) async-start(), calls=%async_computation.3 | async-start | bytes 2359296 | tf_op jit(solution)/shard_map/all_gather | solution.py:214
  7.9 13.4 %copy-start.9 = (bf16[4,4096]{1,0:T(4,128)(2,1)S(1)}, bf16[4,4096]{1,0:T(4,128)(2,1)}, u32[]{:S(2)}) copy-start(bf16[4,4096]{1,0:T(4,128)(2,1)} %param.8) | copy-start | bytes 98308
  7.9 13.4 %copy-start.10 = (bf16[4,4096]{1,0:T(4,128)(2,1)S(1)}, bf16[4,4096]{1,0:T(4,128)(2,1)}, u32[]{:S(2)}) copy-start(bf16[4,4096]{1,0:T(4,128)(2,1)} %param.7) | copy-start | bytes 98308
  9.8 67.1 %copy-start.8 = (bf16[64,64]{1,0:T(8,128)(2,1)S(1)}, bf16[64,64]{1,0:T(8,128)(2,1)}, u32[]{:S(2)}) copy-start(bf16[64,64]{1,0:T(8,128)(2,1)} %constant.19.clone.pick) | copy-start | bytes 24580
  9.8 57.9 %collective-permute-start.4 = (bf16[4096,256]{1,0:T(8,128)(2,1)S(1)}, bf16[4096,256]{1,0:T(8,128)(2,1)}, u32[]{:S(2)}, u32[]{:S(2)}) collective-permute-start(bf16[4096,256]{1,0:T(8,128)(2,1)S(1)} %broadcast_select_fusion), channel_id=1, source_target_pairs={{0,32},{32,0},{96,192},{192,96},{128,160},{160,128},{224,320},{320... | collective-permute-start | bytes 6291464 | tf_op jit(solution)/shard_map/ppermute | solution.py:44
  40.8 12.0 %collective-permute-start.2 = (bf16[64,4096]{1,0:T(8,128)(2,1)S(1)}, bf16[64,4096]{1,0:T(8,128)(2,1)S(1)}, u32[]{:S(2)}, u32[]{:S(2)}) collective-permute-start(bf16[64,4096]{1,0:T(8,128)(2,1)S(1)} %bitcast.5), channel_id=1, source_target_pairs={{0,3},{1,0},{2,1},{3,2},{4,7},{5,4},{6,5},{7,6},{8,11},{9,8},{10,9... | collective-permute-start | bytes 1572872 | tf_op jit(solution)/shard_map/ppermute | solution.py:35
  45.2 13.4 %collective-permute-start = (bf16[64,4096]{1,0:T(8,128)(2,1)S(1)}, bf16[64,4096]{1,0:T(8,128)(2,1)S(1)}, u32[]{:S(2)}, u32[]{:S(2)}) collective-permute-start(bf16[64,4096]{1,0:T(8,128)(2,1)S(1)} %bitcast.6), channel_id=1, source_target_pairs={{0,1},{1,2},{2,3},{3,0},{4,5},{5,6},{6,7},{7,4},{8,9},{9,10},{10,1... | collective-permute-start | bytes 1572872 | tf_op jit(solution)/shard_map/ppermute | solution.py:35
  52.8 8.7 %collective-permute-start.3 = (bf16[32,4096]{1,0:T(8,128)(2,1)S(1)}, bf16[32,4096]{1,0:T(8,128)(2,1)S(1)}, u32[]{:S(2)}, u32[]{:S(2)}) collective-permute-start(bf16[32,4096]{1,0:T(8,128)(2,1)S(1)} %slice.17), channel_id=1, source_target_pairs={{0,3},{1,0},{2,1},{3,2},{4,7},{5,4},{6,5},{7,6},{8,11},{9,8},{10,9... | collective-permute-start | bytes 786440 | tf_op jit(solution)/shard_map/ppermute | solution.py:35
  58.5 9.1 %copy-start.1 = (bf16[64,4096]{1,0:T(8,128)(2,1)}, bf16[64,4096]{1,0:T(8,128)(2,1)S(1)}, u32[]{:S(2)}) copy-start(bf16[64,4096]{1,0:T(8,128)(2,1)S(1)} %collective-permute-done.r1) | copy-start | bytes 1572868
  58.6 8.3 %collective-permute-start.1 = (bf16[32,4096]{1,0:T(8,128)(2,1)S(1)}, bf16[32,4096]{1,0:T(8,128)(2,1)S(1)}, u32[]{:S(2)}, u32[]{:S(2)}) collective-permute-start(bf16[32,4096]{1,0:T(8,128)(2,1)S(1)} %slice.16), channel_id=1, source_target_pairs={{0,1},{1,2},{2,3},{3,0},{4,5},{5,6},{6,7},{7,4},{8,9},{9,10},{10,1... | collective-permute-start | bytes 786440 | tf_op jit(solution)/shard_map/ppermute | solution.py:35
  66.9 0.7 copy-start.3
  67.6 6.4 %collective-permute-start.6 = (bf16[4,512,512]{2,1,0:T(8,128)(2,1)}, bf16[4,512,512]{2,1,0:T(8,128)(2,1)}, u32[]{:S(2)}, u32[]{:S(2)}) collective-permute-start(bf16[4,512,512]{2,1,0:T(8,128)(2,1)} %bitcast.8), channel_id=1, source_target_pairs={{0,64},{64,0},{1,65},{65,1},{2,66},{66,2},{3,67},{67,3},{4,68},{68... | collective-permute-start | bytes 6291464 | tf_op jit(solution)/shard_map/ppermute | solution.py:30
  69.6 7.3 %collective-permute-start.5 = (bf16[4096,256]{1,0:T(8,128)(2,1)}, bf16[4096,256]{1,0:T(8,128)(2,1)S(1)}, u32[]{:S(2)}, u32[]{:S(2)}) collective-permute-start(bf16[4096,256]{1,0:T(8,128)(2,1)} %collective-permute-done.4.mw.refs_4_.refs_5_), channel_id=1, source_target_pairs={{0,64},{64,0},{1,65},{65,1},{2,66},{66,2},{3,67},{67,3},{4,68},{68... | collective-permute-start | bytes 6291464 | tf_op jit(solution)/shard_map/ppermute | solution.py:30
  76.9 1.0 copy-start.2
  77.9 0.9 copy-start.4
  89.8 1.2 copy-start
  91.0 0.7 copy-start.5
  91.7 8.6 %copy-start.7 = (bf16[256,256]{1,0:T(8,128)(2,1)S(1)}, bf16[256,256]{1,0:T(8,128)(2,1)}, u32[]{:S(2)}) copy-start(bf16[256,256]{1,0:T(8,128)(2,1)} %constant.20.clone.pick) | copy-start | bytes 393220
  91.7 8.6 %copy-start.6 = (bf16[128,1024]{1,0:T(8,128)(2,1)S(1)}, bf16[128,1024]{1,0:T(8,128)(2,1)}, u32[]{:S(2)}) copy-start(bf16[128,1024]{1,0:T(8,128)(2,1)} %copy-done.5) | copy-start | bytes 786436
  91.7 34.7 %all-to-all-start.1 = ((bf16[4,3,128,512]{3,2,1,0:T(8,128)(2,1)}), bf16[4,3,128,512]{3,2,1,0:T(8,128)(2,1)}, u32[]{:S(2)}, u32[]{:S(2)}) async-start(bf16[4,3,128,512]{3,2,1,0:T(8,128)(2,1)} %copy-done), calls=%async_computation.1 | async-start | bytes 3145728 | tf_op jit(solution)/shard_map/all_to_all | solution.py:225
  106.3 9.1 %collective-permute-start.7 = (bf16[64,2048]{1,0:T(8,128)(2,1)S(1)}, bf16[64,2048]{1,0:T(8,128)(2,1)S(1)}, u32[]{:S(2)}, u32[]{:S(2)}) collective-permute-start(bf16[64,2048]{1,0:T(8,128)(2,1)S(1)} %get-tuple-element.28), channel_id=1, source_target_pairs={{0,3},{1,0},{2,1},{3,2},{4,7},{5,4},{6,5},{7,6},{8,11},{9,8},{10,9... | collective-permute-start | bytes 786440 | tf_op jit(solution)/shard_map/ppermute | solution.py:35
  108.2 10.7 %collective-permute-start.8 = (bf16[64,2048]{1,0:T(8,128)(2,1)S(1)}, bf16[64,2048]{1,0:T(8,128)(2,1)S(1)}, u32[]{:S(2)}, u32[]{:S(2)}) collective-permute-start(bf16[64,2048]{1,0:T(8,128)(2,1)S(1)} %get-tuple-element.29), channel_id=1, source_target_pairs={{0,2},{1,3},{2,0},{3,1},{4,6},{5,7},{6,4},{7,5},{8,10},{9,11},{10,... | collective-permute-start | bytes 786440 | tf_op jit(solution)/shard_map/ppermute | solution.py:35
  110.5 15.1 %collective-permute-start.9 = (bf16[64,2048]{1,0:T(8,128)(2,1)S(1)}, bf16[64,2048]{1,0:T(8,128)(2,1)S(1)}, u32[]{:S(2)}, u32[]{:S(2)}) collective-permute-start(bf16[64,2048]{1,0:T(8,128)(2,1)S(1)} %get-tuple-element.30), channel_id=1, source_target_pairs={{0,1},{1,2},{2,3},{3,0},{4,5},{5,6},{6,7},{7,4},{8,9},{9,10},{10,1... | collective-permute-start | bytes 786440 | tf_op jit(solution)/shard_map/ppermute | solution.py:35
  129.1 24.2 %collective-permute-start.10 = (bf16[256,512]{1,0:T(8,128)(2,1)S(1)}, bf16[256,512]{1,0:T(8,128)(2,1)S(1)}, u32[]{:S(2)}, u32[]{:S(2)}) collective-permute-start(bf16[256,512]{1,0:T(8,128)(2,1)S(1)} %get-tuple-element.35), channel_id=1, source_target_pairs={{0,64},{64,0},{1,65},{65,1},{2,66},{66,2},{3,67},{67,3},{4,68},{68... | collective-permute-start | bytes 786440 | tf_op jit(solution)/shard_map/ppermute | solution.py:30
  132.9 21.0 %collective-permute-start.11 = (bf16[256,512]{1,0:T(8,128)(2,1)S(1)}, bf16[256,512]{1,0:T(8,128)(2,1)S(1)}, u32[]{:S(2)}, u32[]{:S(2)}) collective-permute-start(bf16[256,512]{1,0:T(8,128)(2,1)S(1)} %get-tuple-element.36), channel_id=1, source_target_pairs={{0,32},{32,0},{1,33},{33,1},{2,34},{34,2},{3,35},{35,3},{4,36},{36... | collective-permute-start | bytes 786440 | tf_op jit(solution)/shard_map/ppermute | solution.py:30
  147.3 12.5 %collective-permute-start.12 = (bf16[256,512]{1,0:T(8,128)(2,1)S(1)}, bf16[256,512]{1,0:T(8,128)(2,1)S(1)}, u32[]{:S(2)}, u32[]{:S(2)}) collective-permute-start(bf16[256,512]{1,0:T(8,128)(2,1)S(1)} %get-tuple-element.37), channel_id=1, source_target_pairs={{0,96},{96,0},{32,64},{64,32},{1,97},{97,1},{33,65},{65,33},{2,98}... | collective-permute-start | bytes 786440 | tf_op jit(solution)/shard_map/ppermute | solution.py:240
  149.2 15.0 %all-to-all-start.2 = ((bf16[8,8,2048]{2,1,0:T(8,128)(2,1)}), bf16[8,8,2048]{2,1,0:T(8,128)(2,1)S(1)}, u32[]{:S(2)}, u32[]{:S(2)}) async-start(bf16[8,8,2048]{2,1,0:T(8,128)(2,1)} %bitcast.4), calls=%async_computation.2 | async-start | bytes 524288 | tf_op jit(solution)/shard_map/all_to_all | solution.py:231
Sparse Core Ops, SparseCore 0:
  10.1 54.1 all-gather.2

commit v12 on v9

--- a/solution.py
+++ b/solution.py
@@ -213,20 +213,20 @@
     )(where, merge(), dd, gw, gw, uw, uw, mw, mw, ow, ow)
 
 
-def grads_body(hn, hf, cn, cf, keep, send):
+def grads_body(where, h, cn, cf, keep, send):
     total = None
     for z in range(NZ):
-        part = contract(hn[z], cn[z, 0], 0, 0) + contract(hf[z], cf[z], 0, 0)
+        part = contract(h[z, 0], cn[z, 0], 0, 0) + contract(h[z, 1], cf[z], 0, 0)
         total = part if total is None else total + part
     keep[...] = total[:HID]
     send[...] = total[HID:].astype(BF16)
 
 
-def grads(hid_near, hid_far, cot_near, cot_far):
+def grads(where, hidden, cot_near, cot_far):
     vmem = pl.BlockSpec(memory_space=pltpu.MemorySpace.VMEM)
     return pl.pallas_call(
         grads_body,
-        in_specs=[vmem] * 4,
+        in_specs=[pl.BlockSpec(memory_space=pltpu.MemorySpace.SMEM)] + [vmem] * 3,
         out_specs=[vmem] * 2,
         out_shape=[
             jax.ShapeDtypeStruct((HID, FEATS), F32),
@@ -234,7 +234,7 @@
         ],
         compiler_params=pltpu.CompilerParams(vmem_limit_bytes=32 * 2**20),
         name="grads",
-    )(hid_near, hid_far, cot_near, cot_far)
+    )(where, hidden, cot_near, cot_far)
 
 
 def selection(shape, order):
@@ -271,16 +271,15 @@
     tok, mine, down_near = lax.optimization_barrier((tok, mine, down_near))
     other, down_far = swap(mine, "c"), swap(down_near, "c")
     hidden, factors = gates(where, tok, gate_weight, up_weight, mine, other)
+    hidden = lax.all_gather(jnp.stack([hidden, swap(hidden, "c")]), "zh", axis=0)
     dd = down(where, cot, down_near, down_far, factors)
 
     parts = term(where, dd, gate_weight, up_weight, mine, other)
-    parts, hidden = lax.optimization_barrier((parts, hidden))
     parts = lax.all_to_all(parts.reshape(NX * NY, 2 * ROWS, D // 2), ("x", "y"), 0, 0)
     total = jnp.sum(parts.astype(F32), axis=0).astype(BF16)
     input_grad = jnp.concatenate([total[:ROWS], total[ROWS:]], axis=1)
 
-    hid_near = lax.all_gather(hidden, "zh", axis=0)
-    keep, send = grads(hid_near, swap(hid_near, "c"), cot_near, cot_far)
+    keep, send = grads(where, hidden, cot_near, cot_far)
     down_grad = keep + swap(send, "zl").astype(F32)
     return (input_grad, down_grad)
 

time: 160 us -> 156 us (0.975)
  blocking collectives: 39.7 us -> 19.4 us
  waiting for transfers between devices: 18.6 us -> 33.5 us
  local copies, waits for them, and re-layouts: 0.14 us -> 3.19 us
  starting transfers between devices: 56.3 us -> 53.6 us
    all_gather x1 -> x0, blocking collectives: 20.3 us -> none  [on_device(): hid_near = lax.all_gather(hidden, 'zh', axis=0)]
    all_gather x0 -> x1, waiting for transfers between devices: none -> 14.4 us  [on_device(): lax.all_gather(jnp.stack([hidden, swap(hidden, 'c')]), 'zh', axis=0)]
    unnamed x8 -> x14, local copies, waits for them, and re-layouts: 0.02 us -> 3.06 us
    ppermute x5, starting transfers between devices: 16.7 us -> 14 us  [swap(): return lax.ppermute(value, axis, [(0, 1), (1, 0)])]
  transfers between devices with their start and end apart: 13 -> 14, of which waited for: 6 -> 8; matrix products, arithmetic and copies ran while one was open for 3% -> 3% of each run, Pallas kernels for 16% -> 17%
where the time goes in v12:
time: 156 us; the launch traced here: 155 us
  starting transfers between devices  53.6 us (34%)
  waiting for transfers between devices  33.5 us (21%)
  Pallas kernels  25.7 us (16%)
  blocking collectives  19.4 us (12%)
  between operations  14.3 us (9%)
  other arithmetic  5.71 us (4%)
  local copies, waits for them, and re-layouts  3.19 us (2%)
    all_to_all x1, blocking collectives, spread(): lax.all_to_all(jnp.broadcast_to(block[None], (n, *block.shape)), axis, 0, 0)  19.4 us
    all_gather x1, waiting for transfers between devices, on_device(): lax.all_gather(jnp.stack([hidden, swap(hidden, 'c')]), 'zh', axis=0)  14.4 us
    ppermute x5, starting transfers between devices, swap(): return lax.ppermute(value, axis, [(0, 1), (1, 0)])  14 us
    ppermute x4, starting transfers between devices, shift(): return lax.ppermute(value, axis, [(i, (i + k) % n) for i in range(n)])  13 us
    ppermute x1, starting transfers between devices, neighbours(): return lax.ppermute(value, ('zh', 'c', 'zl'), pairs)  11.6 us
    ppermute x4, waiting for transfers between devices, shift(): return lax.ppermute(value, axis, [(i, (i + k) % n) for i in range(n)])  10 us
    ppermute x5, waiting for transfers between devices, swap(): return lax.ppermute(value, axis, [(0, 1), (1, 0)])  8.28 us
    all_to_all x1, starting transfers between devices, on_device(): cot_near = lax.all_to_all(cot, 'zh', 0, 0)  8.06 us
  transfers between devices with their start and end apart: 14, of which 8 were waited for; matrix products, arithmetic and copies ran while one was open for 3% of the time, Pallas kernels for 17%

profile of v12, /device:TPU:1, one launch (start us, length us, event | category | flops | bytes accessed | tf_op | source)
XLA Modules:
  0.0 155.4 jit_solution(8125724404016655102)
XLA Ops:
  7.2 0.0 all-gather.5.cloned.1.call-start
  7.2 0.7 all-gather.5.cloned.1.call-update
  7.9 0.0 copy-start.5
  7.9 0.0 copy-start.6
  7.9 3.2 %broadcast_select_fusion = bf16[4096,256]{1,0:T(8,128)(2,1)} fusion(bf16[4096,256]{1,0:T(8,128)(2,1)} %refs_1_.1, bf16[4096,256]{1,0:T(8,128)(2,1)} %refs_3_.1, pred[]{:T(512)S(6)} %eq.3), kind=kLoop, calls=%fused_computation | loop fusion | flops 1048576 | bytes 6291457 | tf_op jit(solution)/shard_map/jit(_where)/select_n | solution.py:258
  11.1 0.0 copy-start.4
  11.1 11.6 %collective-permute-start.4 = (bf16[4096,256]{1,0:T(8,128)(2,1)}, bf16[4096,256]{1,0:T(8,128)(2,1)}, u32[]{:S(2)}, u32[]{:S(2)}) collective-permute-start(bf16[4096,256]{1,0:T(8,128)(2,1)} %broadcast_select_fusion), channel_id=1, source_target_pairs={{0,32},{32,0},{96,192},{192,96},{128,160},{160,128},{224,320},{320... | collective-permute-start | bytes 6291464 | tf_op jit(solution)/shard_map/ppermute | solution.py:44
  22.7 0.0 copy-done.5
  22.7 0.0 copy-done.6
  22.8 19.4 %all_to_all.15 = bf16[8,8,4096]{2,1,0:T(8,128)(2,1)S(1)} all-to-all(bf16[8,8,4096]{2,1,0:T(8,128)(2,1)S(1)} %broadcast_in_dim.2), channel_id=1, replica_groups=mesh['zh'=4,'c'=2,'zl'=2,'y'=8,'x'=4] {'y'}, dimensions={0} | all-to-all | bytes 1048576 | tf_op jit(solution)/shard_map/all_to_all | solution.py:251
  42.2 3.1 %collective-permute-start = (bf16[64,4096]{1,0:T(8,128)(2,1)S(1)}, bf16[64,4096]{1,0:T(8,128)(2,1)S(1)}, u32[]{:S(2)}, u32[]{:S(2)}) collective-permute-start(bf16[64,4096]{1,0:T(8,128)(2,1)S(1)} %bitcast.13), channel_id=1, source_target_pairs={{0,1},{1,2},{2,3},{3,0},{4,5},{5,6},{6,7},{7,4},{8,9},{9,10},{10,1... | collective-permute-start | bytes 1572872 | tf_op jit(solution)/shard_map/ppermute | solution.py:35
  45.4 3.4 %collective-permute-start.2 = (bf16[64,4096]{1,0:T(8,128)(2,1)S(1)}, bf16[64,4096]{1,0:T(8,128)(2,1)S(1)}, u32[]{:S(2)}, u32[]{:S(2)}) collective-permute-start(bf16[64,4096]{1,0:T(8,128)(2,1)S(1)} %bitcast.14), channel_id=1, source_target_pairs={{0,3},{1,0},{2,1},{3,2},{4,7},{5,4},{6,5},{7,6},{8,11},{9,8},{10,9... | collective-permute-start | bytes 1572872 | tf_op jit(solution)/shard_map/ppermute | solution.py:35
  48.7 6.6 %collective-permute-done.r1 = bf16[64,4096]{1,0:T(8,128)(2,1)S(1)} collective-permute-done((bf16[64,4096]{1,0:T(8,128)(2,1)S(1)}, bf16[64,4096]{1,0:T(8,128)(2,1)S(1)}, u32[]{:S(2)}, u32[]{:S(2)}) %collective-permute-start) | collective-permute-done | bytes 524320 | tf_op jit(solution)/shard_map/ppermute | solution.py:35
  55.3 1.9 %collective-permute-start.1 = (bf16[32,4096]{1,0:T(8,128)(2,1)S(1)}, bf16[32,4096]{1,0:T(8,128)(2,1)S(1)}, u32[]{:S(2)}, u32[]{:S(2)}) collective-permute-start(bf16[32,4096]{1,0:T(8,128)(2,1)S(1)} %slice.20), channel_id=1, source_target_pairs={{0,1},{1,2},{2,3},{3,0},{4,5},{5,6},{6,7},{7,4},{8,9},{9,10},{10,1... | collective-permute-start | bytes 786440 | tf_op jit(solution)/shard_map/ppermute | solution.py:35
  57.3 0.2 collective-permute-done.2.r3
  57.5 4.6 %collective-permute-start.3 = (bf16[32,4096]{1,0:T(8,128)(2,1)S(1)}, bf16[32,4096]{1,0:T(8,128)(2,1)S(1)}, u32[]{:S(2)}, u32[]{:S(2)}) collective-permute-start(bf16[32,4096]{1,0:T(8,128)(2,1)S(1)} %slice.21), channel_id=1, source_target_pairs={{0,3},{1,0},{2,1},{3,2},{4,7},{5,4},{6,5},{7,6},{8,11},{9,8},{10,9... | collective-permute-start | bytes 786440 | tf_op jit(solution)/shard_map/ppermute | solution.py:35
  62.1 0.1 pad_add_fusion.where
  62.2 1.7 %collective-permute-done.1.r2a = bf16[32,4096]{1,0:T(8,128)(2,1)S(1)} collective-permute-done((bf16[32,4096]{1,0:T(8,128)(2,1)S(1)}, bf16[32,4096]{1,0:T(8,128)(2,1)S(1)}, u32[]{:S(2)}, u32[]{:S(2)}) %collective-permute-start.1) | collective-permute-done | bytes 262176 | tf_op jit(solution)/shard_map/ppermute | solution.py:35
  63.9 1.5 collective-permute-done.3.r2b
  65.4 0.0 copy-done.4
  65.4 4.8 %split.1 = (bf16[128,4096]{1,0:T(8,128)(2,1)}, bf16[4,2,128,512]{3,2,1,0:T(8,128)(2,1)}) custom-call(s32[3]{0:T(128)S(1)} %pad_add_fusion.where, bf16[64,64]{1,0:T(8,128)(2,1)S(1)} %copy-done.4, bf16[64,4096]{1,0:T(8,128)(2,1)S(1)} %bitcast.15, bf16[64,4096]{1,0:T(8,128)(2,1)S(1)} %collective-permute-done.r1, ...), custom_call_target="tpu_custom_call" | custom-call | tf_op jit(solution)/shard_map/split/pallas_call | solution.py:59
  70.2 0.0 collective-permute-done.4.mw.refs_4_.refs_5_
  70.2 0.0 all-gather.5.cloned.1.call-done
  70.2 1.9 %collective-permute-start.6 = (bf16[4096,256]{1,0:T(8,128)(2,1)}, bf16[4096,256]{1,0:T(8,128)(2,1)S(1)}, u32[]{:S(2)}, u32[]{:S(2)}) collective-permute-start(bf16[4096,256]{1,0:T(8,128)(2,1)} %collective-permute-done.4.mw.refs_4_.refs_5_), channel_id=1, source_target_pairs={{0,64},{64,0},{1,65},{65,1},{2,66},{66,2},{3,67},{67,3},{4,68},{68... | collective-permute-start | bytes 6291464 | tf_op jit(solution)/shard_map/ppermute | solution.py:30
  72.1 2.4 %collective-permute-start.5 = (bf16[4,512,512]{2,1,0:T(8,128)(2,1)}, bf16[4,512,512]{2,1,0:T(8,128)(2,1)}, u32[]{:S(2)}, u32[]{:S(2)}) collective-permute-start(bf16[4,512,512]{2,1,0:T(8,128)(2,1)} %bitcast.19), channel_id=1, source_target_pairs={{0,64},{64,0},{1,65},{65,1},{2,66},{66,2},{3,67},{67,3},{4,68},{68... | collective-permute-start | bytes 6291464 | tf_op jit(solution)/shard_map/ppermute | solution.py:30
  74.5 8.1 %all-to-all-start.2 = ((bf16[4,2,128,512]{3,2,1,0:T(8,128)(2,1)}), bf16[4,2,128,512]{3,2,1,0:T(8,128)(2,1)S(1)}, u32[]{:S(2)}, u32[]{:S(2)}) async-start(bf16[4,2,128,512]{3,2,1,0:T(8,128)(2,1)} %get-tuple-element.14.cot), calls=%async_computation.2 | async-start | bytes 2097152 | tf_op jit(solution)/shard_map/all_to_all | solution.py:269
  82.6 0.0 all-gather.7.cloned.1.call-start
  82.6 0.0 collective-permute-done.6.ow.refs_6_.refs_7_
  82.6 7.2 %gates.1 = (bf16[128,512]{1,0:T(8,128)(2,1)S(1)}, f32[128,1024]{1,0:T(8,128)S(1)}) custom-call(s32[3]{0:T(128)S(1)} %pad_add_fusion.where, bf16[128,4096]{1,0:T(8,128)(2,1)} %get-tuple-element.18.tok, bf16[4096,256]{1,0:T(8,128)(2,1)} %refs_1_.1, bf16[4096,256]{1,0:T(8,128)(2,1)} %refs_3_.1, bf16[4096,256]{1,0:T(8,128)(2,1)} %collective-permute-done.4.mw.refs_4_.refs_5_, ...), custom_call_target="tpu_custom_call" | custom-call | tf_op jit(solution)/shard_map/gates/pallas_call | solution.py:123
  89.8 0.0 copy-start.1
  89.8 0.8 copy-done.1
  90.6 2.7 %collective-permute-start.7 = (bf16[128,512]{1,0:T(8,128)(2,1)S(1)}, bf16[128,512]{1,0:T(8,128)(2,1)S(1)}, u32[]{:S(2)}, u32[]{:S(2)}) collective-permute-start(bf16[128,512]{1,0:T(8,128)(2,1)S(1)} %get-tuple-element.21), channel_id=1, source_target_pairs={{0,64},{64,0},{1,65},{65,1},{2,66},{66,2},{3,67},{67,3},{4,68},{68... | collective-permute-start | bytes 393224 | tf_op jit(solution)/shard_map/ppermute | solution.py:30
  93.3 1.0 collective-permute-done.7
  94.2 0.8 pad_maximum_fusion
  95.0 0.0 all-gather.7.cloned.1.call-update
  95.0 0.0 collective-permute-done.5.df
  95.0 0.0 copy-start.2
  95.0 1.0 copy-done.2
  96.1 0.0 copy-start.3
  96.1 4.7 %down.1.dd = bf16[128,1024]{1,0:T(8,128)(2,1)S(1)} custom-call(s32[3]{0:T(128)S(1)} %pad_add_fusion.where, bf16[4,2,128,512]{3,2,1,0:T(8,128)(2,1)} %get-tuple-element.14.cot, bf16[4,512,512]{2,1,0:T(8,128)(2,1)} %bitcast.20, bf16[4,512,512]{2,1,0:T(8,128)(2,1)} %collective-permute-done.5.df, f32[128,1024]{1,0:T(8,128)S(1)} %copy-done.2), custom_call_target="tpu_custom_call" | custom-call | tf_op jit(solution)/shard_map/down/pallas_call | solution.py:165
  100.8 0.0 copy-done.3
  100.8 7.2 %term.1 = bf16[4,64,2048]{2,1,0:T(8,128)(2,1)} custom-call(s32[3]{0:T(128)S(1)} %pad_add_fusion.where, bf16[256,256]{1,0:T(8,128)(2,1)S(1)} %copy-done.3, bf16[128,1024]{1,0:T(8,128)(2,1)S(1)} %down.1.dd, bf16[4096,256]{1,0:T(8,128)(2,1)} %refs_1_.1, bf16[4096,256]{1,0:T(8,128)(2,1)} %refs_1_.1, bf16[4096,256]{1,0:T(8,128)(2,1)} %refs_3_.1, ...), custom_call_target="tpu_custom_call" | custom-call | tf_op jit(solution)/shard_map/term/pallas_call | solution.py:198
  108.1 0.0 all-to-all-done.2.cn
  108.1 6.9 %all-to-all-start.1 = ((bf16[32,8,2048]{2,1,0:T(8,128)(2,1)}), bf16[32,8,2048]{2,1,0:T(8,128)(2,1)S(1)}, u32[]{:S(2)}, u32[]{:S(2)}) async-start(bf16[32,8,2048]{2,1,0:T(8,128)(2,1)} %bitcast.18), calls=%async_computation.1 | async-start | bytes 2097152 | tf_op jit(solution)/shard_map/all_to_all | solution.py:278
  115.1 2.6 %collective-permute-start.8 = (bf16[4,128,512]{2,1,0:T(8,128)(2,1)S(1)}, bf16[4,128,512]{2,1,0:T(8,128)(2,1)S(1)}, u32[]{:S(2)}, u32[]{:S(2)}) collective-permute-start(bf16[4,128,512]{2,1,0:T(8,128)(2,1)S(1)} %slice_bitcast_fusion), channel_id=1, source_target_pairs={{0,64},{64,0},{1,65},{65,1},{2,66},{66,2},{3,67},{67,3},{4,68},{68... | collective-permute-start | bytes 1572872 | tf_op jit(solution)/shard_map/ppermute | solution.py:30
  117.6 1.5 collective-permute-done.8.cf
  119.2 14.4 %all-gather.7.cloned.1.call-done = bf16[8,128,512]{2,1,0:T(8,128)(2,1)} async-done(((bf16[2,128,512]{2,1,0:T(8,128)(2,1)}), bf16[8,128,512]{2,1,0:T(8,128)(2,1)}) %all-gather.7.cloned.1.call-update) | async-done | bytes 1048592 | tf_op jit(solution)/shard_map/all_gather | solution.py:274
  133.6 0.0 copy-start
  133.6 1.2 copy-done
  134.8 1.8 %grads.1 = (f32[256,512]{1,0:T(8,128)S(1)}, bf16[256,512]{1,0:T(8,128)(2,1)S(1)}) custom-call(s32[3]{0:T(128)S(1)} %pad_add_fusion.where, bf16[4,2,128,512]{3,2,1,0:T(8,128)(2,1)S(1)} %bitcast.16, bf16[4,2,128,512]{3,2,1,0:T(8,128)(2,1)S(1)} %all-to-all-done.2.cn, bf16[4,128,512]{2,1,0:T(8,128)(2,1)S(1)} %collective-permute-done.8.cf), custom_call_target="tpu_custom_call" | custom-call | tf_op jit(solution)/shard_map/grads/pallas_call | solution.py:227
  136.6 4.4 %collective-permute-start.9 = (bf16[256,512]{1,0:T(8,128)(2,1)S(1)}, bf16[256,512]{1,0:T(8,128)(2,1)S(1)}, u32[]{:S(2)}, u32[]{:S(2)}) collective-permute-start(bf16[256,512]{1,0:T(8,128)(2,1)S(1)} %get-tuple-element.23), channel_id=1, source_target_pairs={{0,32},{32,0},{1,33},{33,1},{2,34},{34,2},{3,35},{35,3},{4,36},{36... | collective-permute-start | bytes 786440 | tf_op jit(solution)/shard_map/ppermute | solution.py:30
  141.1 5.8 %collective-permute-done.9 = bf16[256,512]{1,0:T(8,128)(2,1)S(1)} collective-permute-done((bf16[256,512]{1,0:T(8,128)(2,1)S(1)}, bf16[256,512]{1,0:T(8,128)(2,1)S(1)}, u32[]{:S(2)}, u32[]{:S(2)}) %collective-permute-start.9) | collective-permute-done | bytes 262176 | tf_op jit(solution)/shard_map/ppermute | solution.py:30
  146.9 0.9 convert_add_fusion
  147.7 0.0 all-to-all-done.1
  147.7 0.2 reduce_sum.12
  147.9 0.6 pad_maximum_fusion.2
  (6 shorter events, 0.2 us)
Async XLA Ops:
  7.2 63.1 %all-gather.5.cloned.1.call-start = ((), (), s32[]{:S(2)}) async-start(), calls=%async_computation.3 | async-start | bytes 2359296 | tf_op jit(solution)/shard_map/all_gather | solution.py:261
  7.9 14.8 %copy-start.5 = (bf16[4,4096]{1,0:T(4,128)(2,1)S(1)}, bf16[4,4096]{1,0:T(4,128)(2,1)}, u32[]{:S(2)}) copy-start(bf16[4,4096]{1,0:T(4,128)(2,1)} %param.8) | copy-start | bytes 98308
  7.9 14.8 %copy-start.6 = (bf16[4,4096]{1,0:T(4,128)(2,1)S(1)}, bf16[4,4096]{1,0:T(4,128)(2,1)}, u32[]{:S(2)}) copy-start(bf16[4,4096]{1,0:T(4,128)(2,1)} %param.7) | copy-start | bytes 98308
  11.1 54.3 %copy-start.4 = (bf16[64,64]{1,0:T(8,128)(2,1)S(1)}, bf16[64,64]{1,0:T(8,128)(2,1)}, u32[]{:S(2)}) copy-start(bf16[64,64]{1,0:T(8,128)(2,1)} %constant.23.clone.pick) | copy-start | bytes 24580
  11.1 59.1 %collective-permute-start.4 = (bf16[4096,256]{1,0:T(8,128)(2,1)}, bf16[4096,256]{1,0:T(8,128)(2,1)}, u32[]{:S(2)}, u32[]{:S(2)}) collective-permute-start(bf16[4096,256]{1,0:T(8,128)(2,1)} %broadcast_select_fusion), channel_id=1, source_target_pairs={{0,32},{32,0},{96,192},{192,96},{128,160},{160,128},{224,320},{320... | collective-permute-start | bytes 6291464 | tf_op jit(solution)/shard_map/ppermute | solution.py:44
  42.2 13.1 %collective-permute-start = (bf16[64,4096]{1,0:T(8,128)(2,1)S(1)}, bf16[64,4096]{1,0:T(8,128)(2,1)S(1)}, u32[]{:S(2)}, u32[]{:S(2)}) collective-permute-start(bf16[64,4096]{1,0:T(8,128)(2,1)S(1)} %bitcast.13), channel_id=1, source_target_pairs={{0,1},{1,2},{2,3},{3,0},{4,5},{5,6},{6,7},{7,4},{8,9},{9,10},{10,1... | collective-permute-start | bytes 1572872 | tf_op jit(solution)/shard_map/ppermute | solution.py:35
  45.4 12.2 %collective-permute-start.2 = (bf16[64,4096]{1,0:T(8,128)(2,1)S(1)}, bf16[64,4096]{1,0:T(8,128)(2,1)S(1)}, u32[]{:S(2)}, u32[]{:S(2)}) collective-permute-start(bf16[64,4096]{1,0:T(8,128)(2,1)S(1)} %bitcast.14), channel_id=1, source_target_pairs={{0,3},{1,0},{2,1},{3,2},{4,7},{5,4},{6,5},{7,6},{8,11},{9,8},{10,9... | collective-permute-start | bytes 1572872 | tf_op jit(solution)/shard_map/ppermute | solution.py:35
  55.3 8.6 %collective-permute-start.1 = (bf16[32,4096]{1,0:T(8,128)(2,1)S(1)}, bf16[32,4096]{1,0:T(8,128)(2,1)S(1)}, u32[]{:S(2)}, u32[]{:S(2)}) collective-permute-start(bf16[32,4096]{1,0:T(8,128)(2,1)S(1)} %slice.20), channel_id=1, source_target_pairs={{0,1},{1,2},{2,3},{3,0},{4,5},{5,6},{6,7},{7,4},{8,9},{9,10},{10,1... | collective-permute-start | bytes 786440 | tf_op jit(solution)/shard_map/ppermute | solution.py:35
  57.5 7.9 %collective-permute-start.3 = (bf16[32,4096]{1,0:T(8,128)(2,1)S(1)}, bf16[32,4096]{1,0:T(8,128)(2,1)S(1)}, u32[]{:S(2)}, u32[]{:S(2)}) collective-permute-start(bf16[32,4096]{1,0:T(8,128)(2,1)S(1)} %slice.21), channel_id=1, source_target_pairs={{0,3},{1,0},{2,1},{3,2},{4,7},{5,4},{6,5},{7,6},{8,11},{9,8},{10,9... | collective-permute-start | bytes 786440 | tf_op jit(solution)/shard_map/ppermute | solution.py:35
  70.2 12.4 %collective-permute-start.6 = (bf16[4096,256]{1,0:T(8,128)(2,1)}, bf16[4096,256]{1,0:T(8,128)(2,1)S(1)}, u32[]{:S(2)}, u32[]{:S(2)}) collective-permute-start(bf16[4096,256]{1,0:T(8,128)(2,1)} %collective-permute-done.4.mw.refs_4_.refs_5_), channel_id=1, source_target_pairs={{0,64},{64,0},{1,65},{65,1},{2,66},{66,2},{3,67},{67,3},{4,68},{68... | collective-permute-start | bytes 6291464 | tf_op jit(solution)/shard_map/ppermute | solution.py:30
  72.1 22.9 %collective-permute-start.5 = (bf16[4,512,512]{2,1,0:T(8,128)(2,1)}, bf16[4,512,512]{2,1,0:T(8,128)(2,1)}, u32[]{:S(2)}, u32[]{:S(2)}) collective-permute-start(bf16[4,512,512]{2,1,0:T(8,128)(2,1)} %bitcast.19), channel_id=1, source_target_pairs={{0,64},{64,0},{1,65},{65,1},{2,66},{66,2},{3,67},{67,3},{4,68},{68... | collective-permute-start | bytes 6291464 | tf_op jit(solution)/shard_map/ppermute | solution.py:30
  74.5 33.5 %all-to-all-start.2 = ((bf16[4,2,128,512]{3,2,1,0:T(8,128)(2,1)}), bf16[4,2,128,512]{3,2,1,0:T(8,128)(2,1)S(1)}, u32[]{:S(2)}, u32[]{:S(2)}) async-start(bf16[4,2,128,512]{3,2,1,0:T(8,128)(2,1)} %get-tuple-element.14.cot), calls=%async_computation.2 | async-start | bytes 2097152 | tf_op jit(solution)/shard_map/all_to_all | solution.py:269
  82.6 51.0 %all-gather.7.cloned.1.call-start = ((), (), s32[]{:S(2)}) async-start(), calls=%async_computation.4 | async-start | bytes 1310720 | tf_op jit(solution)/shard_map/all_gather | solution.py:274
  89.8 0.8 copy-start.1
  90.6 3.6 %collective-permute-start.7 = (bf16[128,512]{1,0:T(8,128)(2,1)S(1)}, bf16[128,512]{1,0:T(8,128)(2,1)S(1)}, u32[]{:S(2)}, u32[]{:S(2)}) collective-permute-start(bf16[128,512]{1,0:T(8,128)(2,1)S(1)} %get-tuple-element.21), channel_id=1, source_target_pairs={{0,64},{64,0},{1,65},{65,1},{2,66},{66,2},{3,67},{67,3},{4,68},{68... | collective-permute-start | bytes 393224 | tf_op jit(solution)/shard_map/ppermute | solution.py:30
  95.0 1.0 copy-start.2
  96.1 4.8 %copy-start.3 = (bf16[256,256]{1,0:T(8,128)(2,1)S(1)}, bf16[256,256]{1,0:T(8,128)(2,1)}, u32[]{:S(2)}) copy-start(bf16[256,256]{1,0:T(8,128)(2,1)} %constant.24.clone.pick) | copy-start | bytes 393220
  108.1 39.6 %all-to-all-start.1 = ((bf16[32,8,2048]{2,1,0:T(8,128)(2,1)}), bf16[32,8,2048]{2,1,0:T(8,128)(2,1)S(1)}, u32[]{:S(2)}, u32[]{:S(2)}) async-start(bf16[32,8,2048]{2,1,0:T(8,128)(2,1)} %bitcast.18), calls=%async_computation.1 | async-start | bytes 2097152 | tf_op jit(solution)/shard_map/all_to_all | solution.py:278
  115.1 4.1 %collective-permute-start.8 = (bf16[4,128,512]{2,1,0:T(8,128)(2,1)S(1)}, bf16[4,128,512]{2,1,0:T(8,128)(2,1)S(1)}, u32[]{:S(2)}, u32[]{:S(2)}) collective-permute-start(bf16[4,128,512]{2,1,0:T(8,128)(2,1)S(1)} %slice_bitcast_fusion), channel_id=1, source_target_pairs={{0,64},{64,0},{1,65},{65,1},{2,66},{66,2},{3,67},{67,3},{4,68},{68... | collective-permute-start | bytes 1572872 | tf_op jit(solution)/shard_map/ppermute | solution.py:30
  133.6 1.2 copy-start
  136.6 10.2 %collective-permute-start.9 = (bf16[256,512]{1,0:T(8,128)(2,1)S(1)}, bf16[256,512]{1,0:T(8,128)(2,1)S(1)}, u32[]{:S(2)}, u32[]{:S(2)}) collective-permute-start(bf16[256,512]{1,0:T(8,128)(2,1)S(1)} %get-tuple-element.23), channel_id=1, source_target_pairs={{0,32},{32,0},{1,33},{33,1},{2,34},{34,2},{3,35},{35,3},{4,36},{36... | collective-permute-start | bytes 786440 | tf_op jit(solution)/shard_map/ppermute | solution.py:30
Sparse Core Ops, SparseCore 0:
  10.1 54.1 all-gather.4
  95.1 38.4 all-gather.6

commit v13 on v12

--- a/solution.py
+++ b/solution.py
@@ -214,9 +214,9 @@
 
 
 def grads_body(where, h, cn, cf, keep, send):
-    total = None
+    total, core = None, where[0]
     for z in range(NZ):
-        part = contract(h[z, 0], cn[z, 0], 0, 0) + contract(h[z, 1], cf[z], 0, 0)
+        part = contract(h[z, core], cn[z, 0], 0, 0) + contract(h[z, 1 - core], cf[z], 0, 0)
         total = part if total is None else total + part
     keep[...] = total[:HID]
     send[...] = total[HID:].astype(BF16)
@@ -267,20 +267,20 @@
 
     tok, cot = split(where, pieces)
     cot_near = lax.all_to_all(cot, "zh", 0, 0)
-    cot_far = swap(cot_near[:, 1], "c")
     tok, mine, down_near = lax.optimization_barrier((tok, mine, down_near))
     other, down_far = swap(mine, "c"), swap(down_near, "c")
     hidden, factors = gates(where, tok, gate_weight, up_weight, mine, other)
-    hidden = lax.all_gather(jnp.stack([hidden, swap(hidden, "c")]), "zh", axis=0)
+    hidden = lax.all_gather(hidden, DP, axis=0).reshape(NZ, 2, HALF, 2 * HID)
     dd = down(where, cot, down_near, down_far, factors)
 
     parts = term(where, dd, gate_weight, up_weight, mine, other)
     parts = lax.all_to_all(parts.reshape(NX * NY, 2 * ROWS, D // 2), ("x", "y"), 0, 0)
+    hidden, cot_near = lax.optimization_barrier((hidden, cot_near))
+    keep, send = grads(where, hidden, cot_near, swap(cot_near[:, 1], "c"))
+    parts, received = lax.optimization_barrier((parts, swap(send, "zl")))
     total = jnp.sum(parts.astype(F32), axis=0).astype(BF16)
     input_grad = jnp.concatenate([total[:ROWS], total[ROWS:]], axis=1)
-
-    keep, send = grads(where, hidden, cot_near, cot_far)
-    down_grad = keep + swap(send, "zl").astype(F32)
+    down_grad = keep + received.astype(F32)
     return (input_grad, down_grad)
 
 

time: 156 us -> 154 us (0.987)
  starting transfers between devices: 53.6 us -> 48.1 us
  waiting for transfers between devices: 33.5 us -> 35.9 us
    ppermute x5 -> x4, starting transfers between devices: 14 us -> 8.39 us  [swap(): return lax.ppermute(value, axis, [(0, 1), (1, 0)])]
    ppermute x5 -> x4, waiting for transfers between devices: 8.28 us -> 9.26 us  [swap(): return lax.ppermute(value, axis, [(0, 1), (1, 0)])]
  transfers between devices with their start and end apart: 14 -> 13, of which waited for: 8 -> 7; matrix products, arithmetic and copies ran while one was open for 3% -> 2% of each run, Pallas kernels for 17% -> 17%
where the time goes in v13:
time: 154 us; the launch traced here: 152 us
  starting transfers between devices  48.1 us (31%)
  waiting for transfers between devices  35.9 us (23%)
  Pallas kernels  26.3 us (17%)
  blocking collectives  19.4 us (13%)
  between operations  14.2 us (9%)
  other arithmetic  4.95 us (3%)
  local copies, waits for them, and re-layouts  3.19 us (2%)
    all_to_all x1, blocking collectives, spread(): lax.all_to_all(jnp.broadcast_to(block[None], (n, *block.shape)), axis, 0, 0)  19.4 us
    all_gather x1, waiting for transfers between devices, on_device(): hidden = lax.all_gather(hidden, DP, axis=0).reshape(NZ, 2, HALF, 2 * HID)  15.9 us
    ppermute x4, starting transfers between devices, shift(): return lax.ppermute(value, axis, [(i, (i + k) % n) for i in range(n)])  13 us
    ppermute x1, starting transfers between devices, neighbours(): return lax.ppermute(value, ('zh', 'c', 'zl'), pairs)  11.6 us
    ppermute x4, waiting for transfers between devices, shift(): return lax.ppermute(value, axis, [(i, (i + k) % n) for i in range(n)])  10 us
    ppermute x4, waiting for transfers between devices, swap(): return lax.ppermute(value, axis, [(0, 1), (1, 0)])  9.26 us
    ppermute x4, starting transfers between devices, swap(): return lax.ppermute(value, axis, [(0, 1), (1, 0)])  8.39 us
    all_to_all x1, starting transfers between devices, on_device(): cot_near = lax.all_to_all(cot, 'zh', 0, 0)  8.12 us
  transfers between devices with their start and end apart: 13, of which 7 were waited for; matrix products, arithmetic and copies ran while one was open for 2% of the time, Pallas kernels for 17%

profile of v13, /device:TPU:1, one launch (start us, length us, event | category | flops | bytes accessed | tf_op | source)
XLA Modules:
  0.0 152.1 jit_solution(11612536311307034385)
XLA Ops:
  7.2 0.0 all-gather.5.cloned.1.call-start
  7.2 0.7 all-gather.5.cloned.1.call-update
  7.9 0.0 copy-start.5
  7.9 0.0 copy-start.6
  7.9 3.2 %broadcast_select_fusion = bf16[4096,256]{1,0:T(8,128)(2,1)} fusion(bf16[4096,256]{1,0:T(8,128)(2,1)} %refs_1_.1, bf16[4096,256]{1,0:T(8,128)(2,1)} %refs_3_.1, pred[]{:T(512)S(6)} %eq.3), kind=kLoop, calls=%fused_computation | loop fusion | flops 1048576 | bytes 6291457 | tf_op jit(solution)/shard_map/jit(_where)/select_n | solution.py:258
  11.1 0.0 copy-start.4
  11.1 11.6 %collective-permute-start.4 = (bf16[4096,256]{1,0:T(8,128)(2,1)}, bf16[4096,256]{1,0:T(8,128)(2,1)}, u32[]{:S(2)}, u32[]{:S(2)}) collective-permute-start(bf16[4096,256]{1,0:T(8,128)(2,1)} %broadcast_select_fusion), channel_id=1, source_target_pairs={{0,32},{32,0},{96,192},{192,96},{128,160},{160,128},{224,320},{320... | collective-permute-start | bytes 6291464 | tf_op jit(solution)/shard_map/ppermute | solution.py:44
  22.7 0.0 copy-done.5
  22.7 0.0 copy-done.6
  22.8 19.4 %all_to_all.15 = bf16[8,8,4096]{2,1,0:T(8,128)(2,1)S(1)} all-to-all(bf16[8,8,4096]{2,1,0:T(8,128)(2,1)S(1)} %broadcast_in_dim.2), channel_id=1, replica_groups=mesh['zh'=4,'c'=2,'zl'=2,'y'=8,'x'=4] {'y'}, dimensions={0} | all-to-all | bytes 1048576 | tf_op jit(solution)/shard_map/all_to_all | solution.py:251
  42.2 3.1 %collective-permute-start = (bf16[64,4096]{1,0:T(8,128)(2,1)S(1)}, bf16[64,4096]{1,0:T(8,128)(2,1)S(1)}, u32[]{:S(2)}, u32[]{:S(2)}) collective-permute-start(bf16[64,4096]{1,0:T(8,128)(2,1)S(1)} %bitcast.9), channel_id=1, source_target_pairs={{0,1},{1,2},{2,3},{3,0},{4,5},{5,6},{6,7},{7,4},{8,9},{9,10},{10,1... | collective-permute-start | bytes 1572872 | tf_op jit(solution)/shard_map/ppermute | solution.py:35
  45.4 3.4 %collective-permute-start.2 = (bf16[64,4096]{1,0:T(8,128)(2,1)S(1)}, bf16[64,4096]{1,0:T(8,128)(2,1)S(1)}, u32[]{:S(2)}, u32[]{:S(2)}) collective-permute-start(bf16[64,4096]{1,0:T(8,128)(2,1)S(1)} %bitcast.10), channel_id=1, source_target_pairs={{0,3},{1,0},{2,1},{3,2},{4,7},{5,4},{6,5},{7,6},{8,11},{9,8},{10,9... | collective-permute-start | bytes 1572872 | tf_op jit(solution)/shard_map/ppermute | solution.py:35
  48.7 6.6 %collective-permute-done.r1 = bf16[64,4096]{1,0:T(8,128)(2,1)S(1)} collective-permute-done((bf16[64,4096]{1,0:T(8,128)(2,1)S(1)}, bf16[64,4096]{1,0:T(8,128)(2,1)S(1)}, u32[]{:S(2)}, u32[]{:S(2)}) %collective-permute-start) | collective-permute-done | bytes 524320 | tf_op jit(solution)/shard_map/ppermute | solution.py:35
  55.4 1.9 %collective-permute-start.1 = (bf16[32,4096]{1,0:T(8,128)(2,1)S(1)}, bf16[32,4096]{1,0:T(8,128)(2,1)S(1)}, u32[]{:S(2)}, u32[]{:S(2)}) collective-permute-start(bf16[32,4096]{1,0:T(8,128)(2,1)S(1)} %slice.20), channel_id=1, source_target_pairs={{0,1},{1,2},{2,3},{3,0},{4,5},{5,6},{6,7},{7,4},{8,9},{9,10},{10,1... | collective-permute-start | bytes 786440 | tf_op jit(solution)/shard_map/ppermute | solution.py:35
  57.3 0.2 collective-permute-done.2.r3
  57.5 4.6 %collective-permute-start.3 = (bf16[32,4096]{1,0:T(8,128)(2,1)S(1)}, bf16[32,4096]{1,0:T(8,128)(2,1)S(1)}, u32[]{:S(2)}, u32[]{:S(2)}) collective-permute-start(bf16[32,4096]{1,0:T(8,128)(2,1)S(1)} %slice.21), channel_id=1, source_target_pairs={{0,3},{1,0},{2,1},{3,2},{4,7},{5,4},{6,5},{7,6},{8,11},{9,8},{10,9... | collective-permute-start | bytes 786440 | tf_op jit(solution)/shard_map/ppermute | solution.py:35
  62.1 0.1 pad_add_fusion.where
  62.2 1.7 %collective-permute-done.1.r2a = bf16[32,4096]{1,0:T(8,128)(2,1)S(1)} collective-permute-done((bf16[32,4096]{1,0:T(8,128)(2,1)S(1)}, bf16[32,4096]{1,0:T(8,128)(2,1)S(1)}, u32[]{:S(2)}, u32[]{:S(2)}) %collective-permute-start.1) | collective-permute-done | bytes 262176 | tf_op jit(solution)/shard_map/ppermute | solution.py:35
  63.9 1.5 %collective-permute-done.3.r2b = bf16[32,4096]{1,0:T(8,128)(2,1)S(1)} collective-permute-done((bf16[32,4096]{1,0:T(8,128)(2,1)S(1)}, bf16[32,4096]{1,0:T(8,128)(2,1)S(1)}, u32[]{:S(2)}, u32[]{:S(2)}) %collective-permute-start.3) | collective-permute-done | bytes 262176 | tf_op jit(solution)/shard_map/ppermute | solution.py:35
  65.4 0.0 copy-done.4
  65.4 4.7 %split.1 = (bf16[128,4096]{1,0:T(8,128)(2,1)}, bf16[4,2,128,512]{3,2,1,0:T(8,128)(2,1)}) custom-call(s32[3]{0:T(128)S(1)} %pad_add_fusion.where, bf16[64,64]{1,0:T(8,128)(2,1)S(1)} %copy-done.4, bf16[64,4096]{1,0:T(8,128)(2,1)S(1)} %bitcast.11, bf16[64,4096]{1,0:T(8,128)(2,1)S(1)} %collective-permute-done.r1, ...), custom_call_target="tpu_custom_call" | custom-call | tf_op jit(solution)/shard_map/split/pallas_call | solution.py:59
  70.2 0.0 collective-permute-done.4.mw.refs_4_.refs_5_
  70.2 0.0 all-gather.5.cloned.1.call-done
  70.2 1.9 %collective-permute-start.6 = (bf16[4096,256]{1,0:T(8,128)(2,1)}, bf16[4096,256]{1,0:T(8,128)(2,1)S(1)}, u32[]{:S(2)}, u32[]{:S(2)}) collective-permute-start(bf16[4096,256]{1,0:T(8,128)(2,1)} %collective-permute-done.4.mw.refs_4_.refs_5_), channel_id=1, source_target_pairs={{0,64},{64,0},{1,65},{65,1},{2,66},{66,2},{3,67},{67,3},{4,68},{68... | collective-permute-start | bytes 6291464 | tf_op jit(solution)/shard_map/ppermute | solution.py:30
  72.1 2.4 %collective-permute-start.5 = (bf16[4,512,512]{2,1,0:T(8,128)(2,1)}, bf16[4,512,512]{2,1,0:T(8,128)(2,1)}, u32[]{:S(2)}, u32[]{:S(2)}) collective-permute-start(bf16[4,512,512]{2,1,0:T(8,128)(2,1)} %bitcast.14), channel_id=1, source_target_pairs={{0,64},{64,0},{1,65},{65,1},{2,66},{66,2},{3,67},{67,3},{4,68},{68... | collective-permute-start | bytes 6291464 | tf_op jit(solution)/shard_map/ppermute | solution.py:30
  74.5 8.1 %all-to-all-start.2 = ((bf16[4,2,128,512]{3,2,1,0:T(8,128)(2,1)}), bf16[4,2,128,512]{3,2,1,0:T(8,128)(2,1)S(1)}, u32[]{:S(2)}, u32[]{:S(2)}) async-start(bf16[4,2,128,512]{3,2,1,0:T(8,128)(2,1)} %get-tuple-element.18.cot), calls=%async_computation.2 | async-start | bytes 2097152 | tf_op jit(solution)/shard_map/all_to_all | solution.py:269
  82.6 0.0 all-gather.7.cloned.1.call-start
  82.6 0.0 collective-permute-done.6.ow.refs_6_.refs_7_
  82.6 7.8 %gates.1 = (bf16[128,512]{1,0:T(8,128)(2,1)}, f32[128,1024]{1,0:T(8,128)S(1)}) custom-call(s32[3]{0:T(128)S(1)} %pad_add_fusion.where, bf16[128,4096]{1,0:T(8,128)(2,1)} %get-tuple-element.22.tok, bf16[4096,256]{1,0:T(8,128)(2,1)} %refs_1_.1, bf16[4096,256]{1,0:T(8,128)(2,1)} %refs_3_.1, bf16[4096,256]{1,0:T(8,128)(2,1)} %collective-permute-done.4.mw.refs_4_.refs_5_, ...), custom_call_target="tpu_custom_call" | custom-call | tf_op jit(solution)/shard_map/gates/pallas_call | solution.py:123
  90.4 0.0 copy-start.1
  90.4 0.8 copy-done.1
  91.2 0.0 all-gather.7.cloned.1.call-update
  91.3 0.0 collective-permute-done.5.df
  91.3 0.0 copy-start.2
  91.3 1.0 copy-done.2
  92.3 0.0 copy-start.3
  92.3 4.7 %down.1.dd = bf16[128,1024]{1,0:T(8,128)(2,1)S(1)} custom-call(s32[3]{0:T(128)S(1)} %pad_add_fusion.where, bf16[4,2,128,512]{3,2,1,0:T(8,128)(2,1)} %get-tuple-element.18.cot, bf16[4,512,512]{2,1,0:T(8,128)(2,1)} %bitcast.15, bf16[4,512,512]{2,1,0:T(8,128)(2,1)} %collective-permute-done.5.df, f32[128,1024]{1,0:T(8,128)S(1)} %copy-done.2), custom_call_target="tpu_custom_call" | custom-call | tf_op jit(solution)/shard_map/down/pallas_call | solution.py:165
  97.1 0.0 copy-done.3
  97.1 7.2 %term.1 = bf16[4,64,2048]{2,1,0:T(8,128)(2,1)} custom-call(s32[3]{0:T(128)S(1)} %pad_add_fusion.where, bf16[256,256]{1,0:T(8,128)(2,1)S(1)} %copy-done.3, bf16[128,1024]{1,0:T(8,128)(2,1)S(1)} %down.1.dd, bf16[4096,256]{1,0:T(8,128)(2,1)} %refs_1_.1, bf16[4096,256]{1,0:T(8,128)(2,1)} %refs_1_.1, bf16[4096,256]{1,0:T(8,128)(2,1)} %refs_3_.1, ...), custom_call_target="tpu_custom_call" | custom-call | tf_op jit(solution)/shard_map/term/pallas_call | solution.py:198
  104.3 0.0 all-to-all-done.2.cn
  104.3 6.9 %all-to-all-start.1 = ((bf16[32,8,2048]{2,1,0:T(8,128)(2,1)}), bf16[32,8,2048]{2,1,0:T(8,128)(2,1)S(1)}, u32[]{:S(2)}, u32[]{:S(2)}) async-start(bf16[32,8,2048]{2,1,0:T(8,128)(2,1)} %bitcast.13), calls=%async_computation.1 | async-start | bytes 2097152 | tf_op jit(solution)/shard_map/all_to_all | solution.py:277
  111.3 15.9 %all-gather.7.cloned.1.call-done = bf16[1024,512]{1,0:T(8,128)(2,1)} async-done(((bf16[128,512]{1,0:T(8,128)(2,1)}), bf16[1024,512]{1,0:T(8,128)(2,1)}) %all-gather.7.cloned.1.call-update) | async-done | bytes 1048592 | tf_op jit(solution)/shard_map/all_gather | solution.py:273
  127.2 2.2 %collective-permute-start.7 = (bf16[4,128,512]{2,1,0:T(8,128)(2,1)S(1)}, bf16[4,128,512]{2,1,0:T(8,128)(2,1)S(1)}, u32[]{:S(2)}, u32[]{:S(2)}) collective-permute-start(bf16[4,128,512]{2,1,0:T(8,128)(2,1)S(1)} %slice_bitcast_fusion), channel_id=1, source_target_pairs={{0,64},{64,0},{1,65},{65,1},{2,66},{66,2},{3,67},{67,3},{4,68},{68... | collective-permute-start | bytes 1572872 | tf_op jit(solution)/shard_map/ppermute | solution.py:30
  129.4 1.6 %collective-permute-done.7.cf = bf16[4,128,512]{2,1,0:T(8,128)(2,1)S(1)} collective-permute-done((bf16[4,128,512]{2,1,0:T(8,128)(2,1)S(1)}, bf16[4,128,512]{2,1,0:T(8,128)(2,1)S(1)}, u32[]{:S(2)}, u32[]{:S(2)}) %collective-permute-start.7) | collective-permute-done | bytes 524320 | tf_op jit(solution)/shard_map/ppermute | solution.py:30
  131.0 0.0 copy-start
  131.0 1.2 copy-done
  132.3 1.8 %grads.1 = (f32[256,512]{1,0:T(8,128)S(1)}, bf16[256,512]{1,0:T(8,128)(2,1)S(1)}) custom-call(s32[3]{0:T(128)S(1)} %pad_add_fusion.where, bf16[4,2,128,512]{3,2,1,0:T(8,128)(2,1)S(1)} %bitcast.12, bf16[4,2,128,512]{3,2,1,0:T(8,128)(2,1)S(1)} %all-to-all-done.2.cn, bf16[4,128,512]{2,1,0:T(8,128)(2,1)S(1)} %collective-permute-done.7.cf), custom_call_target="tpu_custom_call" | custom-call | tf_op jit(solution)/shard_map/grads/pallas_call | solution.py:227
  134.1 1.9 %collective-permute-start.8 = (bf16[256,512]{1,0:T(8,128)(2,1)S(1)}, bf16[256,512]{1,0:T(8,128)(2,1)S(1)}, u32[]{:S(2)}, u32[]{:S(2)}) collective-permute-start(bf16[256,512]{1,0:T(8,128)(2,1)S(1)} %get-tuple-element.28), channel_id=1, source_target_pairs={{0,32},{32,0},{1,33},{33,1},{2,34},{34,2},{3,35},{35,3},{4,36},{36... | collective-permute-start | bytes 786440 | tf_op jit(solution)/shard_map/ppermute | solution.py:30
  136.0 0.0 all-to-all-done.1
  136.0 7.6 %collective-permute-done.8 = bf16[256,512]{1,0:T(8,128)(2,1)S(1)} collective-permute-done((bf16[256,512]{1,0:T(8,128)(2,1)S(1)}, bf16[256,512]{1,0:T(8,128)(2,1)S(1)}, u32[]{:S(2)}, u32[]{:S(2)}) %collective-permute-start.8) | collective-permute-done | bytes 262176 | tf_op jit(solution)/shard_map/ppermute | solution.py:30
  143.6 0.2 reduce_sum.12
  143.8 0.6 pad_maximum_fusion.1
  144.4 0.9 convert_add_fusion
  (6 shorter events, 0.2 us)
Async XLA Ops:
  7.2 63.0 %all-gather.5.cloned.1.call-start = ((), (), s32[]{:S(2)}) async-start(), calls=%async_computation.3 | async-start | bytes 2359296 | tf_op jit(solution)/shard_map/all_gather | solution.py:261
  7.9 14.8 %copy-start.5 = (bf16[4,4096]{1,0:T(4,128)(2,1)S(1)}, bf16[4,4096]{1,0:T(4,128)(2,1)}, u32[]{:S(2)}) copy-start(bf16[4,4096]{1,0:T(4,128)(2,1)} %param.8) | copy-start | bytes 98308
  7.9 14.8 %copy-start.6 = (bf16[4,4096]{1,0:T(4,128)(2,1)S(1)}, bf16[4,4096]{1,0:T(4,128)(2,1)}, u32[]{:S(2)}) copy-start(bf16[4,4096]{1,0:T(4,128)(2,1)} %param.7) | copy-start | bytes 98308
  11.1 54.3 %copy-start.4 = (bf16[64,64]{1,0:T(8,128)(2,1)S(1)}, bf16[64,64]{1,0:T(8,128)(2,1)}, u32[]{:S(2)}) copy-start(bf16[64,64]{1,0:T(8,128)(2,1)} %constant.23.clone.pick) | copy-start | bytes 24580
  11.1 59.1 %collective-permute-start.4 = (bf16[4096,256]{1,0:T(8,128)(2,1)}, bf16[4096,256]{1,0:T(8,128)(2,1)}, u32[]{:S(2)}, u32[]{:S(2)}) collective-permute-start(bf16[4096,256]{1,0:T(8,128)(2,1)} %broadcast_select_fusion), channel_id=1, source_target_pairs={{0,32},{32,0},{96,192},{192,96},{128,160},{160,128},{224,320},{320... | collective-permute-start | bytes 6291464 | tf_op jit(solution)/shard_map/ppermute | solution.py:44
  42.2 13.1 %collective-permute-start = (bf16[64,4096]{1,0:T(8,128)(2,1)S(1)}, bf16[64,4096]{1,0:T(8,128)(2,1)S(1)}, u32[]{:S(2)}, u32[]{:S(2)}) collective-permute-start(bf16[64,4096]{1,0:T(8,128)(2,1)S(1)} %bitcast.9), channel_id=1, source_target_pairs={{0,1},{1,2},{2,3},{3,0},{4,5},{5,6},{6,7},{7,4},{8,9},{9,10},{10,1... | collective-permute-start | bytes 1572872 | tf_op jit(solution)/shard_map/ppermute | solution.py:35
  45.4 12.2 %collective-permute-start.2 = (bf16[64,4096]{1,0:T(8,128)(2,1)S(1)}, bf16[64,4096]{1,0:T(8,128)(2,1)S(1)}, u32[]{:S(2)}, u32[]{:S(2)}) collective-permute-start(bf16[64,4096]{1,0:T(8,128)(2,1)S(1)} %bitcast.10), channel_id=1, source_target_pairs={{0,3},{1,0},{2,1},{3,2},{4,7},{5,4},{6,5},{7,6},{8,11},{9,8},{10,9... | collective-permute-start | bytes 1572872 | tf_op jit(solution)/shard_map/ppermute | solution.py:35
  55.4 8.6 %collective-permute-start.1 = (bf16[32,4096]{1,0:T(8,128)(2,1)S(1)}, bf16[32,4096]{1,0:T(8,128)(2,1)S(1)}, u32[]{:S(2)}, u32[]{:S(2)}) collective-permute-start(bf16[32,4096]{1,0:T(8,128)(2,1)S(1)} %slice.20), channel_id=1, source_target_pairs={{0,1},{1,2},{2,3},{3,0},{4,5},{5,6},{6,7},{7,4},{8,9},{9,10},{10,1... | collective-permute-start | bytes 786440 | tf_op jit(solution)/shard_map/ppermute | solution.py:35
  57.5 7.9 %collective-permute-start.3 = (bf16[32,4096]{1,0:T(8,128)(2,1)S(1)}, bf16[32,4096]{1,0:T(8,128)(2,1)S(1)}, u32[]{:S(2)}, u32[]{:S(2)}) collective-permute-start(bf16[32,4096]{1,0:T(8,128)(2,1)S(1)} %slice.21), channel_id=1, source_target_pairs={{0,3},{1,0},{2,1},{3,2},{4,7},{5,4},{6,5},{7,6},{8,11},{9,8},{10,9... | collective-permute-start | bytes 786440 | tf_op jit(solution)/shard_map/ppermute | solution.py:35
  70.2 12.5 %collective-permute-start.6 = (bf16[4096,256]{1,0:T(8,128)(2,1)}, bf16[4096,256]{1,0:T(8,128)(2,1)S(1)}, u32[]{:S(2)}, u32[]{:S(2)}) collective-permute-start(bf16[4096,256]{1,0:T(8,128)(2,1)} %collective-permute-done.4.mw.refs_4_.refs_5_), channel_id=1, source_target_pairs={{0,64},{64,0},{1,65},{65,1},{2,66},{66,2},{3,67},{67,3},{4,68},{68... | collective-permute-start | bytes 6291464 | tf_op jit(solution)/shard_map/ppermute | solution.py:30
  72.1 19.2 %collective-permute-start.5 = (bf16[4,512,512]{2,1,0:T(8,128)(2,1)}, bf16[4,512,512]{2,1,0:T(8,128)(2,1)}, u32[]{:S(2)}, u32[]{:S(2)}) collective-permute-start(bf16[4,512,512]{2,1,0:T(8,128)(2,1)} %bitcast.14), channel_id=1, source_target_pairs={{0,64},{64,0},{1,65},{65,1},{2,66},{66,2},{3,67},{67,3},{4,68},{68... | collective-permute-start | bytes 6291464 | tf_op jit(solution)/shard_map/ppermute | solution.py:30
  74.5 29.8 %all-to-all-start.2 = ((bf16[4,2,128,512]{3,2,1,0:T(8,128)(2,1)}), bf16[4,2,128,512]{3,2,1,0:T(8,128)(2,1)S(1)}, u32[]{:S(2)}, u32[]{:S(2)}) async-start(bf16[4,2,128,512]{3,2,1,0:T(8,128)(2,1)} %get-tuple-element.18.cot), calls=%async_computation.2 | async-start | bytes 2097152 | tf_op jit(solution)/shard_map/all_to_all | solution.py:269
  82.6 44.6 %all-gather.7.cloned.1.call-start = ((), (), s32[]{:S(2)}) async-start(), calls=%async_computation.4 | async-start | bytes 1179648 | tf_op jit(solution)/shard_map/all_gather | solution.py:273
  90.4 0.8 copy-start.1
  91.3 1.0 copy-start.2
  92.3 4.8 %copy-start.3 = (bf16[256,256]{1,0:T(8,128)(2,1)S(1)}, bf16[256,256]{1,0:T(8,128)(2,1)}, u32[]{:S(2)}) copy-start(bf16[256,256]{1,0:T(8,128)(2,1)} %constant.24.clone.pick) | copy-start | bytes 393220
  104.3 31.7 %all-to-all-start.1 = ((bf16[32,8,2048]{2,1,0:T(8,128)(2,1)}), bf16[32,8,2048]{2,1,0:T(8,128)(2,1)S(1)}, u32[]{:S(2)}, u32[]{:S(2)}) async-start(bf16[32,8,2048]{2,1,0:T(8,128)(2,1)} %bitcast.13), calls=%async_computation.1 | async-start | bytes 2097152 | tf_op jit(solution)/shard_map/all_to_all | solution.py:277
  127.2 3.8 %collective-permute-start.7 = (bf16[4,128,512]{2,1,0:T(8,128)(2,1)S(1)}, bf16[4,128,512]{2,1,0:T(8,128)(2,1)S(1)}, u32[]{:S(2)}, u32[]{:S(2)}) collective-permute-start(bf16[4,128,512]{2,1,0:T(8,128)(2,1)S(1)} %slice_bitcast_fusion), channel_id=1, source_target_pairs={{0,64},{64,0},{1,65},{65,1},{2,66},{66,2},{3,67},{67,3},{4,68},{68... | collective-permute-start | bytes 1572872 | tf_op jit(solution)/shard_map/ppermute | solution.py:30
  131.0 1.2 copy-start
  134.1 9.6 %collective-permute-start.8 = (bf16[256,512]{1,0:T(8,128)(2,1)S(1)}, bf16[256,512]{1,0:T(8,128)(2,1)S(1)}, u32[]{:S(2)}, u32[]{:S(2)}) collective-permute-start(bf16[256,512]{1,0:T(8,128)(2,1)S(1)} %get-tuple-element.28), channel_id=1, source_target_pairs={{0,32},{32,0},{1,33},{33,1},{2,34},{34,2},{3,35},{35,3},{4,36},{36... | collective-permute-start | bytes 786440 | tf_op jit(solution)/shard_map/ppermute | solution.py:30
Sparse Core Ops, SparseCore 0:
  10.1 54.1 all-gather.4
  91.4 35.7 all-gather.6

commit v14 on v13

--- a/solution.py
+++ b/solution.py
@@ -44,16 +44,30 @@
     return lax.ppermute(value, ("zh", "c", "zl"), pairs)
 
 
-def split_body(where, pick, r0, r1, r2a, r2b, r3, tok, cot):
+def split_body(where, pick, r0, r1, r2a, r2b, r3, gw, uw, tok, cot, pre, acc):
+    step = pl.program_id(0)
+
+    @pl.when(step == 0)
+    def _():
+        acc[...] = jnp.zeros_like(acc)
+
     n = NY * ROWS
     r2 = jnp.concatenate([r2a[...], r2b[...]], axis=0)
     for i, piece in enumerate((r0[...], r1[...], r2, r3[...])):
         rows = contract(pick[...], piece, 1, 0).astype(BF16)
         tok[i * n : (i + 1) * n] = rows[:n]
         cot[0, 0, i * n : (i + 1) * n] = rows[n:]
-
-
-def split(where, pieces):
+    t = tok[...]
+    acc[:, :HID] += contract(t, gw[...], 1, 0)
+    acc[:, HID:] += contract(t, uw[...], 1, 0)
+
+    @pl.when(step == STEPS - 1)
+    def _():
+        pre[...] = acc[...]
+
+
+def split(where, pieces, gw, uw):
+    weight = pl.BlockSpec((FEATS, HID), lambda j, s: (j, 0))
     piece = pl.BlockSpec((PIECE, FEATS), lambda j, s: (0, j))
     part = pl.BlockSpec((PIECE // 2, FEATS), lambda j, s: (0, j))
     return pl.pallas_call(
@@ -61,19 +75,23 @@
         grid_spec=pltpu.PrefetchScalarGridSpec(
             num_scalar_prefetch=1,
             grid=(STEPS,),
-            in_specs=[pl.BlockSpec((PIECE, PIECE), lambda j, s: (0, 0)), piece, piece, part, part, piece],
+            in_specs=[pl.BlockSpec((PIECE, PIECE), lambda j, s: (0, 0)), piece, piece, part, part, piece]
+            + [weight] * 2,
             out_specs=[
                 pl.BlockSpec((HALF, FEATS), lambda j, s: (0, j)),
                 pl.BlockSpec((1, 1, HALF, FEATS), lambda j, s: (j // 2, flip(j % 2, s[0]), 0, 0)),
+                pl.BlockSpec((HALF, 2 * HID), lambda j, s: (0, 0)),
             ],
+            scratch_shapes=[pltpu.VMEM((HALF, 2 * HID), F32)],
         ),
         out_shape=[
             hbm((HALF, D), BF16),
             hbm((NZ, 2, HALF, FEATS), BF16),
+            hbm((HALF, 2 * HID), F32),
         ],
         compiler_params=pltpu.CompilerParams(vmem_limit_bytes=32 * 2**20),
         name="split",
-    )(where, selection((NY, 2, ROWS), (1, 0, 2)), *pieces)
+    )(where, selection((NY, 2, ROWS), (1, 0, 2)), *pieces, *pinned(gw, uw))
 
 
 def hbm(shape, dtype):
@@ -88,7 +106,7 @@
     return a + b - 2 * a * b
 
 
-def gates_body(where, tok, gw, uw, mw, ow, hid, fac, acc):
+def gates_body(where, tok, mw, ow, pre, hid, fac, acc):
     step = pl.program_id(0)
 
     @pl.when(step == 0)
@@ -96,15 +114,15 @@
         acc[...] = jnp.zeros_like(acc)
 
     t = tok[...]
-    for i, w in enumerate((gw, uw, mw, ow)):
+    for i, w in enumerate((mw, ow)):
         acc[:, i * HID : (i + 1) * HID] += contract(t, w[...], 1, 0)
 
     @pl.when(step == STEPS - 1)
     def _():
         first = where[0] == 0
-        pm, po = acc[:, 2 * HID : 3 * HID], acc[:, 3 * HID :]
+        pm, po = acc[:, :HID], acc[:, HID:]
         sides = (
-            (acc[:, :HID], acc[:, HID : 2 * HID]),
+            (pre[:, :HID], pre[:, HID:]),
             (jnp.where(first, pm, po), jnp.where(first, po, pm)),
         )
         for i, (gate, up) in enumerate(sides):
@@ -118,27 +136,28 @@
             fac[:, (2 * i + 1) * HID : (2 * i + 2) * HID] = silu
 
 
-def gates(where, tok, gw, uw, mw, ow):
+def gates(where, tok, mw, ow, pre):
     weight = pl.BlockSpec((FEATS, HID), lambda j, s: (j, 0))
     return pl.pallas_call(
         gates_body,
         grid_spec=pltpu.PrefetchScalarGridSpec(
             num_scalar_prefetch=1,
             grid=(STEPS,),
-            in_specs=[pl.BlockSpec((HALF, FEATS), lambda j, s: (0, j))] + [weight] * 4,
+            in_specs=[pl.BlockSpec((HALF, FEATS), lambda j, s: (0, j))] + [weight] * 2
+            + [pl.BlockSpec((HALF, 2 * HID), lambda j, s: (0, 0))],
             out_specs=[
                 pl.BlockSpec((HALF, 2 * HID), lambda j, s: (0, 0)),
                 pl.BlockSpec((HALF, 4 * HID), lambda j, s: (0, 0)),
             ],
-            scratch_shapes=[pltpu.VMEM((HALF, 4 * HID), F32)],
+            scratch_shapes=[pltpu.VMEM((HALF, 2 * HID), F32)],
         ),
         out_shape=[
             jax.ShapeDtypeStruct((HALF, 2 * HID), BF16),
-            jax.ShapeDtypeStruct((HALF, 4 * HID), F32),
+            hbm((HALF, 4 * HID), F32),
         ],
         compiler_params=pltpu.CompilerParams(vmem_limit_bytes=32 * 2**20),
         name="gates",
-    )(where, *pinned(tok, gw, uw, mw), ow)
+    )(where, *pinned(tok, mw), ow, *pinned(pre))
 
 
 def down_body(where, cot, dn, df, fac, dd, acc):
@@ -174,7 +193,7 @@
         out_shape=jax.ShapeDtypeStruct((HALF, 4 * HID), BF16),
         compiler_params=pltpu.CompilerParams(vmem_limit_bytes=32 * 2**20),
         name="down",
-    )(where, *pinned(cot, dn), df, fac)
+    )(where, *pinned(cot, dn), df, *pinned(fac))
 
 
 def term_body(where, pick, dd, *refs):
@@ -192,20 +211,20 @@
 
 
 def term(where, dd, gw, uw, mw, ow):
-    low = pl.BlockSpec((FEATS, HID), lambda j, s: (j, 0))
-    high = pl.BlockSpec((FEATS, HID), lambda j, s: (j + NZ, 0))
+    low = pl.BlockSpec((2 * FEATS, HID), lambda j, s: (j, 0))
+    high = pl.BlockSpec((2 * FEATS, HID), lambda j, s: (j + 2, 0))
     gw, uw, mw = pinned(gw, uw, mw)
     return pl.pallas_call(
         term_body,
         grid_spec=pltpu.PrefetchScalarGridSpec(
             num_scalar_prefetch=1,
-            grid=(STEPS // 2,),
+            grid=(STEPS // 4,),
             in_specs=[
                 pl.BlockSpec((2 * HALF, 2 * HALF), lambda j, s: (0, 0)),
                 pl.BlockSpec((HALF, 4 * HID), lambda j, s: (0, 0)),
             ]
             + [low, high] * 4,
-            out_specs=pl.BlockSpec((NX, PIECE, FEATS), lambda j, s: (0, 0, j)),
+            out_specs=pl.BlockSpec((NX, PIECE, 2 * FEATS), lambda j, s: (0, 0, j)),
         ),
         out_shape=hbm((NX, PIECE, D // 2), BF16),
         compiler_params=pltpu.CompilerParams(vmem_limit_bytes=32 * 2**20),
@@ -265,11 +284,11 @@
     n = PIECE // 2
     pieces = (block, left, shift(left[:n], "x", 1), shift(right[n:], "x", -1), right)
 
-    tok, cot = split(where, pieces)
+    tok, cot, pre = split(where, pieces, gate_weight, up_weight)
     cot_near = lax.all_to_all(cot, "zh", 0, 0)
     tok, mine, down_near = lax.optimization_barrier((tok, mine, down_near))
     other, down_far = swap(mine, "c"), swap(down_near, "c")
-    hidden, factors = gates(where, tok, gate_weight, up_weight, mine, other)
+    hidden, factors = gates(where, tok, mine, other, pre)
     hidden = lax.all_gather(hidden, DP, axis=0).reshape(NZ, 2, HALF, 2 * HID)
     dd = down(where, cot, down_near, down_far, factors)
 

time: 154 us -> 158 us (1.026)
  the two profiles are of different devices: /device:TPU:1 before, /device:TPU:72 now
where the time goes in v14:
time: 158 us; the launch traced here: 157 us
  starting transfers between devices  42.5 us (27%)
  waiting for transfers between devices  39.8 us (25%)
  Pallas kernels  28.7 us (18%)
  blocking collectives  25.2 us (16%)
  between operations  14.3 us (9%)
  other arithmetic  4.94 us (3%)
    all_to_all x1, blocking collectives, spread(): lax.all_to_all(jnp.broadcast_to(block[None], (n, *block.shape)), axis, 0, 0)  25.2 us
    ppermute x4, waiting for transfers between devices, shift(): return lax.ppermute(value, axis, [(i, (i + k) % n) for i in range(n)])  14.6 us
    ppermute x4, starting transfers between devices, shift(): return lax.ppermute(value, axis, [(i, (i + k) % n) for i in range(n)])  14.1 us
    all_to_all x1, waiting for transfers between devices, on_device(): lax.all_to_all(parts.reshape(NX * NY, 2 * ROWS, D // 2), ('x', 'y'), 0, 0)  12 us
    ppermute x4, starting transfers between devices, swap(): return lax.ppermute(value, axis, [(0, 1), (1, 0)])  10.2 us
    all_to_all x1, starting transfers between devices, on_device(): lax.all_to_all(parts.reshape(NX * NY, 2 * ROWS, D // 2), ('x', 'y'), 0, 0)  9.63 us
    pallas_call x1, Pallas kernels, split(): pl.pallas_call(split_body, grid_spec=pltpu.PrefetchScalarGridSpec(num_sca...  8.16 us
    pallas_call x1, Pallas kernels, gates(): pl.pallas_call(gates_body, grid_spec=pltpu.PrefetchScalarGridSpec(num_sca...  7.06 us
  transfers between devices with their start and end apart: 13, of which 7 were waited for; matrix products, arithmetic and copies ran while one was open for 2% of the time, Pallas kernels for 18%

profile of v14, /device:TPU:72, one launch (start us, length us, event | category | flops | bytes accessed | tf_op | source)
XLA Modules:
  0.0 156.8 jit_solution(4698322216736912895)
XLA Ops:
  7.2 0.0 all-gather.5.cloned.1.call-start
  7.2 0.7 all-gather.5.cloned.1.call-update
  7.9 0.0 copy-start.3
  7.9 0.0 copy-start.4
  7.9 3.2 %broadcast_select_fusion = bf16[4096,256]{1,0:T(8,128)(2,1)} fusion(bf16[4096,256]{1,0:T(8,128)(2,1)} %refs_1_.1, bf16[4096,256]{1,0:T(8,128)(2,1)} %refs_3_.1, pred[]{:T(512)S(6)} %eq.3), kind=kLoop, calls=%fused_computation | loop fusion | flops 1048576 | bytes 6291457 | tf_op jit(solution)/shard_map/jit(_where)/select_n | solution.py:277
  11.1 0.0 copy-start.2
  11.1 2.0 %collective-permute-start.4 = (bf16[4096,256]{1,0:T(8,128)(2,1)}, bf16[4096,256]{1,0:T(8,128)(2,1)}, u32[]{:S(2)}, u32[]{:S(2)}) collective-permute-start(bf16[4096,256]{1,0:T(8,128)(2,1)} %broadcast_select_fusion), channel_id=1, source_target_pairs={{0,32},{32,0},{96,192},{192,96},{128,160},{160,128},{224,320},{320... | collective-permute-start | bytes 6291464 | tf_op jit(solution)/shard_map/ppermute | solution.py:44
  13.1 0.0 copy-done.3
  13.2 0.0 copy-done.4
  13.3 25.2 %all_to_all.15 = bf16[8,8,4096]{2,1,0:T(8,128)(2,1)S(1)} all-to-all(bf16[8,8,4096]{2,1,0:T(8,128)(2,1)S(1)} %broadcast_in_dim.2), channel_id=1, replica_groups=mesh['zh'=4,'c'=2,'zl'=2,'y'=8,'x'=4] {'y'}, dimensions={0} | all-to-all | bytes 1048576 | tf_op jit(solution)/shard_map/all_to_all | solution.py:270
  38.4 1.9 %collective-permute-start = (bf16[64,4096]{1,0:T(8,128)(2,1)S(1)}, bf16[64,4096]{1,0:T(8,128)(2,1)S(1)}, u32[]{:S(2)}, u32[]{:S(2)}) collective-permute-start(bf16[64,4096]{1,0:T(8,128)(2,1)S(1)} %bitcast.9), channel_id=1, source_target_pairs={{0,1},{1,2},{2,3},{3,0},{4,5},{5,6},{6,7},{7,4},{8,9},{9,10},{10,1... | collective-permute-start | bytes 1572872 | tf_op jit(solution)/shard_map/ppermute | solution.py:35
  40.4 5.1 %collective-permute-start.2 = (bf16[64,4096]{1,0:T(8,128)(2,1)S(1)}, bf16[64,4096]{1,0:T(8,128)(2,1)S(1)}, u32[]{:S(2)}, u32[]{:S(2)}) collective-permute-start(bf16[64,4096]{1,0:T(8,128)(2,1)S(1)} %bitcast.10), channel_id=1, source_target_pairs={{0,3},{1,0},{2,1},{3,2},{4,7},{5,4},{6,5},{7,6},{8,11},{9,8},{10,9... | collective-permute-start | bytes 1572872 | tf_op jit(solution)/shard_map/ppermute | solution.py:35
  45.5 10.0 %collective-permute-done.r1 = bf16[64,4096]{1,0:T(8,128)(2,1)S(1)} collective-permute-done((bf16[64,4096]{1,0:T(8,128)(2,1)S(1)}, bf16[64,4096]{1,0:T(8,128)(2,1)S(1)}, u32[]{:S(2)}, u32[]{:S(2)}) %collective-permute-start) | collective-permute-done | bytes 524320 | tf_op jit(solution)/shard_map/ppermute | solution.py:35
  55.5 1.9 %collective-permute-start.1 = (bf16[32,4096]{1,0:T(8,128)(2,1)S(1)}, bf16[32,4096]{1,0:T(8,128)(2,1)S(1)}, u32[]{:S(2)}, u32[]{:S(2)}) collective-permute-start(bf16[32,4096]{1,0:T(8,128)(2,1)S(1)} %slice.20), channel_id=1, source_target_pairs={{0,1},{1,2},{2,3},{3,0},{4,5},{5,6},{6,7},{7,4},{8,9},{9,10},{10,1... | collective-permute-start | bytes 786440 | tf_op jit(solution)/shard_map/ppermute | solution.py:35
  57.4 0.0 collective-permute-done.2.r3
  57.5 5.1 %collective-permute-start.3 = (bf16[32,4096]{1,0:T(8,128)(2,1)S(1)}, bf16[32,4096]{1,0:T(8,128)(2,1)S(1)}, u32[]{:S(2)}, u32[]{:S(2)}) collective-permute-start(bf16[32,4096]{1,0:T(8,128)(2,1)S(1)} %slice.21), channel_id=1, source_target_pairs={{0,3},{1,0},{2,1},{3,2},{4,7},{5,4},{6,5},{7,6},{8,11},{9,8},{10,9... | collective-permute-start | bytes 786440 | tf_op jit(solution)/shard_map/ppermute | solution.py:35
  62.6 0.1 pad_add_fusion.where
  62.7 3.4 %collective-permute-done.1.r2a = bf16[32,4096]{1,0:T(8,128)(2,1)S(1)} collective-permute-done((bf16[32,4096]{1,0:T(8,128)(2,1)S(1)}, bf16[32,4096]{1,0:T(8,128)(2,1)S(1)}, u32[]{:S(2)}, u32[]{:S(2)}) %collective-permute-start.1) | collective-permute-done | bytes 262176 | tf_op jit(solution)/shard_map/ppermute | solution.py:35
  66.1 1.2 collective-permute-done.3.r2b
  67.3 0.0 copy-done.2
  67.3 8.2 %split.1 = (bf16[128,4096]{1,0:T(8,128)(2,1)}, bf16[4,2,128,512]{3,2,1,0:T(8,128)(2,1)}, f32[128,512]{1,0:T(8,128)}) custom-call(s32[3]{0:T(128)S(1)} %pad_add_fusion.where, bf16[64,64]{1,0:T(8,128)(2,1)S(1)} %copy-done.2, bf16[64,4096]{1,0:T(8,128)(2,1)S(1)} %bitcast.11, bf16[64,4096]{1,0:T(8,128)(2,1)S(1)} %collective-permute-done.r1, ...), custom_call_target="tpu_custom_call" | custom-call | tf_op jit(solution)/shard_map/split/pallas_call | solution.py:73
  75.5 0.0 collective-permute-done.4.mw.refs_4_.refs_5_
  75.5 0.0 all-gather.5.cloned.1.call-done
  75.5 1.9 %collective-permute-start.6 = (bf16[4096,256]{1,0:T(8,128)(2,1)}, bf16[4096,256]{1,0:T(8,128)(2,1)S(1)}, u32[]{:S(2)}, u32[]{:S(2)}) collective-permute-start(bf16[4096,256]{1,0:T(8,128)(2,1)} %collective-permute-done.4.mw.refs_4_.refs_5_), channel_id=1, source_target_pairs={{0,64},{64,0},{1,65},{65,1},{2,66},{66,2},{3,67},{67,3},{4,68},{68... | collective-permute-start | bytes 6291464 | tf_op jit(solution)/shard_map/ppermute | solution.py:30
  77.4 2.4 %collective-permute-start.5 = (bf16[4,512,512]{2,1,0:T(8,128)(2,1)}, bf16[4,512,512]{2,1,0:T(8,128)(2,1)}, u32[]{:S(2)}, u32[]{:S(2)}) collective-permute-start(bf16[4,512,512]{2,1,0:T(8,128)(2,1)} %bitcast.14), channel_id=1, source_target_pairs={{0,64},{64,0},{1,65},{65,1},{2,66},{66,2},{3,67},{67,3},{4,68},{68... | collective-permute-start | bytes 6291464 | tf_op jit(solution)/shard_map/ppermute | solution.py:30
  79.9 6.5 %all-to-all-start.2 = ((bf16[4,2,128,512]{3,2,1,0:T(8,128)(2,1)}), bf16[4,2,128,512]{3,2,1,0:T(8,128)(2,1)S(1)}, u32[]{:S(2)}, u32[]{:S(2)}) async-start(bf16[4,2,128,512]{3,2,1,0:T(8,128)(2,1)} %get-tuple-element.19.cot), calls=%async_computation.2 | async-start | bytes 2097152 | tf_op jit(solution)/shard_map/all_to_all | solution.py:288
  86.4 0.0 all-gather.7.cloned.1.call-start
  86.4 0.0 collective-permute-done.6.ow.refs_6_.refs_7_
  86.4 7.1 %gates.1 = (bf16[128,512]{1,0:T(8,128)(2,1)}, f32[128,1024]{1,0:T(8,128)}) custom-call(s32[3]{0:T(128)S(1)} %pad_add_fusion.where, bf16[128,4096]{1,0:T(8,128)(2,1)} %get-tuple-element.23.tok, bf16[4096,256]{1,0:T(8,128)(2,1)} %collective-permute-done.4.mw.refs_4_.refs_5_, bf16[4096,256]{1,0:T(8,128)(2,1)S(1)} %collective-permute-done.6.ow.refs_6_.refs_7_, ...), custom_call_target="tpu_custom_call" | custom-call | tf_op jit(solution)/shard_map/gates/pallas_call | solution.py:141
  93.5 0.0 all-gather.7.cloned.1.call-update
  93.5 0.0 collective-permute-done.5.df
  93.5 0.0 copy-start.1
  93.5 5.1 %down.1.dd = bf16[128,1024]{1,0:T(8,128)(2,1)S(1)} custom-call(s32[3]{0:T(128)S(1)} %pad_add_fusion.where, bf16[4,2,128,512]{3,2,1,0:T(8,128)(2,1)} %get-tuple-element.19.cot, bf16[4,512,512]{2,1,0:T(8,128)(2,1)} %bitcast.15, bf16[4,512,512]{2,1,0:T(8,128)(2,1)} %collective-permute-done.5.df, f32[128,1024]{1,0:T(8,128)} %get-tuple-element.26.fac), custom_call_target="tpu_custom_call" | custom-call | tf_op jit(solution)/shard_map/down/pallas_call | solution.py:184
  98.6 0.0 copy-done.1
  98.6 6.6 %term.1 = bf16[4,64,2048]{2,1,0:T(8,128)(2,1)} custom-call(s32[3]{0:T(128)S(1)} %pad_add_fusion.where, bf16[256,256]{1,0:T(8,128)(2,1)S(1)} %copy-done.1, bf16[128,1024]{1,0:T(8,128)(2,1)S(1)} %down.1.dd, bf16[4096,256]{1,0:T(8,128)(2,1)} %refs_1_.1, bf16[4096,256]{1,0:T(8,128)(2,1)} %refs_1_.1, bf16[4096,256]{1,0:T(8,128)(2,1)} %refs_3_.1, ...), custom_call_target="tpu_custom_call" | custom-call | tf_op jit(solution)/shard_map/term/pallas_call | solution.py:217
  105.2 4.8 %all-to-all-done.2.cn = bf16[4,2,128,512]{3,2,1,0:T(8,128)(2,1)S(1)} async-done(((bf16[4,2,128,512]{3,2,1,0:T(8,128)(2,1)}), bf16[4,2,128,512]{3,2,1,0:T(8,128)(2,1)S(1)}, u32[]{:S(2)}, u32[]{:S(2)}) %all-to-all-start.2) | async-done | bytes 1048608 | tf_op jit(solution)/shard_map/all_to_all | solution.py:288
  110.0 9.6 %all-to-all-start.1 = ((bf16[32,8,2048]{2,1,0:T(8,128)(2,1)}), bf16[32,8,2048]{2,1,0:T(8,128)(2,1)S(1)}, u32[]{:S(2)}, u32[]{:S(2)}) async-start(bf16[32,8,2048]{2,1,0:T(8,128)(2,1)} %bitcast.13), calls=%async_computation.1 | async-start | bytes 2097152 | tf_op jit(solution)/shard_map/all_to_all | solution.py:296
  119.7 6.1 %all-gather.7.cloned.1.call-done = bf16[1024,512]{1,0:T(8,128)(2,1)} async-done(((bf16[128,512]{1,0:T(8,128)(2,1)}), bf16[1024,512]{1,0:T(8,128)(2,1)}) %all-gather.7.cloned.1.call-update) | async-done | bytes 1048592 | tf_op jit(solution)/shard_map/all_gather | solution.py:292
  125.8 2.2 %collective-permute-start.7 = (bf16[4,128,512]{2,1,0:T(8,128)(2,1)S(1)}, bf16[4,128,512]{2,1,0:T(8,128)(2,1)S(1)}, u32[]{:S(2)}, u32[]{:S(2)}) collective-permute-start(bf16[4,128,512]{2,1,0:T(8,128)(2,1)S(1)} %slice_bitcast_fusion), channel_id=1, source_target_pairs={{0,64},{64,0},{1,65},{65,1},{2,66},{66,2},{3,67},{67,3},{4,68},{68... | collective-permute-start | bytes 1572872 | tf_op jit(solution)/shard_map/ppermute | solution.py:30
  128.0 1.6 %collective-permute-done.7.cf = bf16[4,128,512]{2,1,0:T(8,128)(2,1)S(1)} collective-permute-done((bf16[4,128,512]{2,1,0:T(8,128)(2,1)S(1)}, bf16[4,128,512]{2,1,0:T(8,128)(2,1)S(1)}, u32[]{:S(2)}, u32[]{:S(2)}) %collective-permute-start.7) | collective-permute-done | bytes 524320 | tf_op jit(solution)/shard_map/ppermute | solution.py:30
  129.6 0.0 copy-start
  129.6 1.2 copy-done
  130.8 1.8 %grads.1 = (f32[256,512]{1,0:T(8,128)S(1)}, bf16[256,512]{1,0:T(8,128)(2,1)S(1)}) custom-call(s32[3]{0:T(128)S(1)} %pad_add_fusion.where, bf16[4,2,128,512]{3,2,1,0:T(8,128)(2,1)S(1)} %bitcast.12, bf16[4,2,128,512]{3,2,1,0:T(8,128)(2,1)S(1)} %all-to-all-done.2.cn, bf16[4,128,512]{2,1,0:T(8,128)(2,1)S(1)} %collective-permute-done.7.cf), custom_call_target="tpu_custom_call" | custom-call | tf_op jit(solution)/shard_map/grads/pallas_call | solution.py:246
  132.6 3.7 %collective-permute-start.8 = (bf16[256,512]{1,0:T(8,128)(2,1)S(1)}, bf16[256,512]{1,0:T(8,128)(2,1)S(1)}, u32[]{:S(2)}, u32[]{:S(2)}) collective-permute-start(bf16[256,512]{1,0:T(8,128)(2,1)S(1)} %get-tuple-element.30), channel_id=1, source_target_pairs={{0,32},{32,0},{1,33},{33,1},{2,34},{34,2},{3,35},{35,3},{4,36},{36... | collective-permute-start | bytes 786440 | tf_op jit(solution)/shard_map/ppermute | solution.py:30
  136.3 12.0 %all-to-all-done.1 = bf16[32,8,2048]{2,1,0:T(8,128)(2,1)S(1)} async-done(((bf16[32,8,2048]{2,1,0:T(8,128)(2,1)}), bf16[32,8,2048]{2,1,0:T(8,128)(2,1)S(1)}, u32[]{:S(2)}, u32[]{:S(2)}) %all-to-all-start.1) | async-done | bytes 1048608 | tf_op jit(solution)/shard_map/all_to_all | solution.py:296
  148.3 0.0 collective-permute-done.8
  148.3 0.2 reduce_sum.12
  148.5 0.9 convert_add_fusion
  149.4 0.6 pad_maximum_fusion.1
  (6 shorter events, 0.2 us)
Async XLA Ops:
  7.2 68.3 %all-gather.5.cloned.1.call-start = ((), (), s32[]{:S(2)}) async-start(), calls=%async_computation.3 | async-start | bytes 2359296 | tf_op jit(solution)/shard_map/all_gather | solution.py:280
  7.9 5.2 %copy-start.3 = (bf16[4,4096]{1,0:T(4,128)(2,1)S(1)}, bf16[4,4096]{1,0:T(4,128)(2,1)}, u32[]{:S(2)}) copy-start(bf16[4,4096]{1,0:T(4,128)(2,1)} %param.8) | copy-start | bytes 98308
  7.9 5.2 %copy-start.4 = (bf16[4,4096]{1,0:T(4,128)(2,1)S(1)}, bf16[4,4096]{1,0:T(4,128)(2,1)}, u32[]{:S(2)}) copy-start(bf16[4,4096]{1,0:T(4,128)(2,1)} %param.7) | copy-start | bytes 98308
  11.1 56.2 %copy-start.2 = (bf16[64,64]{1,0:T(8,128)(2,1)S(1)}, bf16[64,64]{1,0:T(8,128)(2,1)}, u32[]{:S(2)}) copy-start(bf16[64,64]{1,0:T(8,128)(2,1)} %constant.23.clone.pick) | copy-start | bytes 24580
  11.1 64.4 %collective-permute-start.4 = (bf16[4096,256]{1,0:T(8,128)(2,1)}, bf16[4096,256]{1,0:T(8,128)(2,1)}, u32[]{:S(2)}, u32[]{:S(2)}) collective-permute-start(bf16[4096,256]{1,0:T(8,128)(2,1)} %broadcast_select_fusion), channel_id=1, source_target_pairs={{0,32},{32,0},{96,192},{192,96},{128,160},{160,128},{224,320},{320... | collective-permute-start | bytes 6291464 | tf_op jit(solution)/shard_map/ppermute | solution.py:44
  38.4 17.0 %collective-permute-start = (bf16[64,4096]{1,0:T(8,128)(2,1)S(1)}, bf16[64,4096]{1,0:T(8,128)(2,1)S(1)}, u32[]{:S(2)}, u32[]{:S(2)}) collective-permute-start(bf16[64,4096]{1,0:T(8,128)(2,1)S(1)} %bitcast.9), channel_id=1, source_target_pairs={{0,1},{1,2},{2,3},{3,0},{4,5},{5,6},{6,7},{7,4},{8,9},{9,10},{10,1... | collective-permute-start | bytes 1572872 | tf_op jit(solution)/shard_map/ppermute | solution.py:35
  40.4 17.1 %collective-permute-start.2 = (bf16[64,4096]{1,0:T(8,128)(2,1)S(1)}, bf16[64,4096]{1,0:T(8,128)(2,1)S(1)}, u32[]{:S(2)}, u32[]{:S(2)}) collective-permute-start(bf16[64,4096]{1,0:T(8,128)(2,1)S(1)} %bitcast.10), channel_id=1, source_target_pairs={{0,3},{1,0},{2,1},{3,2},{4,7},{5,4},{6,5},{7,6},{8,11},{9,8},{10,9... | collective-permute-start | bytes 1572872 | tf_op jit(solution)/shard_map/ppermute | solution.py:35
  55.5 10.6 %collective-permute-start.1 = (bf16[32,4096]{1,0:T(8,128)(2,1)S(1)}, bf16[32,4096]{1,0:T(8,128)(2,1)S(1)}, u32[]{:S(2)}, u32[]{:S(2)}) collective-permute-start(bf16[32,4096]{1,0:T(8,128)(2,1)S(1)} %slice.20), channel_id=1, source_target_pairs={{0,1},{1,2},{2,3},{3,0},{4,5},{5,6},{6,7},{7,4},{8,9},{9,10},{10,1... | collective-permute-start | bytes 786440 | tf_op jit(solution)/shard_map/ppermute | solution.py:35
  57.5 9.8 %collective-permute-start.3 = (bf16[32,4096]{1,0:T(8,128)(2,1)S(1)}, bf16[32,4096]{1,0:T(8,128)(2,1)S(1)}, u32[]{:S(2)}, u32[]{:S(2)}) collective-permute-start(bf16[32,4096]{1,0:T(8,128)(2,1)S(1)} %slice.21), channel_id=1, source_target_pairs={{0,3},{1,0},{2,1},{3,2},{4,7},{5,4},{6,5},{7,6},{8,11},{9,8},{10,9... | collective-permute-start | bytes 786440 | tf_op jit(solution)/shard_map/ppermute | solution.py:35
  75.5 10.9 %collective-permute-start.6 = (bf16[4096,256]{1,0:T(8,128)(2,1)}, bf16[4096,256]{1,0:T(8,128)(2,1)S(1)}, u32[]{:S(2)}, u32[]{:S(2)}) collective-permute-start(bf16[4096,256]{1,0:T(8,128)(2,1)} %collective-permute-done.4.mw.refs_4_.refs_5_), channel_id=1, source_target_pairs={{0,64},{64,0},{1,65},{65,1},{2,66},{66,2},{3,67},{67,3},{4,68},{68... | collective-permute-start | bytes 6291464 | tf_op jit(solution)/shard_map/ppermute | solution.py:30
  77.4 16.0 %collective-permute-start.5 = (bf16[4,512,512]{2,1,0:T(8,128)(2,1)}, bf16[4,512,512]{2,1,0:T(8,128)(2,1)}, u32[]{:S(2)}, u32[]{:S(2)}) collective-permute-start(bf16[4,512,512]{2,1,0:T(8,128)(2,1)} %bitcast.14), channel_id=1, source_target_pairs={{0,64},{64,0},{1,65},{65,1},{2,66},{66,2},{3,67},{67,3},{4,68},{68... | collective-permute-start | bytes 6291464 | tf_op jit(solution)/shard_map/ppermute | solution.py:30
  79.9 30.2 %all-to-all-start.2 = ((bf16[4,2,128,512]{3,2,1,0:T(8,128)(2,1)}), bf16[4,2,128,512]{3,2,1,0:T(8,128)(2,1)S(1)}, u32[]{:S(2)}, u32[]{:S(2)}) async-start(bf16[4,2,128,512]{3,2,1,0:T(8,128)(2,1)} %get-tuple-element.19.cot), calls=%async_computation.2 | async-start | bytes 2097152 | tf_op jit(solution)/shard_map/all_to_all | solution.py:288
  86.4 39.3 %all-gather.7.cloned.1.call-start = ((), (), s32[]{:S(2)}) async-start(), calls=%async_computation.4 | async-start | bytes 1179648 | tf_op jit(solution)/shard_map/all_gather | solution.py:292
  93.5 5.1 %copy-start.1 = (bf16[256,256]{1,0:T(8,128)(2,1)S(1)}, bf16[256,256]{1,0:T(8,128)(2,1)}, u32[]{:S(2)}) copy-start(bf16[256,256]{1,0:T(8,128)(2,1)} %constant.24.clone.pick) | copy-start | bytes 393220
  110.0 38.3 %all-to-all-start.1 = ((bf16[32,8,2048]{2,1,0:T(8,128)(2,1)}), bf16[32,8,2048]{2,1,0:T(8,128)(2,1)S(1)}, u32[]{:S(2)}, u32[]{:S(2)}) async-start(bf16[32,8,2048]{2,1,0:T(8,128)(2,1)} %bitcast.13), calls=%async_computation.1 | async-start | bytes 2097152 | tf_op jit(solution)/shard_map/all_to_all | solution.py:296
  125.8 3.8 %collective-permute-start.7 = (bf16[4,128,512]{2,1,0:T(8,128)(2,1)S(1)}, bf16[4,128,512]{2,1,0:T(8,128)(2,1)S(1)}, u32[]{:S(2)}, u32[]{:S(2)}) collective-permute-start(bf16[4,128,512]{2,1,0:T(8,128)(2,1)S(1)} %slice_bitcast_fusion), channel_id=1, source_target_pairs={{0,64},{64,0},{1,65},{65,1},{2,66},{66,2},{3,67},{67,3},{4,68},{68... | collective-permute-start | bytes 1572872 | tf_op jit(solution)/shard_map/ppermute | solution.py:30
  129.6 1.2 copy-start
  132.6 15.7 %collective-permute-start.8 = (bf16[256,512]{1,0:T(8,128)(2,1)S(1)}, bf16[256,512]{1,0:T(8,128)(2,1)S(1)}, u32[]{:S(2)}, u32[]{:S(2)}) collective-permute-start(bf16[256,512]{1,0:T(8,128)(2,1)S(1)} %get-tuple-element.30), channel_id=1, source_target_pairs={{0,32},{32,0},{1,33},{33,1},{2,34},{34,2},{3,35},{35,3},{4,36},{36... | collective-permute-start | bytes 786440 | tf_op jit(solution)/shard_map/ppermute | solution.py:30
Sparse Core Ops, SparseCore 0:
  10.1 51.3 all-gather.4
  93.6 32.0 all-gather.6

commit v15 on v13

--- a/solution.py
+++ b/solution.py
@@ -99,7 +99,7 @@
     for i, w in enumerate((gw, uw, mw, ow)):
         acc[:, i * HID : (i + 1) * HID] += contract(t, w[...], 1, 0)
 
-    @pl.when(step == STEPS - 1)
+    @pl.when(step == STEPS // 2 - 1)
     def _():
         first = where[0] == 0
         pm, po = acc[:, 2 * HID : 3 * HID], acc[:, 3 * HID :]
@@ -119,13 +119,13 @@
 
 
 def gates(where, tok, gw, uw, mw, ow):
-    weight = pl.BlockSpec((FEATS, HID), lambda j, s: (j, 0))
+    weight = pl.BlockSpec((2 * FEATS, HID), lambda j, s: (j, 0))
     return pl.pallas_call(
         gates_body,
         grid_spec=pltpu.PrefetchScalarGridSpec(
             num_scalar_prefetch=1,
-            grid=(STEPS,),
-            in_specs=[pl.BlockSpec((HALF, FEATS), lambda j, s: (0, j))] + [weight] * 4,
+            grid=(STEPS // 2,),
+            in_specs=[pl.BlockSpec((HALF, 2 * FEATS), lambda j, s: (0, j))] + [weight] * 4,
             out_specs=[
                 pl.BlockSpec((HALF, 2 * HID), lambda j, s: (0, 0)),
                 pl.BlockSpec((HALF, 4 * HID), lambda j, s: (0, 0)),
@@ -134,7 +134,7 @@
         ),
         out_shape=[
             jax.ShapeDtypeStruct((HALF, 2 * HID), BF16),
-            jax.ShapeDtypeStruct((HALF, 4 * HID), F32),
+            hbm((HALF, 4 * HID), F32),
         ],
         compiler_params=pltpu.CompilerParams(vmem_limit_bytes=32 * 2**20),
         name="gates",
@@ -148,9 +148,10 @@
     def _():
         acc[...] = jnp.zeros_like(acc)
 
-    acc[...] += contract(cot[0, 0], dn[0], 1, 1) + contract(cot[0, 1], df[0], 1, 1)
-
-    @pl.when(step == NZ - 1)
+    for z in range(2):
+        acc[...] += contract(cot[z, 0], dn[z], 1, 1) + contract(cot[z, 1], df[z], 1, 1)
+
+    @pl.when(step == NZ // 2 - 1)
     def _():
         low = where[1] == 0
         dl, dh = acc[:, :HID], acc[:, HID:]
@@ -160,21 +161,21 @@
 
 
 def down(where, cot, dn, df, fac):
-    plane = pl.BlockSpec((1, 2 * HID, FEATS), lambda j, s: (j, 0, 0))
+    plane = pl.BlockSpec((2, 2 * HID, FEATS), lambda j, s: (j, 0, 0))
     block = pl.BlockSpec((HALF, 4 * HID), lambda j, s: (0, 0))
     return pl.pallas_call(
         down_body,
         grid_spec=pltpu.PrefetchScalarGridSpec(
             num_scalar_prefetch=1,
-            grid=(NZ,),
-            in_specs=[pl.BlockSpec((1, 2, HALF, FEATS), lambda j, s: (j, 0, 0, 0)), plane, plane, block],
+            grid=(NZ // 2,),
+            in_specs=[pl.BlockSpec((2, 2, HALF, FEATS), lambda j, s: (j, 0, 0, 0)), plane, plane, block],
             out_specs=block,
             scratch_shapes=[pltpu.VMEM((HALF, 2 * HID), F32)],
         ),
         out_shape=jax.ShapeDtypeStruct((HALF, 4 * HID), BF16),
         compiler_params=pltpu.CompilerParams(vmem_limit_bytes=32 * 2**20),
         name="down",
-    )(where, *pinned(cot, dn), df, fac)
+    )(where, *pinned(cot, dn), df, *pinned(fac))
 
 
 def term_body(where, pick, dd, *refs):
@@ -192,20 +193,20 @@
 
 
 def term(where, dd, gw, uw, mw, ow):
-    low = pl.BlockSpec((FEATS, HID), lambda j, s: (j, 0))
-    high = pl.BlockSpec((FEATS, HID), lambda j, s: (j + NZ, 0))
+    low = pl.BlockSpec((2 * FEATS, HID), lambda j, s: (j, 0))
+    high = pl.BlockSpec((2 * FEATS, HID), lambda j, s: (j + 2, 0))
     gw, uw, mw = pinned(gw, uw, mw)
     return pl.pallas_call(
         term_body,
         grid_spec=pltpu.PrefetchScalarGridSpec(
             num_scalar_prefetch=1,
-            grid=(STEPS // 2,),
+            grid=(STEPS // 4,),
             in_specs=[
                 pl.BlockSpec((2 * HALF, 2 * HALF), lambda j, s: (0, 0)),
                 pl.BlockSpec((HALF, 4 * HID), lambda j, s: (0, 0)),
             ]
             + [low, high] * 4,
-            out_specs=pl.BlockSpec((NX, PIECE, FEATS), lambda j, s: (0, 0, j)),
+            out_specs=pl.BlockSpec((NX, PIECE, 2 * FEATS), lambda j, s: (0, 0, j)),
         ),
         out_shape=hbm((NX, PIECE, D // 2), BF16),
         compiler_params=pltpu.CompilerParams(vmem_limit_bytes=32 * 2**20),

time: 154 us -> 154 us (level)
  the two profiles are of different devices: /device:TPU:1 before, /device:TPU:72 now
where the time goes in v15:
time: 154 us; the launch traced here: 153 us
  waiting for transfers between devices  42.6 us (28%)
  starting transfers between devices  41.5 us (27%)
  blocking collectives  25.2 us (16%)
  Pallas kernels  23.6 us (15%)
  between operations  14.2 us (9%)
  other arithmetic  4.94 us (3%)
    all_to_all x1, blocking collectives, spread(): lax.all_to_all(jnp.broadcast_to(block[None], (n, *block.shape)), axis, 0, 0)  25.2 us
    ppermute x4, waiting for transfers between devices, shift(): return lax.ppermute(value, axis, [(i, (i + k) % n) for i in range(n)])  14.6 us
    ppermute x4, starting transfers between devices, shift(): return lax.ppermute(value, axis, [(i, (i + k) % n) for i in range(n)])  14.1 us
    all_to_all x1, waiting for transfers between devices, on_device(): lax.all_to_all(parts.reshape(NX * NY, 2 * ROWS, D // 2), ('x', 'y'), 0, 0)  13.3 us
    all_to_all x1, starting transfers between devices, on_device(): lax.all_to_all(parts.reshape(NX * NY, 2 * ROWS, D // 2), ('x', 'y'), 0, 0)  9.63 us
    ppermute x4, starting transfers between devices, swap(): return lax.ppermute(value, axis, [(0, 1), (1, 0)])  9.12 us
    pallas_call x1, Pallas kernels, term(): pl.pallas_call(term_body, grid_spec=pltpu.PrefetchScalarGridSpec(num_scal...  6.59 us
    all_to_all x1, starting transfers between devices, on_device(): cot_near = lax.all_to_all(cot, 'zh', 0, 0)  6.55 us
  transfers between devices with their start and end apart: 13, of which 7 were waited for; matrix products, arithmetic and copies ran while one was open for 2% of the time, Pallas kernels for 15%

profile of v15, /device:TPU:72, one launch (start us, length us, event | category | flops | bytes accessed | tf_op | source)
XLA Modules:
  0.0 153.3 jit_solution(11150647578826174620)
XLA Ops:
  7.2 0.0 all-gather.5.cloned.1.call-start
  7.2 0.7 all-gather.5.cloned.1.call-update
  7.9 0.0 copy-start.3
  7.9 0.0 copy-start.4
  7.9 3.2 %broadcast_select_fusion = bf16[4096,256]{1,0:T(8,128)(2,1)} fusion(bf16[4096,256]{1,0:T(8,128)(2,1)} %refs_1_.1, bf16[4096,256]{1,0:T(8,128)(2,1)} %refs_3_.1, pred[]{:T(512)S(6)} %eq.3), kind=kLoop, calls=%fused_computation | loop fusion | flops 1048576 | bytes 6291457 | tf_op jit(solution)/shard_map/jit(_where)/select_n | solution.py:259
  11.1 0.0 copy-start.2
  11.1 2.0 %collective-permute-start.4 = (bf16[4096,256]{1,0:T(8,128)(2,1)}, bf16[4096,256]{1,0:T(8,128)(2,1)}, u32[]{:S(2)}, u32[]{:S(2)}) collective-permute-start(bf16[4096,256]{1,0:T(8,128)(2,1)} %broadcast_select_fusion), channel_id=1, source_target_pairs={{0,32},{32,0},{96,192},{192,96},{128,160},{160,128},{224,320},{320... | collective-permute-start | bytes 6291464 | tf_op jit(solution)/shard_map/ppermute | solution.py:44
  13.1 0.0 copy-done.3
  13.2 0.0 copy-done.4
  13.3 25.2 %all_to_all.15 = bf16[8,8,4096]{2,1,0:T(8,128)(2,1)S(1)} all-to-all(bf16[8,8,4096]{2,1,0:T(8,128)(2,1)S(1)} %broadcast_in_dim.2), channel_id=1, replica_groups=mesh['zh'=4,'c'=2,'zl'=2,'y'=8,'x'=4] {'y'}, dimensions={0} | all-to-all | bytes 1048576 | tf_op jit(solution)/shard_map/all_to_all | solution.py:252
  38.4 1.9 %collective-permute-start = (bf16[64,4096]{1,0:T(8,128)(2,1)S(1)}, bf16[64,4096]{1,0:T(8,128)(2,1)S(1)}, u32[]{:S(2)}, u32[]{:S(2)}) collective-permute-start(bf16[64,4096]{1,0:T(8,128)(2,1)S(1)} %bitcast.9), channel_id=1, source_target_pairs={{0,1},{1,2},{2,3},{3,0},{4,5},{5,6},{6,7},{7,4},{8,9},{9,10},{10,1... | collective-permute-start | bytes 1572872 | tf_op jit(solution)/shard_map/ppermute | solution.py:35
  40.4 5.1 %collective-permute-start.2 = (bf16[64,4096]{1,0:T(8,128)(2,1)S(1)}, bf16[64,4096]{1,0:T(8,128)(2,1)S(1)}, u32[]{:S(2)}, u32[]{:S(2)}) collective-permute-start(bf16[64,4096]{1,0:T(8,128)(2,1)S(1)} %bitcast.10), channel_id=1, source_target_pairs={{0,3},{1,0},{2,1},{3,2},{4,7},{5,4},{6,5},{7,6},{8,11},{9,8},{10,9... | collective-permute-start | bytes 1572872 | tf_op jit(solution)/shard_map/ppermute | solution.py:35
  45.5 10.0 %collective-permute-done.r1 = bf16[64,4096]{1,0:T(8,128)(2,1)S(1)} collective-permute-done((bf16[64,4096]{1,0:T(8,128)(2,1)S(1)}, bf16[64,4096]{1,0:T(8,128)(2,1)S(1)}, u32[]{:S(2)}, u32[]{:S(2)}) %collective-permute-start) | collective-permute-done | bytes 524320 | tf_op jit(solution)/shard_map/ppermute | solution.py:35
  55.5 1.9 %collective-permute-start.1 = (bf16[32,4096]{1,0:T(8,128)(2,1)S(1)}, bf16[32,4096]{1,0:T(8,128)(2,1)S(1)}, u32[]{:S(2)}, u32[]{:S(2)}) collective-permute-start(bf16[32,4096]{1,0:T(8,128)(2,1)S(1)} %slice.20), channel_id=1, source_target_pairs={{0,1},{1,2},{2,3},{3,0},{4,5},{5,6},{6,7},{7,4},{8,9},{9,10},{10,1... | collective-permute-start | bytes 786440 | tf_op jit(solution)/shard_map/ppermute | solution.py:35
  57.4 0.0 collective-permute-done.2.r3
  57.5 5.1 %collective-permute-start.3 = (bf16[32,4096]{1,0:T(8,128)(2,1)S(1)}, bf16[32,4096]{1,0:T(8,128)(2,1)S(1)}, u32[]{:S(2)}, u32[]{:S(2)}) collective-permute-start(bf16[32,4096]{1,0:T(8,128)(2,1)S(1)} %slice.21), channel_id=1, source_target_pairs={{0,3},{1,0},{2,1},{3,2},{4,7},{5,4},{6,5},{7,6},{8,11},{9,8},{10,9... | collective-permute-start | bytes 786440 | tf_op jit(solution)/shard_map/ppermute | solution.py:35
  62.6 0.1 pad_add_fusion.where
  62.7 3.4 %collective-permute-done.1.r2a = bf16[32,4096]{1,0:T(8,128)(2,1)S(1)} collective-permute-done((bf16[32,4096]{1,0:T(8,128)(2,1)S(1)}, bf16[32,4096]{1,0:T(8,128)(2,1)S(1)}, u32[]{:S(2)}, u32[]{:S(2)}) %collective-permute-start.1) | collective-permute-done | bytes 262176 | tf_op jit(solution)/shard_map/ppermute | solution.py:35
  66.1 1.2 collective-permute-done.3.r2b
  67.3 0.0 copy-done.2
  67.3 4.7 %split.1 = (bf16[128,4096]{1,0:T(8,128)(2,1)}, bf16[4,2,128,512]{3,2,1,0:T(8,128)(2,1)}) custom-call(s32[3]{0:T(128)S(1)} %pad_add_fusion.where, bf16[64,64]{1,0:T(8,128)(2,1)S(1)} %copy-done.2, bf16[64,4096]{1,0:T(8,128)(2,1)S(1)} %bitcast.11, bf16[64,4096]{1,0:T(8,128)(2,1)S(1)} %collective-permute-done.r1, ...), custom_call_target="tpu_custom_call" | custom-call | tf_op jit(solution)/shard_map/split/pallas_call | solution.py:59
  72.0 0.0 collective-permute-done.4.mw.refs_4_.refs_5_
  72.0 0.0 all-gather.5.cloned.1.call-done
  72.0 1.9 %collective-permute-start.6 = (bf16[4096,256]{1,0:T(8,128)(2,1)}, bf16[4096,256]{1,0:T(8,128)(2,1)S(1)}, u32[]{:S(2)}, u32[]{:S(2)}) collective-permute-start(bf16[4096,256]{1,0:T(8,128)(2,1)} %collective-permute-done.4.mw.refs_4_.refs_5_), channel_id=1, source_target_pairs={{0,64},{64,0},{1,65},{65,1},{2,66},{66,2},{3,67},{67,3},{4,68},{68... | collective-permute-start | bytes 6291464 | tf_op jit(solution)/shard_map/ppermute | solution.py:30
  74.0 2.4 %collective-permute-start.5 = (bf16[4,512,512]{2,1,0:T(8,128)(2,1)}, bf16[4,512,512]{2,1,0:T(8,128)(2,1)}, u32[]{:S(2)}, u32[]{:S(2)}) collective-permute-start(bf16[4,512,512]{2,1,0:T(8,128)(2,1)} %bitcast.14), channel_id=1, source_target_pairs={{0,64},{64,0},{1,65},{65,1},{2,66},{66,2},{3,67},{67,3},{4,68},{68... | collective-permute-start | bytes 6291464 | tf_op jit(solution)/shard_map/ppermute | solution.py:30
  76.4 6.5 %all-to-all-start.2 = ((bf16[4,2,128,512]{3,2,1,0:T(8,128)(2,1)}), bf16[4,2,128,512]{3,2,1,0:T(8,128)(2,1)S(1)}, u32[]{:S(2)}, u32[]{:S(2)}) async-start(bf16[4,2,128,512]{3,2,1,0:T(8,128)(2,1)} %get-tuple-element.18.cot), calls=%async_computation.2 | async-start | bytes 2097152 | tf_op jit(solution)/shard_map/all_to_all | solution.py:270
  82.9 0.0 all-gather.7.cloned.1.call-start
  82.9 0.0 collective-permute-done.6.ow.refs_6_.refs_7_
  82.9 6.0 %gates.1 = (bf16[128,512]{1,0:T(8,128)(2,1)}, f32[128,1024]{1,0:T(8,128)}) custom-call(s32[3]{0:T(128)S(1)} %pad_add_fusion.where, bf16[128,4096]{1,0:T(8,128)(2,1)} %get-tuple-element.22.tok, bf16[4096,256]{1,0:T(8,128)(2,1)} %refs_1_.1, bf16[4096,256]{1,0:T(8,128)(2,1)} %refs_3_.1, bf16[4096,256]{1,0:T(8,128)(2,1)} %collective-permute-done.4.mw.refs_4_.refs_5_, ...), custom_call_target="tpu_custom_call" | custom-call | tf_op jit(solution)/shard_map/gates/pallas_call | solution.py:123
  89.0 0.0 all-gather.7.cloned.1.call-update
  89.0 0.0 collective-permute-done.5.df
  89.0 0.0 copy-start.1
  89.0 4.4 %down.1.dd = bf16[128,1024]{1,0:T(8,128)(2,1)S(1)} custom-call(s32[3]{0:T(128)S(1)} %pad_add_fusion.where, bf16[4,2,128,512]{3,2,1,0:T(8,128)(2,1)} %get-tuple-element.18.cot, bf16[4,512,512]{2,1,0:T(8,128)(2,1)} %bitcast.15, bf16[4,512,512]{2,1,0:T(8,128)(2,1)} %collective-permute-done.5.df, f32[128,1024]{1,0:T(8,128)} %get-tuple-element.24.fac), custom_call_target="tpu_custom_call" | custom-call | tf_op jit(solution)/shard_map/down/pallas_call | solution.py:166
  93.4 0.0 copy-done.1
  93.5 6.6 %term.1 = bf16[4,64,2048]{2,1,0:T(8,128)(2,1)} custom-call(s32[3]{0:T(128)S(1)} %pad_add_fusion.where, bf16[256,256]{1,0:T(8,128)(2,1)S(1)} %copy-done.1, bf16[128,1024]{1,0:T(8,128)(2,1)S(1)} %down.1.dd, bf16[4096,256]{1,0:T(8,128)(2,1)} %refs_1_.1, bf16[4096,256]{1,0:T(8,128)(2,1)} %refs_1_.1, bf16[4096,256]{1,0:T(8,128)(2,1)} %refs_3_.1, ...), custom_call_target="tpu_custom_call" | custom-call | tf_op jit(solution)/shard_map/term/pallas_call | solution.py:199
  100.0 6.5 %all-to-all-done.2.cn = bf16[4,2,128,512]{3,2,1,0:T(8,128)(2,1)S(1)} async-done(((bf16[4,2,128,512]{3,2,1,0:T(8,128)(2,1)}), bf16[4,2,128,512]{3,2,1,0:T(8,128)(2,1)S(1)}, u32[]{:S(2)}, u32[]{:S(2)}) %all-to-all-start.2) | async-done | bytes 1048608 | tf_op jit(solution)/shard_map/all_to_all | solution.py:270
  106.6 9.6 %all-to-all-start.1 = ((bf16[32,8,2048]{2,1,0:T(8,128)(2,1)}), bf16[32,8,2048]{2,1,0:T(8,128)(2,1)S(1)}, u32[]{:S(2)}, u32[]{:S(2)}) async-start(bf16[32,8,2048]{2,1,0:T(8,128)(2,1)} %bitcast.13), calls=%async_computation.1 | async-start | bytes 2097152 | tf_op jit(solution)/shard_map/all_to_all | solution.py:278
  116.2 5.8 %all-gather.7.cloned.1.call-done = bf16[1024,512]{1,0:T(8,128)(2,1)} async-done(((bf16[128,512]{1,0:T(8,128)(2,1)}), bf16[1024,512]{1,0:T(8,128)(2,1)}) %all-gather.7.cloned.1.call-update) | async-done | bytes 1048592 | tf_op jit(solution)/shard_map/all_gather | solution.py:274
  122.0 2.1 %collective-permute-start.7 = (bf16[4,128,512]{2,1,0:T(8,128)(2,1)S(1)}, bf16[4,128,512]{2,1,0:T(8,128)(2,1)S(1)}, u32[]{:S(2)}, u32[]{:S(2)}) collective-permute-start(bf16[4,128,512]{2,1,0:T(8,128)(2,1)S(1)} %slice_bitcast_fusion), channel_id=1, source_target_pairs={{0,64},{64,0},{1,65},{65,1},{2,66},{66,2},{3,67},{67,3},{4,68},{68... | collective-permute-start | bytes 1572872 | tf_op jit(solution)/shard_map/ppermute | solution.py:30
  124.1 1.7 %collective-permute-done.7.cf = bf16[4,128,512]{2,1,0:T(8,128)(2,1)S(1)} collective-permute-done((bf16[4,128,512]{2,1,0:T(8,128)(2,1)S(1)}, bf16[4,128,512]{2,1,0:T(8,128)(2,1)S(1)}, u32[]{:S(2)}, u32[]{:S(2)}) %collective-permute-start.7) | collective-permute-done | bytes 524320 | tf_op jit(solution)/shard_map/ppermute | solution.py:30
  125.8 0.0 copy-start
  125.8 1.2 copy-done
  127.0 1.8 %grads.1 = (f32[256,512]{1,0:T(8,128)S(1)}, bf16[256,512]{1,0:T(8,128)(2,1)S(1)}) custom-call(s32[3]{0:T(128)S(1)} %pad_add_fusion.where, bf16[4,2,128,512]{3,2,1,0:T(8,128)(2,1)S(1)} %bitcast.12, bf16[4,2,128,512]{3,2,1,0:T(8,128)(2,1)S(1)} %all-to-all-done.2.cn, bf16[4,128,512]{2,1,0:T(8,128)(2,1)S(1)} %collective-permute-done.7.cf), custom_call_target="tpu_custom_call" | custom-call | tf_op jit(solution)/shard_map/grads/pallas_call | solution.py:228
  128.9 2.7 %collective-permute-start.8 = (bf16[256,512]{1,0:T(8,128)(2,1)S(1)}, bf16[256,512]{1,0:T(8,128)(2,1)S(1)}, u32[]{:S(2)}, u32[]{:S(2)}) collective-permute-start(bf16[256,512]{1,0:T(8,128)(2,1)S(1)} %get-tuple-element.28), channel_id=1, source_target_pairs={{0,32},{32,0},{1,33},{33,1},{2,34},{34,2},{3,35},{35,3},{4,36},{36... | collective-permute-start | bytes 786440 | tf_op jit(solution)/shard_map/ppermute | solution.py:30
  131.5 13.3 %all-to-all-done.1 = bf16[32,8,2048]{2,1,0:T(8,128)(2,1)S(1)} async-done(((bf16[32,8,2048]{2,1,0:T(8,128)(2,1)}), bf16[32,8,2048]{2,1,0:T(8,128)(2,1)S(1)}, u32[]{:S(2)}, u32[]{:S(2)}) %all-to-all-start.1) | async-done | bytes 1048608 | tf_op jit(solution)/shard_map/all_to_all | solution.py:278
  144.8 0.0 collective-permute-done.8
  144.8 0.2 reduce_sum.12
  145.0 0.6 pad_maximum_fusion.1
  145.6 0.9 convert_add_fusion
  (6 shorter events, 0.2 us)
Async XLA Ops:
  7.2 64.9 %all-gather.5.cloned.1.call-start = ((), (), s32[]{:S(2)}) async-start(), calls=%async_computation.3 | async-start | bytes 2359296 | tf_op jit(solution)/shard_map/all_gather | solution.py:262
  7.9 5.2 %copy-start.3 = (bf16[4,4096]{1,0:T(4,128)(2,1)S(1)}, bf16[4,4096]{1,0:T(4,128)(2,1)}, u32[]{:S(2)}) copy-start(bf16[4,4096]{1,0:T(4,128)(2,1)} %param.8) | copy-start | bytes 98308
  7.9 5.2 %copy-start.4 = (bf16[4,4096]{1,0:T(4,128)(2,1)S(1)}, bf16[4,4096]{1,0:T(4,128)(2,1)}, u32[]{:S(2)}) copy-start(bf16[4,4096]{1,0:T(4,128)(2,1)} %param.7) | copy-start | bytes 98308
  11.1 56.2 %copy-start.2 = (bf16[64,64]{1,0:T(8,128)(2,1)S(1)}, bf16[64,64]{1,0:T(8,128)(2,1)}, u32[]{:S(2)}) copy-start(bf16[64,64]{1,0:T(8,128)(2,1)} %constant.23.clone.pick) | copy-start | bytes 24580
  11.1 60.9 %collective-permute-start.4 = (bf16[4096,256]{1,0:T(8,128)(2,1)}, bf16[4096,256]{1,0:T(8,128)(2,1)}, u32[]{:S(2)}, u32[]{:S(2)}) collective-permute-start(bf16[4096,256]{1,0:T(8,128)(2,1)} %broadcast_select_fusion), channel_id=1, source_target_pairs={{0,32},{32,0},{96,192},{192,96},{128,160},{160,128},{224,320},{320... | collective-permute-start | bytes 6291464 | tf_op jit(solution)/shard_map/ppermute | solution.py:44
  38.4 17.0 %collective-permute-start = (bf16[64,4096]{1,0:T(8,128)(2,1)S(1)}, bf16[64,4096]{1,0:T(8,128)(2,1)S(1)}, u32[]{:S(2)}, u32[]{:S(2)}) collective-permute-start(bf16[64,4096]{1,0:T(8,128)(2,1)S(1)} %bitcast.9), channel_id=1, source_target_pairs={{0,1},{1,2},{2,3},{3,0},{4,5},{5,6},{6,7},{7,4},{8,9},{9,10},{10,1... | collective-permute-start | bytes 1572872 | tf_op jit(solution)/shard_map/ppermute | solution.py:35
  40.4 17.1 %collective-permute-start.2 = (bf16[64,4096]{1,0:T(8,128)(2,1)S(1)}, bf16[64,4096]{1,0:T(8,128)(2,1)S(1)}, u32[]{:S(2)}, u32[]{:S(2)}) collective-permute-start(bf16[64,4096]{1,0:T(8,128)(2,1)S(1)} %bitcast.10), channel_id=1, source_target_pairs={{0,3},{1,0},{2,1},{3,2},{4,7},{5,4},{6,5},{7,6},{8,11},{9,8},{10,9... | collective-permute-start | bytes 1572872 | tf_op jit(solution)/shard_map/ppermute | solution.py:35
  55.5 10.6 %collective-permute-start.1 = (bf16[32,4096]{1,0:T(8,128)(2,1)S(1)}, bf16[32,4096]{1,0:T(8,128)(2,1)S(1)}, u32[]{:S(2)}, u32[]{:S(2)}) collective-permute-start(bf16[32,4096]{1,0:T(8,128)(2,1)S(1)} %slice.20), channel_id=1, source_target_pairs={{0,1},{1,2},{2,3},{3,0},{4,5},{5,6},{6,7},{7,4},{8,9},{9,10},{10,1... | collective-permute-start | bytes 786440 | tf_op jit(solution)/shard_map/ppermute | solution.py:35
  57.5 9.8 %collective-permute-start.3 = (bf16[32,4096]{1,0:T(8,128)(2,1)S(1)}, bf16[32,4096]{1,0:T(8,128)(2,1)S(1)}, u32[]{:S(2)}, u32[]{:S(2)}) collective-permute-start(bf16[32,4096]{1,0:T(8,128)(2,1)S(1)} %slice.21), channel_id=1, source_target_pairs={{0,3},{1,0},{2,1},{3,2},{4,7},{5,4},{6,5},{7,6},{8,11},{9,8},{10,9... | collective-permute-start | bytes 786440 | tf_op jit(solution)/shard_map/ppermute | solution.py:35
  72.0 10.9 %collective-permute-start.6 = (bf16[4096,256]{1,0:T(8,128)(2,1)}, bf16[4096,256]{1,0:T(8,128)(2,1)S(1)}, u32[]{:S(2)}, u32[]{:S(2)}) collective-permute-start(bf16[4096,256]{1,0:T(8,128)(2,1)} %collective-permute-done.4.mw.refs_4_.refs_5_), channel_id=1, source_target_pairs={{0,64},{64,0},{1,65},{65,1},{2,66},{66,2},{3,67},{67,3},{4,68},{68... | collective-permute-start | bytes 6291464 | tf_op jit(solution)/shard_map/ppermute | solution.py:30
  74.0 15.0 %collective-permute-start.5 = (bf16[4,512,512]{2,1,0:T(8,128)(2,1)}, bf16[4,512,512]{2,1,0:T(8,128)(2,1)}, u32[]{:S(2)}, u32[]{:S(2)}) collective-permute-start(bf16[4,512,512]{2,1,0:T(8,128)(2,1)} %bitcast.14), channel_id=1, source_target_pairs={{0,64},{64,0},{1,65},{65,1},{2,66},{66,2},{3,67},{67,3},{4,68},{68... | collective-permute-start | bytes 6291464 | tf_op jit(solution)/shard_map/ppermute | solution.py:30
  76.4 30.2 %all-to-all-start.2 = ((bf16[4,2,128,512]{3,2,1,0:T(8,128)(2,1)}), bf16[4,2,128,512]{3,2,1,0:T(8,128)(2,1)S(1)}, u32[]{:S(2)}, u32[]{:S(2)}) async-start(bf16[4,2,128,512]{3,2,1,0:T(8,128)(2,1)} %get-tuple-element.18.cot), calls=%async_computation.2 | async-start | bytes 2097152 | tf_op jit(solution)/shard_map/all_to_all | solution.py:270
  82.9 39.0 %all-gather.7.cloned.1.call-start = ((), (), s32[]{:S(2)}) async-start(), calls=%async_computation.4 | async-start | bytes 1179648 | tf_op jit(solution)/shard_map/all_gather | solution.py:274
  89.0 4.5 %copy-start.1 = (bf16[256,256]{1,0:T(8,128)(2,1)S(1)}, bf16[256,256]{1,0:T(8,128)(2,1)}, u32[]{:S(2)}) copy-start(bf16[256,256]{1,0:T(8,128)(2,1)} %constant.24.clone.pick) | copy-start | bytes 393220
  106.6 38.3 %all-to-all-start.1 = ((bf16[32,8,2048]{2,1,0:T(8,128)(2,1)}), bf16[32,8,2048]{2,1,0:T(8,128)(2,1)S(1)}, u32[]{:S(2)}, u32[]{:S(2)}) async-start(bf16[32,8,2048]{2,1,0:T(8,128)(2,1)} %bitcast.13), calls=%async_computation.1 | async-start | bytes 2097152 | tf_op jit(solution)/shard_map/all_to_all | solution.py:278
  122.0 3.8 %collective-permute-start.7 = (bf16[4,128,512]{2,1,0:T(8,128)(2,1)S(1)}, bf16[4,128,512]{2,1,0:T(8,128)(2,1)S(1)}, u32[]{:S(2)}, u32[]{:S(2)}) collective-permute-start(bf16[4,128,512]{2,1,0:T(8,128)(2,1)S(1)} %slice_bitcast_fusion), channel_id=1, source_target_pairs={{0,64},{64,0},{1,65},{65,1},{2,66},{66,2},{3,67},{67,3},{4,68},{68... | collective-permute-start | bytes 1572872 | tf_op jit(solution)/shard_map/ppermute | solution.py:30
  125.8 1.2 copy-start
  128.9 16.0 %collective-permute-start.8 = (bf16[256,512]{1,0:T(8,128)(2,1)S(1)}, bf16[256,512]{1,0:T(8,128)(2,1)S(1)}, u32[]{:S(2)}, u32[]{:S(2)}) collective-permute-start(bf16[256,512]{1,0:T(8,128)(2,1)S(1)} %get-tuple-element.28), channel_id=1, source_target_pairs={{0,32},{32,0},{1,33},{33,1},{2,34},{34,2},{3,35},{35,3},{4,36},{36... | collective-permute-start | bytes 786440 | tf_op jit(solution)/shard_map/ppermute | solution.py:30
Sparse Core Ops, SparseCore 0:
  10.1 51.3 all-gather.4
  89.1 32.8 all-gather.6

commit v16 on v15

--- a/solution.py
+++ b/solution.py
@@ -256,12 +256,15 @@
     core = lax.axis_index("c")
     where = jnp.stack([core, lax.axis_index("zl"), lax.axis_index("x")]).astype(jnp.int32)
 
+    block = jnp.concatenate([tokens, cotangent], axis=0)
+    block = jnp.broadcast_to(block[None], (NY, 2 * ROWS, D))
+    block, core = lax.optimization_barrier((block, core))
     picked = jnp.where(core == 0, gate_weight, up_weight)
-    picked, tokens = lax.optimization_barrier((picked, tokens))
+    down_near = lax.all_gather(down_weight, ("zh", "zl"), axis=0).reshape(NZ, 2 * HID, FEATS)
+
+    block = lax.all_to_all(block, "y", 0, 0).reshape(PIECE, D)
+    block, picked = lax.optimization_barrier((block, picked))
     mine = neighbours(picked)
-    down_near = lax.all_gather(down_weight, ("zh", "zl"), axis=0).reshape(NZ, 2 * HID, FEATS)
-
-    block = spread(jnp.concatenate([tokens, cotangent], axis=0), "y").reshape(PIECE, D)
     left, right = shift(block, "x", 1), shift(block, "x", -1)
     n = PIECE // 2
     pieces = (block, left, shift(left[:n], "x", 1), shift(right[n:], "x", -1), right)

time: 154 us -> 159 us (1.032)
  the two profiles are of different devices: /device:TPU:72 before, /device:TPU:64 now
where the time goes in v16:
time: 159 us; the launch traced here: 158 us
  waiting for transfers between devices  68.2 us (43%)
  starting transfers between devices  44.3 us (28%)
  Pallas kernels  23.6 us (15%)
  between operations  14.2 us (9%)
  other arithmetic  5.71 us (4%)
  local copies, waits for them, and re-layouts  2.15 us (1%)
    ppermute x4, waiting for transfers between devices, shift(): return lax.ppermute(value, axis, [(i, (i + k) % n) for i in range(n)])  16.3 us
    all_to_all x1, waiting for transfers between devices, on_device(): lax.all_to_all(parts.reshape(NX * NY, 2 * ROWS, D // 2), ('x', 'y'), 0, 0)  15.2 us
    all_to_all x1, waiting for transfers between devices, on_device(): block = lax.all_to_all(block, 'y', 0, 0).reshape(PIECE, D)  14.3 us
    ppermute x4, starting transfers between devices, shift(): return lax.ppermute(value, axis, [(i, (i + k) % n) for i in range(n)])  14.1 us
    all_to_all x1, waiting for transfers between devices, on_device(): cot_near = lax.all_to_all(cot, 'zh', 0, 0)  13.1 us
    ppermute x4, starting transfers between devices, swap(): return lax.ppermute(value, axis, [(0, 1), (1, 0)])  9.19 us
    all_to_all x1, starting transfers between devices, on_device(): block = lax.all_to_all(block, 'y', 0, 0).reshape(PIECE, D)  7.1 us
    pallas_call x1, Pallas kernels, term(): pl.pallas_call(term_body, grid_spec=pltpu.PrefetchScalarGridSpec(num_scal...  6.59 us
  transfers between devices with their start and end apart: 14, of which 10 were waited for; matrix products, arithmetic and copies ran while one was open for 3% of the time, Pallas kernels for 15%

profile of v16, /device:TPU:64, one launch (start us, length us, event | category | flops | bytes accessed | tf_op | source)
XLA Modules:
  0.0 158.1 jit_solution(14713506244085167864)
XLA Ops:
  7.2 0.0 all-gather.5.cloned.1.call-start
  7.2 0.7 all-gather.5.cloned.1.call-update
  7.9 0.8 pad_maximum_fusion
  8.7 0.8 broadcast_in_dim.2
  9.5 7.1 %all-to-all-start = ((bf16[8,8,4096]{2,1,0:T(8,128)(2,1)}), bf16[8,8,4096]{2,1,0:T(8,128)(2,1)S(1)}, u32[]{:S(2)}, u32[]{:S(2)}) async-start(bf16[8,8,4096]{2,1,0:T(8,128)(2,1)} %broadcast_in_dim.2), calls=%async_computation | async-start | bytes 1048576 | tf_op jit(solution)/shard_map/all_to_all | solution.py:265
  16.6 0.0 copy-start.2
  16.7 3.2 %broadcast_select_fusion = bf16[4096,256]{1,0:T(8,128)(2,1)} fusion(bf16[4096,256]{1,0:T(8,128)(2,1)} %refs_1_.1, bf16[4096,256]{1,0:T(8,128)(2,1)} %refs_3_.1, pred[]{:T(512)S(6)} %eq.3), kind=kLoop, calls=%fused_computation | loop fusion | flops 1048576 | bytes 6291457 | tf_op jit(solution)/shard_map/jit(_where)/select_n | solution.py:262
  19.8 14.3 %all-to-all-done = bf16[8,8,4096]{2,1,0:T(8,128)(2,1)S(1)} async-done(((bf16[8,8,4096]{2,1,0:T(8,128)(2,1)}), bf16[8,8,4096]{2,1,0:T(8,128)(2,1)S(1)}, u32[]{:S(2)}, u32[]{:S(2)}) %all-to-all-start) | async-done | bytes 524320 | tf_op jit(solution)/shard_map/all_to_all | solution.py:265
  34.1 1.9 %collective-permute-start.4 = (bf16[4096,256]{1,0:T(8,128)(2,1)}, bf16[4096,256]{1,0:T(8,128)(2,1)}, u32[]{:S(2)}, u32[]{:S(2)}) collective-permute-start(bf16[4096,256]{1,0:T(8,128)(2,1)} %broadcast_select_fusion), channel_id=1, source_target_pairs={{0,32},{32,0},{96,192},{192,96},{128,160},{160,128},{224,320},{320... | collective-permute-start | bytes 6291464 | tf_op jit(solution)/shard_map/ppermute | solution.py:44
  36.1 3.4 %collective-permute-start = (bf16[64,4096]{1,0:T(8,128)(2,1)S(1)}, bf16[64,4096]{1,0:T(8,128)(2,1)S(1)}, u32[]{:S(2)}, u32[]{:S(2)}) collective-permute-start(bf16[64,4096]{1,0:T(8,128)(2,1)S(1)} %bitcast.9), channel_id=1, source_target_pairs={{0,1},{1,2},{2,3},{3,0},{4,5},{5,6},{6,7},{7,4},{8,9},{9,10},{10,1... | collective-permute-start | bytes 1572872 | tf_op jit(solution)/shard_map/ppermute | solution.py:35
  39.5 3.7 %collective-permute-start.2 = (bf16[64,4096]{1,0:T(8,128)(2,1)S(1)}, bf16[64,4096]{1,0:T(8,128)(2,1)S(1)}, u32[]{:S(2)}, u32[]{:S(2)}) collective-permute-start(bf16[64,4096]{1,0:T(8,128)(2,1)S(1)} %bitcast.10), channel_id=1, source_target_pairs={{0,3},{1,0},{2,1},{3,2},{4,7},{5,4},{6,5},{7,6},{8,11},{9,8},{10,9... | collective-permute-start | bytes 1572872 | tf_op jit(solution)/shard_map/ppermute | solution.py:35
  43.1 9.7 %collective-permute-done.r1 = bf16[64,4096]{1,0:T(8,128)(2,1)S(1)} collective-permute-done((bf16[64,4096]{1,0:T(8,128)(2,1)S(1)}, bf16[64,4096]{1,0:T(8,128)(2,1)S(1)}, u32[]{:S(2)}, u32[]{:S(2)}) %collective-permute-start) | collective-permute-done | bytes 524320 | tf_op jit(solution)/shard_map/ppermute | solution.py:35
  52.8 2.2 %collective-permute-start.1 = (bf16[32,4096]{1,0:T(8,128)(2,1)S(1)}, bf16[32,4096]{1,0:T(8,128)(2,1)S(1)}, u32[]{:S(2)}, u32[]{:S(2)}) collective-permute-start(bf16[32,4096]{1,0:T(8,128)(2,1)S(1)} %slice.20), channel_id=1, source_target_pairs={{0,1},{1,2},{2,3},{3,0},{4,5},{5,6},{6,7},{7,4},{8,9},{9,10},{10,1... | collective-permute-start | bytes 786440 | tf_op jit(solution)/shard_map/ppermute | solution.py:35
  55.0 0.3 collective-permute-done.2.r3
  55.4 4.9 %collective-permute-start.3 = (bf16[32,4096]{1,0:T(8,128)(2,1)S(1)}, bf16[32,4096]{1,0:T(8,128)(2,1)S(1)}, u32[]{:S(2)}, u32[]{:S(2)}) collective-permute-start(bf16[32,4096]{1,0:T(8,128)(2,1)S(1)} %slice.21), channel_id=1, source_target_pairs={{0,3},{1,0},{2,1},{3,2},{4,7},{5,4},{6,5},{7,6},{8,11},{9,8},{10,9... | collective-permute-start | bytes 786440 | tf_op jit(solution)/shard_map/ppermute | solution.py:35
  60.2 0.1 pad_add_fusion.where
  60.3 4.8 %collective-permute-done.1.r2a = bf16[32,4096]{1,0:T(8,128)(2,1)S(1)} collective-permute-done((bf16[32,4096]{1,0:T(8,128)(2,1)S(1)}, bf16[32,4096]{1,0:T(8,128)(2,1)S(1)}, u32[]{:S(2)}, u32[]{:S(2)}) %collective-permute-start.1) | collective-permute-done | bytes 262176 | tf_op jit(solution)/shard_map/ppermute | solution.py:35
  65.1 1.5 collective-permute-done.3.r2b
  66.6 0.0 copy-done.2
  66.6 4.7 %split.1 = (bf16[128,4096]{1,0:T(8,128)(2,1)}, bf16[4,2,128,512]{3,2,1,0:T(8,128)(2,1)}) custom-call(s32[3]{0:T(128)S(1)} %pad_add_fusion.where, bf16[64,64]{1,0:T(8,128)(2,1)S(1)} %copy-done.2, bf16[64,4096]{1,0:T(8,128)(2,1)S(1)} %bitcast.11, bf16[64,4096]{1,0:T(8,128)(2,1)S(1)} %collective-permute-done.r1, ...), custom_call_target="tpu_custom_call" | custom-call | tf_op jit(solution)/shard_map/split/pallas_call | solution.py:59
  71.3 3.7 %collective-permute-done.4.mw.refs_4_.refs_5_ = bf16[4096,256]{1,0:T(8,128)(2,1)} collective-permute-done((bf16[4096,256]{1,0:T(8,128)(2,1)}, bf16[4096,256]{1,0:T(8,128)(2,1)}, u32[]{:S(2)}, u32[]{:S(2)}) %collective-permute-start.4) | collective-permute-done | bytes 2097184 | tf_op jit(solution)/shard_map/ppermute | solution.py:44
  75.0 0.0 all-gather.5.cloned.1.call-done
  75.0 2.1 %collective-permute-start.6 = (bf16[4096,256]{1,0:T(8,128)(2,1)}, bf16[4096,256]{1,0:T(8,128)(2,1)S(1)}, u32[]{:S(2)}, u32[]{:S(2)}) collective-permute-start(bf16[4096,256]{1,0:T(8,128)(2,1)} %collective-permute-done.4.mw.refs_4_.refs_5_), channel_id=1, source_target_pairs={{0,64},{64,0},{1,65},{65,1},{2,66},{66,2},{3,67},{67,3},{4,68},{68... | collective-permute-start | bytes 6291464 | tf_op jit(solution)/shard_map/ppermute | solution.py:30
  77.1 2.2 %collective-permute-start.5 = (bf16[4,512,512]{2,1,0:T(8,128)(2,1)}, bf16[4,512,512]{2,1,0:T(8,128)(2,1)}, u32[]{:S(2)}, u32[]{:S(2)}) collective-permute-start(bf16[4,512,512]{2,1,0:T(8,128)(2,1)} %bitcast.14), channel_id=1, source_target_pairs={{0,64},{64,0},{1,65},{65,1},{2,66},{66,2},{3,67},{67,3},{4,68},{68... | collective-permute-start | bytes 6291464 | tf_op jit(solution)/shard_map/ppermute | solution.py:30
  79.4 5.6 %all-to-all-start.2 = ((bf16[4,2,128,512]{3,2,1,0:T(8,128)(2,1)}), bf16[4,2,128,512]{3,2,1,0:T(8,128)(2,1)S(1)}, u32[]{:S(2)}, u32[]{:S(2)}) async-start(bf16[4,2,128,512]{3,2,1,0:T(8,128)(2,1)} %get-tuple-element.22.cot), calls=%async_computation.2 | async-start | bytes 2097152 | tf_op jit(solution)/shard_map/all_to_all | solution.py:273
  85.0 0.0 all-gather.7.cloned.1.call-start
  85.0 0.0 collective-permute-done.6.ow.refs_6_.refs_7_
  85.0 6.0 %gates.1 = (bf16[128,512]{1,0:T(8,128)(2,1)}, f32[128,1024]{1,0:T(8,128)}) custom-call(s32[3]{0:T(128)S(1)} %pad_add_fusion.where, bf16[128,4096]{1,0:T(8,128)(2,1)} %get-tuple-element.26.tok, bf16[4096,256]{1,0:T(8,128)(2,1)} %refs_1_.1, bf16[4096,256]{1,0:T(8,128)(2,1)} %refs_3_.1, bf16[4096,256]{1,0:T(8,128)(2,1)} %collective-permute-done.4.mw.refs_4_.refs_5_, ...), custom_call_target="tpu_custom_call" | custom-call | tf_op jit(solution)/shard_map/gates/pallas_call | solution.py:123
  91.0 0.0 all-gather.7.cloned.1.call-update
  91.1 0.0 collective-permute-done.5.df
  91.1 0.0 copy-start.1
  91.1 4.4 %down.1.dd = bf16[128,1024]{1,0:T(8,128)(2,1)S(1)} custom-call(s32[3]{0:T(128)S(1)} %pad_add_fusion.where, bf16[4,2,128,512]{3,2,1,0:T(8,128)(2,1)} %get-tuple-element.22.cot, bf16[4,512,512]{2,1,0:T(8,128)(2,1)} %bitcast.15, bf16[4,512,512]{2,1,0:T(8,128)(2,1)} %collective-permute-done.5.df, f32[128,1024]{1,0:T(8,128)} %get-tuple-element.28.fac), custom_call_target="tpu_custom_call" | custom-call | tf_op jit(solution)/shard_map/down/pallas_call | solution.py:166
  95.5 0.0 copy-done.1
  95.5 6.6 %term.1 = bf16[4,64,2048]{2,1,0:T(8,128)(2,1)} custom-call(s32[3]{0:T(128)S(1)} %pad_add_fusion.where, bf16[256,256]{1,0:T(8,128)(2,1)S(1)} %copy-done.1, bf16[128,1024]{1,0:T(8,128)(2,1)S(1)} %down.1.dd, bf16[4096,256]{1,0:T(8,128)(2,1)} %refs_1_.1, bf16[4096,256]{1,0:T(8,128)(2,1)} %refs_1_.1, bf16[4096,256]{1,0:T(8,128)(2,1)} %refs_3_.1, ...), custom_call_target="tpu_custom_call" | custom-call | tf_op jit(solution)/shard_map/term/pallas_call | solution.py:199
  102.1 13.1 %all-to-all-done.2.cn = bf16[4,2,128,512]{3,2,1,0:T(8,128)(2,1)S(1)} async-done(((bf16[4,2,128,512]{3,2,1,0:T(8,128)(2,1)}), bf16[4,2,128,512]{3,2,1,0:T(8,128)(2,1)S(1)}, u32[]{:S(2)}, u32[]{:S(2)}) %all-to-all-start.2) | async-done | bytes 1048608 | tf_op jit(solution)/shard_map/all_to_all | solution.py:273
  115.2 6.3 %all-to-all-start.1 = ((bf16[32,8,2048]{2,1,0:T(8,128)(2,1)}), bf16[32,8,2048]{2,1,0:T(8,128)(2,1)S(1)}, u32[]{:S(2)}, u32[]{:S(2)}) async-start(bf16[32,8,2048]{2,1,0:T(8,128)(2,1)} %bitcast.13), calls=%async_computation.1 | async-start | bytes 2097152 | tf_op jit(solution)/shard_map/all_to_all | solution.py:281
  121.5 3.3 %all-gather.7.cloned.1.call-done = bf16[1024,512]{1,0:T(8,128)(2,1)} async-done(((bf16[128,512]{1,0:T(8,128)(2,1)}), bf16[1024,512]{1,0:T(8,128)(2,1)}) %all-gather.7.cloned.1.call-update) | async-done | bytes 1048592 | tf_op jit(solution)/shard_map/all_gather | solution.py:277
  124.8 2.1 %collective-permute-start.7 = (bf16[4,128,512]{2,1,0:T(8,128)(2,1)S(1)}, bf16[4,128,512]{2,1,0:T(8,128)(2,1)S(1)}, u32[]{:S(2)}, u32[]{:S(2)}) collective-permute-start(bf16[4,128,512]{2,1,0:T(8,128)(2,1)S(1)} %slice_bitcast_fusion), channel_id=1, source_target_pairs={{0,64},{64,0},{1,65},{65,1},{2,66},{66,2},{3,67},{67,3},{4,68},{68... | collective-permute-start | bytes 1572872 | tf_op jit(solution)/shard_map/ppermute | solution.py:30
  127.0 1.7 %collective-permute-done.7.cf = bf16[4,128,512]{2,1,0:T(8,128)(2,1)S(1)} collective-permute-done((bf16[4,128,512]{2,1,0:T(8,128)(2,1)S(1)}, bf16[4,128,512]{2,1,0:T(8,128)(2,1)S(1)}, u32[]{:S(2)}, u32[]{:S(2)}) %collective-permute-start.7) | collective-permute-done | bytes 524320 | tf_op jit(solution)/shard_map/ppermute | solution.py:30
  128.6 0.0 copy-start
  128.6 1.2 copy-done
  129.8 1.8 %grads.1 = (f32[256,512]{1,0:T(8,128)S(1)}, bf16[256,512]{1,0:T(8,128)(2,1)S(1)}) custom-call(s32[3]{0:T(128)S(1)} %pad_add_fusion.where, bf16[4,2,128,512]{3,2,1,0:T(8,128)(2,1)S(1)} %bitcast.12, bf16[4,2,128,512]{3,2,1,0:T(8,128)(2,1)S(1)} %all-to-all-done.2.cn, bf16[4,128,512]{2,1,0:T(8,128)(2,1)S(1)} %collective-permute-done.7.cf), custom_call_target="tpu_custom_call" | custom-call | tf_op jit(solution)/shard_map/grads/pallas_call | solution.py:228
  131.7 2.7 %collective-permute-start.8 = (bf16[256,512]{1,0:T(8,128)(2,1)S(1)}, bf16[256,512]{1,0:T(8,128)(2,1)S(1)}, u32[]{:S(2)}, u32[]{:S(2)}) collective-permute-start(bf16[256,512]{1,0:T(8,128)(2,1)S(1)} %get-tuple-element.32), channel_id=1, source_target_pairs={{0,32},{32,0},{1,33},{33,1},{2,34},{34,2},{3,35},{35,3},{4,36},{36... | collective-permute-start | bytes 786440 | tf_op jit(solution)/shard_map/ppermute | solution.py:30
  134.4 15.2 %all-to-all-done.1 = bf16[32,8,2048]{2,1,0:T(8,128)(2,1)S(1)} async-done(((bf16[32,8,2048]{2,1,0:T(8,128)(2,1)}), bf16[32,8,2048]{2,1,0:T(8,128)(2,1)S(1)}, u32[]{:S(2)}, u32[]{:S(2)}) %all-to-all-start.1) | async-done | bytes 1048608 | tf_op jit(solution)/shard_map/all_to_all | solution.py:281
  149.6 0.0 collective-permute-done.8
  149.6 0.2 reduce_sum.12
  149.8 0.6 pad_maximum_fusion.1
  150.4 0.9 convert_add_fusion
  (4 shorter events, 0.1 us)
Async XLA Ops:
  7.2 67.9 %all-gather.5.cloned.1.call-start = ((), (), s32[]{:S(2)}) async-start(), calls=%async_computation.3 | async-start | bytes 2359296 | tf_op jit(solution)/shard_map/all_gather | solution.py:263
  9.5 24.6 %all-to-all-start = ((bf16[8,8,4096]{2,1,0:T(8,128)(2,1)}), bf16[8,8,4096]{2,1,0:T(8,128)(2,1)S(1)}, u32[]{:S(2)}, u32[]{:S(2)}) async-start(bf16[8,8,4096]{2,1,0:T(8,128)(2,1)} %broadcast_in_dim.2), calls=%async_computation | async-start | bytes 1048576 | tf_op jit(solution)/shard_map/all_to_all | solution.py:265
  16.6 49.9 %copy-start.2 = (bf16[64,64]{1,0:T(8,128)(2,1)S(1)}, bf16[64,64]{1,0:T(8,128)(2,1)}, u32[]{:S(2)}) copy-start(bf16[64,64]{1,0:T(8,128)(2,1)} %constant.23.clone.pick) | copy-start | bytes 24580
  34.1 40.9 %collective-permute-start.4 = (bf16[4096,256]{1,0:T(8,128)(2,1)}, bf16[4096,256]{1,0:T(8,128)(2,1)}, u32[]{:S(2)}, u32[]{:S(2)}) collective-permute-start(bf16[4096,256]{1,0:T(8,128)(2,1)} %broadcast_select_fusion), channel_id=1, source_target_pairs={{0,32},{32,0},{96,192},{192,96},{128,160},{160,128},{224,320},{320... | collective-permute-start | bytes 6291464 | tf_op jit(solution)/shard_map/ppermute | solution.py:44
  36.1 16.8 %collective-permute-start = (bf16[64,4096]{1,0:T(8,128)(2,1)S(1)}, bf16[64,4096]{1,0:T(8,128)(2,1)S(1)}, u32[]{:S(2)}, u32[]{:S(2)}) collective-permute-start(bf16[64,4096]{1,0:T(8,128)(2,1)S(1)} %bitcast.9), channel_id=1, source_target_pairs={{0,1},{1,2},{2,3},{3,0},{4,5},{5,6},{6,7},{7,4},{8,9},{9,10},{10,1... | collective-permute-start | bytes 1572872 | tf_op jit(solution)/shard_map/ppermute | solution.py:35
  39.5 15.9 %collective-permute-start.2 = (bf16[64,4096]{1,0:T(8,128)(2,1)S(1)}, bf16[64,4096]{1,0:T(8,128)(2,1)S(1)}, u32[]{:S(2)}, u32[]{:S(2)}) collective-permute-start(bf16[64,4096]{1,0:T(8,128)(2,1)S(1)} %bitcast.10), channel_id=1, source_target_pairs={{0,3},{1,0},{2,1},{3,2},{4,7},{5,4},{6,5},{7,6},{8,11},{9,8},{10,9... | collective-permute-start | bytes 1572872 | tf_op jit(solution)/shard_map/ppermute | solution.py:35
  52.8 12.3 %collective-permute-start.1 = (bf16[32,4096]{1,0:T(8,128)(2,1)S(1)}, bf16[32,4096]{1,0:T(8,128)(2,1)S(1)}, u32[]{:S(2)}, u32[]{:S(2)}) collective-permute-start(bf16[32,4096]{1,0:T(8,128)(2,1)S(1)} %slice.20), channel_id=1, source_target_pairs={{0,1},{1,2},{2,3},{3,0},{4,5},{5,6},{6,7},{7,4},{8,9},{9,10},{10,1... | collective-permute-start | bytes 786440 | tf_op jit(solution)/shard_map/ppermute | solution.py:35
  55.4 11.2 %collective-permute-start.3 = (bf16[32,4096]{1,0:T(8,128)(2,1)S(1)}, bf16[32,4096]{1,0:T(8,128)(2,1)S(1)}, u32[]{:S(2)}, u32[]{:S(2)}) collective-permute-start(bf16[32,4096]{1,0:T(8,128)(2,1)S(1)} %slice.21), channel_id=1, source_target_pairs={{0,3},{1,0},{2,1},{3,2},{4,7},{5,4},{6,5},{7,6},{8,11},{9,8},{10,9... | collective-permute-start | bytes 786440 | tf_op jit(solution)/shard_map/ppermute | solution.py:35
  75.0 10.0 %collective-permute-start.6 = (bf16[4096,256]{1,0:T(8,128)(2,1)}, bf16[4096,256]{1,0:T(8,128)(2,1)S(1)}, u32[]{:S(2)}, u32[]{:S(2)}) collective-permute-start(bf16[4096,256]{1,0:T(8,128)(2,1)} %collective-permute-done.4.mw.refs_4_.refs_5_), channel_id=1, source_target_pairs={{0,64},{64,0},{1,65},{65,1},{2,66},{66,2},{3,67},{67,3},{4,68},{68... | collective-permute-start | bytes 6291464 | tf_op jit(solution)/shard_map/ppermute | solution.py:30
  77.1 13.9 %collective-permute-start.5 = (bf16[4,512,512]{2,1,0:T(8,128)(2,1)}, bf16[4,512,512]{2,1,0:T(8,128)(2,1)}, u32[]{:S(2)}, u32[]{:S(2)}) collective-permute-start(bf16[4,512,512]{2,1,0:T(8,128)(2,1)} %bitcast.14), channel_id=1, source_target_pairs={{0,64},{64,0},{1,65},{65,1},{2,66},{66,2},{3,67},{67,3},{4,68},{68... | collective-permute-start | bytes 6291464 | tf_op jit(solution)/shard_map/ppermute | solution.py:30
  79.4 35.8 %all-to-all-start.2 = ((bf16[4,2,128,512]{3,2,1,0:T(8,128)(2,1)}), bf16[4,2,128,512]{3,2,1,0:T(8,128)(2,1)S(1)}, u32[]{:S(2)}, u32[]{:S(2)}) async-start(bf16[4,2,128,512]{3,2,1,0:T(8,128)(2,1)} %get-tuple-element.22.cot), calls=%async_computation.2 | async-start | bytes 2097152 | tf_op jit(solution)/shard_map/all_to_all | solution.py:273
  85.0 39.8 %all-gather.7.cloned.1.call-start = ((), (), s32[]{:S(2)}) async-start(), calls=%async_computation.4 | async-start | bytes 1179648 | tf_op jit(solution)/shard_map/all_gather | solution.py:277
  91.1 4.5 %copy-start.1 = (bf16[256,256]{1,0:T(8,128)(2,1)S(1)}, bf16[256,256]{1,0:T(8,128)(2,1)}, u32[]{:S(2)}) copy-start(bf16[256,256]{1,0:T(8,128)(2,1)} %constant.24.clone.pick) | copy-start | bytes 393220
  115.2 34.4 %all-to-all-start.1 = ((bf16[32,8,2048]{2,1,0:T(8,128)(2,1)}), bf16[32,8,2048]{2,1,0:T(8,128)(2,1)S(1)}, u32[]{:S(2)}, u32[]{:S(2)}) async-start(bf16[32,8,2048]{2,1,0:T(8,128)(2,1)} %bitcast.13), calls=%async_computation.1 | async-start | bytes 2097152 | tf_op jit(solution)/shard_map/all_to_all | solution.py:281
  124.8 3.8 %collective-permute-start.7 = (bf16[4,128,512]{2,1,0:T(8,128)(2,1)S(1)}, bf16[4,128,512]{2,1,0:T(8,128)(2,1)S(1)}, u32[]{:S(2)}, u32[]{:S(2)}) collective-permute-start(bf16[4,128,512]{2,1,0:T(8,128)(2,1)S(1)} %slice_bitcast_fusion), channel_id=1, source_target_pairs={{0,64},{64,0},{1,65},{65,1},{2,66},{66,2},{3,67},{67,3},{4,68},{68... | collective-permute-start | bytes 1572872 | tf_op jit(solution)/shard_map/ppermute | solution.py:30
  128.6 1.2 copy-start
  131.7 17.9 %collective-permute-start.8 = (bf16[256,512]{1,0:T(8,128)(2,1)S(1)}, bf16[256,512]{1,0:T(8,128)(2,1)S(1)}, u32[]{:S(2)}, u32[]{:S(2)}) collective-permute-start(bf16[256,512]{1,0:T(8,128)(2,1)S(1)} %get-tuple-element.32), channel_id=1, source_target_pairs={{0,32},{32,0},{1,33},{33,1},{2,34},{34,2},{3,35},{35,3},{4,36},{36... | collective-permute-start | bytes 786440 | tf_op jit(solution)/shard_map/ppermute | solution.py:30
Sparse Core Ops, SparseCore 0:
  10.1 50.4 all-gather.4
  91.2 33.5 all-gather.6

commit v17 on v15

--- a/solution.py
+++ b/solution.py
@@ -50,21 +50,22 @@
     for i, piece in enumerate((r0[...], r1[...], r2, r3[...])):
         rows = contract(pick[...], piece, 1, 0).astype(BF16)
         tok[i * n : (i + 1) * n] = rows[:n]
-        cot[0, 0, i * n : (i + 1) * n] = rows[n:]
+        for k in range(2):
+            cot[0, flip(k, where[0]), i * n : (i + 1) * n] = rows[n:, k * FEATS : (k + 1) * FEATS]
 
 
 def split(where, pieces):
-    piece = pl.BlockSpec((PIECE, FEATS), lambda j, s: (0, j))
-    part = pl.BlockSpec((PIECE // 2, FEATS), lambda j, s: (0, j))
+    piece = pl.BlockSpec((PIECE, 2 * FEATS), lambda j, s: (0, j))
+    part = pl.BlockSpec((PIECE // 2, 2 * FEATS), lambda j, s: (0, j))
     return pl.pallas_call(
         split_body,
         grid_spec=pltpu.PrefetchScalarGridSpec(
             num_scalar_prefetch=1,
-            grid=(STEPS,),
+            grid=(NZ,),
             in_specs=[pl.BlockSpec((PIECE, PIECE), lambda j, s: (0, 0)), piece, piece, part, part, piece],
             out_specs=[
-                pl.BlockSpec((HALF, FEATS), lambda j, s: (0, j)),
-                pl.BlockSpec((1, 1, HALF, FEATS), lambda j, s: (j // 2, flip(j % 2, s[0]), 0, 0)),
+                pl.BlockSpec((HALF, 2 * FEATS), lambda j, s: (0, j)),
+                pl.BlockSpec((1, 2, HALF, FEATS), lambda j, s: (j, 0, 0, 0)),
             ],
         ),
         out_shape=[
@@ -99,7 +100,7 @@
     for i, w in enumerate((gw, uw, mw, ow)):
         acc[:, i * HID : (i + 1) * HID] += contract(t, w[...], 1, 0)
 
-    @pl.when(step == STEPS // 2 - 1)
+    @pl.when(step == STEPS // 4 - 1)
     def _():
         first = where[0] == 0
         pm, po = acc[:, 2 * HID : 3 * HID], acc[:, 3 * HID :]
@@ -119,13 +120,13 @@
 
 
 def gates(where, tok, gw, uw, mw, ow):
-    weight = pl.BlockSpec((2 * FEATS, HID), lambda j, s: (j, 0))
+    weight = pl.BlockSpec((4 * FEATS, HID), lambda j, s: (j, 0))
     return pl.pallas_call(
         gates_body,
         grid_spec=pltpu.PrefetchScalarGridSpec(
             num_scalar_prefetch=1,
-            grid=(STEPS // 2,),
-            in_specs=[pl.BlockSpec((HALF, 2 * FEATS), lambda j, s: (0, j))] + [weight] * 4,
+            grid=(STEPS // 4,),
+            in_specs=[pl.BlockSpec((HALF, 4 * FEATS), lambda j, s: (0, j))] + [weight] * 4,
             out_specs=[
                 pl.BlockSpec((HALF, 2 * HID), lambda j, s: (0, 0)),
                 pl.BlockSpec((HALF, 4 * HID), lambda j, s: (0, 0)),

time: 154 us -> 152 us (0.987)
  Pallas kernels: 23.6 us -> 21.4 us
  transfers between devices with their start and end apart: 13 -> 13, of which waited for: 7 -> 7; matrix products, arithmetic and copies ran while one was open for 2% -> 2% of each run, Pallas kernels for 15% -> 14%
where the time goes in v17:
time: 152 us
  waiting for transfers between devices  43.3 us (28%)
  starting transfers between devices  41.4 us (27%)
  blocking collectives  25.2 us (17%)
  Pallas kernels  21.4 us (14%)
  between operations  14.2 us (9%)
  other arithmetic  4.94 us (3%)
    all_to_all x1, blocking collectives, spread(): lax.all_to_all(jnp.broadcast_to(block[None], (n, *block.shape)), axis, 0, 0)  25.2 us
    ppermute x4, waiting for transfers between devices, shift(): return lax.ppermute(value, axis, [(i, (i + k) % n) for i in range(n)])  14.6 us
    ppermute x4, starting transfers between devices, shift(): return lax.ppermute(value, axis, [(i, (i + k) % n) for i in range(n)])  14.1 us
    all_to_all x1, waiting for transfers between devices, on_device(): lax.all_to_all(parts.reshape(NX * NY, 2 * ROWS, D // 2), ('x', 'y'), 0, 0)  13.8 us
    all_to_all x1, starting transfers between devices, on_device(): lax.all_to_all(parts.reshape(NX * NY, 2 * ROWS, D // 2), ('x', 'y'), 0, 0)  9.56 us
    ppermute x4, starting transfers between devices, swap(): return lax.ppermute(value, axis, [(0, 1), (1, 0)])  9.07 us
    all_to_all x1, waiting for transfers between devices, on_device(): cot_near = lax.all_to_all(cot, 'zh', 0, 0)  7.19 us
    pallas_call x1, Pallas kernels, term(): pl.pallas_call(term_body, grid_spec=pltpu.PrefetchScalarGridSpec(num_scal...  6.6 us
  transfers between devices with their start and end apart: 13, of which 7 were waited for; matrix products, arithmetic and copies ran while one was open for 2% of the time, Pallas kernels for 14%

profile of v17, /device:TPU:72, one launch (start us, length us, event | category | flops | bytes accessed | tf_op | source)
XLA Modules:
  0.0 151.8 jit_solution(11853302446586165874)
XLA Ops:
  7.2 0.0 all-gather.5.cloned.1.call-start
  7.2 0.7 all-gather.5.cloned.1.call-update
  7.9 0.0 copy-start.3
  7.9 0.0 copy-start.4
  7.9 3.2 %broadcast_select_fusion = bf16[4096,256]{1,0:T(8,128)(2,1)} fusion(bf16[4096,256]{1,0:T(8,128)(2,1)} %refs_1_.1, bf16[4096,256]{1,0:T(8,128)(2,1)} %refs_3_.1, pred[]{:T(512)S(6)} %eq.3), kind=kLoop, calls=%fused_computation | loop fusion | flops 1048576 | bytes 6291457 | tf_op jit(solution)/shard_map/jit(_where)/select_n | solution.py:260
  11.1 0.0 copy-start.2
  11.1 2.0 %collective-permute-start.4 = (bf16[4096,256]{1,0:T(8,128)(2,1)}, bf16[4096,256]{1,0:T(8,128)(2,1)}, u32[]{:S(2)}, u32[]{:S(2)}) collective-permute-start(bf16[4096,256]{1,0:T(8,128)(2,1)} %broadcast_select_fusion), channel_id=1, source_target_pairs={{0,32},{32,0},{96,192},{192,96},{128,160},{160,128},{224,320},{320... | collective-permute-start | bytes 6291464 | tf_op jit(solution)/shard_map/ppermute | solution.py:44
  13.1 0.0 copy-done.3
  13.2 0.0 copy-done.4
  13.3 25.2 %all_to_all.15 = bf16[8,8,4096]{2,1,0:T(8,128)(2,1)S(1)} all-to-all(bf16[8,8,4096]{2,1,0:T(8,128)(2,1)S(1)} %broadcast_in_dim.2), channel_id=1, replica_groups=mesh['zh'=4,'c'=2,'zl'=2,'y'=8,'x'=4] {'y'}, dimensions={0} | all-to-all | bytes 1048576 | tf_op jit(solution)/shard_map/all_to_all | solution.py:253
  38.4 1.9 %collective-permute-start = (bf16[64,4096]{1,0:T(8,128)(2,1)S(1)}, bf16[64,4096]{1,0:T(8,128)(2,1)S(1)}, u32[]{:S(2)}, u32[]{:S(2)}) collective-permute-start(bf16[64,4096]{1,0:T(8,128)(2,1)S(1)} %bitcast.9), channel_id=1, source_target_pairs={{0,1},{1,2},{2,3},{3,0},{4,5},{5,6},{6,7},{7,4},{8,9},{9,10},{10,1... | collective-permute-start | bytes 1572872 | tf_op jit(solution)/shard_map/ppermute | solution.py:35
  40.4 5.1 %collective-permute-start.2 = (bf16[64,4096]{1,0:T(8,128)(2,1)S(1)}, bf16[64,4096]{1,0:T(8,128)(2,1)S(1)}, u32[]{:S(2)}, u32[]{:S(2)}) collective-permute-start(bf16[64,4096]{1,0:T(8,128)(2,1)S(1)} %bitcast.10), channel_id=1, source_target_pairs={{0,3},{1,0},{2,1},{3,2},{4,7},{5,4},{6,5},{7,6},{8,11},{9,8},{10,9... | collective-permute-start | bytes 1572872 | tf_op jit(solution)/shard_map/ppermute | solution.py:35
  45.5 10.0 %collective-permute-done.r1 = bf16[64,4096]{1,0:T(8,128)(2,1)S(1)} collective-permute-done((bf16[64,4096]{1,0:T(8,128)(2,1)S(1)}, bf16[64,4096]{1,0:T(8,128)(2,1)S(1)}, u32[]{:S(2)}, u32[]{:S(2)}) %collective-permute-start) | collective-permute-done | bytes 524320 | tf_op jit(solution)/shard_map/ppermute | solution.py:35
  55.5 1.9 %collective-permute-start.1 = (bf16[32,4096]{1,0:T(8,128)(2,1)S(1)}, bf16[32,4096]{1,0:T(8,128)(2,1)S(1)}, u32[]{:S(2)}, u32[]{:S(2)}) collective-permute-start(bf16[32,4096]{1,0:T(8,128)(2,1)S(1)} %slice.20), channel_id=1, source_target_pairs={{0,1},{1,2},{2,3},{3,0},{4,5},{5,6},{6,7},{7,4},{8,9},{9,10},{10,1... | collective-permute-start | bytes 786440 | tf_op jit(solution)/shard_map/ppermute | solution.py:35
  57.4 0.0 collective-permute-done.2.r3
  57.5 5.1 %collective-permute-start.3 = (bf16[32,4096]{1,0:T(8,128)(2,1)S(1)}, bf16[32,4096]{1,0:T(8,128)(2,1)S(1)}, u32[]{:S(2)}, u32[]{:S(2)}) collective-permute-start(bf16[32,4096]{1,0:T(8,128)(2,1)S(1)} %slice.21), channel_id=1, source_target_pairs={{0,3},{1,0},{2,1},{3,2},{4,7},{5,4},{6,5},{7,6},{8,11},{9,8},{10,9... | collective-permute-start | bytes 786440 | tf_op jit(solution)/shard_map/ppermute | solution.py:35
  62.6 0.1 pad_add_fusion.where
  62.7 3.4 %collective-permute-done.1.r2a = bf16[32,4096]{1,0:T(8,128)(2,1)S(1)} collective-permute-done((bf16[32,4096]{1,0:T(8,128)(2,1)S(1)}, bf16[32,4096]{1,0:T(8,128)(2,1)S(1)}, u32[]{:S(2)}, u32[]{:S(2)}) %collective-permute-start.1) | collective-permute-done | bytes 262176 | tf_op jit(solution)/shard_map/ppermute | solution.py:35
  66.1 1.2 collective-permute-done.3.r2b
  67.3 0.0 copy-done.2
  67.3 3.2 %split.1 = (bf16[128,4096]{1,0:T(8,128)(2,1)}, bf16[4,2,128,512]{3,2,1,0:T(8,128)(2,1)}) custom-call(s32[3]{0:T(128)S(1)} %pad_add_fusion.where, bf16[64,64]{1,0:T(8,128)(2,1)S(1)} %copy-done.2, bf16[64,4096]{1,0:T(8,128)(2,1)S(1)} %bitcast.11, bf16[64,4096]{1,0:T(8,128)(2,1)S(1)} %collective-permute-done.r1, ...), custom_call_target="tpu_custom_call" | custom-call | tf_op jit(solution)/shard_map/split/pallas_call | solution.py:60
  70.5 0.0 collective-permute-done.4.mw.refs_4_.refs_5_
  70.5 0.0 all-gather.5.cloned.1.call-done
  70.5 1.9 %collective-permute-start.6 = (bf16[4096,256]{1,0:T(8,128)(2,1)}, bf16[4096,256]{1,0:T(8,128)(2,1)S(1)}, u32[]{:S(2)}, u32[]{:S(2)}) collective-permute-start(bf16[4096,256]{1,0:T(8,128)(2,1)} %collective-permute-done.4.mw.refs_4_.refs_5_), channel_id=1, source_target_pairs={{0,64},{64,0},{1,65},{65,1},{2,66},{66,2},{3,67},{67,3},{4,68},{68... | collective-permute-start | bytes 6291464 | tf_op jit(solution)/shard_map/ppermute | solution.py:30
  72.4 2.4 %collective-permute-start.5 = (bf16[4,512,512]{2,1,0:T(8,128)(2,1)}, bf16[4,512,512]{2,1,0:T(8,128)(2,1)}, u32[]{:S(2)}, u32[]{:S(2)}) collective-permute-start(bf16[4,512,512]{2,1,0:T(8,128)(2,1)} %bitcast.14), channel_id=1, source_target_pairs={{0,64},{64,0},{1,65},{65,1},{2,66},{66,2},{3,67},{67,3},{4,68},{68... | collective-permute-start | bytes 6291464 | tf_op jit(solution)/shard_map/ppermute | solution.py:30
  74.8 6.5 %all-to-all-start.2 = ((bf16[4,2,128,512]{3,2,1,0:T(8,128)(2,1)}), bf16[4,2,128,512]{3,2,1,0:T(8,128)(2,1)S(1)}, u32[]{:S(2)}, u32[]{:S(2)}) async-start(bf16[4,2,128,512]{3,2,1,0:T(8,128)(2,1)} %get-tuple-element.18.cot), calls=%async_computation.2 | async-start | bytes 2097152 | tf_op jit(solution)/shard_map/all_to_all | solution.py:271
  81.4 0.0 all-gather.7.cloned.1.call-start
  81.4 0.0 collective-permute-done.6.ow.refs_6_.refs_7_
  81.4 5.4 %gates.1 = (bf16[128,512]{1,0:T(8,128)(2,1)}, f32[128,1024]{1,0:T(8,128)}) custom-call(s32[3]{0:T(128)S(1)} %pad_add_fusion.where, bf16[128,4096]{1,0:T(8,128)(2,1)} %get-tuple-element.22.tok, bf16[4096,256]{1,0:T(8,128)(2,1)} %refs_1_.1, bf16[4096,256]{1,0:T(8,128)(2,1)} %refs_3_.1, bf16[4096,256]{1,0:T(8,128)(2,1)} %collective-permute-done.4.mw.refs_4_.refs_5_, ...), custom_call_target="tpu_custom_call" | custom-call | tf_op jit(solution)/shard_map/gates/pallas_call | solution.py:124
  86.8 0.0 all-gather.7.cloned.1.call-update
  86.8 0.0 collective-permute-done.5.df
  86.8 0.0 copy-start.1
  86.8 4.4 %down.1.dd = bf16[128,1024]{1,0:T(8,128)(2,1)S(1)} custom-call(s32[3]{0:T(128)S(1)} %pad_add_fusion.where, bf16[4,2,128,512]{3,2,1,0:T(8,128)(2,1)} %get-tuple-element.18.cot, bf16[4,512,512]{2,1,0:T(8,128)(2,1)} %bitcast.15, bf16[4,512,512]{2,1,0:T(8,128)(2,1)} %collective-permute-done.5.df, f32[128,1024]{1,0:T(8,128)} %get-tuple-element.24.fac), custom_call_target="tpu_custom_call" | custom-call | tf_op jit(solution)/shard_map/down/pallas_call | solution.py:167
  91.2 0.0 copy-done.1
  91.2 6.6 %term.1 = bf16[4,64,2048]{2,1,0:T(8,128)(2,1)} custom-call(s32[3]{0:T(128)S(1)} %pad_add_fusion.where, bf16[256,256]{1,0:T(8,128)(2,1)S(1)} %copy-done.1, bf16[128,1024]{1,0:T(8,128)(2,1)S(1)} %down.1.dd, bf16[4096,256]{1,0:T(8,128)(2,1)} %refs_1_.1, bf16[4096,256]{1,0:T(8,128)(2,1)} %refs_1_.1, bf16[4096,256]{1,0:T(8,128)(2,1)} %refs_3_.1, ...), custom_call_target="tpu_custom_call" | custom-call | tf_op jit(solution)/shard_map/term/pallas_call | solution.py:200
  97.8 7.2 %all-to-all-done.2.cn = bf16[4,2,128,512]{3,2,1,0:T(8,128)(2,1)S(1)} async-done(((bf16[4,2,128,512]{3,2,1,0:T(8,128)(2,1)}), bf16[4,2,128,512]{3,2,1,0:T(8,128)(2,1)S(1)}, u32[]{:S(2)}, u32[]{:S(2)}) %all-to-all-start.2) | async-done | bytes 1048608 | tf_op jit(solution)/shard_map/all_to_all | solution.py:271
  105.0 9.6 %all-to-all-start.1 = ((bf16[32,8,2048]{2,1,0:T(8,128)(2,1)}), bf16[32,8,2048]{2,1,0:T(8,128)(2,1)S(1)}, u32[]{:S(2)}, u32[]{:S(2)}) async-start(bf16[32,8,2048]{2,1,0:T(8,128)(2,1)} %bitcast.13), calls=%async_computation.1 | async-start | bytes 2097152 | tf_op jit(solution)/shard_map/all_to_all | solution.py:279
  114.6 5.3 %all-gather.7.cloned.1.call-done = bf16[1024,512]{1,0:T(8,128)(2,1)} async-done(((bf16[128,512]{1,0:T(8,128)(2,1)}), bf16[1024,512]{1,0:T(8,128)(2,1)}) %all-gather.7.cloned.1.call-update) | async-done | bytes 1048592 | tf_op jit(solution)/shard_map/all_gather | solution.py:275
  120.0 2.1 %collective-permute-start.7 = (bf16[4,128,512]{2,1,0:T(8,128)(2,1)S(1)}, bf16[4,128,512]{2,1,0:T(8,128)(2,1)S(1)}, u32[]{:S(2)}, u32[]{:S(2)}) collective-permute-start(bf16[4,128,512]{2,1,0:T(8,128)(2,1)S(1)} %slice_bitcast_fusion), channel_id=1, source_target_pairs={{0,64},{64,0},{1,65},{65,1},{2,66},{66,2},{3,67},{67,3},{4,68},{68... | collective-permute-start | bytes 1572872 | tf_op jit(solution)/shard_map/ppermute | solution.py:30
  122.1 1.7 %collective-permute-done.7.cf = bf16[4,128,512]{2,1,0:T(8,128)(2,1)S(1)} collective-permute-done((bf16[4,128,512]{2,1,0:T(8,128)(2,1)S(1)}, bf16[4,128,512]{2,1,0:T(8,128)(2,1)S(1)}, u32[]{:S(2)}, u32[]{:S(2)}) %collective-permute-start.7) | collective-permute-done | bytes 524320 | tf_op jit(solution)/shard_map/ppermute | solution.py:30
  123.8 0.0 copy-start
  123.8 1.2 copy-done
  125.0 1.8 %grads.1 = (f32[256,512]{1,0:T(8,128)S(1)}, bf16[256,512]{1,0:T(8,128)(2,1)S(1)}) custom-call(s32[3]{0:T(128)S(1)} %pad_add_fusion.where, bf16[4,2,128,512]{3,2,1,0:T(8,128)(2,1)S(1)} %bitcast.12, bf16[4,2,128,512]{3,2,1,0:T(8,128)(2,1)S(1)} %all-to-all-done.2.cn, bf16[4,128,512]{2,1,0:T(8,128)(2,1)S(1)} %collective-permute-done.7.cf), custom_call_target="tpu_custom_call" | custom-call | tf_op jit(solution)/shard_map/grads/pallas_call | solution.py:229
  126.8 2.6 %collective-permute-start.8 = (bf16[256,512]{1,0:T(8,128)(2,1)S(1)}, bf16[256,512]{1,0:T(8,128)(2,1)S(1)}, u32[]{:S(2)}, u32[]{:S(2)}) collective-permute-start(bf16[256,512]{1,0:T(8,128)(2,1)S(1)} %get-tuple-element.28), channel_id=1, source_target_pairs={{0,32},{32,0},{1,33},{33,1},{2,34},{34,2},{3,35},{35,3},{4,36},{36... | collective-permute-start | bytes 786440 | tf_op jit(solution)/shard_map/ppermute | solution.py:30
  129.4 13.8 %all-to-all-done.1 = bf16[32,8,2048]{2,1,0:T(8,128)(2,1)S(1)} async-done(((bf16[32,8,2048]{2,1,0:T(8,128)(2,1)}), bf16[32,8,2048]{2,1,0:T(8,128)(2,1)S(1)}, u32[]{:S(2)}, u32[]{:S(2)}) %all-to-all-start.1) | async-done | bytes 1048608 | tf_op jit(solution)/shard_map/all_to_all | solution.py:279
  143.3 0.0 collective-permute-done.8
  143.3 0.2 reduce_sum.12
  143.5 0.6 pad_maximum_fusion.1
  144.1 0.9 convert_add_fusion
  (6 shorter events, 0.2 us)
Async XLA Ops:
  7.2 63.4 %all-gather.5.cloned.1.call-start = ((), (), s32[]{:S(2)}) async-start(), calls=%async_computation.3 | async-start | bytes 2359296 | tf_op jit(solution)/shard_map/all_gather | solution.py:263
  7.9 5.2 %copy-start.3 = (bf16[4,4096]{1,0:T(4,128)(2,1)S(1)}, bf16[4,4096]{1,0:T(4,128)(2,1)}, u32[]{:S(2)}) copy-start(bf16[4,4096]{1,0:T(4,128)(2,1)} %param.8) | copy-start | bytes 98308
  7.9 5.2 %copy-start.4 = (bf16[4,4096]{1,0:T(4,128)(2,1)S(1)}, bf16[4,4096]{1,0:T(4,128)(2,1)}, u32[]{:S(2)}) copy-start(bf16[4,4096]{1,0:T(4,128)(2,1)} %param.7) | copy-start | bytes 98308
  11.1 56.2 %copy-start.2 = (bf16[64,64]{1,0:T(8,128)(2,1)S(1)}, bf16[64,64]{1,0:T(8,128)(2,1)}, u32[]{:S(2)}) copy-start(bf16[64,64]{1,0:T(8,128)(2,1)} %constant.23.clone.pick) | copy-start | bytes 24580
  11.1 59.4 %collective-permute-start.4 = (bf16[4096,256]{1,0:T(8,128)(2,1)}, bf16[4096,256]{1,0:T(8,128)(2,1)}, u32[]{:S(2)}, u32[]{:S(2)}) collective-permute-start(bf16[4096,256]{1,0:T(8,128)(2,1)} %broadcast_select_fusion), channel_id=1, source_target_pairs={{0,32},{32,0},{96,192},{192,96},{128,160},{160,128},{224,320},{320... | collective-permute-start | bytes 6291464 | tf_op jit(solution)/shard_map/ppermute | solution.py:44
  38.4 17.0 %collective-permute-start = (bf16[64,4096]{1,0:T(8,128)(2,1)S(1)}, bf16[64,4096]{1,0:T(8,128)(2,1)S(1)}, u32[]{:S(2)}, u32[]{:S(2)}) collective-permute-start(bf16[64,4096]{1,0:T(8,128)(2,1)S(1)} %bitcast.9), channel_id=1, source_target_pairs={{0,1},{1,2},{2,3},{3,0},{4,5},{5,6},{6,7},{7,4},{8,9},{9,10},{10,1... | collective-permute-start | bytes 1572872 | tf_op jit(solution)/shard_map/ppermute | solution.py:35
  40.4 17.1 %collective-permute-start.2 = (bf16[64,4096]{1,0:T(8,128)(2,1)S(1)}, bf16[64,4096]{1,0:T(8,128)(2,1)S(1)}, u32[]{:S(2)}, u32[]{:S(2)}) collective-permute-start(bf16[64,4096]{1,0:T(8,128)(2,1)S(1)} %bitcast.10), channel_id=1, source_target_pairs={{0,3},{1,0},{2,1},{3,2},{4,7},{5,4},{6,5},{7,6},{8,11},{9,8},{10,9... | collective-permute-start | bytes 1572872 | tf_op jit(solution)/shard_map/ppermute | solution.py:35
  55.5 10.6 %collective-permute-start.1 = (bf16[32,4096]{1,0:T(8,128)(2,1)S(1)}, bf16[32,4096]{1,0:T(8,128)(2,1)S(1)}, u32[]{:S(2)}, u32[]{:S(2)}) collective-permute-start(bf16[32,4096]{1,0:T(8,128)(2,1)S(1)} %slice.20), channel_id=1, source_target_pairs={{0,1},{1,2},{2,3},{3,0},{4,5},{5,6},{6,7},{7,4},{8,9},{9,10},{10,1... | collective-permute-start | bytes 786440 | tf_op jit(solution)/shard_map/ppermute | solution.py:35
  57.5 9.8 %collective-permute-start.3 = (bf16[32,4096]{1,0:T(8,128)(2,1)S(1)}, bf16[32,4096]{1,0:T(8,128)(2,1)S(1)}, u32[]{:S(2)}, u32[]{:S(2)}) collective-permute-start(bf16[32,4096]{1,0:T(8,128)(2,1)S(1)} %slice.21), channel_id=1, source_target_pairs={{0,3},{1,0},{2,1},{3,2},{4,7},{5,4},{6,5},{7,6},{8,11},{9,8},{10,9... | collective-permute-start | bytes 786440 | tf_op jit(solution)/shard_map/ppermute | solution.py:35
  70.5 10.9 %collective-permute-start.6 = (bf16[4096,256]{1,0:T(8,128)(2,1)}, bf16[4096,256]{1,0:T(8,128)(2,1)S(1)}, u32[]{:S(2)}, u32[]{:S(2)}) collective-permute-start(bf16[4096,256]{1,0:T(8,128)(2,1)} %collective-permute-done.4.mw.refs_4_.refs_5_), channel_id=1, source_target_pairs={{0,64},{64,0},{1,65},{65,1},{2,66},{66,2},{3,67},{67,3},{4,68},{68... | collective-permute-start | bytes 6291464 | tf_op jit(solution)/shard_map/ppermute | solution.py:30
  72.4 14.4 %collective-permute-start.5 = (bf16[4,512,512]{2,1,0:T(8,128)(2,1)}, bf16[4,512,512]{2,1,0:T(8,128)(2,1)}, u32[]{:S(2)}, u32[]{:S(2)}) collective-permute-start(bf16[4,512,512]{2,1,0:T(8,128)(2,1)} %bitcast.14), channel_id=1, source_target_pairs={{0,64},{64,0},{1,65},{65,1},{2,66},{66,2},{3,67},{67,3},{4,68},{68... | collective-permute-start | bytes 6291464 | tf_op jit(solution)/shard_map/ppermute | solution.py:30
  74.8 30.2 %all-to-all-start.2 = ((bf16[4,2,128,512]{3,2,1,0:T(8,128)(2,1)}), bf16[4,2,128,512]{3,2,1,0:T(8,128)(2,1)S(1)}, u32[]{:S(2)}, u32[]{:S(2)}) async-start(bf16[4,2,128,512]{3,2,1,0:T(8,128)(2,1)} %get-tuple-element.18.cot), calls=%async_computation.2 | async-start | bytes 2097152 | tf_op jit(solution)/shard_map/all_to_all | solution.py:271
  81.4 38.5 %all-gather.7.cloned.1.call-start = ((), (), s32[]{:S(2)}) async-start(), calls=%async_computation.4 | async-start | bytes 1179648 | tf_op jit(solution)/shard_map/all_gather | solution.py:275
  86.8 4.4 %copy-start.1 = (bf16[256,256]{1,0:T(8,128)(2,1)S(1)}, bf16[256,256]{1,0:T(8,128)(2,1)}, u32[]{:S(2)}) copy-start(bf16[256,256]{1,0:T(8,128)(2,1)} %constant.24.clone.pick) | copy-start | bytes 393220
  105.0 38.3 %all-to-all-start.1 = ((bf16[32,8,2048]{2,1,0:T(8,128)(2,1)}), bf16[32,8,2048]{2,1,0:T(8,128)(2,1)S(1)}, u32[]{:S(2)}, u32[]{:S(2)}) async-start(bf16[32,8,2048]{2,1,0:T(8,128)(2,1)} %bitcast.13), calls=%async_computation.1 | async-start | bytes 2097152 | tf_op jit(solution)/shard_map/all_to_all | solution.py:279
  120.0 3.8 %collective-permute-start.7 = (bf16[4,128,512]{2,1,0:T(8,128)(2,1)S(1)}, bf16[4,128,512]{2,1,0:T(8,128)(2,1)S(1)}, u32[]{:S(2)}, u32[]{:S(2)}) collective-permute-start(bf16[4,128,512]{2,1,0:T(8,128)(2,1)S(1)} %slice_bitcast_fusion), channel_id=1, source_target_pairs={{0,64},{64,0},{1,65},{65,1},{2,66},{66,2},{3,67},{67,3},{4,68},{68... | collective-permute-start | bytes 1572872 | tf_op jit(solution)/shard_map/ppermute | solution.py:30
  123.8 1.2 copy-start
  126.8 16.5 %collective-permute-start.8 = (bf16[256,512]{1,0:T(8,128)(2,1)S(1)}, bf16[256,512]{1,0:T(8,128)(2,1)S(1)}, u32[]{:S(2)}, u32[]{:S(2)}) collective-permute-start(bf16[256,512]{1,0:T(8,128)(2,1)S(1)} %get-tuple-element.28), channel_id=1, source_target_pairs={{0,32},{32,0},{1,33},{33,1},{2,34},{34,2},{3,35},{35,3},{4,36},{36... | collective-permute-start | bytes 786440 | tf_op jit(solution)/shard_map/ppermute | solution.py:30
Sparse Core Ops, SparseCore 0:
  10.1 51.3 all-gather.4
  86.9 32.9 all-gather.6

commit v18 on v17

--- a/solution.py
+++ b/solution.py
@@ -50,22 +50,22 @@
     for i, piece in enumerate((r0[...], r1[...], r2, r3[...])):
         rows = contract(pick[...], piece, 1, 0).astype(BF16)
         tok[i * n : (i + 1) * n] = rows[:n]
-        for k in range(2):
-            cot[0, flip(k, where[0]), i * n : (i + 1) * n] = rows[n:, k * FEATS : (k + 1) * FEATS]
+        for k in range(4):
+            cot[k // 2, flip(k % 2, where[0]), i * n : (i + 1) * n] = rows[n:, k * FEATS : (k + 1) * FEATS]
 
 
 def split(where, pieces):
-    piece = pl.BlockSpec((PIECE, 2 * FEATS), lambda j, s: (0, j))
-    part = pl.BlockSpec((PIECE // 2, 2 * FEATS), lambda j, s: (0, j))
+    piece = pl.BlockSpec((PIECE, 4 * FEATS), lambda j, s: (0, j))
+    part = pl.BlockSpec((PIECE // 2, 4 * FEATS), lambda j, s: (0, j))
     return pl.pallas_call(
         split_body,
         grid_spec=pltpu.PrefetchScalarGridSpec(
             num_scalar_prefetch=1,
-            grid=(NZ,),
+            grid=(NZ // 2,),
             in_specs=[pl.BlockSpec((PIECE, PIECE), lambda j, s: (0, 0)), piece, piece, part, part, piece],
             out_specs=[
-                pl.BlockSpec((HALF, 2 * FEATS), lambda j, s: (0, j)),
-                pl.BlockSpec((1, 2, HALF, FEATS), lambda j, s: (j, 0, 0, 0)),
+                pl.BlockSpec((HALF, 4 * FEATS), lambda j, s: (0, j)),
+                pl.BlockSpec((2, 2, HALF, FEATS), lambda j, s: (j, 0, 0, 0)),
             ],
         ),
         out_shape=[

time: 152 us -> 152 us (level)
  no operation moved by 1% of the time
where the time goes in v18:
time: 152 us; the launch traced here: 151 us
  waiting for transfers between devices  43.3 us (28%)
  starting transfers between devices  41.3 us (27%)
  blocking collectives  25.2 us (17%)
  Pallas kernels  20.7 us (14%)
  between operations  14.2 us (9%)
  other arithmetic  4.94 us (3%)
    all_to_all x1, blocking collectives, spread(): lax.all_to_all(jnp.broadcast_to(block[None], (n, *block.shape)), axis, 0, 0)  25.2 us
    ppermute x4, waiting for transfers between devices, shift(): return lax.ppermute(value, axis, [(i, (i + k) % n) for i in range(n)])  14.6 us
    ppermute x4, starting transfers between devices, shift(): return lax.ppermute(value, axis, [(i, (i + k) % n) for i in range(n)])  14.1 us
    all_to_all x1, waiting for transfers between devices, on_device(): lax.all_to_all(parts.reshape(NX * NY, 2 * ROWS, D // 2), ('x', 'y'), 0, 0)  13.8 us
    all_to_all x1, starting transfers between devices, on_device(): lax.all_to_all(parts.reshape(NX * NY, 2 * ROWS, D // 2), ('x', 'y'), 0, 0)  9.54 us
    ppermute x4, starting transfers between devices, swap(): return lax.ppermute(value, axis, [(0, 1), (1, 0)])  9.07 us
    all_to_all x1, waiting for transfers between devices, on_device(): cot_near = lax.all_to_all(cot, 'zh', 0, 0)  7.18 us
    pallas_call x1, Pallas kernels, term(): pl.pallas_call(term_body, grid_spec=pltpu.PrefetchScalarGridSpec(num_scal...  6.59 us
  transfers between devices with their start and end apart: 13, of which 7 were waited for; matrix products, arithmetic and copies ran while one was open for 2% of the time, Pallas kernels for 14%

profile of v18, /device:TPU:72, one launch (start us, length us, event | category | flops | bytes accessed | tf_op | source)
XLA Modules:
  0.0 151.1 jit_solution(7845215644947484642)
XLA Ops:
  7.2 0.0 all-gather.5.cloned.1.call-start
  7.2 0.7 all-gather.5.cloned.1.call-update
  7.9 0.0 copy-start.3
  7.9 0.0 copy-start.4
  7.9 3.2 %broadcast_select_fusion = bf16[4096,256]{1,0:T(8,128)(2,1)} fusion(bf16[4096,256]{1,0:T(8,128)(2,1)} %refs_1_.1, bf16[4096,256]{1,0:T(8,128)(2,1)} %refs_3_.1, pred[]{:T(512)S(6)} %eq.3), kind=kLoop, calls=%fused_computation | loop fusion | flops 1048576 | bytes 6291457 | tf_op jit(solution)/shard_map/jit(_where)/select_n | solution.py:260
  11.1 0.0 copy-start.2
  11.1 2.0 %collective-permute-start.4 = (bf16[4096,256]{1,0:T(8,128)(2,1)}, bf16[4096,256]{1,0:T(8,128)(2,1)}, u32[]{:S(2)}, u32[]{:S(2)}) collective-permute-start(bf16[4096,256]{1,0:T(8,128)(2,1)} %broadcast_select_fusion), channel_id=1, source_target_pairs={{0,32},{32,0},{96,192},{192,96},{128,160},{160,128},{224,320},{320... | collective-permute-start | bytes 6291464 | tf_op jit(solution)/shard_map/ppermute | solution.py:44
  13.1 0.0 copy-done.3
  13.2 0.0 copy-done.4
  13.3 25.2 %all_to_all.15 = bf16[8,8,4096]{2,1,0:T(8,128)(2,1)S(1)} all-to-all(bf16[8,8,4096]{2,1,0:T(8,128)(2,1)S(1)} %broadcast_in_dim.2), channel_id=1, replica_groups=mesh['zh'=4,'c'=2,'zl'=2,'y'=8,'x'=4] {'y'}, dimensions={0} | all-to-all | bytes 1048576 | tf_op jit(solution)/shard_map/all_to_all | solution.py:253
  38.4 1.9 %collective-permute-start = (bf16[64,4096]{1,0:T(8,128)(2,1)S(1)}, bf16[64,4096]{1,0:T(8,128)(2,1)S(1)}, u32[]{:S(2)}, u32[]{:S(2)}) collective-permute-start(bf16[64,4096]{1,0:T(8,128)(2,1)S(1)} %bitcast.9), channel_id=1, source_target_pairs={{0,1},{1,2},{2,3},{3,0},{4,5},{5,6},{6,7},{7,4},{8,9},{9,10},{10,1... | collective-permute-start | bytes 1572872 | tf_op jit(solution)/shard_map/ppermute | solution.py:35
  40.4 5.1 %collective-permute-start.2 = (bf16[64,4096]{1,0:T(8,128)(2,1)S(1)}, bf16[64,4096]{1,0:T(8,128)(2,1)S(1)}, u32[]{:S(2)}, u32[]{:S(2)}) collective-permute-start(bf16[64,4096]{1,0:T(8,128)(2,1)S(1)} %bitcast.10), channel_id=1, source_target_pairs={{0,3},{1,0},{2,1},{3,2},{4,7},{5,4},{6,5},{7,6},{8,11},{9,8},{10,9... | collective-permute-start | bytes 1572872 | tf_op jit(solution)/shard_map/ppermute | solution.py:35
  45.5 10.0 %collective-permute-done.r1 = bf16[64,4096]{1,0:T(8,128)(2,1)S(1)} collective-permute-done((bf16[64,4096]{1,0:T(8,128)(2,1)S(1)}, bf16[64,4096]{1,0:T(8,128)(2,1)S(1)}, u32[]{:S(2)}, u32[]{:S(2)}) %collective-permute-start) | collective-permute-done | bytes 524320 | tf_op jit(solution)/shard_map/ppermute | solution.py:35
  55.5 1.9 %collective-permute-start.1 = (bf16[32,4096]{1,0:T(8,128)(2,1)S(1)}, bf16[32,4096]{1,0:T(8,128)(2,1)S(1)}, u32[]{:S(2)}, u32[]{:S(2)}) collective-permute-start(bf16[32,4096]{1,0:T(8,128)(2,1)S(1)} %slice.20), channel_id=1, source_target_pairs={{0,1},{1,2},{2,3},{3,0},{4,5},{5,6},{6,7},{7,4},{8,9},{9,10},{10,1... | collective-permute-start | bytes 786440 | tf_op jit(solution)/shard_map/ppermute | solution.py:35
  57.4 0.0 collective-permute-done.2.r3
  57.5 5.1 %collective-permute-start.3 = (bf16[32,4096]{1,0:T(8,128)(2,1)S(1)}, bf16[32,4096]{1,0:T(8,128)(2,1)S(1)}, u32[]{:S(2)}, u32[]{:S(2)}) collective-permute-start(bf16[32,4096]{1,0:T(8,128)(2,1)S(1)} %slice.21), channel_id=1, source_target_pairs={{0,3},{1,0},{2,1},{3,2},{4,7},{5,4},{6,5},{7,6},{8,11},{9,8},{10,9... | collective-permute-start | bytes 786440 | tf_op jit(solution)/shard_map/ppermute | solution.py:35
  62.6 0.1 pad_add_fusion.where
  62.7 3.4 %collective-permute-done.1.r2a = bf16[32,4096]{1,0:T(8,128)(2,1)S(1)} collective-permute-done((bf16[32,4096]{1,0:T(8,128)(2,1)S(1)}, bf16[32,4096]{1,0:T(8,128)(2,1)S(1)}, u32[]{:S(2)}, u32[]{:S(2)}) %collective-permute-start.1) | collective-permute-done | bytes 262176 | tf_op jit(solution)/shard_map/ppermute | solution.py:35
  66.1 1.2 collective-permute-done.3.r2b
  67.3 0.0 copy-done.2
  67.3 2.5 %split.1 = (bf16[128,4096]{1,0:T(8,128)(2,1)}, bf16[4,2,128,512]{3,2,1,0:T(8,128)(2,1)}) custom-call(s32[3]{0:T(128)S(1)} %pad_add_fusion.where, bf16[64,64]{1,0:T(8,128)(2,1)S(1)} %copy-done.2, bf16[64,4096]{1,0:T(8,128)(2,1)S(1)} %bitcast.11, bf16[64,4096]{1,0:T(8,128)(2,1)S(1)} %collective-permute-done.r1, ...), custom_call_target="tpu_custom_call" | custom-call | tf_op jit(solution)/shard_map/split/pallas_call | solution.py:60
  69.9 0.0 collective-permute-done.4.mw.refs_4_.refs_5_
  69.9 0.0 all-gather.5.cloned.1.call-done
  69.9 1.9 %collective-permute-start.6 = (bf16[4096,256]{1,0:T(8,128)(2,1)}, bf16[4096,256]{1,0:T(8,128)(2,1)S(1)}, u32[]{:S(2)}, u32[]{:S(2)}) collective-permute-start(bf16[4096,256]{1,0:T(8,128)(2,1)} %collective-permute-done.4.mw.refs_4_.refs_5_), channel_id=1, source_target_pairs={{0,64},{64,0},{1,65},{65,1},{2,66},{66,2},{3,67},{67,3},{4,68},{68... | collective-permute-start | bytes 6291464 | tf_op jit(solution)/shard_map/ppermute | solution.py:30
  71.8 2.4 %collective-permute-start.5 = (bf16[4,512,512]{2,1,0:T(8,128)(2,1)}, bf16[4,512,512]{2,1,0:T(8,128)(2,1)}, u32[]{:S(2)}, u32[]{:S(2)}) collective-permute-start(bf16[4,512,512]{2,1,0:T(8,128)(2,1)} %bitcast.14), channel_id=1, source_target_pairs={{0,64},{64,0},{1,65},{65,1},{2,66},{66,2},{3,67},{67,3},{4,68},{68... | collective-permute-start | bytes 6291464 | tf_op jit(solution)/shard_map/ppermute | solution.py:30
  74.2 6.5 %all-to-all-start.2 = ((bf16[4,2,128,512]{3,2,1,0:T(8,128)(2,1)}), bf16[4,2,128,512]{3,2,1,0:T(8,128)(2,1)S(1)}, u32[]{:S(2)}, u32[]{:S(2)}) async-start(bf16[4,2,128,512]{3,2,1,0:T(8,128)(2,1)} %get-tuple-element.18.cot), calls=%async_computation.2 | async-start | bytes 2097152 | tf_op jit(solution)/shard_map/all_to_all | solution.py:271
  80.7 0.0 all-gather.7.cloned.1.call-start
  80.7 0.0 collective-permute-done.6.ow.refs_6_.refs_7_
  80.8 5.4 %gates.1 = (bf16[128,512]{1,0:T(8,128)(2,1)}, f32[128,1024]{1,0:T(8,128)}) custom-call(s32[3]{0:T(128)S(1)} %pad_add_fusion.where, bf16[128,4096]{1,0:T(8,128)(2,1)} %get-tuple-element.22.tok, bf16[4096,256]{1,0:T(8,128)(2,1)} %refs_1_.1, bf16[4096,256]{1,0:T(8,128)(2,1)} %refs_3_.1, bf16[4096,256]{1,0:T(8,128)(2,1)} %collective-permute-done.4.mw.refs_4_.refs_5_, ...), custom_call_target="tpu_custom_call" | custom-call | tf_op jit(solution)/shard_map/gates/pallas_call | solution.py:124
  86.1 0.0 all-gather.7.cloned.1.call-update
  86.1 0.0 collective-permute-done.5.df
  86.1 0.0 copy-start.1
  86.2 4.4 %down.1.dd = bf16[128,1024]{1,0:T(8,128)(2,1)S(1)} custom-call(s32[3]{0:T(128)S(1)} %pad_add_fusion.where, bf16[4,2,128,512]{3,2,1,0:T(8,128)(2,1)} %get-tuple-element.18.cot, bf16[4,512,512]{2,1,0:T(8,128)(2,1)} %bitcast.15, bf16[4,512,512]{2,1,0:T(8,128)(2,1)} %collective-permute-done.5.df, f32[128,1024]{1,0:T(8,128)} %get-tuple-element.24.fac), custom_call_target="tpu_custom_call" | custom-call | tf_op jit(solution)/shard_map/down/pallas_call | solution.py:167
  90.6 0.0 copy-done.1
  90.6 6.6 %term.1 = bf16[4,64,2048]{2,1,0:T(8,128)(2,1)} custom-call(s32[3]{0:T(128)S(1)} %pad_add_fusion.where, bf16[256,256]{1,0:T(8,128)(2,1)S(1)} %copy-done.1, bf16[128,1024]{1,0:T(8,128)(2,1)S(1)} %down.1.dd, bf16[4096,256]{1,0:T(8,128)(2,1)} %refs_1_.1, bf16[4096,256]{1,0:T(8,128)(2,1)} %refs_1_.1, bf16[4096,256]{1,0:T(8,128)(2,1)} %refs_3_.1, ...), custom_call_target="tpu_custom_call" | custom-call | tf_op jit(solution)/shard_map/term/pallas_call | solution.py:200
  97.2 7.2 %all-to-all-done.2.cn = bf16[4,2,128,512]{3,2,1,0:T(8,128)(2,1)S(1)} async-done(((bf16[4,2,128,512]{3,2,1,0:T(8,128)(2,1)}), bf16[4,2,128,512]{3,2,1,0:T(8,128)(2,1)S(1)}, u32[]{:S(2)}, u32[]{:S(2)}) %all-to-all-start.2) | async-done | bytes 1048608 | tf_op jit(solution)/shard_map/all_to_all | solution.py:271
  104.4 9.5 %all-to-all-start.1 = ((bf16[32,8,2048]{2,1,0:T(8,128)(2,1)}), bf16[32,8,2048]{2,1,0:T(8,128)(2,1)S(1)}, u32[]{:S(2)}, u32[]{:S(2)}) async-start(bf16[32,8,2048]{2,1,0:T(8,128)(2,1)} %bitcast.13), calls=%async_computation.1 | async-start | bytes 2097152 | tf_op jit(solution)/shard_map/all_to_all | solution.py:279
  113.9 5.3 %all-gather.7.cloned.1.call-done = bf16[1024,512]{1,0:T(8,128)(2,1)} async-done(((bf16[128,512]{1,0:T(8,128)(2,1)}), bf16[1024,512]{1,0:T(8,128)(2,1)}) %all-gather.7.cloned.1.call-update) | async-done | bytes 1048592 | tf_op jit(solution)/shard_map/all_gather | solution.py:275
  119.3 2.1 %collective-permute-start.7 = (bf16[4,128,512]{2,1,0:T(8,128)(2,1)S(1)}, bf16[4,128,512]{2,1,0:T(8,128)(2,1)S(1)}, u32[]{:S(2)}, u32[]{:S(2)}) collective-permute-start(bf16[4,128,512]{2,1,0:T(8,128)(2,1)S(1)} %slice_bitcast_fusion), channel_id=1, source_target_pairs={{0,64},{64,0},{1,65},{65,1},{2,66},{66,2},{3,67},{67,3},{4,68},{68... | collective-permute-start | bytes 1572872 | tf_op jit(solution)/shard_map/ppermute | solution.py:30
  121.5 1.7 %collective-permute-done.7.cf = bf16[4,128,512]{2,1,0:T(8,128)(2,1)S(1)} collective-permute-done((bf16[4,128,512]{2,1,0:T(8,128)(2,1)S(1)}, bf16[4,128,512]{2,1,0:T(8,128)(2,1)S(1)}, u32[]{:S(2)}, u32[]{:S(2)}) %collective-permute-start.7) | collective-permute-done | bytes 524320 | tf_op jit(solution)/shard_map/ppermute | solution.py:30
  123.1 0.0 copy-start
  123.1 1.2 copy-done
  124.3 1.8 %grads.1 = (f32[256,512]{1,0:T(8,128)S(1)}, bf16[256,512]{1,0:T(8,128)(2,1)S(1)}) custom-call(s32[3]{0:T(128)S(1)} %pad_add_fusion.where, bf16[4,2,128,512]{3,2,1,0:T(8,128)(2,1)S(1)} %bitcast.12, bf16[4,2,128,512]{3,2,1,0:T(8,128)(2,1)S(1)} %all-to-all-done.2.cn, bf16[4,128,512]{2,1,0:T(8,128)(2,1)S(1)} %collective-permute-done.7.cf), custom_call_target="tpu_custom_call" | custom-call | tf_op jit(solution)/shard_map/grads/pallas_call | solution.py:229
  126.2 2.6 %collective-permute-start.8 = (bf16[256,512]{1,0:T(8,128)(2,1)S(1)}, bf16[256,512]{1,0:T(8,128)(2,1)S(1)}, u32[]{:S(2)}, u32[]{:S(2)}) collective-permute-start(bf16[256,512]{1,0:T(8,128)(2,1)S(1)} %get-tuple-element.28), channel_id=1, source_target_pairs={{0,32},{32,0},{1,33},{33,1},{2,34},{34,2},{3,35},{35,3},{4,36},{36... | collective-permute-start | bytes 786440 | tf_op jit(solution)/shard_map/ppermute | solution.py:30
  128.8 13.8 %all-to-all-done.1 = bf16[32,8,2048]{2,1,0:T(8,128)(2,1)S(1)} async-done(((bf16[32,8,2048]{2,1,0:T(8,128)(2,1)}), bf16[32,8,2048]{2,1,0:T(8,128)(2,1)S(1)}, u32[]{:S(2)}, u32[]{:S(2)}) %all-to-all-start.1) | async-done | bytes 1048608 | tf_op jit(solution)/shard_map/all_to_all | solution.py:279
  142.6 0.0 collective-permute-done.8
  142.6 0.2 reduce_sum.12
  142.8 0.6 pad_maximum_fusion.1
  143.4 0.9 convert_add_fusion
  (6 shorter events, 0.2 us)
Async XLA Ops:
  7.2 62.7 %all-gather.5.cloned.1.call-start = ((), (), s32[]{:S(2)}) async-start(), calls=%async_computation.3 | async-start | bytes 2359296 | tf_op jit(solution)/shard_map/all_gather | solution.py:263
  7.9 5.2 %copy-start.3 = (bf16[4,4096]{1,0:T(4,128)(2,1)S(1)}, bf16[4,4096]{1,0:T(4,128)(2,1)}, u32[]{:S(2)}) copy-start(bf16[4,4096]{1,0:T(4,128)(2,1)} %param.8) | copy-start | bytes 98308
  7.9 5.2 %copy-start.4 = (bf16[4,4096]{1,0:T(4,128)(2,1)S(1)}, bf16[4,4096]{1,0:T(4,128)(2,1)}, u32[]{:S(2)}) copy-start(bf16[4,4096]{1,0:T(4,128)(2,1)} %param.7) | copy-start | bytes 98308
  11.1 56.2 %copy-start.2 = (bf16[64,64]{1,0:T(8,128)(2,1)S(1)}, bf16[64,64]{1,0:T(8,128)(2,1)}, u32[]{:S(2)}) copy-start(bf16[64,64]{1,0:T(8,128)(2,1)} %constant.23.clone.pick) | copy-start | bytes 24580
  11.1 58.8 %collective-permute-start.4 = (bf16[4096,256]{1,0:T(8,128)(2,1)}, bf16[4096,256]{1,0:T(8,128)(2,1)}, u32[]{:S(2)}, u32[]{:S(2)}) collective-permute-start(bf16[4096,256]{1,0:T(8,128)(2,1)} %broadcast_select_fusion), channel_id=1, source_target_pairs={{0,32},{32,0},{96,192},{192,96},{128,160},{160,128},{224,320},{320... | collective-permute-start | bytes 6291464 | tf_op jit(solution)/shard_map/ppermute | solution.py:44
  38.4 17.0 %collective-permute-start = (bf16[64,4096]{1,0:T(8,128)(2,1)S(1)}, bf16[64,4096]{1,0:T(8,128)(2,1)S(1)}, u32[]{:S(2)}, u32[]{:S(2)}) collective-permute-start(bf16[64,4096]{1,0:T(8,128)(2,1)S(1)} %bitcast.9), channel_id=1, source_target_pairs={{0,1},{1,2},{2,3},{3,0},{4,5},{5,6},{6,7},{7,4},{8,9},{9,10},{10,1... | collective-permute-start | bytes 1572872 | tf_op jit(solution)/shard_map/ppermute | solution.py:35
  40.4 17.1 %collective-permute-start.2 = (bf16[64,4096]{1,0:T(8,128)(2,1)S(1)}, bf16[64,4096]{1,0:T(8,128)(2,1)S(1)}, u32[]{:S(2)}, u32[]{:S(2)}) collective-permute-start(bf16[64,4096]{1,0:T(8,128)(2,1)S(1)} %bitcast.10), channel_id=1, source_target_pairs={{0,3},{1,0},{2,1},{3,2},{4,7},{5,4},{6,5},{7,6},{8,11},{9,8},{10,9... | collective-permute-start | bytes 1572872 | tf_op jit(solution)/shard_map/ppermute | solution.py:35
  55.5 10.6 %collective-permute-start.1 = (bf16[32,4096]{1,0:T(8,128)(2,1)S(1)}, bf16[32,4096]{1,0:T(8,128)(2,1)S(1)}, u32[]{:S(2)}, u32[]{:S(2)}) collective-permute-start(bf16[32,4096]{1,0:T(8,128)(2,1)S(1)} %slice.20), channel_id=1, source_target_pairs={{0,1},{1,2},{2,3},{3,0},{4,5},{5,6},{6,7},{7,4},{8,9},{9,10},{10,1... | collective-permute-start | bytes 786440 | tf_op jit(solution)/shard_map/ppermute | solution.py:35
  57.5 9.8 %collective-permute-start.3 = (bf16[32,4096]{1,0:T(8,128)(2,1)S(1)}, bf16[32,4096]{1,0:T(8,128)(2,1)S(1)}, u32[]{:S(2)}, u32[]{:S(2)}) collective-permute-start(bf16[32,4096]{1,0:T(8,128)(2,1)S(1)} %slice.21), channel_id=1, source_target_pairs={{0,3},{1,0},{2,1},{3,2},{4,7},{5,4},{6,5},{7,6},{8,11},{9,8},{10,9... | collective-permute-start | bytes 786440 | tf_op jit(solution)/shard_map/ppermute | solution.py:35
  69.9 10.9 %collective-permute-start.6 = (bf16[4096,256]{1,0:T(8,128)(2,1)}, bf16[4096,256]{1,0:T(8,128)(2,1)S(1)}, u32[]{:S(2)}, u32[]{:S(2)}) collective-permute-start(bf16[4096,256]{1,0:T(8,128)(2,1)} %collective-permute-done.4.mw.refs_4_.refs_5_), channel_id=1, source_target_pairs={{0,64},{64,0},{1,65},{65,1},{2,66},{66,2},{3,67},{67,3},{4,68},{68... | collective-permute-start | bytes 6291464 | tf_op jit(solution)/shard_map/ppermute | solution.py:30
  71.8 14.4 %collective-permute-start.5 = (bf16[4,512,512]{2,1,0:T(8,128)(2,1)}, bf16[4,512,512]{2,1,0:T(8,128)(2,1)}, u32[]{:S(2)}, u32[]{:S(2)}) collective-permute-start(bf16[4,512,512]{2,1,0:T(8,128)(2,1)} %bitcast.14), channel_id=1, source_target_pairs={{0,64},{64,0},{1,65},{65,1},{2,66},{66,2},{3,67},{67,3},{4,68},{68... | collective-permute-start | bytes 6291464 | tf_op jit(solution)/shard_map/ppermute | solution.py:30
  74.2 30.2 %all-to-all-start.2 = ((bf16[4,2,128,512]{3,2,1,0:T(8,128)(2,1)}), bf16[4,2,128,512]{3,2,1,0:T(8,128)(2,1)S(1)}, u32[]{:S(2)}, u32[]{:S(2)}) async-start(bf16[4,2,128,512]{3,2,1,0:T(8,128)(2,1)} %get-tuple-element.18.cot), calls=%async_computation.2 | async-start | bytes 2097152 | tf_op jit(solution)/shard_map/all_to_all | solution.py:271
  80.7 38.5 %all-gather.7.cloned.1.call-start = ((), (), s32[]{:S(2)}) async-start(), calls=%async_computation.4 | async-start | bytes 1179648 | tf_op jit(solution)/shard_map/all_gather | solution.py:275
  86.1 4.5 %copy-start.1 = (bf16[256,256]{1,0:T(8,128)(2,1)S(1)}, bf16[256,256]{1,0:T(8,128)(2,1)}, u32[]{:S(2)}) copy-start(bf16[256,256]{1,0:T(8,128)(2,1)} %constant.24.clone.pick) | copy-start | bytes 393220
  104.4 38.2 %all-to-all-start.1 = ((bf16[32,8,2048]{2,1,0:T(8,128)(2,1)}), bf16[32,8,2048]{2,1,0:T(8,128)(2,1)S(1)}, u32[]{:S(2)}, u32[]{:S(2)}) async-start(bf16[32,8,2048]{2,1,0:T(8,128)(2,1)} %bitcast.13), calls=%async_computation.1 | async-start | bytes 2097152 | tf_op jit(solution)/shard_map/all_to_all | solution.py:279
  119.3 3.8 %collective-permute-start.7 = (bf16[4,128,512]{2,1,0:T(8,128)(2,1)S(1)}, bf16[4,128,512]{2,1,0:T(8,128)(2,1)S(1)}, u32[]{:S(2)}, u32[]{:S(2)}) collective-permute-start(bf16[4,128,512]{2,1,0:T(8,128)(2,1)S(1)} %slice_bitcast_fusion), channel_id=1, source_target_pairs={{0,64},{64,0},{1,65},{65,1},{2,66},{66,2},{3,67},{67,3},{4,68},{68... | collective-permute-start | bytes 1572872 | tf_op jit(solution)/shard_map/ppermute | solution.py:30
  123.1 1.2 copy-start
  126.2 16.4 %collective-permute-start.8 = (bf16[256,512]{1,0:T(8,128)(2,1)S(1)}, bf16[256,512]{1,0:T(8,128)(2,1)S(1)}, u32[]{:S(2)}, u32[]{:S(2)}) collective-permute-start(bf16[256,512]{1,0:T(8,128)(2,1)S(1)} %get-tuple-element.28), channel_id=1, source_target_pairs={{0,32},{32,0},{1,33},{33,1},{2,34},{34,2},{3,35},{35,3},{4,36},{36... | collective-permute-start | bytes 786440 | tf_op jit(solution)/shard_map/ppermute | solution.py:30
Sparse Core Ops, SparseCore 0:
  10.1 51.3 all-gather.4
  86.3 32.9 all-gather.6
